TPU v7x, 32 devices: a whole 2x2x4 slice. The times are simulated.
32 devices in a mesh: section: 2 (over y), fsdp: 4 (over z), replica: 4 (over x, core).
Axes of the slice: x: 2, y: 2, z: 4, core: 2. Of those that a mesh axis runs over, the one named last changes fastest.
Arguments:
- inputs: bfloat16 [2, 4096, 2048], P(None, ('replica', 'fsdp')), may hold values from -6 to 6
- cotangent: bfloat16 [2, 4096, 2048], P(None, ('replica', 'fsdp')), may hold values from -6 to 6
- norm_gains: bfloat16 [2, 2, 2048], P('section'), may hold values from 0.099609375 to 1.8984375
- norm_biases: bfloat16 [2, 2, 2048], P('section'), may hold values from -1.5 to 1.5
- w_attn: bfloat16 [2, 2048, 2304], P('section', None, 'fsdp'), may hold values from -0.125 to 0.125
- w_out: bfloat16 [2, 2048, 2048], P('section', None, 'fsdp'), may hold values from -2 to 2
- w_up: bfloat16 [2, 2048, 8192], P('section', None, 'fsdp'), may hold values from -0.125 to 0.125
- w_down: bfloat16 [2, 8192, 2048], P('section', 'fsdp'), may hold values from -0.0625 to 0.0625
- down_attn: bfloat16 [2, 8, 16, 2048], P('section', None, None, 'fsdp'), may hold values from -0.125 to 0.125
- up_attn: bfloat16 [2, 8, 16, 2304], P('section', None, None, 'fsdp'), may hold values from -0.375 to 0.375
- down_out: bfloat16 [2, 8, 16, 2048], P('section', None, None, 'fsdp'), may hold values from -2 to 2
- up_out: bfloat16 [2, 8, 16, 2048], P('section', None, None, 'fsdp'), may hold values from -0.375 to 0.375
- down_up: bfloat16 [2, 8, 16, 2048], P('section', None, None, 'fsdp'), may hold values from -0.125 to 0.125
- up_up: bfloat16 [2, 8, 16, 8192], P('section', None, None, 'fsdp'), may hold values from -0.375 to 0.375
- down_down: bfloat16 [2, 8, 16, 8192], P('section', None, None, 'fsdp'), may hold values from -0.0625 to 0.0625
- up_down: bfloat16 [2, 8, 16, 2048], P('section', None, None, 'fsdp'), may hold values from -0.375 to 0.375
- seg_lengths: int32 [2, 4, 5], P(None, 'replica'), may hold values from 1 to 512, 1024 in all within a row
- parent_ids: int32 [2, 4, 5], P(None, 'replica'), may hold values from 0 to 3, as said below
- adapter_ids: int32 [2, 4, 1], P(None, 'replica'), may hold values from 0 to 7
Outputs:
- layer_outputs: bfloat16 [2, 2, 4096, 2048], P('section', None, ('replica', 'fsdp'))
- input_grads: bfloat16 [2, 2, 4096, 2048], P('section', None, ('replica', 'fsdp'))
- grad_down_attn: float32 [2, 8, 16, 2048], P('section', None, None, 'fsdp')
- grad_up_attn: float32 [2, 8, 16, 2304], P('section', None, None, 'fsdp')
- grad_down_out: float32 [2, 8, 16, 2048], P('section', None, None, 'fsdp')
- grad_up_out: float32 [2, 8, 16, 2048], P('section', None, None, 'fsdp')
- grad_down_up: float32 [2, 8, 16, 2048], P('section', None, None, 'fsdp')
- grad_up_up: float32 [2, 8, 16, 8192], P('section', None, None, 'fsdp')
- grad_down_down: float32 [2, 8, 16, 8192], P('section', None, None, 'fsdp')
- grad_up_down: float32 [2, 8, 16, 2048], P('section', None, None, 'fsdp')
Inputs may be any that keep to these rules, and one draw needn't show every extreme that they name: `seg_lengths`: for every micro-batch and tree the 5 lengths sum to 1024. parent_ids[m,t,0] is 0; for k > 0, parent_ids[m,t,k] is below k. `adapter_ids`: every adapter index is used by some tree.
All inputs are finite; a program needn't handle non-finite values.
Results may differ from a plain program's by a relative error of at most 0.024.
Values may be sent and summed in bfloat16 or wider, within the bound.
No kernel may reach another device: no remote copies, remote signals or barrier semaphores. Data moves between devices by JAX's collectives and lax.ppermute only.
A program may use at most 448 MiB of HBM per device.

v0:
```python
import jax
import jax.numpy as jnp
from jax import lax
from jax.sharding import PartitionSpec as P

D = 2048
HEADS = 16
HEAD_DIM = 128


HIGH = lax.Precision.HIGHEST
ADAPTER_SCALING = 2.0
NORM_EPS = 1e-05
MASKED = -1e30
SLIM = jnp.bfloat16
WIDE_FEATURES = jnp.float32


def from_behind(value, axis, steps):
    count = lax.axis_size(axis)
    initial, last = (max(0, -steps), min(count, count - steps))
    return lax.ppermute(value, axis, [(source, source + steps) for source in range(initial, last)])


def matrix_product(left_side, right_side):
    return jnp.dot(left_side, right_side, preferred_element_type=WIDE_FEATURES)


def precise_product(left_side, right_side):
    return jnp.dot(left_side, right_side, precision=HIGH, preferred_element_type=WIDE_FEATURES)


def rounded(tensor):
    return lax.optimization_barrier(tensor.astype(SLIM)).astype(WIDE_FEATURES)


def layer_norm(value_rows, gain_vec, shift_vec):
    centre = value_rows - jnp.mean(value_rows, axis=-1, keepdims=True)
    spread = jnp.mean(centre * centre, axis=-1, keepdims=True)
    return centre * lax.rsqrt(spread + NORM_EPS) * gain_vec + shift_vec


def gelu_fn(value_rows):
    return jax.nn.gelu(value_rows, approximate=True)


def segment_of(places, lengths):
    ends = jnp.cumsum(lengths, dtype=jnp.int32)
    return jnp.sum((places[:, None] >= ends[None, :]).astype(jnp.int32), axis=1, dtype=jnp.int32)


def ancestry(parents):
    seg_ids = jnp.arange(parents.shape[0], dtype=jnp.int32)
    current = seg_ids
    reach = current[:, None] == seg_ids[None, :]
    for sweep in range(parents.shape[0] - 1):
        current = jnp.sum(
            jnp.where(current[:, None] == seg_ids[None, :], parents[None, :], 0),
            axis=1,
            dtype=jnp.int32,
        )
        reach = reach | (current[:, None] == seg_ids[None, :])
    return reach.astype(WIDE_FEATURES)


def permitted(seg_query, place_query, seg_key, place_key, ancestors):
    seg_ids = jnp.arange(ancestors.shape[0], dtype=jnp.int32)
    anc_rows = jnp.dot((seg_query[:, None] == seg_ids[None, :]).astype(WIDE_FEATURES), ancestors)
    reach = jnp.dot(anc_rows, (seg_key[:, None] == seg_ids[None, :]).astype(WIDE_FEATURES).T)
    return (reach > 0.5) & (place_key[None, :] <= place_query[:, None])


def adapter_forward(value_rows, down_projector, up_projector):
    inner_hidden = matrix_product(value_rows, down_projector.T)
    return (
        inner_hidden,
        ADAPTER_SCALING * precise_product(inner_hidden, up_projector.astype(WIDE_FEATURES)),
    )


def adapter_backward(output_gradient, value_rows, inner_hidden, down_projector, up_projector):
    inner_gradient = ADAPTER_SCALING * matrix_product(output_gradient, up_projector.T)
    up_gradient = ADAPTER_SCALING * precise_product(inner_hidden.T, output_gradient)
    grad_down = precise_product(inner_gradient.T, value_rows)
    grad_values = precise_product(inner_gradient, down_projector.astype(WIDE_FEATURES))
    return (grad_values, grad_down, up_gradient)


def pick_one(stacked, chosen):
    return lax.dynamic_index_in_dim(stacked, chosen, 0, keepdims=False)


def add_slab(stacked, chosen, addend):
    slab = lax.dynamic_index_in_dim(stacked, chosen, 0, keepdims=False) + addend
    return lax.dynamic_update_index_in_dim(stacked, slab, chosen, 0)


def local(
    inputs,
    cotangent,
    norm_gains,
    norm_biases,
    w_attn,
    w_out,
    w_up,
    w_down,
    down_attn,
    up_attn,
    down_out,
    up_out,
    down_up,
    up_up,
    down_down,
    up_down,
    seg_lengths,
    parent_ids,
    adapter_ids,
):
    section_at = lax.axis_index("section")
    shard_at = lax.axis_index("fsdp")
    shard_count = lax.axis_size("fsdp")
    micro_count = inputs.shape[0]
    row_count = inputs.shape[1]
    inv_root = HEAD_DIM ** (-0.5)
    norm_gain = norm_gains[0].astype(WIDE_FEATURES)
    norm_shift = norm_biases[0].astype(WIDE_FEATURES)
    (
        attn_full,
        out_full,
        up_weight,
        down_weight,
        attn_down,
        attn_up,
        proj_down,
        proj_up,
        widen_down,
        widen_up,
        narrow_down,
        narrow_up,
    ) = (
        lax.all_gather(w_attn[0], "fsdp", axis=1, tiled=True),
        lax.all_gather(w_out[0], "fsdp", axis=1, tiled=True),
        lax.all_gather(w_up[0], "fsdp", axis=1, tiled=True),
        lax.all_gather(w_down[0], "fsdp", axis=0, tiled=True),
        lax.all_gather(down_attn[0], "fsdp", axis=2, tiled=True),
        lax.all_gather(up_attn[0], "fsdp", axis=2, tiled=True),
        lax.all_gather(down_out[0], "fsdp", axis=2, tiled=True),
        lax.all_gather(up_out[0], "fsdp", axis=2, tiled=True),
        lax.all_gather(down_up[0], "fsdp", axis=2, tiled=True),
        lax.all_gather(up_up[0], "fsdp", axis=2, tiled=True),
        lax.all_gather(down_down[0], "fsdp", axis=2, tiled=True),
        lax.all_gather(up_down[0], "fsdp", axis=2, tiled=True),
    )
    query_places = shard_at * row_count + jnp.arange(row_count, dtype=jnp.int32)

    def tree_info(micro_at):
        lengths = lax.dynamic_index_in_dim(seg_lengths, micro_at, 0, keepdims=False)[0]
        parents = lax.dynamic_index_in_dim(parent_ids, micro_at, 0, keepdims=False)[0]
        chosen = lax.dynamic_index_in_dim(adapter_ids, micro_at, 0, keepdims=False)[0, 0]
        return (lengths, ancestry(parents), chosen)

    def mlp_backward(grad_branch, stored, chosen):
        second_kept, pre_act, gelu_out, inner_in, inner_out = stored
        gelu_back = jax.vjp(gelu_fn, pre_act)[1]
        extra_term, narrow_down_grad, narrow_up_grad = adapter_backward(
            grad_branch,
            gelu_out,
            inner_out,
            pick_one(narrow_down, chosen),
            pick_one(narrow_up, chosen),
        )
        grad_gelu = rounded(matrix_product(grad_branch, down_weight.T) + extra_term)
        grad_pre = gelu_back(grad_gelu)[0].astype(SLIM)
        extra_in, widen_down_grad, widen_up_grad = adapter_backward(
            grad_pre,
            second_kept,
            inner_in,
            pick_one(widen_down, chosen),
            pick_one(widen_up, chosen),
        )
        grad_second = matrix_product(grad_pre, up_weight.T) + extra_in
        return (grad_second, (widen_down_grad, widen_up_grad, narrow_down_grad, narrow_up_grad))

    def backward(grad_output, stored, micro_at):
        lengths, ancestors, chosen = tree_info(micro_at)
        (
            residual,
            normed,
            inner_qkv,
            queries,
            keys_vals,
            log_total,
            mixed_out,
            inner_proj,
            middle,
            mlp_kept,
        ) = stored
        grad_second, mlp_grads = mlp_backward(grad_output.astype(SLIM), mlp_kept, chosen)
        norm_two_back = jax.vjp(
            lambda value_rows: layer_norm(value_rows, norm_gain[1], norm_shift[1]), middle
        )[1]
        grad_middle = grad_output + norm_two_back(rounded(grad_second))[0]
        grad_branch = grad_middle.astype(SLIM)
        extra_term, proj_down_grad, proj_up_grad = adapter_backward(
            grad_branch,
            mixed_out,
            inner_proj,
            pick_one(proj_down, chosen),
            pick_one(proj_up, chosen),
        )
        grad_mixed = (
            (matrix_product(grad_branch, out_full.T) + extra_term)
            .astype(SLIM)
            .reshape(row_count * HEADS, HEAD_DIM)
        )
        keys_all = lax.all_gather(keys_vals, "fsdp", axis=0, tiled=True)
        key_count = keys_all.shape[0]
        key_places = jnp.arange(key_count, dtype=jnp.int32)
        segments = segment_of(query_places, lengths)
        visible = permitted(
            segments, query_places, segment_of(key_places, lengths), key_places, ancestors
        )[:, None, :]
        scores = (matrix_product(queries, keys_all[:, :HEAD_DIM].T) * inv_root).reshape(
            row_count, HEADS, key_count
        )
        scores = jnp.where(visible, scores, MASKED)
        attn_probs = jnp.where(visible, jnp.exp(scores - log_total[:, :, None]), 0.0)
        grad_probs = matrix_product(grad_mixed, keys_all[:, HEAD_DIM:].T).reshape(
            row_count, HEADS, key_count
        )
        row_delta = jnp.sum(attn_probs * grad_probs, axis=2)
        grad_scores = (
            (attn_probs * (grad_probs - row_delta[:, :, None]))
            .astype(SLIM)
            .reshape(row_count * HEADS, key_count)
        )
        probs_low = attn_probs.astype(SLIM).reshape(row_count * HEADS, key_count)
        grad_queries = matrix_product(grad_scores, keys_all[:, :HEAD_DIM]) * inv_root
        grad_keys = matrix_product(grad_scores.T, queries) * inv_root
        grad_values = matrix_product(probs_low.T, grad_mixed)
        grad_kv = lax.psum_scatter(
            jnp.concatenate([grad_keys, grad_values], axis=1).astype(jnp.bfloat16),
            "fsdp",
            scatter_dimension=0,
            tiled=True,
        ).astype(jnp.float32)
        grad_joined = jnp.concatenate(
            [grad_queries.reshape(row_count, D).astype(SLIM), grad_kv.astype(SLIM)], axis=1
        )
        extra_qkv, attn_down_grad, attn_up_grad = adapter_backward(
            grad_joined, normed, inner_qkv, pick_one(attn_down, chosen), pick_one(attn_up, chosen)
        )
        grad_normed = rounded(matrix_product(grad_joined, attn_full.T) + extra_qkv)
        norm_one_back = jax.vjp(
            lambda value_rows: layer_norm(value_rows, norm_gain[0], norm_shift[0]), residual
        )[1]
        grad_in = grad_middle + norm_one_back(grad_normed)[0]
        widen_down_grad, widen_up_grad, narrow_down_grad, narrow_up_grad = mlp_grads
        return (
            grad_in,
            (
                attn_down_grad,
                attn_up_grad,
                proj_down_grad,
                proj_up_grad,
                widen_down_grad,
                widen_up_grad,
                narrow_down_grad,
                narrow_up_grad,
            ),
            chosen,
        )

    forward_outs = []
    saved_all = []
    received = jnp.zeros((row_count, D), WIDE_FEATURES)
    for step_at in range(micro_count + 1):
        micro_at = jnp.clip(step_at - section_at, 0, micro_count - 1)
        own_rows = inputs[min(step_at, micro_count - 1)].astype(WIDE_FEATURES)
        layer_in = jnp.where(section_at == 0, own_rows, received)
        forward_lengths, forward_ancestors, forward_chosen = tree_info(micro_at)
        forward_normed = layer_norm(layer_in, norm_gain[0], norm_shift[0]).astype(SLIM)
        forward_inner_qkv, forward_extra_qkv = adapter_forward(
            forward_normed, pick_one(attn_down, forward_chosen), pick_one(attn_up, forward_chosen)
        )
        joined_out = matrix_product(forward_normed, attn_full) + forward_extra_qkv
        forward_queries = joined_out[:, :D].astype(SLIM).reshape(row_count * HEADS, HEAD_DIM)
        forward_keys_vals = joined_out[:, D:].astype(SLIM)
        forward_segments = segment_of(query_places, forward_lengths)
        forward_keys_all = lax.all_gather(forward_keys_vals, "fsdp", axis=0, tiled=True)
        forward_key_count = forward_keys_all.shape[0]
        forward_key_places = jnp.arange(forward_key_count, dtype=jnp.int32)
        forward_visible = permitted(
            forward_segments,
            query_places,
            segment_of(forward_key_places, forward_lengths),
            forward_key_places,
            forward_ancestors,
        )[:, None, :]
        forward_scores = (
            matrix_product(forward_queries, forward_keys_all[:, :HEAD_DIM].T) * inv_root
        ).reshape(row_count, HEADS, forward_key_count)
        forward_scores = jnp.where(forward_visible, forward_scores, MASKED)
        row_top = jnp.max(forward_scores, axis=2)
        exp_terms = jnp.where(forward_visible, jnp.exp(forward_scores - row_top[:, :, None]), 0.0)
        row_total = jnp.sum(exp_terms, axis=2)
        forward_attn_probs = exp_terms / row_total[:, :, None]
        forward_log_total = row_top + jnp.log(row_total)
        forward_probs_low = forward_attn_probs.astype(SLIM).reshape(
            row_count * HEADS, forward_key_count
        )
        forward_mixed_out = (
            matrix_product(forward_probs_low, forward_keys_all[:, HEAD_DIM:])
            .reshape(row_count, D)
            .astype(SLIM)
        )
        forward_inner_proj, extra_proj = adapter_forward(
            forward_mixed_out,
            pick_one(proj_down, forward_chosen),
            pick_one(proj_up, forward_chosen),
        )
        forward_middle = layer_in + (matrix_product(forward_mixed_out, out_full) + extra_proj)
        forward_second = layer_norm(forward_middle, norm_gain[1], norm_shift[1]).astype(SLIM)
        mlp_inner_in, mlp_extra_in = adapter_forward(
            forward_second, pick_one(widen_down, forward_chosen), pick_one(widen_up, forward_chosen)
        )
        mlp_pre_act = matrix_product(forward_second, up_weight) + mlp_extra_in
        mlp_gelu_out = gelu_fn(mlp_pre_act).astype(SLIM)
        mlp_inner_out, extra_out = adapter_forward(
            mlp_gelu_out, pick_one(narrow_down, forward_chosen), pick_one(narrow_up, forward_chosen)
        )
        branch = matrix_product(mlp_gelu_out, down_weight) + extra_out
        forward_mlp_kept = (forward_second, mlp_pre_act, mlp_gelu_out, mlp_inner_in, mlp_inner_out)
        output = forward_middle + branch
        output, stored = (
            output,
            (
                layer_in,
                forward_normed,
                forward_inner_qkv,
                forward_queries,
                forward_keys_vals,
                forward_log_total,
                forward_mixed_out,
                forward_inner_proj,
                forward_middle,
                forward_mlp_kept,
            ),
        )
        output_low = output.astype(SLIM)
        forward_outs.append(output_low)
        saved_all.append(stored)
        if step_at < micro_count:
            received = from_behind(output_low, "section", 1).astype(WIDE_FEATURES)
    stack_shapes = [
        (arr.shape[1], arr.shape[2], arr.shape[3] * shard_count)
        for arr in (down_attn, up_attn, down_out, up_out, down_up, up_up, down_down, up_down)
    ]
    totals = [jnp.zeros(shape_now, WIDE_FEATURES) for shape_now in stack_shapes]
    backward_outs = []
    incoming = jnp.zeros((row_count, D), WIDE_FEATURES)
    for step_at in range(micro_count + 1):
        micro_raw = step_at - 1 + section_at
        valid = ((micro_raw >= 0) & (micro_raw < micro_count)).astype(WIDE_FEATURES)
        micro_at = jnp.clip(micro_raw, 0, micro_count - 1)
        cot_rows = cotangent[min(step_at, micro_count - 1)].astype(WIDE_FEATURES)
        grad_output = jnp.where(section_at == 1, cot_rows, incoming)
        stored = jax.tree.map(
            lambda earlier, later: jnp.where(section_at == 1, later, earlier),
            saved_all[max(step_at - 1, 0)],
            saved_all[min(step_at + 1, micro_count)],
        )
        grad_in, grad_list, chosen = backward(grad_output, stored, micro_at)
        grad_low = grad_in.astype(SLIM)
        backward_outs.append(grad_low)
        totals = [
            add_slab(running, chosen, grad_now * valid)
            for running, grad_now in zip(totals, grad_list)
        ]
        if step_at < micro_count:
            incoming = from_behind(grad_low, "section", -1).astype(WIDE_FEATURES)
    local_sums = (
        lax.psum_scatter(
            totals[0].astype(jnp.bfloat16), "fsdp", scatter_dimension=2, tiled=True
        ).astype(jnp.float32),
        lax.psum_scatter(
            totals[1].astype(jnp.bfloat16), "fsdp", scatter_dimension=2, tiled=True
        ).astype(jnp.float32),
        lax.psum_scatter(
            totals[2].astype(jnp.bfloat16), "fsdp", scatter_dimension=2, tiled=True
        ).astype(jnp.float32),
        lax.psum_scatter(
            totals[3].astype(jnp.bfloat16), "fsdp", scatter_dimension=2, tiled=True
        ).astype(jnp.float32),
        lax.psum_scatter(
            totals[4].astype(jnp.bfloat16), "fsdp", scatter_dimension=2, tiled=True
        ).astype(jnp.float32),
        lax.psum_scatter(
            totals[5].astype(jnp.bfloat16), "fsdp", scatter_dimension=2, tiled=True
        ).astype(jnp.float32),
        lax.psum_scatter(
            totals[6].astype(jnp.bfloat16), "fsdp", scatter_dimension=2, tiled=True
        ).astype(jnp.float32),
        lax.psum_scatter(
            totals[7].astype(jnp.bfloat16), "fsdp", scatter_dimension=2, tiled=True
        ).astype(jnp.float32),
    )
    finals = (
        lax.psum(local_sums[0].astype(jnp.bfloat16), "replica").astype(jnp.float32),
        lax.psum(local_sums[1].astype(jnp.bfloat16), "replica").astype(jnp.float32),
        lax.psum(local_sums[2].astype(jnp.bfloat16), "replica").astype(jnp.float32),
        lax.psum(local_sums[3].astype(jnp.bfloat16), "replica").astype(jnp.float32),
        lax.psum(local_sums[4].astype(jnp.bfloat16), "replica").astype(jnp.float32),
        lax.psum(local_sums[5].astype(jnp.bfloat16), "replica").astype(jnp.float32),
        lax.psum(local_sums[6].astype(jnp.bfloat16), "replica").astype(jnp.float32),
        lax.psum(local_sums[7].astype(jnp.bfloat16), "replica").astype(jnp.float32),
    )
    layer_outputs = jnp.stack(
        [
            jnp.where(section_at == 0, forward_outs[micro_index], forward_outs[micro_index + 1])
            for micro_index in range(micro_count)
        ]
    )[None]
    input_grads = jnp.stack(
        [
            jnp.where(section_at == 1, backward_outs[micro_index], backward_outs[micro_index + 1])
            for micro_index in range(micro_count)
        ]
    )[None]
    return (
        layer_outputs,
        input_grads,
        finals[0][None],
        finals[1][None],
        finals[2][None],
        finals[3][None],
        finals[4][None],
        finals[5][None],
        finals[6][None],
        finals[7][None],
    )


def solution(mesh):
    placed = (
        P(None, ("replica", "fsdp"), None),
        P(None, ("replica", "fsdp"), None),
        P("section", None, None),
        P("section", None, None),
        P("section", None, "fsdp"),
        P("section", None, "fsdp"),
        P("section", None, "fsdp"),
        P("section", "fsdp", None),
        P("section", None, None, "fsdp"),
        P("section", None, None, "fsdp"),
        P("section", None, None, "fsdp"),
        P("section", None, None, "fsdp"),
        P("section", None, None, "fsdp"),
        P("section", None, None, "fsdp"),
        P("section", None, None, "fsdp"),
        P("section", None, None, "fsdp"),
        P(None, "replica", None),
        P(None, "replica", None),
        P(None, "replica", None),
    )
    return jax.shard_map(
        local,
        mesh=mesh,
        in_specs=placed,
        out_specs=(
            P("section", None, ("replica", "fsdp"), None),
            P("section", None, ("replica", "fsdp"), None),
            P("section", None, None, "fsdp"),
            P("section", None, None, "fsdp"),
            P("section", None, None, "fsdp"),
            P("section", None, None, "fsdp"),
            P("section", None, None, "fsdp"),
            P("section", None, None, "fsdp"),
            P("section", None, None, "fsdp"),
            P("section", None, None, "fsdp"),
        ),
        check_vma=False,
    )
```

profile of v0, /device:TPU:0, one launch (start us, length us, event | category | flops | bytes accessed | tf_op | source)
XLA Modules:
  0.0 2851.4 jit_solution(4499084613932903647)
XLA Ops:
  42.5 30.7 %all-gather.1 = bf16[1,8,16,2048]{3,2,1,0:T(8,128)(2,1)} all-gather(bf16[1,8,16,512]{3,2,1,0:T(8,128)(2,1)S(1)} %copy-done.164), channel_id=3, replica_groups=mesh['section'=2,'fsdp'=4,'replica'=4] {'fsdp'}, dimensions={3}, use_global_device_ids=true | all-gather | bytes 655360 | tf_op jit(solution)/shard_map/all_gather | solution.py:145
  74.1 153.1 %all-gather.2 = bf16[1,8,16,2304]{2,1,0,3:T(8,128)(2,1)} all-gather(bf16[1,8,16,576]{2,1,0,3:T(8,128)(2,1)S(1)} %copy.163), channel_id=4, replica_groups=mesh['section'=2,'fsdp'=4,'replica'=4] {'fsdp'}, dimensions={3}, use_global_device_ids=true | all-gather | bytes 737280 | tf_op jit(solution)/shard_map/all_gather | solution.py:146
  231.0 18.8 constant_dynamic-slice_fusion.16
  252.2 20.7 all-gather.4
  272.9 22.7 all-gather.5
  295.6 27.0 all-gather.7
  322.6 26.3 all-gather.11
  423.3 23.3 all_gather.57
  457.1 11.9 fusion.187
  483.4 525.9 %all-gather.23.cloned.1.call-done = bf16[1,2048,8192]{2,1,0:T(8,128)(2,1)} async-done(((bf16[1,2048,2048]{2,1,0:T(8,128)(2,1)}), bf16[1,2048,8192]{2,1,0:T(8,128)(2,1)}) %all-gather.23.cloned.1.call-update) | async-done | bytes 33554448 | tf_op jit(solution)/shard_map/all_gather | solution.py:143
  1009.3 17.8 fusion.25
  1027.1 27.8 all-gather.25.cloned.1.call-done
  1054.9 13.2 fusion.135
  1068.2 548.3 %all-gather.27.cloned.1.call-done = bf16[1,8192,2048]{2,1,0:T(8,128)(2,1)} async-done(((bf16[1,2048,2048]{2,1,0:T(8,128)(2,1)}), bf16[1,8192,2048]{2,1,0:T(8,128)(2,1)}) %all-gather.27.cloned.1.call-update) | async-done | bytes 33554448 | tf_op jit(solution)/shard_map/all_gather | solution.py:144
  1616.5 18.1 fusion.13
  1634.6 27.5 all-gather.29.cloned.1.call-done
  1672.7 18.5 fusion.7
  1691.3 7.6 fusion.60
  1709.4 15.9 all_gather.67
  1736.2 10.4 fusion.186
  1761.1 17.3 fusion.23
  1778.4 19.4 fusion.100
  1797.7 17.9 fusion.11
  1822.4 17.0 fusion.19
  1869.2 15.4 all_gather.68
  1895.3 10.4 fusion.185
  1935.7 14.9 all_gather.69
  1951.4 8.2 convolution_multiply_fusion.11
  1959.6 17.5 copy.174
  1977.3 38.7 %multiply_convert_fusion.2 = bf16[256,16,1024]{2,0,1:T(8,128)(2,1)} fusion(f32[256,16,1024]{2,1,0:T(8,128)} %bitcast.657, f32[256,16]{0,1:T(8,128)S(1)} %copy.176, pred[256,1024]{1,0:T(8,128)(4,1)} %fusion.307, bf16[1024,256]{1,0:T(8,128)(2,1)} %copy-done.107, bf16[256,2048]{1,0:T(8,128)(2,1)} %fusion.236), kind=kOutput, calls=%fused_computation.48 | convolution fusion | flops 2189431808 | bytes 45121536 | tf_op jit(solution)/shard_map/sub | solution.py:233
  2015.9 11.4 copy.178
  2029.6 6.9 fusion.182
  2039.0 8.1 fusion.299
  2050.3 17.9 all_gather.70
  2068.9 8.1 convolution_multiply_fusion.10
  2077.0 17.4 copy.185
  2097.0 17.2 fusion.21
  2114.3 14.8 all_gather.71
  2129.9 8.2 convolution_multiply_fusion.9
  2138.1 17.5 copy.196
  2175.3 6.9 fusion.51
  2182.2 7.0 collective-permute-done.2
  2198.7 19.6 fusion.64
  2218.3 8.9 fusion.105
  2227.2 17.4 fusion.17
  2265.8 36.4 %multiply_convert_fusion.1 = bf16[256,16,1024]{2,0,1:T(8,128)(2,1)} fusion(f32[256,16,1024]{2,1,0:T(8,128)} %bitcast.656, f32[256,16]{0,1:T(8,128)S(1)} %copy.187, pred[256,1024]{1,0:T(8,128)(4,1)S(1)} %copy-done.138, bf16[1024,256]{1,0:T(8,128)(2,1)S(1)} %copy-done.106, bf16[256,2048]{1,0:T(8,128)(2,1)} %fusion.229), kind=kOutput, calls=%fused_computation.44 | convolution fusion | flops 2189431808 | bytes 45121536 | tf_op jit(solution)/shard_map/sub | solution.py:233
  2302.2 11.5 copy.189
  2313.7 11.2 fusion.298
  2329.5 6.9 fusion.183
  2338.2 9.5 reduce-scatter.16.cloned.1.call-done
  2368.7 19.6 collective-permute-done.3
  2397.4 19.6 fusion.61
  2416.9 13.1 fusion.110
  2430.0 17.7 fusion.15
  2466.2 39.1 %multiply_convert_fusion = bf16[256,16,1024]{2,0,1:T(8,128)(2,1)} fusion(f32[256,16,1024]{2,1,0:T(8,128)} %bitcast.655, f32[256,16]{0,1:T(8,128)S(1)} %copy-done.200, pred[256,1024]{1,0:T(8,128)(4,1)S(1)} %copy-done.137, bf16[1024,256]{1,0:T(8,128)(2,1)S(1)} %copy-done.104, bf16[256,2048]{1,0:T(8,128)(2,1)S(1)} %fusion.226), kind=kOutput, calls=%fused_computation.40 | convolution fusion | flops 2189431808 | bytes 45121536 | tf_op jit(solution)/shard_map/sub | solution.py:233
  2505.3 11.5 copy.200
  2516.8 8.5 fusion.297
  2538.1 9.6 reduce-scatter.18.cloned.1.call-done
  2619.5 16.5 fusion.9
  2654.2 15.2 reduce-scatter.32.cloned.1.call-done
  2669.4 22.1 reduce-scatter.20.cloned.1.call-done
  2691.5 44.4 %reduce-scatter.28.cloned.1.call-done = bf16[8,16,2048]{2,1,0:T(8,128)(2,1)} async-done(((bf16[8,16,8192]{2,1,0:T(8,128)(2,1)}), bf16[8,16,2048]{2,1,0:T(8,128)(2,1)}) %reduce-scatter.28.cloned.1.call-update) | async-done | bytes 524304 | tf_op jit(solution)/shard_map/reduce_scatter | solution.py:398
  2735.9 45.5 %reduce-scatter.30.cloned.1.call-done = bf16[8,16,2048]{2,1,0:T(8,128)(2,1)} async-done(((bf16[8,16,8192]{2,1,0:T(8,128)(2,1)}), bf16[8,16,2048]{2,1,0:T(8,128)(2,1)}) %reduce-scatter.30.cloned.1.call-update) | async-done | bytes 524304 | tf_op jit(solution)/shard_map/reduce_scatter | solution.py:401
  2786.7 46.2 %all-reduce.3.cloned.1.call-done = (bf16[1,8,16,512]{3,2,1,0:T(8,128)(2,1)}, bf16[1,8,16,576]{3,2,1,0:T(8,128)(2,1)}, bf16[1,8,16,512]{3,2,1,0:T(8,128)(2,1)}, b...) async-done(((bf16[1,8,16,512]{3,2,1,0:T(8,128)(2,1)}, ...) | async-done | bytes 1851408 | tf_op jit(solution)/shard_map/psum | solution.py:409
  (803 shorter events, 488.6 us)
Async XLA Ops:
  7.2 405.3 %all-gather.19.cloned.1.call-start = ((), (), s32[]{:S(2)}) async-start(), calls=%async_computation.21 | async-start | bytes 11796480 | tf_op jit(solution)/shard_map/all_gather | solution.py:141
  7.9 464.0 %all-gather.21.cloned.1.call-start = ((), (), s32[]{:S(2)}) async-start(), calls=%async_computation.22 | async-start | bytes 10485760 | tf_op jit(solution)/shard_map/all_gather | solution.py:142
  8.7 1000.7 %all-gather.23.cloned.1.call-start = ((), (), s32[]{:S(2)}) async-start(), calls=%async_computation.23 | async-start | bytes 41943040 | tf_op jit(solution)/shard_map/all_gather | solution.py:143
  9.4 1045.5 %all-gather.25.cloned.1.call-start = ((), (), s32[]{:S(2)}) async-start(), calls=%async_computation.24 | async-start | bytes 2621440 | tf_op jit(solution)/shard_map/all_gather | solution.py:150
  10.0 11.8 copy-start.202
  10.0 1606.5 %all-gather.27.cloned.1.call-start = ((), (), s32[]{:S(2)}) async-start(), calls=%async_computation.25 | async-start | bytes 41943040 | tf_op jit(solution)/shard_map/all_gather | solution.py:144
  10.6 1651.5 %all-gather.29.cloned.1.call-start = ((), (), s32[]{:S(2)}) async-start(), calls=%async_computation.26 | async-start | bytes 2621440 | tf_op jit(solution)/shard_map/all_gather | solution.py:151
  11.2 2147.5 %reduce-scatter.14.cloned.1.call-start = ((), (), s32[]{:S(2)}) async-start(), calls=%async_computation.11 | async-start | bytes 655360 | tf_op jit(solution)/shard_map/reduce_scatter | solution.py:241
  41.1 32.2 %copy-start.141 = (bf16[1,8,16,576]{3,2,1,0:T(8,128)(2,1)S(1)}, bf16[1,8,16,576]{3,2,1,0:T(8,128)(2,1)}, u32[]{:S(2)}) copy-start(bf16[1,8,16,576]{3,2,1,0:T(8,128)(2,1)} %param.28) | copy-start | bytes 442372
  41.1 1658.6 %copy-start.173 = (f32[1,1,2048]{2,1,0:T(1,128)}, f32[1,1,2048]{2,1,0:T(1,128)S(1)}, u32[]{:S(2)}) copy-start(f32[1,1,2048]{2,1,0:T(1,128)S(1)} %get-tuple-element.90) | copy-start | bytes 24580
  41.1 1718.2 %copy-start.171 = (f32[1,1,2048]{2,1,0:T(1,128)}, f32[1,1,2048]{2,1,0:T(1,128)S(1)}, u32[]{:S(2)}) copy-start(f32[1,1,2048]{2,1,0:T(1,128)S(1)} %get-tuple-element.89) | copy-start | bytes 24580
  41.2 1658.6 %copy-start.108 = (f32[1,1,2048]{2,1,0:T(1,128)}, f32[1,1,2048]{2,1,0:T(1,128)S(1)}, u32[]{:S(2)}) copy-start(f32[1,1,2048]{2,1,0:T(1,128)S(1)} %get-tuple-element.88) | copy-start | bytes 24580
  41.2 1718.1 %copy-start.121 = (f32[1,1,2048]{2,1,0:T(1,128)}, f32[1,1,2048]{2,1,0:T(1,128)S(1)}, u32[]{:S(2)}) copy-start(f32[1,1,2048]{2,1,0:T(1,128)S(1)} %get-tuple-element.87) | copy-start | bytes 24580
  41.5 371.0 %copy-start.203 = (f32[256]{0:T(256)}, f32[256]{0:T(256)S(1)}, u32[]{:S(2)}) copy-start(f32[256]{0:T(256)S(1)} %broadcast_multiply_fusion.11) | copy-start | bytes 3076
  231.0 21.2 copy-start.165
  411.0 1280.3 %copy-start.179 = (f32[256,16]{0,1:T(8,128)}, f32[256,16]{0,1:T(8,128)S(1)}, u32[]{:S(2)}) copy-start(f32[256,16]{0,1:T(8,128)S(1)} %convolution_multiply_fusion.53) | copy-start | bytes 49156
  423.3 28.8 %copy-start.26 = (bf16[4096,128]{1,0:T(8,128)(2,1)}, bf16[4096,128]{1,0:T(8,128)(2,1)S(1)}, u32[]{:S(2)}) copy-start(bf16[4096,128]{1,0:T(8,128)(2,1)S(1)} %reshape.715) | copy-start | bytes 3145732
  457.1 11.9 copy-start.185
  482.1 545.0 %copy-start.42 = (bf16[256,2048]{1,0:T(8,128)(2,1)}, bf16[256,2048]{1,0:T(8,128)(2,1)S(1)}, u32[]{:S(2)}) copy-start(bf16[256,2048]{1,0:T(8,128)(2,1)S(1)} %add_convert_fusion.7) | copy-start | bytes 3145732
  483.4 571.5 %copy-start.145 = (f32[256,16]{0,1:T(8,128)}, f32[256,16]{0,1:T(8,128)S(1)}, u32[]{:S(2)}) copy-start(f32[256,16]{0,1:T(8,128)S(1)} %fusion.483) | copy-start | bytes 49156
  1669.3 29.6 %collective-permute-start = (bf16[256,2048]{1,0:T(8,128)(2,1)}, bf16[256,2048]{1,0:T(8,128)(2,1)S(1)}, u32[]{:S(2)}, u32[]{:S(2)}) collective-permute-start(bf16[256,2048]{1,0:T(8,128)(2,1)} %fusion.232), channel_id=1, source_target_pairs={{0,16},{1,17},{2,18},{3,19},{4,20},{5,21},{6,22},{7,23},{8,24},{9,... | collective-permute-start | bytes 3145736 | tf_op jit(solution)/shard_map/ppermute | solution.py:22
  1758.9 59.0 %copy-start.6 = (f32[256,2048]{1,0:T(8,128)}, f32[256,2048]{1,0:T(8,128)S(1)}, u32[]{:S(2)}) copy-start(f32[256,2048]{1,0:T(8,128)S(1)} %get-tuple-element.130) | copy-start | bytes 6291460
  1759.8 18.6 copy-start.48
  1761.1 87.7 %copy-start.148 = (f32[256,16]{0,1:T(8,128)}, f32[256,16]{0,1:T(8,128)S(1)}, u32[]{:S(2)}) copy-start(f32[256,16]{0,1:T(8,128)S(1)} %fusion.475) | copy-start | bytes 49156
  1797.7 17.9 copy-start.9
  1818.0 33.8 %copy-start.150 = (f32[256,16]{0,1:T(8,128)}, f32[256,16]{0,1:T(8,128)S(1)}, u32[]{:S(2)}) copy-start(f32[256,16]{0,1:T(8,128)S(1)} %fusion.413) | copy-start | bytes 49156
  1821.0 32.8 %collective-permute-start.1 = (bf16[256,2048]{1,0:T(8,128)(2,1)}, bf16[256,2048]{1,0:T(8,128)(2,1)S(1)}, u32[]{:S(2)}, u32[]{:S(2)}) collective-permute-start(bf16[256,2048]{1,0:T(8,128)(2,1)} %fusion.233), channel_id=1, source_target_pairs={{0,16},{1,17},{2,18},{3,19},{4,20},{5,21},{6,22},{7,23},{8,24},{9,... | collective-permute-start | bytes 3145736 | tf_op jit(solution)/shard_map/ppermute | solution.py:22
  1850.0 10.5 slice-start.5
  1869.2 21.0 copy-start.29
  1895.3 10.4 copy-start.161
  1905.8 249.8 %copy-start.189 = (f32[4096]{0:T(1024)}, f32[4096]{0:T(1024)S(1)}, u32[]{:S(2)}) copy-start(f32[4096]{0:T(1024)S(1)} %get-tuple-element.84) | copy-start | bytes 49156
  1909.0 19.0 slice-start.8
  1917.5 10.5 slice-start.9
  1930.4 21.0 copy-start.27
  2047.9 299.9 %reduce-scatter.16.cloned.1.call-start = ((), (), s32[]{:S(2)}) async-start(), calls=%async_computation.12 | async-start | bytes 655360 | tf_op jit(solution)/shard_map/reduce_scatter | solution.py:241
  2097.0 17.2 copy-start.126
  2097.0 32.9 %copy-start.28 = (bf16[4096,128]{1,0:T(8,128)(2,1)S(1)}, bf16[4096,128]{1,0:T(8,128)(2,1)}, u32[]{:S(2)}) copy-start(bf16[4096,128]{1,0:T(8,128)(2,1)} %reshape.718) | copy-start | bytes 3145732
  2097.0 32.9 %copy-start.30 = (bf16[4096,128]{1,0:T(8,128)(2,1)S(1)}, bf16[4096,128]{1,0:T(8,128)(2,1)}, u32[]{:S(2)}) copy-start(bf16[4096,128]{1,0:T(8,128)(2,1)} %copy-done.29) | copy-start | bytes 3145732
  2159.7 15.6 slice-start
  2161.5 13.8 slice-start.1
  2172.6 16.7 collective-permute-start.2
  2227.2 17.4 copy-start.14
  2302.1 11.5 copy-start.119
  2313.6 11.2 copy-start.82
  2313.6 11.2 copy-start.117
  2327.1 220.5 %reduce-scatter.18.cloned.1.call-start = ((), (), s32[]{:S(2)}) async-start(), calls=%async_computation.13 | async-start | bytes 655360 | tf_op jit(solution)/shard_map/reduce_scatter | solution.py:241
  2329.5 20.0 copy-start.177
  2338.2 17.8 copy-start.116
  2363.2 25.2 collective-permute-start.3
  2430.0 17.7 copy-start.15
  2505.3 11.5 copy-start.91
  2505.3 11.5 copy-start.190
  2527.7 121.1 %reduce-scatter.34.cloned.1.call-start = ((), (), s32[]{:S(2)}) async-start(), calls=%async_computation.27 | async-start | bytes 737280
  2538.1 10.6 copy-start.112
  2560.3 93.9 %reduce-scatter.22.cloned.1.call-start = ((), (), s32[]{:S(2)}) async-start(), calls=%async_computation.15 | async-start | bytes 655360 | tf_op jit(solution)/shard_map/reduce_scatter | solution.py:389
  2569.3 85.0 %reduce-scatter.24.cloned.1.call-start = ((), (), s32[]{:S(2)}) async-start(), calls=%async_computation.16 | async-start | bytes 655360 | tf_op jit(solution)/shard_map/reduce_scatter | solution.py:392
  2576.7 77.6 %reduce-scatter.26.cloned.1.call-start = ((), (), s32[]{:S(2)}) async-start(), calls=%async_computation.17 | async-start | bytes 655360 | tf_op jit(solution)/shard_map/reduce_scatter | solution.py:395
  2585.4 84.0 %reduce-scatter.32.cloned.1.call-start = ((), (), s32[]{:S(2)}) async-start(), calls=%async_computation.20 | async-start | bytes 655360 | tf_op jit(solution)/shard_map/reduce_scatter | solution.py:404
  2591.2 100.3 %reduce-scatter.20.cloned.1.call-start = ((), (), s32[]{:S(2)}) async-start(), calls=%async_computation.14 | async-start | bytes 655360 | tf_op jit(solution)/shard_map/reduce_scatter | solution.py:383
  2598.1 137.8 %reduce-scatter.28.cloned.1.call-start = ((), (), s32[]{:S(2)}) async-start(), calls=%async_computation.18 | async-start | bytes 2621440 | tf_op jit(solution)/shard_map/reduce_scatter | solution.py:398
  2607.7 173.7 %reduce-scatter.30.cloned.1.call-start = ((), (), s32[]{:S(2)}) async-start(), calls=%async_computation.19 | async-start | bytes 2621440 | tf_op jit(solution)/shard_map/reduce_scatter | solution.py:401
  2619.2 16.8 copy-start.17
  2619.2 213.8 %all-reduce.3.cloned.1.call-start = ((), (), s32[]{:S(2)}) async-start(), calls=%async_computation.28 | async-start | bytes 3735552 | tf_op jit(solution)/shard_map/psum | solution.py:409
  2648.8 132.6 %copy-start.23 = (bf16[2,256,2048]{2,1,0:T(8,128)(2,1)S(1)}, bf16[2,256,2048]{2,1,0:T(8,128)(2,1)}, u32[]{:S(2)}) copy-start(bf16[2,256,2048]{2,1,0:T(8,128)(2,1)} %param.20) | copy-start | bytes 6291460
  (182 other events, 761.7 us)
Sparse Core Ops, SparseCore 0:
  9.6 260.3 all-gather.18
  271.5 175.3 all-gather.20
  448.5 560.7 all-gather.22
  1010.8 44.1 all-gather.24
  1056.4 560.0 all-gather.26
  1617.9 44.1 all-gather.28
  2048.0 21.0 reduce-scatter.13
  2327.3 20.4 reduce-scatter.15
  2527.9 19.7 reduce-scatter.17
  2560.5 20.1 reduce-scatter.33
  2582.9 20.1 reduce-scatter.21
  2605.2 19.9 reduce-scatter.23
  2627.4 19.8 reduce-scatter.25
  2649.5 19.8 reduce-scatter.31
  2671.5 19.9 reduce-scatter.19
  2693.7 42.1 reduce-scatter.27
  2738.2 43.1 reduce-scatter.29
  2784.7 48.2 all-reduce.2
where the time goes:
time: 2860 us; the launch traced here: 2850 us
  waiting for transfers between devices  1350 us (47%)
  matrix products  702 us (25%)
  blocking collectives  383 us (13%)
  local copies, waits for them, and re-layouts  266 us (9%)
  other arithmetic  110 us (4%)
  between operations  29.5 us (1%)
    all_gather x1, waiting for transfers between devices, local(): lax.all_gather(w_down[0], 'fsdp', axis=0, tiled=True)  548 us
    all_gather x1, waiting for transfers between devices, local(): lax.all_gather(w_up[0], 'fsdp', axis=1, tiled=True)  526 us
    dot_general x66, matrix products, matrix_product(): return jnp.dot(left_side, right_side, preferred_element_type=WIDE_FEATURES)  443 us
    all_gather x1, blocking collectives, local(): lax.all_gather(up_attn[0], 'fsdp', axis=2, tiled=True)  153 us
    dot_general x48, matrix products, precise_product(): jnp.dot(left_side, right_side, precision=HIGH, preferred_element_type=WID...  137 us
    sub x3, matrix products, backward(): grad_probs - row_delta[:, :, None]  114 us
    unnamed x459, local copies, waits for them, and re-layouts  57.7 us
  transfers between devices with their start and end apart: 22, of which 13 were waited for; matrix products, arithmetic and copies ran while one was open for 16% of the time, Pallas kernels for 0%

commit v1 on v0

v1 whole, which is shorter than its diff:
```python
import functools
import math

import jax
import jax.numpy as jnp
from jax import lax
from jax.experimental import pallas as pl
from jax.experimental.pallas import tpu as pltpu
from jax.sharding import PartitionSpec as P

D = 2048
HEADS = 16
HEAD_DIM = 128
RANK = 16

NORM_EPS = 1e-05
MASKED = -1e30
BF = jnp.bfloat16
F32 = jnp.float32
INV_ROOT = HEAD_DIM ** (-0.5)
LOG2E = math.log2(math.e)
LN2 = math.log(2.0)
GELU_C = math.sqrt(2.0 / math.pi)
VMEM_LIMIT = 56 * 1024 * 1024

NN = (((1,), (0,)), ((), ()))
NT = (((1,), (1,)), ((), ()))
TN = (((0,), (0,)), ((), ()))


def dot(left, right, dims=NN):
    return lax.dot_general(left, right, dims, preferred_element_type=F32)


def params(steps=1):
    return pltpu.CompilerParams(
        dimension_semantics=("arbitrary",) * steps, vmem_limit_bytes=VMEM_LIMIT
    )


def layer_norm(rows, gain, shift):
    centre = rows - jnp.mean(rows, axis=-1, keepdims=True)
    spread = jnp.mean(centre * centre, axis=-1, keepdims=True)
    return centre * lax.rsqrt(spread + NORM_EPS) * gain + shift


def layer_norm_back(rows, gain, grad):
    centre = rows - jnp.mean(rows, axis=-1, keepdims=True)
    spread = jnp.mean(centre * centre, axis=-1, keepdims=True)
    scale = lax.rsqrt(spread + NORM_EPS)
    unit = centre * scale
    inner = grad * gain
    return scale * (
        inner
        - jnp.mean(inner, axis=-1, keepdims=True)
        - unit * jnp.mean(inner * unit, axis=-1, keepdims=True)
    )


def tree_mask(rows, per_tree):
    row = lax.broadcasted_iota(jnp.int32, (rows, (rows // per_tree) * RANK), 0)
    col = lax.broadcasted_iota(jnp.int32, (rows, (rows // per_tree) * RANK), 1)
    return (row // per_tree) == (col // RANK)


def masked(value, per_tree):
    return jnp.where(tree_mask(value.shape[0], per_tree), 2.0 * value, 0.0).astype(BF)


def attention_forward_kernel(blocks, heads, q_ref, *refs):
    kv_refs, (bias_ref, o_ref, lse_ref) = refs[:blocks], refs[blocks:]
    keys = jnp.concatenate([r[:, :HEAD_DIM] for r in kv_refs], axis=0)
    vals = jnp.concatenate([r[:, HEAD_DIM:] for r in kv_refs], axis=0).T
    for h in range(heads):
        cols = slice(h * HEAD_DIM, (h + 1) * HEAD_DIM)
        scores = dot(keys, q_ref[:, cols], NT) + bias_ref[...]
        top = jnp.max(scores, axis=0, keepdims=True)
        probs = jnp.exp2(scores - top)
        total = jnp.sum(probs, axis=0, keepdims=True)
        mixed = dot(vals, probs.astype(BF)) * (1.0 / total)
        o_ref[:, cols] = mixed.T.astype(BF)
        lse_ref[0, h : h + 1, :] = top + jnp.log2(total)


def attention_forward(q, kv, bias, heads=4):
    rows = q.shape[0]
    blocks = len(kv)
    wide = heads * HEAD_DIM
    steps = HEADS // heads
    whole = lambda i: (0, 0)
    return pl.pallas_call(
        functools.partial(attention_forward_kernel, blocks, heads),
        grid=(steps,),
        in_specs=[pl.BlockSpec((rows, wide), lambda i: (0, i))]
        + [pl.BlockSpec((rows, 2 * HEAD_DIM), whole)] * blocks
        + [pl.BlockSpec((blocks * rows, rows), whole)],
        out_specs=[
            pl.BlockSpec((rows, wide), lambda i: (0, i)),
            pl.BlockSpec((1, heads, rows), lambda i: (i, 0, 0)),
        ],
        out_shape=[
            jax.ShapeDtypeStruct((rows, D), BF),
            jax.ShapeDtypeStruct((steps, heads, rows), F32),
        ],
        compiler_params=params(),
        cost_estimate=pl.CostEstimate(
            flops=4 * rows * rows * blocks * D,
            transcendentals=rows * rows * blocks * HEADS,
            bytes_accessed=4 * rows * D + 4 * rows * rows * blocks,
        ),
        name="attention_forward",
    )(q, *kv, bias)


def attention_backward_kernel(blocks, heads, q_ref, do_ref, o_ref, *refs):
    kv_refs = refs[:blocks]
    bias_ref, lse_ref, dq_ref, dkv_ref, acc_ref = refs[blocks:]
    rows = q_ref.shape[0]
    step = pl.program_id(0)

    @pl.when(step == 0)
    def _():
        acc_ref[...] = jnp.zeros_like(acc_ref)

    keys = jnp.concatenate([r[:, :HEAD_DIM] for r in kv_refs], axis=0)
    vals = jnp.concatenate([r[:, HEAD_DIM:] for r in kv_refs], axis=0)
    keys_t = keys.T
    for h in range(heads):
        cols = slice(h * HEAD_DIM, (h + 1) * HEAD_DIM)
        q, do = q_ref[:, cols], do_ref[:, cols]
        delta = jnp.sum(
            (do.astype(F32) * o_ref[:, cols].astype(F32)).T, axis=0, keepdims=True
        )
        scores = dot(keys, q, NT) + bias_ref[...]
        probs = jnp.exp2(scores - lse_ref[0, h : h + 1, :])
        dprobs = dot(vals, do, NT)
        dscores = (probs * (dprobs - delta)).astype(BF)
        acc_ref[:, :HEAD_DIM] += dot(dscores, q)
        acc_ref[:, HEAD_DIM:] += dot(probs.astype(BF), do)
        dq_ref[:, cols] = (dot(keys_t, dscores) * INV_ROOT).T.astype(BF)

    @pl.when(step == pl.num_programs(0) - 1)
    def _():
        for s in range(blocks):
            part = slice(s * rows, (s + 1) * rows)
            dkv_ref[s, :, :HEAD_DIM] = (acc_ref[part, :HEAD_DIM] * LN2).astype(BF)
            dkv_ref[s, :, HEAD_DIM:] = acc_ref[part, HEAD_DIM:].astype(BF)


def attention_backward(q, do, o, kv, bias, lse, heads=4):
    rows = q.shape[0]
    blocks = len(kv)
    wide = heads * HEAD_DIM
    steps = HEADS // heads
    whole = lambda i: (0, 0)
    return pl.pallas_call(
        functools.partial(attention_backward_kernel, blocks, heads),
        grid=(steps,),
        in_specs=[pl.BlockSpec((rows, wide), lambda i: (0, i))] * 3
        + [pl.BlockSpec((rows, 2 * HEAD_DIM), whole)] * blocks
        + [
            pl.BlockSpec((blocks * rows, rows), whole),
            pl.BlockSpec((1, heads, rows), lambda i: (i, 0, 0)),
        ],
        out_specs=[
            pl.BlockSpec((rows, wide), lambda i: (0, i)),
            pl.BlockSpec((blocks, rows, 2 * HEAD_DIM), lambda i: (0, 0, 0)),
        ],
        out_shape=[
            jax.ShapeDtypeStruct((rows, D), BF),
            jax.ShapeDtypeStruct((blocks, rows, 2 * HEAD_DIM), BF),
        ],
        scratch_shapes=[pltpu.VMEM((blocks * rows, 2 * HEAD_DIM), F32)],
        compiler_params=params(),
        cost_estimate=pl.CostEstimate(
            flops=10 * rows * rows * blocks * D,
            transcendentals=rows * rows * blocks * HEADS,
            bytes_accessed=8 * rows * D + 4 * rows * rows * blocks,
        ),
        name="attention_backward",
    )(q, do, o, *kv, bias, lse)


def mlp_forward_kernel(
    per_tree, b_ref, x2_ref, wu_ref, wd_ref, upu_ref, dnd_ref, dnu_ref, upd_ref,
    y_ref, g_ref, gp_ref, u3_ref, u4_ref, acc_ref,
):
    step = pl.program_id(0)

    @pl.when(step == 0)
    def _():
        u3_ref[...] = masked(dot(b_ref[...], dnu_ref[...], NT), per_tree)
        y_ref[...] = x2_ref[...]
        acc_ref[...] = jnp.zeros_like(acc_ref)

    f = dot(b_ref[...], wu_ref[0]) + dot(u3_ref[...], upu_ref[...])
    square = f * f
    bend = jnp.tanh(GELU_C * f * (1.0 + 0.044715 * square))
    half = 0.5 * (1.0 + bend)
    g = (f * half).astype(BF)
    g_ref[...] = g
    gp_ref[...] = (
        half
        + 0.5 * f * (1.0 - bend * bend) * (GELU_C * (1.0 + 3 * 0.044715 * square))
    ).astype(BF)
    y_ref[...] += dot(g, wd_ref[...])
    acc_ref[...] += dot(g, dnd_ref[...], NT)

    @pl.when(step == pl.num_programs(0) - 1)
    def _():
        u4 = masked(acc_ref[...], per_tree)
        u4_ref[...] = u4
        y_ref[...] += dot(u4, upd_ref[...])


def mlp_forward(b, x2, w_up, w_down, up_up, down_down, down_up, up_down, block=512):
    rows = b.shape[0]
    shards, _, part = w_up.shape
    hidden = shards * part
    trees = down_up.shape[0] // RANK
    wide = trees * RANK
    block = min(block, part)
    per = part // block
    once = lambda j: (0, 0)
    return pl.pallas_call(
        functools.partial(mlp_forward_kernel, rows // trees),
        grid=(hidden // block,),
        in_specs=[
            pl.BlockSpec((rows, D), once, pipeline_mode=pl.Buffered(1)),
            pl.BlockSpec((rows, D), once, pipeline_mode=pl.Buffered(1)),
            pl.BlockSpec((1, D, block), lambda j: (j // per, 0, j % per)),
            pl.BlockSpec((block, D), lambda j: (j, 0)),
            pl.BlockSpec((wide, block), lambda j: (0, j)),
            pl.BlockSpec((wide, block), lambda j: (0, j)),
            pl.BlockSpec((wide, D), once),
            pl.BlockSpec((wide, D), once),
        ],
        out_specs=[
            pl.BlockSpec((rows, D), once),
            pl.BlockSpec((rows, block), lambda j: (0, j)),
            pl.BlockSpec((rows, block), lambda j: (0, j)),
            pl.BlockSpec((rows, wide), once),
            pl.BlockSpec((rows, wide), once),
        ],
        out_shape=[
            jax.ShapeDtypeStruct((rows, D), F32),
            jax.ShapeDtypeStruct((rows, hidden), BF),
            jax.ShapeDtypeStruct((rows, hidden), BF),
            jax.ShapeDtypeStruct((rows, wide), BF),
            jax.ShapeDtypeStruct((rows, wide), BF),
        ],
        scratch_shapes=[pltpu.VMEM((rows, wide), F32)],
        compiler_params=params(),
        cost_estimate=pl.CostEstimate(
            flops=4 * rows * D * hidden,
            transcendentals=rows * hidden,
            bytes_accessed=4 * D * hidden + 4 * rows * hidden + 10 * rows * D,
        ),
        name="mlp_forward",
    )(b, x2, w_up, w_down, up_up, down_down, down_up, up_down)


def mlp_backward_kernel(
    per_tree, dy_ref, b_ref, x2_ref, gain_ref, wu_ref, wd_ref, g_ref, gp_ref, u3_ref, u4_ref,
    upu_ref, dnd_ref, dnu_ref, upd_ref,
    dx2_ref, gupu_ref, gdnd_ref, gdnu_ref, gupd_ref,
    dm_ref, du4_ref, du3_ref,
):
    step = pl.program_id(0)

    @pl.when(step == 0)
    def _():
        dm = dy_ref[...].astype(BF)
        dm_ref[...] = dm
        du4_ref[...] = masked(dot(dm, upd_ref[...], NT), per_tree)
        gupd_ref[...] = dot(u4_ref[...], dm, TN)
        dx2_ref[...] = jnp.zeros_like(dx2_ref)
        du3_ref[...] = jnp.zeros_like(du3_ref)

    du4 = du4_ref[...]
    dg = dot(dm_ref[...], wd_ref[...], NT) + dot(du4, dnd_ref[...])
    df = (gp_ref[...].astype(F32) * dg).astype(BF)
    gdnd_ref[...] = dot(du4, g_ref[...], TN)
    gupu_ref[...] = dot(u3_ref[...], df, TN)
    du3_ref[...] += dot(df, upu_ref[...], NT)
    dx2_ref[...] += dot(df, wu_ref[0], NT)

    @pl.when(step == pl.num_programs(0) - 1)
    def _():
        du3 = masked(du3_ref[...], per_tree)
        gdnu_ref[...] = dot(du3, b_ref[...], TN)
        db = (dx2_ref[...] + dot(du3, dnu_ref[...])).astype(BF).astype(F32)
        dx2_ref[...] = dy_ref[...] + layer_norm_back(x2_ref[...], gain_ref[...], db)


def mlp_backward(
    dy, b, x2, gain, w_up, w_down, g, gp, u3, u4, up_up, down_down, down_up, up_down, block=512
):
    rows = b.shape[0]
    shards, _, part = w_up.shape
    hidden = shards * part
    trees = down_up.shape[0] // RANK
    wide = trees * RANK
    block = min(block, part)
    per = part // block
    once = lambda j: (0, 0)
    single = pl.Buffered(1)
    return pl.pallas_call(
        functools.partial(mlp_backward_kernel, rows // trees),
        grid=(hidden // block,),
        in_specs=[
            pl.BlockSpec((rows, D), once, pipeline_mode=single),
            pl.BlockSpec((rows, D), once, pipeline_mode=single),
            pl.BlockSpec((rows, D), once, pipeline_mode=single),
            pl.BlockSpec((1, D), once),
            pl.BlockSpec((1, D, block), lambda j: (j // per, 0, j % per)),
            pl.BlockSpec((block, D), lambda j: (j, 0)),
            pl.BlockSpec((rows, block), lambda j: (0, j)),
            pl.BlockSpec((rows, block), lambda j: (0, j)),
            pl.BlockSpec((rows, wide), once),
            pl.BlockSpec((rows, wide), once),
            pl.BlockSpec((wide, block), lambda j: (0, j)),
            pl.BlockSpec((wide, block), lambda j: (0, j)),
            pl.BlockSpec((wide, D), once),
            pl.BlockSpec((wide, D), once),
        ],
        out_specs=[
            pl.BlockSpec((rows, D), once),
            pl.BlockSpec((wide, block), lambda j: (0, j)),
            pl.BlockSpec((wide, block), lambda j: (0, j)),
            pl.BlockSpec((wide, D), once),
            pl.BlockSpec((wide, D), once),
        ],
        out_shape=[
            jax.ShapeDtypeStruct((rows, D), F32),
            jax.ShapeDtypeStruct((wide, hidden), F32),
            jax.ShapeDtypeStruct((wide, hidden), F32),
            jax.ShapeDtypeStruct((wide, D), F32),
            jax.ShapeDtypeStruct((wide, D), F32),
        ],
        scratch_shapes=[
            pltpu.VMEM((rows, D), BF),
            pltpu.VMEM((rows, wide), BF),
            pltpu.VMEM((rows, wide), F32),
        ],
        compiler_params=params(),
        cost_estimate=pl.CostEstimate(
            flops=4 * rows * D * hidden,
            transcendentals=0,
            bytes_accessed=4 * D * hidden + 4 * rows * hidden + 14 * rows * D,
        ),
        name="mlp_backward",
    )(dy, b, x2, gain, w_up, w_down, g, gp, u3, u4, up_up, down_down, down_up, up_down)


def segment_of(places, lengths):
    order = jnp.arange(lengths.shape[0], dtype=jnp.int32)
    ends = jnp.sum(
        jnp.where(order[None, :] <= order[:, None], lengths[None, :], 0), axis=1, dtype=jnp.int32
    )
    return jnp.sum((places[:, None] >= ends[None, :]).astype(jnp.int32), axis=1, dtype=jnp.int32)


def ancestry(parents):
    seg_ids = jnp.arange(parents.shape[0], dtype=jnp.int32)
    current = seg_ids
    reach = current[:, None] == seg_ids[None, :]
    for sweep in range(parents.shape[0] - 1):
        current = jnp.sum(
            jnp.where(current[:, None] == seg_ids[None, :], parents[None, :], 0),
            axis=1,
            dtype=jnp.int32,
        )
        reach = reach | (current[:, None] == seg_ids[None, :])
    return reach.astype(BF)


def key_bias(lengths, parents, query_places, key_places):
    seg_ids = jnp.arange(parents.shape[0], dtype=jnp.int32)
    of_query = (segment_of(query_places, lengths)[:, None] == seg_ids[None, :]).astype(BF)
    of_key = (segment_of(key_places, lengths)[:, None] == seg_ids[None, :]).astype(BF)
    reach = dot(of_key, dot(of_query, ancestry(parents)).astype(BF), NT)
    allowed = (
        (reach > 0.5)
        & (key_places[:, None] <= query_places[None, :])
        & (key_places[:, None] >= 0)
    )
    return jnp.where(allowed, 0.0, MASKED).astype(F32)


def local(
    inputs, cotangent, norm_gains, norm_biases, w_attn, w_out, w_up, w_down,
    down_attn, up_attn, down_out, up_out, down_up, up_up, down_down, up_down,
    seg_lengths, parent_ids, adapter_ids,
):
    section = lax.axis_index("section")
    shard = lax.axis_index("fsdp")
    member = lax.axis_index("replica")
    shards = lax.axis_size("fsdp")
    members = lax.axis_size("replica")
    trees, per_tree = inputs.shape[0], inputs.shape[1]
    rows = trees * per_tree
    gain = norm_gains[0].astype(F32)
    shift = norm_biases[0].astype(F32)

    def gathered(weight):
        part = weight.shape[0] // members
        own = lax.dynamic_slice_in_dim(weight, member * part, part, 0)
        return lax.all_gather(own, ("fsdp", "replica"), axis=0, tiled=True)

    stacks = (down_attn, up_attn, down_out, up_out, down_up, up_up, down_down, up_down)
    widths = [stack.shape[3] for stack in stacks]
    starts = [sum(widths[:i]) for i in range(len(widths))]
    chosen = adapter_ids[:, 0, 0]
    picked = jnp.concatenate(
        [
            jnp.concatenate(
                [lax.dynamic_index_in_dim(stack[0], chosen[m], 0, keepdims=False) for m in range(trees)],
                axis=0,
            )
            for stack in stacks
        ],
        axis=1,
    )
    maps = lax.all_gather(picked, "fsdp", axis=0)
    maps = [
        jnp.moveaxis(maps[:, :, at : at + width], 0, 1).reshape(trees * RANK, shards * width)
        for at, width in zip(starts, widths)
    ]
    dn_attn, up_attn_, dn_out, up_out_, dn_up, up_up_, dn_down, up_down_ = maps

    attn_parts = gathered(w_attn[0]).reshape(shards, D, w_attn.shape[2])
    attn_full = jnp.moveaxis(attn_parts, 0, 1).reshape(D, shards * w_attn.shape[2])
    w_q, w_kv = attn_full[:, :D], attn_full[:, D:]
    out_parts = gathered(w_out[0]).reshape(shards, D, w_out.shape[2])
    out_full = jnp.moveaxis(out_parts, 0, 1).reshape(D, D)
    up_parts = gathered(w_up[0]).reshape(shards, D, w_up.shape[2])
    down_full = gathered(w_down[0])
    owners = lax.all_gather(chosen, "replica", axis=0, tiled=True)

    query_places = shard * per_tree + jnp.arange(per_tree, dtype=jnp.int32)
    key_places = jnp.concatenate(
        [(shard - s) * per_tree + jnp.arange(per_tree, dtype=jnp.int32) for s in range(shards)]
    )
    biases = [
        key_bias(seg_lengths[m, 0], parent_ids[m, 0], query_places, key_places)
        for m in range(trees)
    ]

    def tree(value, m):
        return value[m * per_tree : (m + 1) * per_tree]

    def to_higher(value, steps):
        return lax.ppermute(value, "fsdp", [(i, i + steps) for i in range(shards - steps)])

    def to_lower(value, steps):
        return lax.ppermute(value, "fsdp", [(i + steps, i) for i in range(shards - steps)])

    def forward(x):
        a = layer_norm(x, gain[0], shift[0]).astype(BF)
        u1 = masked(dot(a, dn_attn, NT), per_tree)
        kv = (dot(a, w_kv) + dot(u1, up_attn_[:, D:])).astype(BF)
        kv_blocks = [
            [tree(kv, m)] + [to_higher(tree(kv, m), s) for s in range(1, shards)]
            for m in range(trees)
        ]
        q = ((dot(a, w_q) + dot(u1, up_attn_[:, :D])) * (INV_ROOT * LOG2E)).astype(BF)
        mixed = [attention_forward(tree(q, m), kv_blocks[m], biases[m]) for m in range(trees)]
        o = jnp.concatenate([part[0] for part in mixed], axis=0)
        u2 = masked(dot(o, dn_out, NT), per_tree)
        x2 = x + (dot(o, out_full) + dot(u2, up_out_))
        b = layer_norm(x2, gain[1], shift[1]).astype(BF)
        y, g, gp, u3, u4 = mlp_forward(
            b, x2, up_parts, down_full, up_up_, dn_down, dn_up, up_down_
        )
        kept = (x, a, u1, q, kv_blocks, mixed, o, u2, x2, b, g, gp, u3, u4)
        return y.astype(BF), kept

    def backward(dy, kept):
        x, a, u1, q, kv_blocks, mixed, o, u2, x2, b, g, gp, u3, u4 = kept
        dx2, g_up_up, g_dn_down, g_dn_up, g_up_down = mlp_backward(
            dy, b, x2, gain[1:2], up_parts, down_full, g, gp, u3, u4,
            up_up_, dn_down, dn_up, up_down_,
        )
        dr = dx2.astype(BF)
        du2 = masked(dot(dr, up_out_, NT), per_tree)
        do = (dot(dr, out_full, NT) + dot(du2, dn_out)).astype(BF)
        g_up_out = dot(u2, dr, TN)
        g_dn_out = dot(du2, o, TN)
        joined = []
        for m in range(trees):
            dq, dkv = attention_backward(
                tree(q, m), tree(do, m), tree(o, m), kv_blocks[m], biases[m], mixed[m][1]
            )
            total = dkv[0].astype(F32)
            for s in range(1, shards):
                total = total + to_lower(dkv[s], s).astype(F32)
            joined.append(jnp.concatenate([dq, total.astype(BF)], axis=1))
        joined = jnp.concatenate(joined, axis=0)
        du1 = masked(dot(joined, up_attn_, NT), per_tree)
        da = (dot(joined, attn_full, NT) + dot(du1, dn_attn)).astype(BF).astype(F32)
        g_up_attn = dot(u1, joined, TN)
        g_dn_attn = dot(du1, a, TN)
        dx = dx2 + layer_norm_back(x, gain[0], da)
        grads = (
            g_dn_attn, g_up_attn, g_dn_out, g_up_out, g_dn_up, g_up_up, g_dn_down, g_up_down
        )
        return dx.astype(BF), grads

    own = inputs.reshape(rows, D)
    first, _ = forward(own.astype(F32))
    arrived = lax.ppermute(first, "section", [(0, 1)])
    layer_out, kept = forward(jnp.where(section == 0, own, arrived).astype(F32))

    own_grad = cotangent.reshape(rows, D)
    last, _ = backward(own_grad.astype(F32), kept)
    arrived = lax.ppermute(last, "section", [(1, 0)])
    in_grad, grads = backward(jnp.where(section == 1, own_grad, arrived).astype(F32), kept)

    slabs = jnp.concatenate(
        [
            grad.astype(BF).reshape(trees * RANK, shards, width)
            for grad, width in zip(grads, widths)
        ],
        axis=2,
    )
    slabs = lax.psum_scatter(
        jnp.moveaxis(slabs, 1, 0), "fsdp", scatter_dimension=0, tiled=False
    )
    slabs = lax.all_gather(slabs, "replica", axis=0)
    slabs = slabs.reshape(members * trees, RANK * sum(widths))
    adapters = down_attn.shape[1]
    pick = (jnp.arange(adapters, dtype=jnp.int32)[:, None] == owners[None, :]).astype(BF)
    totals = dot(pick, slabs).reshape(adapters, RANK, sum(widths))
    finals = [
        totals[None, :, :, at : at + width] for at, width in zip(starts, widths)
    ]
    return (
        layer_out.reshape(1, trees, per_tree, D),
        in_grad.reshape(1, trees, per_tree, D),
        *finals,
    )


def solution(mesh):
    rows = P(None, ("replica", "fsdp"), None)
    stack = P("section", None, None, "fsdp")
    placed = (
        (rows, rows)
        + (P("section", None, None),) * 2
        + (P("section", None, "fsdp"),) * 3
        + (P("section", "fsdp", None),)
        + (stack,) * 8
        + (P(None, "replica", None),) * 3
    )
    return jax.shard_map(
        local,
        mesh=mesh,
        in_specs=placed,
        out_specs=(P("section", None, ("replica", "fsdp"), None),) * 2 + (stack,) * 8,
        check_vma=False,
    )
```

time: 2860 us -> 1270 us (0.44)
  waiting for transfers between devices: 1350 us -> 569 us
  matrix products: 702 us -> 108 us
  blocking collectives: 383 us -> 4.26 us
  Pallas kernels: 0 us -> 351 us
  local copies, waits for them, and re-layouts: 266 us -> 121 us
  other arithmetic: 110 us -> 42.9 us
  starting transfers between devices: 8.89 us -> 46.5 us
    all_gather x6, waiting for transfers between devices: 1130 us -> 426 us  [the longest x4 393 us: gathered(): return lax.all_gather(own, ('fsdp', 'replica'), axis=0, tiled=True)]
    dot_general x120 -> x32, matrix products: 588 us -> 108 us  [dot(): return lax.dot_general(left, right, dims, preferred_element_type=F32)]
    all_gather x12 -> x0, blocking collectives: 383 us -> none  [the longest x1 153 us: local(): lax.all_gather(up_attn[0], 'fsdp', axis=2, tiled=True)]
    pallas_call x0 -> x12, Pallas kernels: none -> 351 us  [the longest x2 121 us: mlp_forward(): pl.pallas_call(functools.partial(mlp_forward_kernel, rows // trees), grid...]
    reduce_scatter x10 -> x1, waiting for transfers between devices: 146 us -> 26.9 us  [local(): lax.psum_scatter(jnp.moveaxis(slabs, 1, 0), 'fsdp', scatter_dimension=0,...]
    sub x3 -> x0, matrix products: 114 us -> none  [backward(): grad_probs - row_delta[:, :, None]]
    ppermute x4 -> x26, waiting for transfers between devices: 26.6 us -> 116 us  [the longest x1 48.6 us: local(): arrived = lax.ppermute(last, 'section', [(1, 0)])]
    mul x3 -> x0, local copies, waits for them, and re-layouts: 52.4 us -> none  [backward(): matrix_product(queries, keys_all[:, :HEAD_DIM].T) * inv_root]
  transfers between devices with their start and end apart: 22 -> 33, of which waited for: 13 -> 17; matrix products, arithmetic and copies ran while one was open for 16% -> 11% of each run, Pallas kernels for 0% -> 5%
where the time goes in v1:
time: 1270 us; the launch traced here: 1260 us
  waiting for transfers between devices  569 us (45%)
  Pallas kernels  351 us (28%)
  local copies, waits for them, and re-layouts  121 us (10%)
  matrix products  108 us (9%)
  starting transfers between devices  46.5 us (4%)
  other arithmetic  42.9 us (3%)
  between operations  20.6 us (2%)
    all_gather x4, waiting for transfers between devices, gathered(): return lax.all_gather(own, ('fsdp', 'replica'), axis=0, tiled=True)  393 us
    pallas_call x2, Pallas kernels, mlp_forward(): pl.pallas_call(functools.partial(mlp_forward_kernel, rows // trees), grid...  121 us
    pallas_call x2, Pallas kernels, mlp_backward(): pl.pallas_call(functools.partial(mlp_backward_kernel, rows // trees), gri...  119 us
    dot_general x32, matrix products, dot(): return lax.dot_general(left, right, dims, preferred_element_type=F32)  108 us
    pallas_call x4, Pallas kernels, attention_forward(): pl.pallas_call(functools.partial(attention_forward_kernel, blocks, heads)...  55.5 us
    pallas_call x4, Pallas kernels, attention_backward(): pl.pallas_call(functools.partial(attention_backward_kernel, blocks, heads...  55.3 us
    ppermute x1, waiting for transfers between devices, local(): arrived = lax.ppermute(last, 'section', [(1, 0)])  48.6 us
    ppermute x1, waiting for transfers between devices, local(): arrived = lax.ppermute(first, 'section', [(0, 1)])  40.9 us
  transfers between devices with their start and end apart: 33, of which 17 were waited for; matrix products, arithmetic and copies ran while one was open for 11% of the time, Pallas kernels for 5%

profile of v1, /device:TPU:0, one launch (start us, length us, event | category | flops | bytes accessed | tf_op | source)
XLA Modules:
  0.0 1263.1 jit_solution(5621275205920946416)
XLA Ops:
  20.7 3.3 constant_dynamic-slice_fusion.1
  24.1 3.3 constant_dynamic-slice_fusion
  36.0 2.2 fusion.33
  38.2 24.3 %all-gather.17.cloned.1.call-done = bf16[128,7232]{1,0:T(8,128)(2,1)} async-done(((bf16[32,7232]{1,0:T(8,128)(2,1)}), bf16[128,7232]{1,0:T(8,128)(2,1)}) %all-gather.17.cloned.1.call-update) | async-done | bytes 1851408 | tf_op jit(solution)/shard_map/all_gather | solution.py:425
  71.1 68.0 %all-gather.19.cloned.1.call-done = bf16[1,8192,512]{2,1,0:T(8,128)(2,1)} async-done(((bf16[1,512,512]{2,1,0:T(8,128)(2,1)}), bf16[1,8192,512]{2,1,0:T(8,128)(2,1)}) %all-gather.19.cloned.1.call-update) | async-done | bytes 8388624 | tf_op jit(solution)/shard_map/all_gather | solution.py:409
  139.1 11.7 copy.115
  150.8 73.6 %all-gather.15.cloned.1.call-done = bf16[1,8192,576]{1,2,0:T(8,128)(2,1)} async-done(((bf16[1,512,576]{1,2,0:T(8,128)(2,1)}), bf16[1,8192,576]{1,2,0:T(8,128)(2,1)}) %all-gather.15.cloned.1.call-update) | async-done | bytes 9437200 | tf_op jit(solution)/shard_map/all_gather | solution.py:409
  224.4 16.4 %reshape.318 = bf16[4,2048,576]{1,0,2:T(4,128)(2,1)} reshape(bf16[1,8192,576]{1,2,0:T(8,128)(2,1)} %all-gather.15.cloned.1.call-done) | data formatting | bytes 18874368 | tf_op jit(solution)/shard_map/reshape | solution.py:432
  240.8 12.6 copy.112
  253.4 2.7 fusion.41
  256.2 3.6 collective-permute-start.5
  261.1 2.5 collective-permute-start.3
  266.2 7.2 fusion.2
  278.3 13.9 %attention_forward.5 = (bf16[256,2048]{1,0:T(8,128)(2,1)}, f32[4,4,256]{2,1,0:T(4,128)}) custom-call(bf16[256,2048]{1,0:T(8,128)(2,1)} %get-tuple-element.135.q_ref, bf16[256,256]{1,0:T(8,128)(2,1)} %copy-done.35, bf16[256,256]{1,0:T(8,128)(2,1)} %copy-done.67, bf16[256,256]{1,0:T(8,128)(2,1)} %copy-done.66, bf16[256,256]{1,0:T(8,128)(2,1)} %copy-done.65, ...), custom_call_target="tpu_custom_call" | custom-call | flops 2147483648 | bytes 3145728 | tf_op jit(solution)/shard_map/attention_forward/pallas_call | solution.py:91
  294.9 14.0 %attention_forward.4 = (bf16[256,2048]{1,0:T(8,128)(2,1)}, f32[4,4,256]{2,1,0:T(4,128)}) custom-call(bf16[256,2048]{1,0:T(8,128)(2,1)} %get-tuple-element.136.q_ref, bf16[256,256]{1,0:T(8,128)(2,1)} %copy-done.34, bf16[256,256]{1,0:T(8,128)(2,1)} %copy-done.68, bf16[256,256]{1,0:T(8,128)(2,1)} %copy-done.64, bf16[256,256]{1,0:T(8,128)(2,1)} %copy-done.63, ...), custom_call_target="tpu_custom_call" | custom-call | flops 2147483648 | bytes 3145728 | tf_op jit(solution)/shard_map/attention_forward/pallas_call | solution.py:91
  308.9 2.3 constant_dynamic-update-slice_fusion.1
  312.3 5.3 fusion.63
  317.5 10.2 fusion.161
  331.8 73.0 %all-gather.21.cloned.1.call-done = bf16[1,8192,2048]{2,1,0:T(8,128)(2,1)} async-done(((bf16[1,512,2048]{2,1,0:T(8,128)(2,1)}), bf16[1,8192,2048]{2,1,0:T(8,128)(2,1)}) %all-gather.21.cloned.1.call-update) | async-done | bytes 33554448 | tf_op jit(solution)/shard_map/all_gather | solution.py:409
  404.7 178.5 %all-gather.23.cloned.1.call-done = bf16[1,8192,2048]{2,1,0:T(8,128)(2,1)} async-done(((bf16[1,512,2048]{2,1,0:T(8,128)(2,1)}), bf16[1,8192,2048]{2,1,0:T(8,128)(2,1)}) %all-gather.23.cloned.1.call-update) | async-done | bytes 33554448 | tf_op jit(solution)/shard_map/all_gather | solution.py:409
  583.2 60.6 %mlp_forward.2 = (f32[512,2048]{1,0:T(8,128)}, bf16[512,8192]{1,0:T(8,128)(2,1)}, bf16[512,8192]{1,0:T(8,128)(2,1)}, bf16[512,32]{1,0:T(8,128)(2,1)}, bf16[512,32]{1,0:T(8,128)(2,1)}) custom-call(bf16[512,2048]{1,0:T(8,128)(2,1)} %add_convert_fusion.5.b_ref, f32[512,2048]{1,0:T(8,128)} %copy-done.8, bf16[4,2048,2048]{2,1,0:T(8,128)(2,1)} %bitcast.322, ...), custom_call_target="tpu_custom_call" | custom-call | flops 34359738368 | bytes 94371840 | tf_op jit(solution)/shard_map/mlp_forward/pallas_call | solution.py:225
  643.8 4.0 convert_element_type.253
  647.7 4.7 collective-permute-start.6
  653.1 2.8 bitcast_convert_fusion.dy_ref
  655.9 40.9 %collective-permute-done.6 = bf16[512,2048]{1,0:T(8,128)(2,1)} collective-permute-done((bf16[512,2048]{1,0:T(8,128)(2,1)}, bf16[512,2048]{1,0:T(8,128)(2,1)}, u32[]{:S(2)}, u32[]{:S(2)}) %collective-permute-start.6) | collective-permute-done | bytes 2097184 | tf_op jit(solution)/shard_map/ppermute | solution.py:512
  696.7 2.3 convert_reduce_fusion
  702.4 5.2 collective-permute-start.12
  711.6 2.5 collective-permute-start.7
  714.1 2.8 fusion.85
  716.9 6.4 multiply_convert_fusion
  727.5 13.9 %attention_forward.6 = (bf16[256,2048]{1,0:T(8,128)(2,1)}, f32[4,4,256]{2,1,0:T(4,128)}) custom-call(bf16[256,2048]{1,0:T(8,128)(2,1)} %get-tuple-element.134.q_ref, bf16[256,256]{1,0:T(8,128)(2,1)} %copy-done.32, bf16[256,256]{1,0:T(8,128)(2,1)} %copy-done.59, bf16[256,256]{1,0:T(8,128)(2,1)} %copy-done.58, bf16[256,256]{1,0:T(8,128)(2,1)} %copy-done.57, ...), custom_call_target="tpu_custom_call" | custom-call | flops 2147483648 | bytes 3145728 | tf_op jit(solution)/shard_map/attention_forward/pallas_call | solution.py:91
  743.4 13.7 %attention_forward.7 = (bf16[256,2048]{1,0:T(8,128)(2,1)}, f32[4,4,256]{2,1,0:T(4,128)}) custom-call(bf16[256,2048]{1,0:T(8,128)(2,1)} %get-tuple-element.133.q_ref, bf16[256,256]{1,0:T(8,128)(2,1)} %copy-done.33, bf16[256,256]{1,0:T(8,128)(2,1)} %copy-done.62, bf16[256,256]{1,0:T(8,128)(2,1)} %copy-done.61, bf16[256,256]{1,0:T(8,128)(2,1)} %copy-done.60, ...), custom_call_target="tpu_custom_call" | custom-call | flops 2147483648 | bytes 3145728 | tf_op jit(solution)/shard_map/attention_forward/pallas_call | solution.py:91
  760.5 7.9 fusion.162
  771.1 60.6 %mlp_forward.3 = (f32[512,2048]{1,0:T(8,128)}, bf16[512,8192]{1,0:T(8,128)(2,1)}, bf16[512,8192]{1,0:T(8,128)(2,1)}, bf16[512,32]{1,0:T(8,128)(2,1)}, bf16[512,32]{1,0:T(8,128)(2,1)}) custom-call(bf16[512,2048]{1,0:T(8,128)(2,1)} %add_convert_fusion.4.b_ref, f32[512,2048]{1,0:T(8,128)} %copy-done.7, bf16[4,2048,2048]{2,1,0:T(8,128)(2,1)} %bitcast.323, ...), custom_call_target="tpu_custom_call" | custom-call | flops 34359738368 | bytes 94371840 | tf_op jit(solution)/shard_map/mlp_forward/pallas_call | solution.py:225
  831.7 59.6 %mlp_backward.2 = (f32[512,2048]{1,0:T(8,128)}, f32[32,8192]{1,0:T(8,128)}, f32[32,8192]{1,0:T(8,128)}, f32[32,2048]{1,0:T(8,128)}, f32[32,2048]{1,0:T(8,128)}) custom-call(f32[512,2048]{1,0:T(8,128)} %bitcast_convert_fusion.dy_ref, bf16[512,2048]{1,0:T(8,128)(2,1)} %add_convert_fusion.4.b_ref, f32[512,2048]{1,0:T(8,128)} %copy-done.7, ...), custom_call_target="tpu_custom_call" | custom-call | flops 34359738368 | bytes 98566144 | tf_op jit(solution)/shard_map/mlp_backward/pallas_call | solution.py:308
  891.3 11.1 fusion.66
  902.4 6.2 add_convert_fusion.3
  908.6 3.2 fusion.153
  911.7 13.8 %attention_backward.4 = (bf16[256,2048]{1,0:T(8,128)(2,1)}, bf16[4,256,256]{2,1,0:T(8,128)(2,1)}) custom-call(bf16[256,2048]{1,0:T(8,128)(2,1)} %get-tuple-element.134.q_ref, bf16[256,2048]{1,0:T(8,128)(2,1)} %get-tuple-element.131.do_ref, bf16[256,2048]{1,0:T(8,128)(2,1)} %get-tuple-element.39.o_ref, bf16[256,256]{1,0:T(8,128)(2,1)} %copy-done.32, ...), custom_call_target="tpu_custom_call" | custom-call | flops 5368709120 | bytes 5242880 | tf_op jit(solution)/shard_map/attention_backward/pallas_call | solution.py:156
  930.5 13.8 %attention_backward.5 = (bf16[256,2048]{1,0:T(8,128)(2,1)}, bf16[4,256,256]{2,1,0:T(8,128)(2,1)}) custom-call(bf16[256,2048]{1,0:T(8,128)(2,1)} %get-tuple-element.133.q_ref, bf16[256,2048]{1,0:T(8,128)(2,1)} %get-tuple-element.132.do_ref, bf16[256,2048]{1,0:T(8,128)(2,1)} %get-tuple-element.40.o_ref, bf16[256,256]{1,0:T(8,128)(2,1)} %copy-done.33, ...), custom_call_target="tpu_custom_call" | custom-call | flops 5368709120 | bytes 5242880 | tf_op jit(solution)/shard_map/attention_backward/pallas_call | solution.py:156
  950.2 2.2 collective-permute-done.16
  952.4 7.1 collective-permute-done.18
  959.5 3.3 collective-permute-done.17
  963.8 9.4 fusion.70
  973.2 6.3 fusion.35
  979.5 4.7 fusion.19
  985.5 48.6 %collective-permute-done.19 = bf16[512,2048]{1,0:T(8,128)(2,1)} collective-permute-done((bf16[512,2048]{1,0:T(8,128)(2,1)}, bf16[512,2048]{1,0:T(8,128)(2,1)}, u32[]{:S(2)}, u32[]{:S(2)}) %collective-permute-start.19) | collective-permute-done | bytes 2097184 | tf_op jit(solution)/shard_map/ppermute | solution.py:517
  1034.1 4.4 fusion.38.dy_ref
  1038.5 59.1 %mlp_backward.3 = (f32[512,2048]{1,0:T(8,128)}, f32[32,8192]{1,0:T(8,128)}, f32[32,8192]{1,0:T(8,128)}, f32[32,2048]{1,0:T(8,128)}, f32[32,2048]{1,0:T(8,128)}) custom-call(f32[512,2048]{1,0:T(8,128)} %fusion.38.dy_ref, bf16[512,2048]{1,0:T(8,128)(2,1)} %add_convert_fusion.4.b_ref, f32[512,2048]{1,0:T(8,128)} %copy-done.7, ...), custom_call_target="tpu_custom_call" | custom-call | flops 34359738368 | bytes 98566144 | tf_op jit(solution)/shard_map/mlp_backward/pallas_call | solution.py:308
  1097.6 8.3 fusion.141
  1113.0 13.9 %attention_backward.7 = (bf16[256,2048]{1,0:T(8,128)(2,1)}, bf16[4,256,256]{2,1,0:T(8,128)(2,1)}) custom-call(bf16[256,2048]{1,0:T(8,128)(2,1)} %get-tuple-element.133.q_ref, bf16[256,2048]{1,0:T(8,128)(2,1)} %get-tuple-element.130.do_ref, bf16[256,2048]{1,0:T(8,128)(2,1)} %get-tuple-element.40.o_ref, bf16[256,256]{1,0:T(8,128)(2,1)} %copy-done.33, ...), custom_call_target="tpu_custom_call" | custom-call | flops 5368709120 | bytes 5242880 | tf_op jit(solution)/shard_map/attention_backward/pallas_call | solution.py:156
  1131.9 13.8 %attention_backward.6 = (bf16[256,2048]{1,0:T(8,128)(2,1)}, bf16[4,256,256]{2,1,0:T(8,128)(2,1)}) custom-call(bf16[256,2048]{1,0:T(8,128)(2,1)} %get-tuple-element.134.q_ref, bf16[256,2048]{1,0:T(8,128)(2,1)} %get-tuple-element.129.do_ref, bf16[256,2048]{1,0:T(8,128)(2,1)} %get-tuple-element.39.o_ref, bf16[256,256]{1,0:T(8,128)(2,1)} %copy-done.32, ...), custom_call_target="tpu_custom_call" | custom-call | flops 5368709120 | bytes 5242880 | tf_op jit(solution)/shard_map/attention_backward/pallas_call | solution.py:156
  1153.9 6.2 collective-permute-done.22
  1160.0 3.8 collective-permute-done.21
  1171.3 3.8 concatenate.79
  1176.5 4.3 all-reduce
  1180.8 3.8 convert_element_type.261
  1184.6 26.9 %reduce-scatter.2.cloned.1.call-done = bf16[1,32,7232]{2,1,0:T(8,128)(2,1)} async-done(((bf16[4,32,7232]{2,1,0:T(8,128)(2,1)}), bf16[1,32,7232]{2,1,0:T(8,128)(2,1)}) %reduce-scatter.2.cloned.1.call-update) | async-done | bytes 462864 | tf_op jit(solution)/shard_map/reduce_scatter | solution.py:527
  1211.6 8.6 fusion.151
  1222.5 2.8 fusion.24
  1225.3 8.3 all-gather.13.cloned.1.call-done
  1233.6 3.6 reshape.363
  1239.2 3.6 reshape.365
  1242.9 3.3 reshape.366
  (348 shorter events, 118.0 us)
Async XLA Ops:
  7.2 55.4 %all-gather.17.cloned.1.call-start = ((), (), s32[]{:S(2)}) async-start(), calls=%async_computation.4 | async-start | bytes 2334720 | tf_op jit(solution)/shard_map/all_gather | solution.py:425
  17.8 121.3 %all-gather.19.cloned.1.call-start = ((), (), s32[]{:S(2)}) async-start(), calls=%async_computation.5 | async-start | bytes 8912896 | tf_op jit(solution)/shard_map/all_gather | solution.py:409
  19.7 204.7 %all-gather.15.cloned.1.call-start = ((), (), s32[]{:S(2)}) async-start(), calls=%async_computation.3 | async-start | bytes 10027008 | tf_op jit(solution)/shard_map/all_gather | solution.py:409
  20.7 384.1 %all-gather.21.cloned.1.call-start = ((), (), s32[]{:S(2)}) async-start(), calls=%async_computation.6 | async-start | bytes 35651584 | tf_op jit(solution)/shard_map/all_gather | solution.py:409
  24.1 559.1 %all-gather.23.cloned.1.call-start = ((), (), s32[]{:S(2)}) async-start(), calls=%async_computation.7 | async-start | bytes 35651584 | tf_op jit(solution)/shard_map/all_gather | solution.py:409
  27.5 1184.1 %reduce-scatter.2.cloned.1.call-start = ((), (), s32[]{:S(2)}) async-start(), calls=%async_computation.1 | async-start | bytes 2334720 | tf_op jit(solution)/shard_map/reduce_scatter | solution.py:527
  28.6 1077.3 %copy-start.46 = (pred[32]{0:T(512)(128)(4,1)}, pred[32]{0:T(512)(128)(4,1)S(1)}, u32[]{:S(2)}) copy-start(pred[32]{0:T(512)(128)(4,1)S(1)} %compare_and_fusion.2) | copy-start | bytes 100
  28.7 1077.3 %copy-start.48 = (pred[512]{0:T(512)(128)(4,1)}, pred[512]{0:T(512)(128)(4,1)S(1)}, u32[]{:S(2)}) copy-start(pred[512]{0:T(512)(128)(4,1)S(1)} %fusion.135) | copy-start | bytes 1540
  28.7 1077.3 %copy-start.50 = (s32[32]{0:T(128)}, s32[32]{0:T(128)S(1)}, u32[]{:S(2)}) copy-start(s32[32]{0:T(128)S(1)} %get-tuple-element.206) | copy-start | bytes 388
  28.7 1077.3 %copy-start.52 = (s32[32]{0:T(128)}, s32[32]{0:T(128)S(1)}, u32[]{:S(2)}) copy-start(s32[32]{0:T(128)S(1)} %get-tuple-element.207) | copy-start | bytes 388
  28.8 1077.2 %copy-start.36 = (s32[512]{0:T(512)}, s32[512]{0:T(512)S(1)}, u32[]{:S(2)}) copy-start(s32[512]{0:T(512)S(1)} %get-tuple-element.204) | copy-start | bytes 6148
  28.8 1077.2 %copy-start.38 = (s32[512]{0:T(512)}, s32[512]{0:T(512)S(1)}, u32[]{:S(2)}) copy-start(s32[512]{0:T(512)S(1)} %get-tuple-element.205) | copy-start | bytes 6148
  33.9 945.6 %copy-start.22 = (f32[1,1,2048]{2,1,0:T(1,128)}, f32[1,1,2048]{2,1,0:T(1,128)S(1)}, u32[]{:S(2)}) copy-start(f32[1,1,2048]{2,1,0:T(1,128)S(1)} %get-tuple-element.177) | copy-start | bytes 24580
  69.3 903.9 %copy-start.14 = (bf16[4,4,8,512]{3,2,0,1:T(8,128)(2,1)}, bf16[4,4,8,512]{3,2,0,1:T(8,128)(2,1)S(1)}, u32[]{:S(2)}) copy-start(bf16[4,4,8,512]{3,2,0,1:T(8,128)(2,1)S(1)} %copy.146) | copy-start | bytes 393220
  256.2 17.2 %copy-start.35 = (bf16[256,256]{1,0:T(8,128)(2,1)}, bf16[256,256]{1,0:T(8,128)(2,1)S(1)}, u32[]{:S(2)}) copy-start(bf16[256,256]{1,0:T(8,128)(2,1)S(1)} %get-tuple-element.162.refs_0_) | copy-start | bytes 393220
  256.2 19.4 %copy-start.34 = (bf16[256,256]{1,0:T(8,128)(2,1)}, bf16[256,256]{1,0:T(8,128)(2,1)S(1)}, u32[]{:S(2)}) copy-start(bf16[256,256]{1,0:T(8,128)(2,1)S(1)} %get-tuple-element.163.refs_0_) | copy-start | bytes 393220
  256.2 19.4 %collective-permute-start.5 = (bf16[256,256]{1,0:T(8,128)(2,1)S(1)}, bf16[256,256]{1,0:T(8,128)(2,1)S(1)}, u32[]{:S(2)}, u32[]{:S(2)}) collective-permute-start(bf16[256,256]{1,0:T(8,128)(2,1)S(1)} %get-tuple-element.162.refs_0_), channel_id=1, source_target_pairs={{0,12},{1,13},{2,14},{3,15},{16,28},{17,29},{18,30},{19,31}} | collective-permute-start | bytes 393224 | tf_op jit(solution)/shard_map/ppermute | solution.py:454
  259.8 17.1 %collective-permute-start.4 = (bf16[256,256]{1,0:T(8,128)(2,1)S(1)}, bf16[256,256]{1,0:T(8,128)(2,1)S(1)}, u32[]{:S(2)}, u32[]{:S(2)}) collective-permute-start(bf16[256,256]{1,0:T(8,128)(2,1)S(1)} %get-tuple-element.162.refs_0_), channel_id=1, source_target_pairs={{0,8},{4,12},{1,9},{5,13},{2,10},{6,14},{3,11},{7,15},{16,24},{20,... | collective-permute-start | bytes 393224 | tf_op jit(solution)/shard_map/ppermute | solution.py:454
  261.1 16.6 %collective-permute-start.3 = (bf16[256,256]{1,0:T(8,128)(2,1)S(1)}, bf16[256,256]{1,0:T(8,128)(2,1)S(1)}, u32[]{:S(2)}, u32[]{:S(2)}) collective-permute-start(bf16[256,256]{1,0:T(8,128)(2,1)S(1)} %get-tuple-element.162.refs_0_), channel_id=1, source_target_pairs={{0,4},{4,8},{8,12},{1,5},{5,9},{9,13},{2,6},{6,10},{10,14},{3,7},{... | collective-permute-start | bytes 393224 | tf_op jit(solution)/shard_map/ppermute | solution.py:454
  263.6 28.7 %collective-permute-start.2 = (bf16[256,256]{1,0:T(8,128)(2,1)S(1)}, bf16[256,256]{1,0:T(8,128)(2,1)S(1)}, u32[]{:S(2)}, u32[]{:S(2)}) collective-permute-start(bf16[256,256]{1,0:T(8,128)(2,1)S(1)} %get-tuple-element.163.refs_0_), channel_id=1, source_target_pairs={{0,12},{1,13},{2,14},{3,15},{16,28},{17,29},{18,30},{19,31}} | collective-permute-start | bytes 393224 | tf_op jit(solution)/shard_map/ppermute | solution.py:454
  264.9 27.4 %collective-permute-start.1 = (bf16[256,256]{1,0:T(8,128)(2,1)S(1)}, bf16[256,256]{1,0:T(8,128)(2,1)S(1)}, u32[]{:S(2)}, u32[]{:S(2)}) collective-permute-start(bf16[256,256]{1,0:T(8,128)(2,1)S(1)} %get-tuple-element.163.refs_0_), channel_id=1, source_target_pairs={{0,8},{4,12},{1,9},{5,13},{2,10},{6,14},{3,11},{7,15},{16,24},{20,... | collective-permute-start | bytes 393224 | tf_op jit(solution)/shard_map/ppermute | solution.py:454
  275.6 18.6 %collective-permute-start = (bf16[256,256]{1,0:T(8,128)(2,1)S(1)}, bf16[256,256]{1,0:T(8,128)(2,1)S(1)}, u32[]{:S(2)}, u32[]{:S(2)}) collective-permute-start(bf16[256,256]{1,0:T(8,128)(2,1)S(1)} %get-tuple-element.163.refs_0_), channel_id=1, source_target_pairs={{0,4},{4,8},{8,12},{1,5},{5,9},{9,13},{2,6},{6,10},{10,14},{3,7},{... | collective-permute-start | bytes 393224 | tf_op jit(solution)/shard_map/ppermute | solution.py:454
  294.9 16.3 %copy-start.18 = (bf16[256,2048]{1,0:T(8,128)(2,1)S(1)}, bf16[256,2048]{1,0:T(8,128)(2,1)}, u32[]{:S(2)}) copy-start(bf16[256,2048]{1,0:T(8,128)(2,1)} %get-tuple-element.37) | copy-start | bytes 3145732
  647.7 49.0 %collective-permute-start.6 = (bf16[512,2048]{1,0:T(8,128)(2,1)}, bf16[512,2048]{1,0:T(8,128)(2,1)}, u32[]{:S(2)}, u32[]{:S(2)}) collective-permute-start(bf16[512,2048]{1,0:T(8,128)(2,1)} %convert_element_type.253), channel_id=1, source_target_pairs={{0,16},{1,17},{2,18},{3,19},{4,20},{5,21},{6,22},{7,23},{8,24},{9,... | collective-permute-start | bytes 6291464 | tf_op jit(solution)/shard_map/ppermute | solution.py:512
  653.1 48.5 %slice-start = ((s8[9437184]{0:T(1024)(128)(4,1)}), s8[4194304]{0:T(1024)(128)(4,1)S(1)}, s32[]{:S(2)}) async-start(s8[9437184]{0:T(1024)(128)(4,1)} %bitcast.247), calls=%async_computation.8 | async-start | bytes 8388608
  655.9 45.7 %slice-start.1 = ((s8[9437184]{0:T(1024)(128)(4,1)}), s8[4194304]{0:T(1024)(128)(4,1)S(1)}, s32[]{:S(2)}) async-start(s8[9437184]{0:T(1024)(128)(4,1)} %bitcast.247), calls=%async_computation.9 | async-start | bytes 8388608
  699.0 280.5 %copy-start.41 = (f32[512]{0:T(512)}, f32[512]{0:T(512)S(1)}, u32[]{:S(2)}) copy-start(f32[512]{0:T(512)S(1)} %broadcast_multiply_fusion.5) | copy-start | bytes 6148
  699.7 279.8 %copy-start.43 = (f32[512]{0:T(512)}, f32[512]{0:T(512)S(1)}, u32[]{:S(2)}) copy-start(f32[512]{0:T(512)S(1)} %add_rsqrt_fusion.1) | copy-start | bytes 6148
  700.6 16.3 %copy-start.5 = (bf16[512,2048]{1,0:T(8,128)(2,1)}, bf16[512,2048]{1,0:T(8,128)(2,1)S(1)}, u32[]{:S(2)}) copy-start(bf16[512,2048]{1,0:T(8,128)(2,1)S(1)} %fusion.14) | copy-start | bytes 6291460
  702.4 20.9 %copy-start.32 = (bf16[256,256]{1,0:T(8,128)(2,1)}, bf16[256,256]{1,0:T(8,128)(2,1)S(1)}, u32[]{:S(2)}) copy-start(bf16[256,256]{1,0:T(8,128)(2,1)S(1)} %get-tuple-element.161.refs_0_) | copy-start | bytes 393220
  702.4 22.4 %copy-start.33 = (bf16[256,256]{1,0:T(8,128)(2,1)}, bf16[256,256]{1,0:T(8,128)(2,1)S(1)}, u32[]{:S(2)}) copy-start(bf16[256,256]{1,0:T(8,128)(2,1)S(1)} %get-tuple-element.160.refs_0_) | copy-start | bytes 393220
  702.4 40.2 %collective-permute-start.12 = (bf16[256,256]{1,0:T(8,128)(2,1)S(1)}, bf16[256,256]{1,0:T(8,128)(2,1)S(1)}, u32[]{:S(2)}, u32[]{:S(2)}) collective-permute-start(bf16[256,256]{1,0:T(8,128)(2,1)S(1)} %get-tuple-element.160.refs_0_), channel_id=1, source_target_pairs={{0,12},{1,13},{2,14},{3,15},{16,28},{17,29},{18,30},{19,31}} | collective-permute-start | bytes 393224 | tf_op jit(solution)/shard_map/ppermute | solution.py:454
  707.7 35.0 %collective-permute-start.11 = (bf16[256,256]{1,0:T(8,128)(2,1)S(1)}, bf16[256,256]{1,0:T(8,128)(2,1)S(1)}, u32[]{:S(2)}, u32[]{:S(2)}) collective-permute-start(bf16[256,256]{1,0:T(8,128)(2,1)S(1)} %get-tuple-element.160.refs_0_), channel_id=1, source_target_pairs={{0,8},{4,12},{1,9},{5,13},{2,10},{6,14},{3,11},{7,15},{16,24},{20,... | collective-permute-start | bytes 393224 | tf_op jit(solution)/shard_map/ppermute | solution.py:454
  709.0 15.8 %collective-permute-start.9 = (bf16[256,256]{1,0:T(8,128)(2,1)S(1)}, bf16[256,256]{1,0:T(8,128)(2,1)S(1)}, u32[]{:S(2)}, u32[]{:S(2)}) collective-permute-start(bf16[256,256]{1,0:T(8,128)(2,1)S(1)} %get-tuple-element.161.refs_0_), channel_id=1, source_target_pairs={{0,12},{1,13},{2,14},{3,15},{16,28},{17,29},{18,30},{19,31}} | collective-permute-start | bytes 393224 | tf_op jit(solution)/shard_map/ppermute | solution.py:454
  710.3 16.5 %collective-permute-start.8 = (bf16[256,256]{1,0:T(8,128)(2,1)S(1)}, bf16[256,256]{1,0:T(8,128)(2,1)S(1)}, u32[]{:S(2)}, u32[]{:S(2)}) collective-permute-start(bf16[256,256]{1,0:T(8,128)(2,1)S(1)} %get-tuple-element.161.refs_0_), channel_id=1, source_target_pairs={{0,8},{4,12},{1,9},{5,13},{2,10},{6,14},{3,11},{7,15},{16,24},{20,... | collective-permute-start | bytes 393224 | tf_op jit(solution)/shard_map/ppermute | solution.py:454
  711.6 15.2 %collective-permute-start.7 = (bf16[256,256]{1,0:T(8,128)(2,1)S(1)}, bf16[256,256]{1,0:T(8,128)(2,1)S(1)}, u32[]{:S(2)}, u32[]{:S(2)}) collective-permute-start(bf16[256,256]{1,0:T(8,128)(2,1)S(1)} %get-tuple-element.161.refs_0_), channel_id=1, source_target_pairs={{0,4},{4,8},{8,12},{1,5},{5,9},{9,13},{2,6},{6,10},{10,14},{3,7},{... | collective-permute-start | bytes 393224 | tf_op jit(solution)/shard_map/ppermute | solution.py:454
  724.8 17.9 %collective-permute-start.10 = (bf16[256,256]{1,0:T(8,128)(2,1)S(1)}, bf16[256,256]{1,0:T(8,128)(2,1)S(1)}, u32[]{:S(2)}, u32[]{:S(2)}) collective-permute-start(bf16[256,256]{1,0:T(8,128)(2,1)S(1)} %get-tuple-element.160.refs_0_), channel_id=1, source_target_pairs={{0,4},{4,8},{8,12},{1,5},{5,9},{9,13},{2,6},{6,10},{10,14},{3,7},{... | collective-permute-start | bytes 393224 | tf_op jit(solution)/shard_map/ppermute | solution.py:454
  926.6 21.4 %collective-permute-start.13 = (bf16[256,256]{1,0:T(8,128)(2,1)S(1)}, bf16[256,256]{1,0:T(8,128)(2,1)S(1)}, u32[]{:S(2)}, u32[]{:S(2)}) collective-permute-start(bf16[256,256]{1,0:T(8,128)(2,1)S(1)} %get-tuple-element.150), channel_id=1, source_target_pairs={{4,0},{8,4},{12,8},{5,1},{9,5},{13,9},{6,2},{10,6},{14,10},{7,3},{... | collective-permute-start | bytes 393224 | tf_op jit(solution)/shard_map/ppermute | solution.py:457
  927.9 21.4 %collective-permute-start.15 = (bf16[256,256]{1,0:T(8,128)(2,1)S(1)}, bf16[256,256]{1,0:T(8,128)(2,1)S(1)}, u32[]{:S(2)}, u32[]{:S(2)}) collective-permute-start(bf16[256,256]{1,0:T(8,128)(2,1)S(1)} %get-tuple-element.151), channel_id=1, source_target_pairs={{12,0},{13,1},{14,2},{15,3},{28,16},{29,17},{30,18},{31,19}} | collective-permute-start | bytes 393224 | tf_op jit(solution)/shard_map/ppermute | solution.py:457
  929.2 20.1 %collective-permute-start.14 = (bf16[256,256]{1,0:T(8,128)(2,1)S(1)}, bf16[256,256]{1,0:T(8,128)(2,1)S(1)}, u32[]{:S(2)}, u32[]{:S(2)}) collective-permute-start(bf16[256,256]{1,0:T(8,128)(2,1)S(1)} %get-tuple-element.152), channel_id=1, source_target_pairs={{8,0},{12,4},{9,1},{13,5},{10,2},{14,6},{11,3},{15,7},{24,16},{28,... | collective-permute-start | bytes 393224 | tf_op jit(solution)/shard_map/ppermute | solution.py:457
  930.5 33.3 %copy-start.72 = (bf16[256,2048]{1,0:T(8,128)(2,1)S(1)}, bf16[256,2048]{1,0:T(8,128)(2,1)}, u32[]{:S(2)}) copy-start(bf16[256,2048]{1,0:T(8,128)(2,1)} %get-tuple-element.48) | copy-start | bytes 3145732
  945.3 7.1 collective-permute-start.16
  946.6 12.9 %collective-permute-start.18 = (bf16[256,256]{1,0:T(8,128)(2,1)S(1)}, bf16[256,256]{1,0:T(8,128)(2,1)S(1)}, u32[]{:S(2)}, u32[]{:S(2)}) collective-permute-start(bf16[256,256]{1,0:T(8,128)(2,1)S(1)} %get-tuple-element.154), channel_id=1, source_target_pairs={{12,0},{13,1},{14,2},{15,3},{28,16},{29,17},{30,18},{31,19}} | collective-permute-start | bytes 393224 | tf_op jit(solution)/shard_map/ppermute | solution.py:457
  947.9 14.8 %collective-permute-start.17 = (bf16[256,256]{1,0:T(8,128)(2,1)S(1)}, bf16[256,256]{1,0:T(8,128)(2,1)S(1)}, u32[]{:S(2)}, u32[]{:S(2)}) collective-permute-start(bf16[256,256]{1,0:T(8,128)(2,1)S(1)} %get-tuple-element.155), channel_id=1, source_target_pairs={{8,0},{12,4},{9,1},{13,5},{10,2},{14,6},{11,3},{15,7},{24,16},{28,... | collective-permute-start | bytes 393224 | tf_op jit(solution)/shard_map/ppermute | solution.py:457
  984.2 49.9 %collective-permute-start.19 = (bf16[512,2048]{1,0:T(8,128)(2,1)}, bf16[512,2048]{1,0:T(8,128)(2,1)}, u32[]{:S(2)}, u32[]{:S(2)}) collective-permute-start(bf16[512,2048]{1,0:T(8,128)(2,1)} %fusion.19), channel_id=1, source_target_pairs={{16,0},{17,1},{18,2},{19,3},{20,4},{21,5},{22,6},{23,7},{24,8},{25... | collective-permute-start | bytes 6291464 | tf_op jit(solution)/shard_map/ppermute | solution.py:517
  1128.0 21.9 %collective-permute-start.23 = (bf16[256,256]{1,0:T(8,128)(2,1)S(1)}, bf16[256,256]{1,0:T(8,128)(2,1)S(1)}, u32[]{:S(2)}, u32[]{:S(2)}) collective-permute-start(bf16[256,256]{1,0:T(8,128)(2,1)S(1)} %get-tuple-element.147), channel_id=1, source_target_pairs={{4,0},{8,4},{12,8},{5,1},{9,5},{13,9},{6,2},{10,6},{14,10},{7,3},{... | collective-permute-start | bytes 393224 | tf_op jit(solution)/shard_map/ppermute | solution.py:457
  1129.3 21.9 %collective-permute-start.25 = (bf16[256,256]{1,0:T(8,128)(2,1)S(1)}, bf16[256,256]{1,0:T(8,128)(2,1)S(1)}, u32[]{:S(2)}, u32[]{:S(2)}) collective-permute-start(bf16[256,256]{1,0:T(8,128)(2,1)S(1)} %get-tuple-element.148), channel_id=1, source_target_pairs={{12,0},{13,1},{14,2},{15,3},{28,16},{29,17},{30,18},{31,19}} | collective-permute-start | bytes 393224 | tf_op jit(solution)/shard_map/ppermute | solution.py:457
  1130.6 20.6 %collective-permute-start.24 = (bf16[256,256]{1,0:T(8,128)(2,1)S(1)}, bf16[256,256]{1,0:T(8,128)(2,1)S(1)}, u32[]{:S(2)}, u32[]{:S(2)}) collective-permute-start(bf16[256,256]{1,0:T(8,128)(2,1)S(1)} %get-tuple-element.149), channel_id=1, source_target_pairs={{8,0},{12,4},{9,1},{13,5},{10,2},{14,6},{11,3},{15,7},{24,16},{28,... | collective-permute-start | bytes 393224 | tf_op jit(solution)/shard_map/ppermute | solution.py:457
  1131.9 17.7 %copy-start.17 = (f32[32,8192]{1,0:T(8,128)S(1)}, f32[32,8192]{1,0:T(8,128)}, u32[]{:S(2)}) copy-start(f32[32,8192]{1,0:T(8,128)} %get-tuple-element.59) | copy-start | bytes 3145732
  1131.9 17.8 %copy-start.16 = (f32[32,8192]{1,0:T(8,128)S(1)}, f32[32,8192]{1,0:T(8,128)}, u32[]{:S(2)}) copy-start(f32[32,8192]{1,0:T(8,128)} %get-tuple-element.60) | copy-start | bytes 3145732
  1145.7 19.1 %copy-start.37 = (s32[512]{0:T(512)S(1)}, s32[512]{0:T(512)}, u32[]{:S(2)}) copy-start(s32[512]{0:T(512)} %copy-done.36) | copy-start | bytes 6148
  1145.7 19.1 %copy-start.39 = (s32[512]{0:T(512)S(1)}, s32[512]{0:T(512)}, u32[]{:S(2)}) copy-start(s32[512]{0:T(512)} %copy-done.38) | copy-start | bytes 6148
  1145.7 19.1 %copy-start.47 = (pred[32]{0:T(512)(128)(4,1)S(1)}, pred[32]{0:T(512)(128)(4,1)}, u32[]{:S(2)}) copy-start(pred[32]{0:T(512)(128)(4,1)} %copy-done.46) | copy-start | bytes 100
  1145.7 19.1 %copy-start.49 = (pred[512]{0:T(512)(128)(4,1)S(1)}, pred[512]{0:T(512)(128)(4,1)}, u32[]{:S(2)}) copy-start(pred[512]{0:T(512)(128)(4,1)} %copy-done.48) | copy-start | bytes 1540
  1145.7 19.1 %copy-start.51 = (s32[32]{0:T(128)S(1)}, s32[32]{0:T(128)}, u32[]{:S(2)}) copy-start(s32[32]{0:T(128)} %copy-done.50) | copy-start | bytes 388
  1145.7 19.1 %copy-start.53 = (s32[32]{0:T(128)S(1)}, s32[32]{0:T(128)}, u32[]{:S(2)}) copy-start(s32[32]{0:T(128)} %copy-done.52) | copy-start | bytes 388
  1145.8 19.1 %copy-start.70 = (bf16[256,2048]{1,0:T(8,128)(2,1)S(1)}, bf16[256,2048]{1,0:T(8,128)(2,1)}, u32[]{:S(2)}) copy-start(bf16[256,2048]{1,0:T(8,128)(2,1)} %get-tuple-element.56) | copy-start | bytes 3145732
  1145.8 19.1 %copy-start.71 = (bf16[256,2048]{1,0:T(8,128)(2,1)S(1)}, bf16[256,2048]{1,0:T(8,128)(2,1)}, u32[]{:S(2)}) copy-start(bf16[256,2048]{1,0:T(8,128)(2,1)} %get-tuple-element.54) | copy-start | bytes 3145732
  1147.0 6.9 collective-permute-start.20
  1148.3 11.7 collective-permute-start.22
  1149.8 14.0 %collective-permute-start.21 = (bf16[256,256]{1,0:T(8,128)(2,1)S(1)}, bf16[256,256]{1,0:T(8,128)(2,1)S(1)}, u32[]{:S(2)}, u32[]{:S(2)}) collective-permute-start(bf16[256,256]{1,0:T(8,128)(2,1)S(1)} %get-tuple-element.146), channel_id=1, source_target_pairs={{8,0},{12,4},{9,1},{13,5},{10,2},{14,6},{11,3},{15,7},{24,16},{28,... | collective-permute-start | bytes 393224 | tf_op jit(solution)/shard_map/ppermute | solution.py:457
  1175.1 36.5 %copy-start.29 = (bf16[256,256]{1,0:T(8,128)(2,1)S(1)}, bf16[256,256]{1,0:T(8,128)(2,1)}, u32[]{:S(2)}) copy-start(bf16[256,256]{1,0:T(8,128)(2,1)} %copy-done.28) | copy-start | bytes 393220
  1175.1 36.5 %copy-start.31 = (bf16[256,256]{1,0:T(8,128)(2,1)S(1)}, bf16[256,256]{1,0:T(8,128)(2,1)}, u32[]{:S(2)}) copy-start(bf16[256,256]{1,0:T(8,128)(2,1)} %copy-done.30) | copy-start | bytes 393220
  1175.1 58.5 %all-gather.13.cloned.1.call-start = ((), (), s32[]{:S(2)}) async-start(), calls=%async_computation.2 | async-start | bytes 2334720 | tf_op jit(solution)/shard_map/all_gather | solution.py:530
  (45 other events, 207.7 us)
Sparse Core Ops, SparseCore 0:
  17.9 44.6 all-gather.16
  65.3 73.7 all-gather.18
  141.8 82.5 all-gather.14
  225.9 178.8 all-gather.20
  406.2 176.9 all-gather.22
  1175.2 36.2 reduce-scatter.1
  1213.1 20.4 all-gather.12

commit v2 on v1

v2 whole, which is shorter than its diff:
```python
import functools
import math

import jax
import jax.numpy as jnp
from jax import lax
from jax.experimental import pallas as pl
from jax.experimental.pallas import tpu as pltpu
from jax.sharding import PartitionSpec as P

D = 2048
HEADS = 16
HEAD_DIM = 128
RANK = 16

NORM_EPS = 1e-05
MASKED = -1e30
BF = jnp.bfloat16
F32 = jnp.float32
INV_ROOT = HEAD_DIM ** (-0.5)
LOG2E = math.log2(math.e)
LN2 = math.log(2.0)
GELU_C = math.sqrt(2.0 / math.pi)
VMEM_LIMIT = 56 * 1024 * 1024

NN = (((1,), (0,)), ((), ()))
NT = (((1,), (1,)), ((), ()))
TN = (((0,), (0,)), ((), ()))


def dot(left, right, dims=NN):
    return lax.dot_general(left, right, dims, preferred_element_type=F32)


def params(steps=1):
    return pltpu.CompilerParams(
        dimension_semantics=("arbitrary",) * steps, vmem_limit_bytes=VMEM_LIMIT
    )


def layer_norm(rows, gain, shift):
    centre = rows - jnp.mean(rows, axis=-1, keepdims=True)
    spread = jnp.mean(centre * centre, axis=-1, keepdims=True)
    return centre * lax.rsqrt(spread + NORM_EPS) * gain + shift


def layer_norm_back(rows, gain, grad):
    centre = rows - jnp.mean(rows, axis=-1, keepdims=True)
    spread = jnp.mean(centre * centre, axis=-1, keepdims=True)
    scale = lax.rsqrt(spread + NORM_EPS)
    unit = centre * scale
    inner = grad * gain
    return scale * (
        inner
        - jnp.mean(inner, axis=-1, keepdims=True)
        - unit * jnp.mean(inner * unit, axis=-1, keepdims=True)
    )


def tree_mask(rows, per_tree):
    row = lax.broadcasted_iota(jnp.int32, (rows, (rows // per_tree) * RANK), 0)
    col = lax.broadcasted_iota(jnp.int32, (rows, (rows // per_tree) * RANK), 1)
    return (row // per_tree) == (col // RANK)


def masked(value, per_tree):
    return jnp.where(tree_mask(value.shape[0], per_tree), 2.0 * value, 0.0).astype(BF)


def attention_forward_kernel(blocks, heads, before, keep, q_ref, *refs):
    kv_refs, (bias_ref, *refs) = refs[:blocks], refs[blocks:]
    o_ref, lse_ref, *kept_refs = refs[before:]
    keys = jnp.concatenate([r[:, :HEAD_DIM] for r in kv_refs], axis=0)
    vals = jnp.concatenate([r[:, HEAD_DIM:] for r in kv_refs], axis=0)
    vals = jnp.concatenate([vals, jnp.ones_like(vals)], axis=1)
    if keep:
        for kept, given in zip(kept_refs, (q_ref, *kv_refs)):
            kept[...] = given[...]
    for h in range(heads):
        cols = slice(h * HEAD_DIM, (h + 1) * HEAD_DIM)
        scores = dot(q_ref[:, cols], keys, NT) + bias_ref[...]
        top = jnp.max(scores, axis=1, keepdims=True)
        probs = jnp.exp2(scores - top)
        mixed = dot(probs.astype(BF), vals)
        total = mixed[:, HEAD_DIM:]
        o_ref[:, cols] = (mixed[:, :HEAD_DIM] / total).astype(BF)
        lse_ref[0, h : h + 1, :] = (top + jnp.log2(total)).T[0:1, :]


def attention_forward(tree, trees, q, kv, bias, before, keep, heads=8):
    rows = q.shape[0]
    blocks = len(kv)
    wide = heads * HEAD_DIM
    steps = HEADS // heads
    whole = lambda i: (0, 0)
    mine = pl.BlockSpec((rows, wide), lambda i: (tree, i))
    pair = pl.BlockSpec((rows, 2 * HEAD_DIM), lambda i: (tree, 0))
    tall = jax.ShapeDtypeStruct((trees * rows, D), BF)
    outs = [tall, jax.ShapeDtypeStruct((trees * steps, heads, rows), F32)]
    out_specs = [mine, pl.BlockSpec((1, heads, rows), lambda i: (tree * steps + i, 0, 0))]
    if keep:
        outs += [tall] + [jax.ShapeDtypeStruct((trees * rows, 2 * HEAD_DIM), BF)] * blocks
        out_specs += [mine] + [pair] * blocks
    return pl.pallas_call(
        functools.partial(attention_forward_kernel, blocks, heads, len(before), keep),
        grid=(steps,),
        in_specs=[pl.BlockSpec((rows, wide), lambda i: (0, i))]
        + [pl.BlockSpec((rows, 2 * HEAD_DIM), whole)] * blocks
        + [pl.BlockSpec((rows, blocks * rows), whole)]
        + [pl.BlockSpec(memory_space=pl.ANY)] * len(before),
        out_specs=out_specs,
        out_shape=outs,
        input_output_aliases={blocks + 2 + i: i for i in range(len(before))},
        compiler_params=params(),
        cost_estimate=pl.CostEstimate(
            flops=8 * rows * rows * blocks * D,
            transcendentals=rows * rows * blocks * HEADS,
            bytes_accessed=4 * rows * D + 4 * rows * rows * blocks,
        ),
        name="attention_forward",
    )(q, *kv, bias, *before)


def attention_backward_kernel(blocks, heads, _, q_ref, do_ref, o_ref, *refs):
    kv_refs = refs[:blocks]
    bias_ref, lse_ref, dq_ref, *dkv_refs, acc_ref = refs[blocks:]
    rows = q_ref.shape[0]
    step = pl.program_id(0)

    @pl.when(step == 0)
    def _():
        acc_ref[...] = jnp.zeros_like(acc_ref)

    keys = jnp.concatenate([r[:, :HEAD_DIM] for r in kv_refs], axis=0)
    vals = jnp.concatenate([r[:, HEAD_DIM:] for r in kv_refs], axis=0)
    keys_t = keys.T
    for h in range(heads):
        cols = slice(h * HEAD_DIM, (h + 1) * HEAD_DIM)
        q, do = q_ref[:, cols], do_ref[:, cols]
        delta = jnp.sum(
            (do.astype(F32) * o_ref[:, cols].astype(F32)).T, axis=0, keepdims=True
        )
        scores = dot(keys, q, NT) + bias_ref[...]
        probs = jnp.exp2(scores - lse_ref[0, h : h + 1, :])
        dprobs = dot(vals, do, NT)
        dscores = (probs * (dprobs - delta)).astype(BF)
        acc_ref[:, :HEAD_DIM] += dot(dscores, q)
        acc_ref[:, HEAD_DIM:] += dot(probs.astype(BF), do)
        dq_ref[:, cols] = (dot(keys_t, dscores) * INV_ROOT).T.astype(BF)

    @pl.when(step == pl.num_programs(0) - 1)
    def _():
        for s in range(blocks):
            part = slice(s * rows, (s + 1) * rows)
            dkv_refs[s][:, :HEAD_DIM] = (acc_ref[part, :HEAD_DIM] * LN2).astype(BF)
            dkv_refs[s][:, HEAD_DIM:] = acc_ref[part, HEAD_DIM:].astype(BF)


def attention_backward(which, q, do, o, kv, bias, lse):
    rows = do.shape[0]
    blocks = len(kv)
    trees = q.shape[0] // rows
    heads = lse.shape[1]
    steps = lse.shape[0] // trees
    wide = heads * HEAD_DIM
    mine = lambda i, w: (w[1], i)
    pair = pl.BlockSpec((rows, 2 * HEAD_DIM), lambda i, w: (0, 0))
    dq, *dkv = pl.pallas_call(
        functools.partial(attention_backward_kernel, blocks, heads),
        grid_spec=pltpu.PrefetchScalarGridSpec(
            num_scalar_prefetch=1,
            grid=(steps,),
            in_specs=[
                pl.BlockSpec((rows, wide), mine),
                pl.BlockSpec((rows, wide), lambda i, w: (0, i)),
                pl.BlockSpec((rows, wide), mine),
            ]
            + [pl.BlockSpec((rows, 2 * HEAD_DIM), lambda i, w: (w[1], 0))] * blocks
            + [
                pl.BlockSpec((blocks * rows, rows), lambda i, w: (w[1], 0)),
                pl.BlockSpec((1, heads, rows), lambda i, w: (w[1] * steps + i, 0, 0)),
            ],
            out_specs=[pl.BlockSpec((rows, wide), lambda i, w: (0, i))] + [pair] * blocks,
            scratch_shapes=[pltpu.VMEM((blocks * rows, 2 * HEAD_DIM), F32)],
        ),
        out_shape=[jax.ShapeDtypeStruct((rows, D), BF)]
        + [jax.ShapeDtypeStruct((rows, 2 * HEAD_DIM), BF)] * blocks,
        compiler_params=params(),
        cost_estimate=pl.CostEstimate(
            flops=20 * rows * rows * blocks * D,
            transcendentals=rows * rows * blocks * HEADS,
            bytes_accessed=8 * rows * D + 4 * rows * rows * blocks,
        ),
        name="attention_backward",
    )(which, q, do, o, *kv, bias, lse)
    return dq, dkv


def assemble_kernel(wide, held_ref, full_ref):
    full_ref[...] = jnp.concatenate(
        [held_ref[z][:, :wide] for z in range(held_ref.shape[0])], axis=1
    )


def assemble(held, start, wide, block=256):
    shards, depth, _ = held.shape
    padded = -(-wide // 128) * 128
    return pl.pallas_call(
        functools.partial(assemble_kernel, wide),
        grid=(depth // block,),
        in_specs=[pl.BlockSpec((shards, block, padded), lambda i: (0, i, start // padded))],
        out_specs=pl.BlockSpec((block, shards * wide), lambda i: (i, 0)),
        out_shape=jax.ShapeDtypeStruct((depth, shards * wide), BF),
        compiler_params=params(),
        cost_estimate=pl.CostEstimate(
            flops=0, transcendentals=0, bytes_accessed=4 * shards * depth * padded
        ),
        name="assemble",
    )(held)


def entry_body(x, norm_ref, dn_ref, up_ref, w_ref, a_ref, u_ref, kv_ref):
    a = layer_norm(x.astype(F32), norm_ref[0:1, :], norm_ref[1:2, :]).astype(BF)
    a_ref[...] = a
    u = (2.0 * dot(a, dn_ref[...], NT)).astype(BF)
    u_ref[...] = u
    kv_ref[...] = (dot(a, w_ref[...]) + dot(u, up_ref[...])).astype(BF)


def entry_own_kernel(own_ref, *refs):
    entry_body(own_ref[...], *refs)


def entry_arrived_kernel(before, flag_ref, own_ref, arrived_ref, *refs):
    given, (a_ref, u_ref, kv_ref, x_all, a_all, u_all) = refs[:4], refs[4 + before :]
    x = jnp.where(flag_ref[0] == 1, own_ref[...], arrived_ref[...])
    x_all[...] = x
    entry_body(x, *given, a_ref, u_ref, kv_ref)
    a_all[...] = a_ref[...]
    u_all[0] = u_ref[...]


def entry(tree, trees, own, norm, dn, up, w, arrived=None, flag=None, before=()):
    rows = own.shape[0] // trees
    wide = 2 * HEAD_DIM
    last = D // wide
    whole = lambda i, *_: (0, 0)
    mine = pl.BlockSpec((rows, D), lambda i, *_: (tree, 0))
    row = pl.BlockSpec((rows, D), whole)
    ins, ins_specs = ([own], [mine]) if arrived is None else ([own, arrived], [mine, row])
    outs = [
        jax.ShapeDtypeStruct((rows, D), BF),
        jax.ShapeDtypeStruct((rows, RANK), BF),
        jax.ShapeDtypeStruct((rows, wide), BF),
    ]
    out_specs = [row, pl.BlockSpec((rows, RANK), whole), pl.BlockSpec((rows, wide), whole)]
    kernel = entry_own_kernel
    if arrived is not None:
        kernel = functools.partial(entry_arrived_kernel, len(before))
        outs += [jax.ShapeDtypeStruct((trees * rows, D), BF)] * 2
        outs += [jax.ShapeDtypeStruct((trees, rows, RANK), BF)]
        out_specs += [mine, mine, pl.BlockSpec((1, rows, RANK), lambda i, *_: (tree, 0, 0))]
    return pl.pallas_call(
        kernel,
        grid_spec=pltpu.PrefetchScalarGridSpec(
            num_scalar_prefetch=0 if arrived is None else 1,
            grid=(1,),
            in_specs=ins_specs
            + [
                pl.BlockSpec((2, D), whole),
                pl.BlockSpec((RANK, D), lambda i, *_: (tree, 0)),
                pl.BlockSpec((RANK, wide), lambda i, *_: (tree, last)),
                pl.BlockSpec((D, wide), lambda i, *_: (0, last)),
            ]
            + [pl.BlockSpec(memory_space=pl.ANY)] * len(before),
            out_specs=out_specs,
        ),
        out_shape=outs,
        input_output_aliases={7 + i: 3 + i for i in range(len(before))},
        compiler_params=params(),
        cost_estimate=pl.CostEstimate(
            flops=3 * rows * D * wide, transcendentals=0, bytes_accessed=8 * rows * D
        ),
        name="entry",
    )(*([] if arrived is None else [flag]), *ins, norm, dn, up, w, *before)


def queries_kernel(a_ref, u_ref, up_ref, w_ref, q_ref):
    q = dot(a_ref[...], w_ref[...]) + dot(u_ref[...], up_ref[...])
    q_ref[...] = (q * (INV_ROOT * LOG2E)).astype(BF)


def queries(tree, a, u, up, w, block=1024):
    rows = a.shape[0]
    return pl.pallas_call(
        queries_kernel,
        grid=(D // block,),
        in_specs=[
            pl.BlockSpec((rows, D), lambda i: (0, 0)),
            pl.BlockSpec((rows, RANK), lambda i: (0, 0)),
            pl.BlockSpec((RANK, block), lambda i: (tree, i)),
            pl.BlockSpec((D, block), lambda i: (0, i)),
        ],
        out_specs=pl.BlockSpec((rows, block), lambda i: (0, i)),
        out_shape=jax.ShapeDtypeStruct((rows, D), BF),
        compiler_params=params(),
        cost_estimate=pl.CostEstimate(
            flops=2 * rows * D * D, transcendentals=0, bytes_accessed=2 * D * D
        ),
        name="queries",
    )(a, u, up, w)


def mix(step, rows, o_ref, x_ref, dn_ref, up_ref, w_ref, u_ref, sum_ref):
    @pl.when(step == 0)
    def _():
        sum_ref[...] = x_ref[...].astype(F32)
        u_ref[...] = masked(dot(o_ref[...], dn_ref[...], NT), rows)

    block = w_ref.shape[2]
    cols = pl.ds(pl.multiple_of(step * block, block), block)
    sum_ref[:, cols] += dot(o_ref[...], w_ref[0]) + dot(u_ref[...], up_ref[...])


def normed(sum_ref, norm_ref):
    return layer_norm(sum_ref[...], norm_ref[0:1, :], norm_ref[1:2, :]).astype(BF)


def mixing_kernel(rows, o_ref, x_ref, norm_ref, dn_ref, up_ref, w_ref, x2_ref, b_ref, u_ref):
    step = pl.program_id(0)
    mix(step, rows, o_ref, x_ref, dn_ref, up_ref, w_ref, u_ref, x2_ref)

    @pl.when(step == pl.num_programs(0) - 1)
    def _():
        b_ref[...] = normed(x2_ref, norm_ref)


def mixing(o, x, norm, dn, up, held, part):
    total, wide = o.shape[0], dn.shape[0]
    shards = held.shape[0]
    block = D // shards
    at = part // block
    whole = lambda i: (0, 0)
    single = pl.Buffered(1)
    return pl.pallas_call(
        functools.partial(mixing_kernel, total * RANK // wide),
        grid=(shards,),
        in_specs=[pl.BlockSpec((total, D), whole, pipeline_mode=single)] * 2
        + [
            pl.BlockSpec((2, D), whole),
            pl.BlockSpec((wide, D), whole),
            pl.BlockSpec((wide, block), lambda i: (0, i)),
            pl.BlockSpec((1, D, block), lambda i: (i, 0, at)),
        ],
        out_specs=[pl.BlockSpec((total, D), whole), pl.BlockSpec((total, D), whole)],
        out_shape=[
            jax.ShapeDtypeStruct((total, D), F32),
            jax.ShapeDtypeStruct((total, D), BF),
        ],
        scratch_shapes=[pltpu.VMEM((total, wide), BF)],
        compiler_params=params(),
        cost_estimate=pl.CostEstimate(
            flops=2 * total * D * D, transcendentals=0, bytes_accessed=2 * D * D + 10 * total * D
        ),
        name="mixing",
    )(o, x, norm, dn, up, held)


def query_leaving_kernel(_, dq_ref, u_ref, up_ref, w_ref, da_ref, du_ref, gup_ref):
    @pl.when(pl.program_id(0) == 0)
    def _():
        du_ref[...] = dot(dq_ref[...], up_ref[...], NT)
        gup_ref[...] = dot(u_ref[0], dq_ref[...], TN).astype(BF)

    da_ref[...] = dot(dq_ref[...], w_ref[...], NT)


def query_leaving(which, dq, u, up, w, block=1024):
    rows = dq.shape[0]
    whole = lambda i, w: (0, 0)
    return pl.pallas_call(
        query_leaving_kernel,
        grid_spec=pltpu.PrefetchScalarGridSpec(
            num_scalar_prefetch=1,
            grid=(D // block,),
            in_specs=[
                pl.BlockSpec((rows, D), whole),
                pl.BlockSpec((1, rows, RANK), lambda i, w: (w[1], 0, 0)),
                pl.BlockSpec((RANK, D), lambda i, w: (w[1], 0)),
                pl.BlockSpec((block, D), lambda i, w: (i, 0)),
            ],
            out_specs=[
                pl.BlockSpec((rows, block), lambda i, w: (0, i)),
                pl.BlockSpec((rows, RANK), whole),
                pl.BlockSpec((RANK, D), whole),
            ],
        ),
        out_shape=[
            jax.ShapeDtypeStruct((rows, D), F32),
            jax.ShapeDtypeStruct((rows, RANK), F32),
            jax.ShapeDtypeStruct((RANK, D), BF),
        ],
        compiler_params=params(),
        cost_estimate=pl.CostEstimate(
            flops=2 * rows * D * D, transcendentals=0, bytes_accessed=2 * D * D
        ),
        name="query_leaving",
    )(which, dq, u, up, w)


def leaving_kernel(blocks, _, da_ref, du_ref, *refs):
    dkv_refs = refs[:blocks]
    (a_ref, u_ref, x_ref, dr_ref, gain_ref, dn_ref, up_ref, w_ref,
     dx_ref, gdn_ref, gup_ref) = refs[blocks:]
    total = dkv_refs[0][...].astype(F32)
    for ref in dkv_refs[1:]:
        total = total + ref[...].astype(F32)
    dkv = total.astype(BF)
    du = (2.0 * (du_ref[...] + dot(dkv, up_ref[...], NT))).astype(BF)
    gup_ref[...] = dot(u_ref[0], dkv, TN).astype(BF)
    gdn_ref[...] = dot(du, a_ref[...], TN).astype(BF)
    da = da_ref[...] + dot(dkv, w_ref[...], NT) + dot(du, dn_ref[...])
    back = layer_norm_back(
        x_ref[...].astype(F32), gain_ref[...], da.astype(BF).astype(F32)
    )
    dx_ref[...] = (dr_ref[...].astype(F32) + back).astype(BF)


def leaving(which, da, du, dkv, a, u, x, dr, gain, dn, up, w):
    rows = da.shape[0]
    wide = 2 * HEAD_DIM
    last = D // wide
    whole = lambda i, w: (0, 0)
    mine = lambda i, w: (w[1], 0)
    return pl.pallas_call(
        functools.partial(leaving_kernel, len(dkv)),
        grid_spec=pltpu.PrefetchScalarGridSpec(
            num_scalar_prefetch=1,
            grid=(1,),
            in_specs=[pl.BlockSpec((rows, D), whole), pl.BlockSpec((rows, RANK), whole)]
            + [pl.BlockSpec((rows, wide), whole)] * len(dkv)
            + [
                pl.BlockSpec((rows, D), mine),
                pl.BlockSpec((1, rows, RANK), lambda i, w: (w[1], 0, 0)),
                pl.BlockSpec((rows, D), mine),
                pl.BlockSpec((rows, D), whole),
                pl.BlockSpec((1, D), whole),
                pl.BlockSpec((RANK, D), mine),
                pl.BlockSpec((RANK, wide), lambda i, w: (w[1], last)),
                pl.BlockSpec((D, wide), lambda i, w: (0, last)),
            ],
            out_specs=[
                pl.BlockSpec((rows, D), whole),
                pl.BlockSpec((RANK, D), whole),
                pl.BlockSpec((RANK, wide), whole),
            ],
        ),
        out_shape=[
            jax.ShapeDtypeStruct((rows, D), BF),
            jax.ShapeDtypeStruct((RANK, D), BF),
            jax.ShapeDtypeStruct((RANK, wide), BF),
        ],
        compiler_params=params(),
        cost_estimate=pl.CostEstimate(
            flops=4 * rows * D * wide, transcendentals=0, bytes_accessed=14 * rows * D
        ),
        name="leaving",
    )(which, da, du, *dkv, a, u, x, dr, gain, dn, up, w)


def gelu_parts(f):
    square = f * f
    half = 0.5 + 0.5 * jnp.tanh(f * (GELU_C + (GELU_C * 0.044715) * square))
    return square, half


def mlp_up_kernel(per_tree, b_ref, wu_ref, upu_ref, dnu_ref, g_ref, u3_ref):
    @pl.when(pl.program_id(0) == 0)
    def _():
        u3_ref[...] = masked(dot(b_ref[...], dnu_ref[...], NT), per_tree)

    f = dot(b_ref[...], wu_ref[0]) + dot(u3_ref[...], upu_ref[...])
    g_ref[...] = (f * gelu_parts(f)[1]).astype(BF)


def mlp_up(b, held, part, up_up, down_up, block=1024):
    rows = b.shape[0]
    shards = held.shape[0]
    hidden = shards * part
    wide = down_up.shape[0]
    block = min(block, part)
    per = part // block
    once = lambda j: (0, 0)
    return pl.pallas_call(
        functools.partial(mlp_up_kernel, rows * RANK // wide),
        grid=(hidden // block,),
        in_specs=[
            pl.BlockSpec((rows, D), once),
            pl.BlockSpec((1, D, block), lambda j: (j // per, 0, j % per)),
            pl.BlockSpec((wide, block), lambda j: (0, j)),
            pl.BlockSpec((wide, D), once),
        ],
        out_specs=pl.BlockSpec((rows, block), lambda j: (0, j)),
        out_shape=jax.ShapeDtypeStruct((rows, hidden), BF),
        scratch_shapes=[pltpu.VMEM((rows, wide), BF)],
        compiler_params=params(),
        cost_estimate=pl.CostEstimate(
            flops=2 * rows * D * hidden,
            transcendentals=rows * hidden,
            bytes_accessed=2 * D * hidden + 2 * rows * hidden,
        ),
        name="mlp_up",
    )(b, held, up_up, down_up)


def mlp_down_kernel(trees, g_ref, x2_ref, wd_ref, dnd_ref, upd_ref, *refs):
    y_refs, (sum_ref, acc_ref) = refs[:trees], refs[trees:]
    step = pl.program_id(0)
    rows = g_ref.shape[0] // trees

    @pl.when(step == 0)
    def _():
        sum_ref[...] = x2_ref[...]
        acc_ref[...] = jnp.zeros_like(acc_ref)

    g = g_ref[...]
    sum_ref[...] += dot(g, wd_ref[...])
    acc_ref[...] += dot(dnd_ref[...], g, NT)

    @pl.when(step == pl.num_programs(0) - 1)
    def _():
        u4 = masked(acc_ref[...].T, rows)
        y = (sum_ref[...] + dot(u4, upd_ref[...])).astype(BF)
        for m in range(trees):
            y_refs[m][...] = y[m * rows : (m + 1) * rows]


def mlp_down(trees, g, x2, w_down, down_down, up_down, block=1024):
    total, hidden = g.shape
    rows, wide = total // trees, trees * RANK
    once = lambda j: (0, 0)
    return pl.pallas_call(
        functools.partial(mlp_down_kernel, trees),
        grid=(hidden // block,),
        in_specs=[
            pl.BlockSpec((total, block), lambda j: (0, j)),
            pl.BlockSpec((total, D), once, pipeline_mode=pl.Buffered(1)),
            pl.BlockSpec((block, D), lambda j: (j, 0)),
            pl.BlockSpec((wide, block), lambda j: (0, j)),
            pl.BlockSpec((wide, D), once),
        ],
        out_specs=[pl.BlockSpec((rows, D), once)] * trees,
        out_shape=[jax.ShapeDtypeStruct((rows, D), BF)] * trees,
        scratch_shapes=[pltpu.VMEM((total, D), F32), pltpu.VMEM((wide, total), F32)],
        compiler_params=params(),
        cost_estimate=pl.CostEstimate(
            flops=2 * total * D * hidden,
            transcendentals=0,
            bytes_accessed=2 * D * hidden + 2 * total * hidden,
        ),
        name="mlp_down",
    )(g, x2, w_down, down_down, up_down)


def by_tree(u_ref, u, rows):
    for m in range(u_ref.shape[0]):
        u_ref[m] = u[m * rows : (m + 1) * rows, m * RANK : (m + 1) * RANK]


def forward_kernel(trees, first, *refs):
    (o_ref, x_ref, norm_ref, dno_ref, upo_ref, wo_ref, wu_ref, wd_ref, upu_ref, dnd_ref, dnu_ref,
     upd_ref, y_ref, x2_ref, b_ref, g_ref, gp_ref, u2_ref, u3_ref, u4_ref,
     sum_ref, acc_ref, mixed_ref, inner_ref) = refs
    step = pl.program_id(0)
    rows = o_ref.shape[0] // trees

    @pl.when(step < first)
    def _():
        mix(step, rows, o_ref, x_ref, dno_ref, upo_ref, wo_ref, mixed_ref, sum_ref)

    @pl.when(step == first - 1)
    def _():
        by_tree(u2_ref, mixed_ref[...], rows)
        x2_ref[...] = sum_ref[...].astype(BF)
        b = normed(sum_ref, norm_ref)
        b_ref[...] = b
        inner = masked(dot(b, dnu_ref[...], NT), rows)
        inner_ref[...] = inner
        by_tree(u3_ref, inner, rows)
        acc_ref[...] = jnp.zeros_like(acc_ref)

    @pl.when(step >= first)
    def _():
        f = dot(b_ref[...], wu_ref[0]) + dot(inner_ref[...], upu_ref[...])
        square, half = gelu_parts(f)
        g = (f * half).astype(BF)
        g_ref[...] = g
        slope = f * ((2 * GELU_C) + (6 * GELU_C * 0.044715) * square)
        gp_ref[...] = (half + (half * (1.0 - half)) * slope).astype(BF)
        sum_ref[...] += dot(g, wd_ref[...])
        acc_ref[...] += dot(dnd_ref[...], g, NT)

    @pl.when(step == pl.num_programs(0) - 1)
    def _():
        u4 = masked(acc_ref[...].T, rows)
        by_tree(u4_ref, u4, rows)
        y_ref[...] = (sum_ref[...] + dot(u4, upd_ref[...])).astype(BF)


def forward_rest(trees, o, x, norm, held, part, w_down, maps, block=512):
    _, _, dn_out, up_out, dn_up, up_up, dn_down, up_down = maps
    total, wide = o.shape[0], trees * RANK
    rows = total // trees
    shards = held.shape[0]
    hidden = shards * part
    block = min(block, part)
    per = part // block
    at = part // (D // shards)
    once = lambda i: (0, 0)
    early = lambda i: jnp.minimum(i, shards - 1)
    late = lambda i: jnp.maximum(i - shards, 0)
    single = pl.Buffered(1)
    full = pl.BlockSpec((total, D), once)
    ranks = pl.BlockSpec((trees, rows, RANK), lambda i: (0, 0, 0))
    return pl.pallas_call(
        functools.partial(forward_kernel, trees, shards),
        grid=(shards + hidden // block,),
        in_specs=[pl.BlockSpec((total, D), once, pipeline_mode=single)] * 2
        + [
            pl.BlockSpec((2, D), once),
            pl.BlockSpec((wide, D), once),
            pl.BlockSpec((wide, D // shards), lambda i: (0, early(i))),
            pl.BlockSpec((1, D, D // shards), lambda i: (early(i), 0, at)),
            pl.BlockSpec((1, D, block), lambda i: (late(i) // per, 0, late(i) % per)),
            pl.BlockSpec((block, D), lambda i: (late(i), 0)),
            pl.BlockSpec((wide, block), lambda i: (0, late(i))),
            pl.BlockSpec((wide, block), lambda i: (0, late(i))),
            pl.BlockSpec((wide, D), once),
            pl.BlockSpec((wide, D), once),
        ],
        out_specs=[
            full,
            full,
            full,
            pl.BlockSpec((total, block), lambda i: (0, late(i))),
            pl.BlockSpec((total, block), lambda i: (0, late(i))),
            ranks,
            ranks,
            ranks,
        ],
        out_shape=[jax.ShapeDtypeStruct((total, D), BF)] * 3
        + [jax.ShapeDtypeStruct((total, hidden), BF)] * 2
        + [jax.ShapeDtypeStruct((trees, rows, RANK), BF)] * 3,
        scratch_shapes=[
            pltpu.VMEM((total, D), F32),
            pltpu.VMEM((wide, total), F32),
            pltpu.VMEM((total, wide), BF),
            pltpu.VMEM((total, wide), BF),
        ],
        compiler_params=params(),
        cost_estimate=pl.CostEstimate(
            flops=4 * total * D * hidden + 2 * total * D * D,
            transcendentals=total * hidden,
            bytes_accessed=4 * D * hidden + 4 * total * hidden + 2 * D * D,
        ),
        name="forward_rest",
    )(o, x, norm, dn_out, up_out, held, held, w_down, up_up, dn_down, dn_up, up_down)


def backward_kernel(given, first, *refs):
    flag_ref, own_ref, *refs = refs
    if given == 2:
        arrived_ref, *refs = refs
    (b_ref, x2_ref, gain_ref, wu_ref, wd_ref, g_ref, gp_ref, u3_ref, u4_ref, upu_ref, dnd_ref,
     dnu_ref, upd_ref, o_ref, u2_ref, dno_ref, upo_ref, wo_ref,
     dr_ref, do_ref, gdno_ref, gupo_ref, gdnu_ref, gupu_ref, gdnd_ref, gupd_ref,
     dy_ref, sum_ref, du4_ref, du3_ref, du2_ref) = refs
    step = pl.program_id(0)

    @pl.when(step == 0)
    def _():
        dy = own_ref[...]
        if given == 2:
            dy = jnp.where(flag_ref[0] == 1, dy, arrived_ref[...])
        dy_ref[...] = dy
        du4_ref[...] = (2.0 * dot(dy, upd_ref[...], NT)).astype(BF)
        gupd_ref[...] = dot(u4_ref[0], dy, TN).astype(BF)
        sum_ref[...] = jnp.zeros_like(sum_ref)
        du3_ref[...] = jnp.zeros_like(du3_ref)

    @pl.when(step < first)
    def _():
        du4 = du4_ref[...]
        dg = dot(dy_ref[...], wd_ref[...], NT) + dot(du4, dnd_ref[...])
        df = (gp_ref[...].astype(F32) * dg).astype(BF)
        gdnd_ref[...] = dot(du4, g_ref[...], TN).astype(BF)
        gupu_ref[...] = dot(u3_ref[0], df, TN).astype(BF)
        du3_ref[...] += dot(upu_ref[...], df, NT)
        sum_ref[...] += dot(df, wu_ref[0], NT)

    @pl.when(step == first - 1)
    def _():
        du3 = (2.0 * du3_ref[...].T).astype(BF)
        gdnu_ref[...] = dot(du3, b_ref[...], TN).astype(BF)
        db = (sum_ref[...] + dot(du3, dnu_ref[...])).astype(BF).astype(F32)
        back = layer_norm_back(x2_ref[...].astype(F32), gain_ref[...], db)
        dr = (dy_ref[...].astype(F32) + back).astype(BF)
        dr_ref[...] = dr
        du2_ref[...] = (2.0 * dot(dr, upo_ref[...], NT)).astype(BF)
        gupo_ref[...] = dot(u2_ref[0], dr, TN).astype(BF)

    @pl.when(step >= first)
    def _():
        wide = wo_ref.shape[2]
        du2 = du2_ref[...]
        do = dot(du2, dno_ref[...])
        for z in range(wo_ref.shape[0]):
            do = do + dot(dr_ref[:, z * wide : (z + 1) * wide], wo_ref[z], NT)
        do_ref[...] = do.astype(BF)
        gdno_ref[...] = dot(du2, o_ref[...], TN).astype(BF)


def backward_rest(
    which, own, b, x2, gain, held, part, w_down, g, gp, u2, u3, u4, o, maps, arrived=None,
    block=1024,
):
    _, _, dn_out, up_out, dn_up, up_up, dn_down, up_down = maps
    rows = u2.shape[1]
    shards = held.shape[0]
    hidden = shards * part
    block = min(block, part)
    per = part // block
    at = part // (D // shards)
    first = hidden // block
    deep = 512
    once = lambda i, w: (0, 0)
    mine = lambda i, w: (w[1], 0)
    early = lambda i: jnp.minimum(i, first - 1)
    late = lambda i: jnp.maximum(i - first, 0)
    single = pl.Buffered(1)
    row = pl.BlockSpec((rows, D), mine, pipeline_mode=single)
    given = 1 if arrived is None else 2
    hid = pl.BlockSpec((rows, block), lambda i, w: (w[1], early(i)))
    thin = pl.BlockSpec((RANK, block), lambda i, w: (w[1], early(i)))
    ranks = pl.BlockSpec((1, rows, RANK), lambda i, w: (w[1], 0, 0))
    across = pl.BlockSpec((RANK, D), mine)
    shape = jax.ShapeDtypeStruct
    dr, do, *grads = pl.pallas_call(
        functools.partial(backward_kernel, given, first),
        grid_spec=pltpu.PrefetchScalarGridSpec(
            num_scalar_prefetch=1,
            grid=(first + D // deep,),
            in_specs=[row]
            + [pl.BlockSpec((rows, D), once, pipeline_mode=single)] * (given - 1)
            + [
                row,
                row,
                pl.BlockSpec((1, D), once),
                pl.BlockSpec((1, D, block), lambda i, w: (early(i) // per, 0, early(i) % per)),
                pl.BlockSpec((block, D), lambda i, w: (early(i), 0)),
                hid,
                hid,
                ranks,
                ranks,
                thin,
                thin,
                across,
                across,
                pl.BlockSpec((rows, deep), lambda i, w: (w[1], late(i))),
                ranks,
                pl.BlockSpec((RANK, deep), lambda i, w: (w[1], late(i))),
                across,
                pl.BlockSpec((shards, deep, D // shards), lambda i, w: (0, late(i), at)),
            ],
            out_specs=[
                pl.BlockSpec((rows, D), once),
                pl.BlockSpec((rows, deep), lambda i, w: (0, late(i))),
                pl.BlockSpec((RANK, deep), lambda i, w: (0, late(i))),
                pl.BlockSpec((RANK, D), once),
                pl.BlockSpec((RANK, D), once),
                pl.BlockSpec((RANK, block), lambda i, w: (0, early(i))),
                pl.BlockSpec((RANK, block), lambda i, w: (0, early(i))),
                pl.BlockSpec((RANK, D), once),
            ],
            scratch_shapes=[
                pltpu.VMEM((rows, D), BF),
                pltpu.VMEM((rows, D), F32),
                pltpu.VMEM((rows, RANK), BF),
                pltpu.VMEM((RANK, rows), F32),
                pltpu.VMEM((rows, RANK), BF),
            ],
        ),
        out_shape=[shape((rows, D), BF)] * 2
        + [shape((RANK, D), BF)] * 3
        + [shape((RANK, hidden), BF)] * 2
        + [shape((RANK, D), BF)],
        compiler_params=params(),
        cost_estimate=pl.CostEstimate(
            flops=4 * rows * D * hidden + 2 * rows * D * D,
            transcendentals=0,
            bytes_accessed=4 * D * hidden + 4 * rows * hidden + 2 * D * D,
        ),
        name="backward_rest",
    )(
        which, own, *([] if arrived is None else [arrived]),
        b, x2, gain, held, w_down, g, gp, u3, u4, up_up, dn_down, dn_up, up_down,
        o, u2, dn_out, up_out, held,
    )
    return dr, do, grads


def segment_of(places, lengths):
    order = jnp.arange(lengths.shape[0], dtype=jnp.int32)
    ends = jnp.sum(
        jnp.where(order[None, :] <= order[:, None], lengths[None, :], 0), axis=1, dtype=jnp.int32
    )
    return jnp.sum((places[:, None] >= ends[None, :]).astype(jnp.int32), axis=1, dtype=jnp.int32)


def ancestry(parents):
    seg_ids = jnp.arange(parents.shape[0], dtype=jnp.int32)
    current = seg_ids
    reach = current[:, None] == seg_ids[None, :]
    for sweep in range(parents.shape[0] - 1):
        current = jnp.sum(
            jnp.where(current[:, None] == seg_ids[None, :], parents[None, :], 0),
            axis=1,
            dtype=jnp.int32,
        )
        reach = reach | (current[:, None] == seg_ids[None, :])
    return reach.astype(BF)


def key_bias(lengths, parents, query_places, key_places):
    seg_ids = jnp.arange(parents.shape[0], dtype=jnp.int32)
    of_query = (segment_of(query_places, lengths)[:, None] == seg_ids[None, :]).astype(BF)
    of_key = (segment_of(key_places, lengths)[:, None] == seg_ids[None, :]).astype(BF)
    known = ancestry(parents)

    def bias(rows_in, rows_out, place_query, place_key):
        reach = dot(rows_in, rows_out, NT)
        allowed = (reach > 0.5) & (place_key <= place_query) & (place_key >= 0)
        return jnp.where(allowed, 0.0, MASKED).astype(F32)

    anc = dot(of_query, known).astype(BF)
    return (
        bias(anc, of_key, query_places[:, None], key_places[None, :]),
        bias(of_key, anc, query_places[None, :], key_places[:, None]),
    )


def shifted(value, axis, steps):
    count = lax.axis_size(axis)
    return lax.ppermute(value, axis, [(i, (i + steps) % count) for i in range(count)])


def local(
    inputs, cotangent, norm_gains, norm_biases, w_attn, w_out, w_up, w_down,
    down_attn, up_attn, down_out, up_out, down_up, up_up, down_down, up_down,
    seg_lengths, parent_ids, adapter_ids,
):
    section = lax.axis_index("section")
    shard = lax.axis_index("fsdp")
    member = lax.axis_index("replica")
    shards = lax.axis_size("fsdp")
    members = lax.axis_size("replica")
    trees, per_tree = inputs.shape[0], inputs.shape[1]
    gain = norm_gains[0].astype(F32)
    shift = norm_biases[0].astype(F32)
    norms = [jnp.stack([gain[i], shift[i]]) for i in range(2)]
    is_first = (section == 0).astype(jnp.int32).reshape(1)

    def quarter(weight):
        part = weight.shape[0] // members
        return lax.dynamic_slice_in_dim(weight, member * part, part, 0)

    def gathered(own):
        return lax.all_gather(own[None], ("fsdp", "replica"), axis=1, tiled=True)[0]

    part, out_wide, attn_wide = w_up.shape[2], w_out.shape[2], w_attn.shape[2]
    padded = -(-attn_wide // 128) * 128
    attn_at = -(-(part + out_wide) // padded) * padded
    each = D // members
    own = jnp.concatenate(
        [
            quarter(w_up[0]),
            quarter(w_out[0]),
            jnp.zeros((each, attn_at - part - out_wide), BF),
            quarter(w_attn[0]),
            jnp.zeros((each, padded - attn_wide), BF),
        ],
        axis=1,
    )
    held = gathered(own).reshape(shards, D, own.shape[1])
    down_full = gathered(quarter(w_down[0]))
    attn_full = assemble(held, attn_at, attn_wide)

    stacks = (down_attn, up_attn, down_out, up_out, down_up, up_up, down_down, up_down)
    widths = [stack.shape[3] for stack in stacks]
    starts = [sum(widths[:i]) for i in range(len(widths))]
    chosen = adapter_ids[:, 0, 0]
    picked = jnp.concatenate(
        [
            jnp.concatenate(
                [lax.dynamic_index_in_dim(stack[0], chosen[m], 0, keepdims=False) for m in range(trees)],
                axis=0,
            )
            for stack in stacks
        ],
        axis=1,
    )
    owners = lax.all_gather(chosen, "replica", axis=0, tiled=True)
    owners, picked = lax.optimization_barrier((owners, picked))
    behind = jnp.stack([picked] + [shifted(picked, "fsdp", k) for k in range(1, shards)])
    ordered = [
        lax.dynamic_index_in_dim(behind, lax.rem(shard - z + shards, shards), 0, keepdims=False)
        for z in range(shards)
    ]
    maps = [
        jnp.concatenate([piece[:, at : at + width] for piece in ordered], axis=1)
        for at, width in zip(starts, widths)
    ]
    dn_attn, up_attn_, dn_out, up_out_, dn_up, up_up_, dn_down, up_down_ = maps

    query_places = shard * per_tree + jnp.arange(per_tree, dtype=jnp.int32)
    key_places = jnp.concatenate(
        [(shard - s) * per_tree + jnp.arange(per_tree, dtype=jnp.int32) for s in range(shards)]
    )
    biases = [
        key_bias(seg_lengths[m, 0], parent_ids[m, 0], query_places, key_places)
        for m in range(trees)
    ]

    def to_higher(value, steps):
        return lax.ppermute(value, "fsdp", [(i, i + steps) for i in range(shards - steps)])

    def to_lower(value, steps):
        return lax.ppermute(value, "fsdp", [(i + steps, i) for i in range(shards - steps)])

    def with_lower(kv):
        return [kv] + [to_higher(kv, s) for s in range(1, shards)]

    own_rows = inputs.reshape(trees * per_tree, D)
    before = ()
    for m in range(trees):
        a, u1, kv = entry(m, trees, own_rows, norms[0], dn_attn, up_attn_, attn_full)
        blocks = with_lower(kv)
        before = attention_forward(
            m, trees, queries(m, a, u1, up_attn_, attn_full), blocks, biases[m][0], before, False
        )
    x2, b = mixing(before[0], own_rows, norms[1], dn_out, up_out_, held, part)
    g = mlp_up(b, held, part, up_up_, dn_up)
    sent = mlp_down(trees, g, x2, down_full, dn_down, up_down_)
    arrived = [lax.ppermute(rows, "section", [(0, 1)]) for rows in sent]
    entered, attended = (), ()
    for m in range(trees):
        rows = arrived[m]
        if m:
            rows, attended = lax.optimization_barrier((rows, attended))
        a, u1, kv, *entered = entry(
            m, trees, own_rows, norms[0], dn_attn, up_attn_, attn_full, rows, is_first, entered
        )
        blocks = with_lower(kv)
        attended = attention_forward(
            m, trees, queries(m, a, u1, up_attn_, attn_full), blocks, biases[m][0], attended, True
        )
    x, a, u1 = entered
    o, lse, q, *blocks = attended
    layer_out, x2, b, g, gp, u2, u3, u4 = forward_rest(
        trees, o, x, norms[1], held, part, down_full, maps
    )
    bias = jnp.concatenate([pair[1] for pair in biases], axis=0)

    def by_shard(grads, parts):
        return jnp.stack(
            [
                jnp.concatenate(
                    [g[:, z * part : (z + 1) * part] for g, part in zip(grads, parts)], axis=1
                )
                for z in range(shards)
            ]
        )

    def scattered(slabs):
        return lax.psum_scatter(slabs, "fsdp", scatter_dimension=0)

    def permuted(slabs):
        total = lax.dynamic_index_in_dim(slabs, shard, 0, keepdims=False).astype(F32)
        for k in range(1, shards):
            part = lax.dynamic_index_in_dim(slabs, lax.rem(shard + k, shards), 0, keepdims=False)
            total = total + shifted(part, "fsdp", k).astype(F32)
        return total.astype(BF)

    def all_replicas(total):
        return jnp.stack([total] + [shifted(total, "replica", i) for i in range(1, members)])

    own_grads = cotangent.reshape(trees * per_tree, D)
    order = lax.rem(member - jnp.arange(members, dtype=jnp.int32) + members, members)
    cyclic = owners.reshape(members, trees)[order].reshape(-1)
    in_grads, sums, arrived, before, total, ready = [], [], None, None, None, None
    for step in range(trees + 1):
        tree = jnp.clip(step - 1 + section, 0, trees - 1)
        which = jnp.stack([section, tree]).astype(jnp.int32)
        if arrived is None:
            which = jnp.array([1, 0], jnp.int32)
        total = None
        if ready is not None:
            arrived, ready = lax.optimization_barrier((arrived, ready))
            in_grads.append(ready[0])
            total = scattered(ready[1])
        dr, do, early = backward_rest(
            which, own_grads, b, x2, gain[1:2], held, part, down_full, g, gp, u2, u3, u4,
            o, maps, arrived,
        )
        if total is not None:
            do, total = lax.optimization_barrier((do, total))
            total = all_replicas(total)
        if step == trees:
            slabs = by_shard(early, widths[2:])
            do, slabs = lax.optimization_barrier((do, slabs))
            early_sum = scattered(slabs)
        dq, dkv = attention_backward(which, q, do, o, blocks, bias, lse)
        dkv = [dkv[0]] + [to_lower(dkv[s], s) for s in range(1, shards)]
        da, du, g_up_q = query_leaving(which, dq, u1, up_attn_, attn_full)
        if total is not None:
            da, total = lax.optimization_barrier((da, total))
            sums.append((step - 2, total))
        dx, g_dn, g_up_kv = leaving(
            which, da, du, dkv, a, u1, x, dr, gain[0:1], dn_attn, up_attn_, attn_full
        )
        if step < trees:
            arrived = lax.ppermute(dx, "section", [(1, 0)])
        late = (g_dn, jnp.concatenate([g_up_q, g_up_kv], axis=1))
        now = (dx, *late, *early)
        ready = None
        if 0 < step < trees:
            dx_ready, *grads = (
                jnp.where(section == 1, was, new) for was, new in zip(before, now)
            )
            ready = (dx_ready, by_shard(grads, widths))
        before = now
    in_grads.append(dx)
    late_sum = permuted(by_shard(late, widths[:2]))
    sums.append((trees - 1, all_replicas(jnp.concatenate([late_sum, early_sum], axis=1))))

    finals = []
    names = jnp.arange(down_attn.shape[1], dtype=jnp.int32)[:, None, None]
    for at, width in zip(starts, widths):
        total = jnp.zeros((down_attn.shape[1], RANK, width), F32)
        for m, slabs in sums:
            for r in range(members):
                addend = slabs[r, :, at : at + width].astype(F32)[None]
                total = total + jnp.where(names == cyclic[r * trees + m], addend, 0.0)
        finals.append(total[None])
    return (
        layer_out.reshape(1, trees, per_tree, D),
        jnp.stack(in_grads)[None],
        *finals,
    )


def solution(mesh):
    rows = P(None, ("replica", "fsdp"), None)
    stack = P("section", None, None, "fsdp")
    placed = (
        (rows, rows)
        + (P("section", None, None),) * 2
        + (P("section", None, "fsdp"),) * 3
        + (P("section", "fsdp", None),)
        + (stack,) * 8
        + (P(None, "replica", None),) * 3
    )
    return jax.shard_map(
        local,
        mesh=mesh,
        in_specs=placed,
        out_specs=(P("section", None, ("replica", "fsdp"), None),) * 2 + (stack,) * 8,
        check_vma=False,
    )
```

time: 1270 us -> 1050 us (0.83)
  waiting for transfers between devices: 569 us -> 392 us
  matrix products: 108 us -> 6.13 us
  Pallas kernels: 351 us -> 439 us
  local copies, waits for them, and re-layouts: 121 us -> 51.4 us
  starting transfers between devices: 46.5 us -> 80.5 us
    all_gather x6 -> x2, waiting for transfers between devices: 426 us -> 276 us  [gathered(): return lax.all_gather(own[None], ('fsdp', 'replica'), axis=1, tiled=True)[0]]
    dot_general x32 -> x6, matrix products: 108 us -> 6.13 us  [dot(): return lax.dot_general(left, right, dims, preferred_element_type=F32)]
    pallas_call x8 -> x26, Pallas kernels: 295 us -> 396 us  [the longest x3 127 us: backward_rest(): pl.pallas_call(functools.partial(backward_kernel, given, first), grid_spe...]
    convert_element_type x19 -> x2, other arithmetic: 35.9 us -> 0.04 us  [the longest x1 0.03 us: permuted(): return total.astype(BF)]
    reshape x19 -> x2, local copies, waits for them, and re-layouts: 27.7 us -> 0.17 us  [local(): cyclic = owners.reshape(members, trees)[order].reshape(-1)]
    reduce_scatter x1 -> x2, waiting for transfers between devices: 26.9 us -> 0.02 us  [scattered(): return lax.psum_scatter(slabs, 'fsdp', scatter_dimension=0)]
    transpose x4 -> x0, local copies, waits for them, and re-layouts: 25.3 us -> none  [the longest x1 12.6 us: local(): jnp.moveaxis(attn_parts, 0, 1).reshape(D, shards * w_attn.shape[2])]
    ppermute x12, starting transfers between devices: 24.7 us -> 46.4 us  [to_higher(): lax.ppermute(value, 'fsdp', [(i, i + steps) for i in range(shards - steps)])]
  transfers between devices with their start and end apart: 33 -> 41, of which waited for: 17 -> 16; matrix products, arithmetic and copies ran while one was open for 11% -> 6% of each run, Pallas kernels for 5% -> 20%
where the time goes in v2:
time: 1050 us; the launch traced here: 1040 us
  Pallas kernels  439 us (42%)
  waiting for transfers between devices  392 us (37%)
  starting transfers between devices  80.5 us (8%)
  local copies, waits for them, and re-layouts  51.4 us (5%)
  other arithmetic  43.2 us (4%)
  between operations  20 us (2%)
    all_gather x2, waiting for transfers between devices, gathered(): return lax.all_gather(own[None], ('fsdp', 'replica'), axis=1, tiled=True)[0]  276 us
    pallas_call x3, Pallas kernels, backward_rest(): pl.pallas_call(functools.partial(backward_kernel, given, first), grid_spe...  127 us
    pallas_call x1, Pallas kernels, forward_rest(): pl.pallas_call(functools.partial(forward_kernel, trees, shards), grid=(sh...  66.1 us
    ppermute x12, waiting for transfers between devices, shifted(): lax.ppermute(value, axis, [(i, (i + steps) % count) for i in range(count)])  57.7 us
    ppermute x12, starting transfers between devices, to_higher(): lax.ppermute(value, 'fsdp', [(i, i + steps) for i in range(shards - steps)])  46.4 us
    pallas_call x3, Pallas kernels, attention_backward(): pl.pallas_call(functools.partial(attention_backward_kernel, blocks, heads...  43.6 us
    pallas_call x4, Pallas kernels, attention_forward(): pl.pallas_call(functools.partial(attention_forward_kernel, blocks, heads,...  35.4 us
    pallas_call x1, Pallas kernels, mlp_up(): pl.pallas_call(functools.partial(mlp_up_kernel, rows * RANK // wide), gri...  28.4 us
  transfers between devices with their start and end apart: 41, of which 16 were waited for; matrix products, arithmetic and copies ran while one was open for 6% of the time, Pallas kernels for 20%

profile of v2, /device:TPU:0, one launch (start us, length us, event | category | flops | bytes accessed | tf_op | source)
XLA Modules:
  0.0 1039.4 jit_solution(16563589346112567439)
XLA Ops:
  7.2 3.3 dynamic-slice_bitcast_fusion
  12.4 3.9 concatenate.127
  16.4 3.1 constant_dynamic-slice_fusion
  21.5 6.9 all-reduce
  39.0 2.6 collective-permute-start.1
  48.6 1.6 fusion.1.refs_4_
  50.2 12.5 %collective-permute-done = bf16[32,7232]{1,0:T(8,128)(2,1)S(1)} collective-permute-done((bf16[32,7232]{1,0:T(8,128)(2,1)S(1)}, bf16[32,7232]{1,0:T(8,128)(2,1)S(1)}, u32[]{:S(2)}, u32[]{:S(2)}) %collective-permute-start) | collective-permute-done | bytes 462880 | tf_op jit(solution)/shard_map/ppermute | solution.py:854
  62.8 19.8 %collective-permute-done.1 = bf16[32,7232]{1,0:T(8,128)(2,1)S(1)} collective-permute-done((bf16[32,7232]{1,0:T(8,128)(2,1)S(1)}, bf16[32,7232]{1,0:T(8,128)(2,1)S(1)}, u32[]{:S(2)}, u32[]{:S(2)}) %collective-permute-start.1) | collective-permute-done | bytes 462880 | tf_op jit(solution)/shard_map/ppermute | solution.py:854
  82.6 17.0 %collective-permute-done.2 = bf16[32,7232]{1,0:T(8,128)(2,1)S(1)} collective-permute-done((bf16[32,7232]{1,0:T(8,128)(2,1)S(1)}, bf16[32,7232]{1,0:T(8,128)(2,1)S(1)}, u32[]{:S(2)}, u32[]{:S(2)}) %collective-permute-start.2) | collective-permute-done | bytes 462880 | tf_op jit(solution)/shard_map/ppermute | solution.py:854
  106.9 199.3 %all-gather.7.cloned.1.call-done = bf16[8192,3200]{1,0:T(8,128)(2,1)} async-done(((bf16[512,3200]{1,0:T(8,128)(2,1)}), bf16[8192,3200]{1,0:T(8,128)(2,1)}) %all-gather.7.cloned.1.call-update) | async-done | bytes 52428816 | tf_op jit(solution)/shard_map/all_gather | solution.py:878
  306.2 10.6 %assemble.1.refs_3_.w_ref.refs_11_ = bf16[2048,2304]{1,0:T(8,128)(2,1)} custom-call(bf16[4,2048,3200]{2,1,0:T(8,128)(2,1)} %bitcast.390), custom_call_target="tpu_custom_call" | custom-call | bytes 20971520 | tf_op jit(solution)/shard_map/assemble/pallas_call | solution.py:208
  316.8 4.1 entry.5
  320.9 13.9 %collective-permute-start.6 = (bf16[256,256]{1,0:T(8,128)(2,1)}, bf16[256,256]{1,0:T(8,128)(2,1)S(1)}, u32[]{:S(2)}, u32[]{:S(2)}) collective-permute-start(bf16[256,256]{1,0:T(8,128)(2,1)} %get-tuple-element.139.refs_0_), channel_id=1, source_target_pairs={{0,4},{4,8},{8,12},{1,5},{5,9},{9,13},{2,6},{6,10},{10,14},{3,7},{... | collective-permute-start | bytes 393224 | tf_op jit(solution)/shard_map/ppermute | solution.py:935
  337.4 4.4 entry.4
  344.3 6.1 queries.5.q_ref
  350.5 6.2 queries.4.q_ref
  359.5 8.8 attention_forward.4
  370.1 8.6 attention_forward.5
  378.7 13.7 %mixing.1 = (f32[512,2048]{1,0:T(8,128)}, bf16[512,2048]{1,0:T(8,128)(2,1)}) custom-call(bf16[512,2048]{1,0:T(8,128)(2,1)} %get-tuple-element.142.o_ref, bf16[512,2048]{1,0:T(8,128)(2,1)} %bitcast.408, f32[2,2048]{1,0:T(2,128)} %pad_maximum_fusion.23.norm_ref.refs_2_, bf16[32,2048]{1,0:T(8,128)(2,1)} %pad_maximum_fusion.12.dn_ref.refs_3_.refs_17_.refs_18_, ...), custom_call_target="tpu_custom_call" | custom-call | flops 4294967296 | bytes 18874368 | tf_op jit(solution)/shard_map/mixing/pallas_call | solution.py:345
  392.4 28.4 %mlp_up.1.g_ref = bf16[512,8192]{1,0:T(8,128)(2,1)} custom-call(bf16[512,2048]{1,0:T(8,128)(2,1)} %get-tuple-element.143.b_ref, bf16[4,2048,3200]{2,1,0:T(8,128)(2,1)} %bitcast.392, bf16[32,8192]{1,0:T(8,128)(2,1)} %pad_maximum_fusion.5.upu_ref.refs_8_.refs_11_.refs_12_, bf16[32,2048]{1,0:T(8,128)(2,1)} %pad_maximum_fusion.14.dnu_ref.refs_10_.refs_13_.refs_14_), custom_call_target="tpu_custom_call" | custom-call | flops 17179869184 | bytes 41943040 | tf_op jit(solution)/shard_map/mlp_up/pallas_call | solution.py:494
  420.8 76.7 %all-gather.5.cloned.1.call-done = bf16[1,8192,2048]{2,1,0:T(8,128)(2,1)} async-done(((bf16[1,512,2048]{2,1,0:T(8,128)(2,1)}), bf16[1,8192,2048]{2,1,0:T(8,128)(2,1)}) %all-gather.5.cloned.1.call-update) | async-done | bytes 33554448 | tf_op jit(solution)/shard_map/all_gather | solution.py:878
  497.5 28.3 %mlp_down.1 = (bf16[256,2048]{1,0:T(8,128)(2,1)}, bf16[256,2048]{1,0:T(8,128)(2,1)}) custom-call(bf16[512,8192]{1,0:T(8,128)(2,1)} %mlp_up.1.g_ref, f32[512,2048]{1,0:T(8,128)} %get-tuple-element.144.x2_ref, bf16[8192,2048]{1,0:T(8,128)(2,1)} %bitcast.401, bf16[32,8192]{1,0:T(8,128)(2,1)} %pad_maximum_fusion.6.dnd_ref.refs_9_.refs_12_.refs_13_, ...), custom_call_target="tpu_custom_call" | custom-call | flops 17179869184 | bytes 41943040 | tf_op jit(solution)/shard_map/mlp_down/pallas_call | solution.py:542
  525.9 3.7 collective-permute-start.10
  530.1 1.9 fusion.7
  534.0 2.7 pad_maximum_fusion.refs_4_
  536.7 16.7 %collective-permute-done.10.arrived_ref = bf16[256,2048]{1,0:T(8,128)(2,1)S(1)} collective-permute-done((bf16[256,2048]{1,0:T(8,128)(2,1)}, bf16[256,2048]{1,0:T(8,128)(2,1)S(1)}, u32[]{:S(2)}, u32[]{:S(2)}) %collective-permute-start.10) | collective-permute-done | bytes 1048608 | tf_op jit(solution)/shard_map/ppermute | solution.py:954
  554.3 4.6 entry.6
  558.9 9.0 collective-permute-start.11
  567.9 5.5 collective-permute-start.12
  574.7 6.1 queries.6.q_ref
  582.1 9.0 attention_forward.6
  592.1 4.6 entry.7
  596.7 3.5 collective-permute-start.14
  600.2 5.2 collective-permute-start.15
  606.7 6.3 queries.7.q_ref
  614.3 9.0 attention_forward.7
  623.3 66.1 %forward_rest.1 = (bf16[512,2048]{1,0:T(8,128)(2,1)}, bf16[512,2048]{1,0:T(8,128)(2,1)}, bf16[512,2048]{1,0:T(8,128)(2,1)}, bf16[512,8192]{1,0:T(8,128)(2,1)}, b...) custom-call(bf16[512,2048]{1,0:T(8,128)(2,1)} %get-tuple-element.171, ...), custom_call_target="tpu_custom_call" | custom-call | flops 38654705664 | bytes 92274688 | tf_op jit(solution)/shard_map/forward_rest/pallas_call | solution.py:625
  689.5 42.4 %backward_rest.3 = (bf16[256,2048]{1,0:T(8,128)(2,1)}, bf16[256,2048]{1,0:T(8,128)(2,1)}, bf16[16,2048]{1,0:T(8,128)(2,1)}, bf16[16,2048]{1,0:T(8,128)(2,1)}, bf...) custom-call(s32[2]{0:T(128)} %constant.148.clone.refs_0_._, ...), custom_call_target="tpu_custom_call" | custom-call | flops 19327352832 | bytes 83886080 | tf_op jit(solution)/shard_map/backward_rest/pallas_call | solution.py:748
  731.9 14.5 %attention_backward.3 = (bf16[256,2048]{1,0:T(8,128)(2,1)}, bf16[256,256]{1,0:T(8,128)(2,1)}, bf16[256,256]{1,0:T(8,128)(2,1)}, bf16[256,256]{1,0:T(8,128)(2,1)}, bf16[256,256]{1,0:T(8,128)(2,1)}) custom-call(s32[2]{0:T(128)} %constant.148.clone.refs_0_._, bf16[512,2048]{1,0:T(8,128)(2,1)} %get-tuple-element.174.q_ref, ...), custom_call_target="tpu_custom_call" | custom-call | flops 10737418240 | bytes 5242880 | tf_op jit(solution)/shard_map/attention_backward/pallas_call | solution.py:168
  750.2 7.4 query_leaving.3
  757.6 2.5 collective-permute-done.18.refs_2_
  760.8 7.1 leaving.3
  780.2 10.3 collective-permute-done.20.refs_2_
  791.5 42.5 %backward_rest.4 = (bf16[256,2048]{1,0:T(8,128)(2,1)}, bf16[256,2048]{1,0:T(8,128)(2,1)}, bf16[16,2048]{1,0:T(8,128)(2,1)}, bf16[16,2048]{1,0:T(8,128)(2,1)}, bf...) custom-call(s32[2]{0:T(128)} %pad_add_fusion.1.refs_0_._, ...), custom_call_target="tpu_custom_call" | custom-call | flops 19327352832 | bytes 83886080 | tf_op jit(solution)/shard_map/backward_rest/pallas_call | solution.py:748
  841.0 14.4 %attention_backward.4 = (bf16[256,2048]{1,0:T(8,128)(2,1)}, bf16[256,256]{1,0:T(8,128)(2,1)}, bf16[256,256]{1,0:T(8,128)(2,1)}, bf16[256,256]{1,0:T(8,128)(2,1)}, bf16[256,256]{1,0:T(8,128)(2,1)}) custom-call(s32[2]{0:T(128)} %pad_add_fusion.1.refs_0_._, bf16[512,2048]{1,0:T(8,128)(2,1)} %get-tuple-element.174.q_ref, ...), custom_call_target="tpu_custom_call" | custom-call | flops 10737418240 | bytes 5242880 | tf_op jit(solution)/shard_map/attention_backward/pallas_call | solution.py:168
  859.2 7.6 query_leaving.4
  868.8 7.1 leaving.4
  881.2 1.8 concatenate.139
  883.0 1.8 concatenate.140
  884.9 1.7 concatenate.141
  886.5 2.3 pad_maximum_fusion.2
  888.8 9.2 collective-permute-done.24.refs_2_
  898.9 42.4 %backward_rest.5 = (bf16[256,2048]{1,0:T(8,128)(2,1)}, bf16[256,2048]{1,0:T(8,128)(2,1)}, bf16[16,2048]{1,0:T(8,128)(2,1)}, bf16[16,2048]{1,0:T(8,128)(2,1)}, bf...) custom-call(s32[2]{0:T(128)} %pad_add_fusion.2.refs_0_._, ...), custom_call_target="tpu_custom_call" | custom-call | flops 19327352832 | bytes 83886080 | tf_op jit(solution)/shard_map/backward_rest/pallas_call | solution.py:748
  947.3 1.9 collective-permute-start.26
  950.6 14.8 %attention_backward.5 = (bf16[256,2048]{1,0:T(8,128)(2,1)}, bf16[256,256]{1,0:T(8,128)(2,1)}, bf16[256,256]{1,0:T(8,128)(2,1)}, bf16[256,256]{1,0:T(8,128)(2,1)}, bf16[256,256]{1,0:T(8,128)(2,1)}) custom-call(s32[2]{0:T(128)} %pad_add_fusion.2.refs_0_._, bf16[512,2048]{1,0:T(8,128)(2,1)} %get-tuple-element.174.q_ref, ...), custom_call_target="tpu_custom_call" | custom-call | flops 10737418240 | bytes 5242880 | tf_op jit(solution)/shard_map/attention_backward/pallas_call | solution.py:168
  965.4 7.5 query_leaving.5
  977.9 2.9 collective-permute-done.28.refs_1_
  980.8 14.1 %collective-permute-done.29.refs_2_ = bf16[256,256]{1,0:T(8,128)(2,1)S(1)} collective-permute-done((bf16[256,256]{1,0:T(8,128)(2,1)S(1)}, bf16[256,256]{1,0:T(8,128)(2,1)S(1)}, u32[]{:S(2)}, u32[]{:S(2)}) %collective-permute-start.29) | collective-permute-done | bytes 131104 | tf_op jit(solution)/shard_map/ppermute | solution.py:938
  995.7 7.1 leaving.5
  1004.7 3.7 collective-permute-start.33
  1014.4 5.2 collective-permute-done.34
  1021.1 2.0 collective-permute-done.36
  1024.3 1.9 select_add_fusion
  1026.2 1.9 select_add_fusion.1
  (356 shorter events, 108.0 us)
Async XLA Ops:
  7.2 299.0 %all-gather.7.cloned.1.call-start = ((), (), s32[]{:S(2)}) async-start(), calls=%async_computation.5 | async-start | bytes 55705600 | tf_op jit(solution)/shard_map/all_gather | solution.py:878
  16.3 481.2 %all-gather.5.cloned.1.call-start = ((), (), s32[]{:S(2)}) async-start(), calls=%async_computation.2 | async-start | bytes 35651584 | tf_op jit(solution)/shard_map/all_gather | solution.py:878
  19.5 23.4 %copy-start.50 = (bf16[1,2,2048]{2,1,0:T(2,128)(2,1)S(1)}, bf16[1,2,2048]{2,1,0:T(2,128)(2,1)}, u32[]{:S(2)}) copy-start(bf16[1,2,2048]{2,1,0:T(2,128)(2,1)} %param.22) | copy-start | bytes 24580
  19.5 23.4 %copy-start.51 = (bf16[1,2,2048]{2,1,0:T(2,128)(2,1)S(1)}, bf16[1,2,2048]{2,1,0:T(2,128)(2,1)}, u32[]{:S(2)}) copy-start(bf16[1,2,2048]{2,1,0:T(2,128)(2,1)} %param.23) | copy-start | bytes 24580
  19.5 23.6 %copy-start.53 = (s32[2,1,5]{2,1,0:T(1,128)S(1)}, s32[2,1,5]{2,1,0:T(1,128)}, u32[]{:S(2)}) copy-start(s32[2,1,5]{2,1,0:T(1,128)} %param.37) | copy-start | bytes 124
  19.5 23.8 %copy-start.54 = (s32[2,1,5]{2,1,0:T(1,128)S(1)}, s32[2,1,5]{2,1,0:T(1,128)}, u32[]{:S(2)}) copy-start(s32[2,1,5]{2,1,0:T(1,128)} %param.36) | copy-start | bytes 124
  19.6 927.7 %reduce-scatter.3.cloned.1.call-start = ((), (), s32[]{:S(2)}) async-start(), calls=%async_computation.3 | async-start | bytes 1167360 | tf_op jit(solution)/shard_map/reduce_scatter | solution.py:985
  37.4 25.4 %collective-permute-start = (bf16[32,7232]{1,0:T(8,128)(2,1)S(1)}, bf16[32,7232]{1,0:T(8,128)(2,1)S(1)}, u32[]{:S(2)}, u32[]{:S(2)}) collective-permute-start(bf16[32,7232]{1,0:T(8,128)(2,1)S(1)} %concatenate.124), channel_id=1, source_target_pairs={{0,4},{4,8},{8,12},{12,0},{1,5},{5,9},{9,13},{13,1},{2,6},{6,10},{... | collective-permute-start | bytes 1388552 | tf_op jit(solution)/shard_map/ppermute | solution.py:854
  39.0 43.6 %collective-permute-start.1 = (bf16[32,7232]{1,0:T(8,128)(2,1)S(1)}, bf16[32,7232]{1,0:T(8,128)(2,1)S(1)}, u32[]{:S(2)}, u32[]{:S(2)}) collective-permute-start(bf16[32,7232]{1,0:T(8,128)(2,1)S(1)} %concatenate.124), channel_id=1, source_target_pairs={{0,8},{4,12},{8,0},{12,4},{1,9},{5,13},{9,1},{13,5},{2,10},{6,14},... | collective-permute-start | bytes 1388552 | tf_op jit(solution)/shard_map/ppermute | solution.py:854
  41.6 58.0 %collective-permute-start.2 = (bf16[32,7232]{1,0:T(8,128)(2,1)S(1)}, bf16[32,7232]{1,0:T(8,128)(2,1)S(1)}, u32[]{:S(2)}, u32[]{:S(2)}) collective-permute-start(bf16[32,7232]{1,0:T(8,128)(2,1)S(1)} %concatenate.124), channel_id=1, source_target_pairs={{0,12},{4,0},{8,4},{12,8},{1,13},{5,1},{9,5},{13,9},{2,14},{6,2},{... | collective-permute-start | bytes 1388552 | tf_op jit(solution)/shard_map/ppermute | solution.py:854
  320.9 35.7 %collective-permute-start.6 = (bf16[256,256]{1,0:T(8,128)(2,1)}, bf16[256,256]{1,0:T(8,128)(2,1)S(1)}, u32[]{:S(2)}, u32[]{:S(2)}) collective-permute-start(bf16[256,256]{1,0:T(8,128)(2,1)} %get-tuple-element.139.refs_0_), channel_id=1, source_target_pairs={{0,4},{4,8},{8,12},{1,5},{5,9},{9,13},{2,6},{6,10},{10,14},{3,7},{... | collective-permute-start | bytes 393224 | tf_op jit(solution)/shard_map/ppermute | solution.py:935
  334.7 23.4 %collective-permute-start.7 = (bf16[256,256]{1,0:T(8,128)(2,1)}, bf16[256,256]{1,0:T(8,128)(2,1)S(1)}, u32[]{:S(2)}, u32[]{:S(2)}) collective-permute-start(bf16[256,256]{1,0:T(8,128)(2,1)} %get-tuple-element.139.refs_0_), channel_id=1, source_target_pairs={{0,8},{4,12},{1,9},{5,13},{2,10},{6,14},{3,11},{7,15},{16,24},{20,... | collective-permute-start | bytes 393224 | tf_op jit(solution)/shard_map/ppermute | solution.py:935
  336.0 22.1 %collective-permute-start.8 = (bf16[256,256]{1,0:T(8,128)(2,1)}, bf16[256,256]{1,0:T(8,128)(2,1)S(1)}, u32[]{:S(2)}, u32[]{:S(2)}) collective-permute-start(bf16[256,256]{1,0:T(8,128)(2,1)} %get-tuple-element.139.refs_0_), channel_id=1, source_target_pairs={{0,12},{1,13},{2,14},{3,15},{16,28},{17,29},{18,30},{19,31}} | collective-permute-start | bytes 393224 | tf_op jit(solution)/shard_map/ppermute | solution.py:935
  341.7 26.6 %collective-permute-start.3 = (bf16[256,256]{1,0:T(8,128)(2,1)}, bf16[256,256]{1,0:T(8,128)(2,1)S(1)}, u32[]{:S(2)}, u32[]{:S(2)}) collective-permute-start(bf16[256,256]{1,0:T(8,128)(2,1)} %get-tuple-element.136.refs_0_), channel_id=1, source_target_pairs={{0,4},{4,8},{8,12},{1,5},{5,9},{9,13},{2,6},{6,10},{10,14},{3,7},{... | collective-permute-start | bytes 393224 | tf_op jit(solution)/shard_map/ppermute | solution.py:935
  343.0 25.3 %collective-permute-start.4 = (bf16[256,256]{1,0:T(8,128)(2,1)}, bf16[256,256]{1,0:T(8,128)(2,1)S(1)}, u32[]{:S(2)}, u32[]{:S(2)}) collective-permute-start(bf16[256,256]{1,0:T(8,128)(2,1)} %get-tuple-element.136.refs_0_), channel_id=1, source_target_pairs={{0,8},{4,12},{1,9},{5,13},{2,10},{6,14},{3,11},{7,15},{16,24},{20,... | collective-permute-start | bytes 393224 | tf_op jit(solution)/shard_map/ppermute | solution.py:935
  356.6 12.8 %collective-permute-start.5 = (bf16[256,256]{1,0:T(8,128)(2,1)S(1)}, bf16[256,256]{1,0:T(8,128)(2,1)S(1)}, u32[]{:S(2)}, u32[]{:S(2)}) collective-permute-start(bf16[256,256]{1,0:T(8,128)(2,1)S(1)} %copy-done.59), channel_id=1, source_target_pairs={{0,12},{1,13},{2,14},{3,15},{16,28},{17,29},{18,30},{19,31}} | collective-permute-start | bytes 393224 | tf_op jit(solution)/shard_map/ppermute | solution.py:935
  525.9 27.5 %collective-permute-start.10 = (bf16[256,2048]{1,0:T(8,128)(2,1)}, bf16[256,2048]{1,0:T(8,128)(2,1)S(1)}, u32[]{:S(2)}, u32[]{:S(2)}) collective-permute-start(bf16[256,2048]{1,0:T(8,128)(2,1)} %get-tuple-element.146), channel_id=1, source_target_pairs={{0,16},{1,17},{2,18},{3,19},{4,20},{5,21},{6,22},{7,23},{8,24},{9,... | collective-permute-start | bytes 3145736 | tf_op jit(solution)/shard_map/ppermute | solution.py:954
  532.0 59.2 %collective-permute-start.9 = (bf16[256,2048]{1,0:T(8,128)(2,1)}, bf16[256,2048]{1,0:T(8,128)(2,1)S(1)}, u32[]{:S(2)}, u32[]{:S(2)}) collective-permute-start(bf16[256,2048]{1,0:T(8,128)(2,1)} %get-tuple-element.145), channel_id=1, source_target_pairs={{0,16},{1,17},{2,18},{3,19},{4,20},{5,21},{6,22},{7,23},{8,24},{9,... | collective-permute-start | bytes 3145736 | tf_op jit(solution)/shard_map/ppermute | solution.py:954
  558.9 21.9 %collective-permute-start.11 = (bf16[256,256]{1,0:T(8,128)(2,1)}, bf16[256,256]{1,0:T(8,128)(2,1)S(1)}, u32[]{:S(2)}, u32[]{:S(2)}) collective-permute-start(bf16[256,256]{1,0:T(8,128)(2,1)} %get-tuple-element.149.refs_0_), channel_id=1, source_target_pairs={{0,4},{4,8},{8,12},{1,5},{5,9},{9,13},{2,6},{6,10},{10,14},{3,7},{... | collective-permute-start | bytes 393224 | tf_op jit(solution)/shard_map/ppermute | solution.py:935
  567.9 12.9 %collective-permute-start.12 = (bf16[256,256]{1,0:T(8,128)(2,1)}, bf16[256,256]{1,0:T(8,128)(2,1)S(1)}, u32[]{:S(2)}, u32[]{:S(2)}) collective-permute-start(bf16[256,256]{1,0:T(8,128)(2,1)} %get-tuple-element.149.refs_0_), channel_id=1, source_target_pairs={{0,8},{4,12},{1,9},{5,13},{2,10},{6,14},{3,11},{7,15},{16,24},{20,... | collective-permute-start | bytes 393224 | tf_op jit(solution)/shard_map/ppermute | solution.py:935
  573.4 7.4 collective-permute-start.13
  596.7 16.3 %collective-permute-start.14 = (bf16[256,256]{1,0:T(8,128)(2,1)}, bf16[256,256]{1,0:T(8,128)(2,1)S(1)}, u32[]{:S(2)}, u32[]{:S(2)}) collective-permute-start(bf16[256,256]{1,0:T(8,128)(2,1)} %get-tuple-element.163.refs_0_), channel_id=1, source_target_pairs={{0,4},{4,8},{8,12},{1,5},{5,9},{9,13},{2,6},{6,10},{10,14},{3,7},{... | collective-permute-start | bytes 393224 | tf_op jit(solution)/shard_map/ppermute | solution.py:935
  600.2 12.8 %collective-permute-start.15 = (bf16[256,256]{1,0:T(8,128)(2,1)}, bf16[256,256]{1,0:T(8,128)(2,1)S(1)}, u32[]{:S(2)}, u32[]{:S(2)}) collective-permute-start(bf16[256,256]{1,0:T(8,128)(2,1)} %get-tuple-element.163.refs_0_), channel_id=1, source_target_pairs={{0,8},{4,12},{1,9},{5,13},{2,10},{6,14},{3,11},{7,15},{16,24},{20,... | collective-permute-start | bytes 393224 | tf_op jit(solution)/shard_map/ppermute | solution.py:935
  605.4 7.6 collective-permute-start.16
  746.3 11.3 %collective-permute-start.17 = (bf16[256,256]{1,0:T(8,128)(2,1)}, bf16[256,256]{1,0:T(8,128)(2,1)S(1)}, u32[]{:S(2)}, u32[]{:S(2)}) collective-permute-start(bf16[256,256]{1,0:T(8,128)(2,1)} %get-tuple-element.193), channel_id=1, source_target_pairs={{4,0},{8,4},{12,8},{5,1},{9,5},{13,9},{6,2},{10,6},{14,10},{7,3},{... | collective-permute-start | bytes 393224 | tf_op jit(solution)/shard_map/ppermute | solution.py:938
  747.6 12.4 %collective-permute-start.18 = (bf16[256,256]{1,0:T(8,128)(2,1)}, bf16[256,256]{1,0:T(8,128)(2,1)S(1)}, u32[]{:S(2)}, u32[]{:S(2)}) collective-permute-start(bf16[256,256]{1,0:T(8,128)(2,1)} %get-tuple-element.194), channel_id=1, source_target_pairs={{8,0},{12,4},{9,1},{13,5},{10,2},{14,6},{11,3},{15,7},{24,16},{28,... | collective-permute-start | bytes 393224 | tf_op jit(solution)/shard_map/ppermute | solution.py:938
  748.9 11.1 %collective-permute-start.19 = (bf16[256,256]{1,0:T(8,128)(2,1)}, bf16[256,256]{1,0:T(8,128)(2,1)S(1)}, u32[]{:S(2)}, u32[]{:S(2)}) collective-permute-start(bf16[256,256]{1,0:T(8,128)(2,1)} %get-tuple-element.195), channel_id=1, source_target_pairs={{12,0},{13,1},{14,2},{15,3},{28,16},{29,17},{30,18},{31,19}} | collective-permute-start | bytes 393224 | tf_op jit(solution)/shard_map/ppermute | solution.py:938
  760.8 8.9 copy-start.55
  767.9 22.6 %collective-permute-start.20 = (bf16[256,2048]{1,0:T(8,128)(2,1)}, bf16[256,2048]{1,0:T(8,128)(2,1)S(1)}, u32[]{:S(2)}, u32[]{:S(2)}) collective-permute-start(bf16[256,2048]{1,0:T(8,128)(2,1)} %get-tuple-element.198), channel_id=1, source_target_pairs={{16,0},{17,1},{18,2},{19,3},{20,4},{21,5},{22,6},{23,7},{24,8},{25... | collective-permute-start | bytes 3145736 | tf_op jit(solution)/shard_map/ppermute | solution.py:1032
  780.2 53.9 %copy-start.31 = (bf16[16,2048]{1,0:T(8,128)(2,1)S(1)}, bf16[16,2048]{1,0:T(8,128)(2,1)}, u32[]{:S(2)}) copy-start(bf16[16,2048]{1,0:T(8,128)(2,1)} %get-tuple-element.225) | copy-start | bytes 196612
  780.2 55.5 %copy-start.11 = (bf16[16,8192]{1,0:T(8,128)(2,1)S(1)}, bf16[16,8192]{1,0:T(8,128)(2,1)}, u32[]{:S(2)}) copy-start(bf16[16,8192]{1,0:T(8,128)(2,1)} %get-tuple-element.223) | copy-start | bytes 786436
  780.2 57.2 %copy-start.10 = (bf16[16,8192]{1,0:T(8,128)(2,1)S(1)}, bf16[16,8192]{1,0:T(8,128)(2,1)}, u32[]{:S(2)}) copy-start(bf16[16,8192]{1,0:T(8,128)(2,1)} %get-tuple-element.221) | copy-start | bytes 786436
  855.3 11.5 %collective-permute-start.21 = (bf16[256,256]{1,0:T(8,128)(2,1)}, bf16[256,256]{1,0:T(8,128)(2,1)S(1)}, u32[]{:S(2)}, u32[]{:S(2)}) collective-permute-start(bf16[256,256]{1,0:T(8,128)(2,1)} %get-tuple-element.204), channel_id=1, source_target_pairs={{4,0},{8,4},{12,8},{5,1},{9,5},{13,9},{6,2},{10,6},{14,10},{7,3},{... | collective-permute-start | bytes 393224 | tf_op jit(solution)/shard_map/ppermute | solution.py:938
  856.6 10.2 collective-permute-start.22
  857.9 10.2 collective-permute-start.23
  868.8 7.1 copy-start.7
  877.4 20.6 %collective-permute-start.24 = (bf16[256,2048]{1,0:T(8,128)(2,1)S(1)}, bf16[256,2048]{1,0:T(8,128)(2,1)S(1)}, u32[]{:S(2)}, u32[]{:S(2)}) collective-permute-start(bf16[256,2048]{1,0:T(8,128)(2,1)S(1)} %copy-done.8), channel_id=1, source_target_pairs={{16,0},{17,1},{18,2},{19,3},{20,4},{21,5},{22,6},{23,7},{24,8},{25... | collective-permute-start | bytes 3145736 | tf_op jit(solution)/shard_map/ppermute | solution.py:1032
  898.0 113.1 %reduce-scatter.5.cloned.1.call-start = ((), (), s32[]{:S(2)}) async-start(), calls=%async_computation.4 | async-start | bytes 983040 | tf_op jit(solution)/shard_map/reduce_scatter | solution.py:985
  947.3 29.2 %collective-permute-start.25 = (bf16[16,7232]{1,0:T(8,128)(2,1)}, bf16[16,7232]{1,0:T(8,128)(2,1)S(1)}, u32[]{:S(2)}, u32[]{:S(2)}) collective-permute-start(bf16[16,7232]{1,0:T(8,128)(2,1)} %bitcast.424), channel_id=1, source_target_pairs={{0,1},{1,2},{2,3},{3,0},{4,5},{5,6},{6,7},{7,4},{8,9},{9,10},{10,1... | collective-permute-start | bytes 694280 | tf_op jit(solution)/shard_map/ppermute | solution.py:854
  947.3 30.5 %collective-permute-start.26 = (bf16[16,7232]{1,0:T(8,128)(2,1)}, bf16[16,7232]{1,0:T(8,128)(2,1)S(1)}, u32[]{:S(2)}, u32[]{:S(2)}) collective-permute-start(bf16[16,7232]{1,0:T(8,128)(2,1)} %bitcast.425), channel_id=1, source_target_pairs={{0,2},{1,3},{2,0},{3,1},{4,6},{5,7},{6,4},{7,5},{8,10},{9,11},{10,... | collective-permute-start | bytes 694280 | tf_op jit(solution)/shard_map/ppermute | solution.py:854
  949.2 28.6 %collective-permute-start.27 = (bf16[16,7232]{1,0:T(8,128)(2,1)}, bf16[16,7232]{1,0:T(8,128)(2,1)S(1)}, u32[]{:S(2)}, u32[]{:S(2)}) collective-permute-start(bf16[16,7232]{1,0:T(8,128)(2,1)} %bitcast.426), channel_id=1, source_target_pairs={{0,3},{1,0},{2,1},{3,2},{4,7},{5,4},{6,5},{7,6},{8,11},{9,8},{10,9... | collective-permute-start | bytes 694280 | tf_op jit(solution)/shard_map/ppermute | solution.py:854
  965.4 7.6 copy-start.58
  965.4 8.8 copy-start.57
  965.4 11.1 %copy-start.56 = (bf16[256,256]{1,0:T(8,128)(2,1)S(1)}, bf16[256,256]{1,0:T(8,128)(2,1)}, u32[]{:S(2)}) copy-start(bf16[256,256]{1,0:T(8,128)(2,1)} %get-tuple-element.247) | copy-start | bytes 393220
  965.4 12.4 %copy-start.13 = (bf16[1,16,7232]{2,1,0:T(8,128)(2,1)S(1)}, bf16[1,16,7232]{2,1,0:T(8,128)(2,1)}, u32[]{:S(2)}) copy-start(bf16[1,16,7232]{2,1,0:T(8,128)(2,1)} %reduce-scatter.3.cloned.1.call-done) | copy-start | bytes 694276
  972.9 7.9 collective-permute-start.28
  974.2 20.8 %collective-permute-start.29 = (bf16[256,256]{1,0:T(8,128)(2,1)S(1)}, bf16[256,256]{1,0:T(8,128)(2,1)S(1)}, u32[]{:S(2)}, u32[]{:S(2)}) collective-permute-start(bf16[256,256]{1,0:T(8,128)(2,1)S(1)} %copy-done.57), channel_id=1, source_target_pairs={{8,0},{12,4},{9,1},{13,5},{10,2},{14,6},{11,3},{15,7},{24,16},{28,... | collective-permute-start | bytes 393224 | tf_op jit(solution)/shard_map/ppermute | solution.py:938
  976.5 18.5 %collective-permute-start.30 = (bf16[256,256]{1,0:T(8,128)(2,1)S(1)}, bf16[256,256]{1,0:T(8,128)(2,1)S(1)}, u32[]{:S(2)}, u32[]{:S(2)}) collective-permute-start(bf16[256,256]{1,0:T(8,128)(2,1)S(1)} %copy-done.56), channel_id=1, source_target_pairs={{12,0},{13,1},{14,2},{15,3},{28,16},{29,17},{30,18},{31,19}} | collective-permute-start | bytes 393224 | tf_op jit(solution)/shard_map/ppermute | solution.py:938
  980.8 14.2 %copy-start.16 = (bf16[256,256]{1,0:T(8,128)(2,1)}, bf16[256,256]{1,0:T(8,128)(2,1)S(1)}, u32[]{:S(2)}) copy-start(bf16[256,256]{1,0:T(8,128)(2,1)S(1)} %collective-permute-done.28.refs_1_) | copy-start | bytes 393220
  995.7 8.0 copy-start.12
  1004.5 6.5 collective-permute-start.31
  1004.6 6.4 collective-permute-start.32
  1004.7 6.3 collective-permute-start.33
  1010.3 13.0 %copy-start.37 = (pred[8]{0:T(512)(128)(4,1)S(1)}, pred[8]{0:T(512)(128)(4,1)}, u32[]{:S(2)}) copy-start(pred[8]{0:T(512)(128)(4,1)} %iota_compare_fusion.24) | copy-start | bytes 28
  1010.3 13.0 %copy-start.38 = (pred[8]{0:T(512)(128)(4,1)S(1)}, pred[8]{0:T(512)(128)(4,1)}, u32[]{:S(2)}) copy-start(pred[8]{0:T(512)(128)(4,1)} %iota_compare_fusion.25) | copy-start | bytes 28
  1010.3 13.0 %copy-start.39 = (pred[8]{0:T(512)(128)(4,1)S(1)}, pred[8]{0:T(512)(128)(4,1)}, u32[]{:S(2)}) copy-start(pred[8]{0:T(512)(128)(4,1)} %iota_compare_fusion.26) | copy-start | bytes 28
  1010.3 13.0 %copy-start.40 = (pred[8]{0:T(512)(128)(4,1)S(1)}, pred[8]{0:T(512)(128)(4,1)}, u32[]{:S(2)}) copy-start(pred[8]{0:T(512)(128)(4,1)} %iota_compare_fusion.27) | copy-start | bytes 28
  1010.3 13.0 %copy-start.42 = (pred[8]{0:T(512)(128)(4,1)S(1)}, pred[8]{0:T(512)(128)(4,1)}, u32[]{:S(2)}) copy-start(pred[8]{0:T(512)(128)(4,1)} %iota_compare_fusion.28) | copy-start | bytes 28
  1010.3 13.0 %copy-start.44 = (pred[8]{0:T(512)(128)(4,1)S(1)}, pred[8]{0:T(512)(128)(4,1)}, u32[]{:S(2)}) copy-start(pred[8]{0:T(512)(128)(4,1)} %iota_compare_fusion.29) | copy-start | bytes 28
  1010.4 13.0 %copy-start.46 = (pred[8]{0:T(512)(128)(4,1)S(1)}, pred[8]{0:T(512)(128)(4,1)}, u32[]{:S(2)}) copy-start(pred[8]{0:T(512)(128)(4,1)} %iota_compare_fusion.30) | copy-start | bytes 28
  1012.1 7.4 collective-permute-start.34
  1012.2 8.6 collective-permute-start.35
  1012.6 10.4 %collective-permute-start.36 = (bf16[16,7232]{1,0:T(8,128)(2,1)S(1)}, bf16[16,7232]{1,0:T(8,128)(2,1)S(1)}, u32[]{:S(2)}, u32[]{:S(2)}) collective-permute-start(bf16[16,7232]{1,0:T(8,128)(2,1)S(1)} %get-tuple-element.372), channel_id=1, source_target_pairs={{0,3},{1,0},{2,1},{3,2},{4,7},{5,4},{6,5},{7,6},{8,11},{9,8},{10,9... | collective-permute-start | bytes 694280 | tf_op jit(solution)/shard_map/ppermute | solution.py:854
  1026.2 6.5 copy-start.1
  (50 other events, 124.6 us)
Sparse Core Ops, SparseCore 0:
  16.5 289.6 all-gather.6
  307.8 189.7 all-gather.4
  898.1 27.7 reduce-scatter.2
  975.7 27.5 reduce-scatter.4

commit v3 on v2

--- a/solution.py
+++ b/solution.py
@@ -74,8 +74,7 @@
     vals = jnp.concatenate([r[:, HEAD_DIM:] for r in kv_refs], axis=0)
     vals = jnp.concatenate([vals, jnp.ones_like(vals)], axis=1)
     if keep:
-        for kept, given in zip(kept_refs, (q_ref, *kv_refs)):
-            kept[...] = given[...]
+        kept_refs[0][...] = q_ref[...]
     for h in range(heads):
         cols = slice(h * HEAD_DIM, (h + 1) * HEAD_DIM)
         scores = dot(q_ref[:, cols], keys, NT) + bias_ref[...]
@@ -92,21 +91,19 @@
     blocks = len(kv)
     wide = heads * HEAD_DIM
     steps = HEADS // heads
-    whole = lambda i: (0, 0)
     mine = pl.BlockSpec((rows, wide), lambda i: (tree, i))
-    pair = pl.BlockSpec((rows, 2 * HEAD_DIM), lambda i: (tree, 0))
     tall = jax.ShapeDtypeStruct((trees * rows, D), BF)
     outs = [tall, jax.ShapeDtypeStruct((trees * steps, heads, rows), F32)]
     out_specs = [mine, pl.BlockSpec((1, heads, rows), lambda i: (tree * steps + i, 0, 0))]
     if keep:
-        outs += [tall] + [jax.ShapeDtypeStruct((trees * rows, 2 * HEAD_DIM), BF)] * blocks
-        out_specs += [mine] + [pair] * blocks
+        outs.append(tall)
+        out_specs.append(mine)
     return pl.pallas_call(
         functools.partial(attention_forward_kernel, blocks, heads, len(before), keep),
         grid=(steps,),
         in_specs=[pl.BlockSpec((rows, wide), lambda i: (0, i))]
-        + [pl.BlockSpec((rows, 2 * HEAD_DIM), whole)] * blocks
-        + [pl.BlockSpec((rows, blocks * rows), whole)]
+        + [pl.BlockSpec((rows, 2 * HEAD_DIM), lambda i: (tree, 0))] * blocks
+        + [pl.BlockSpec((rows, blocks * rows), lambda i: (0, 0))]
         + [pl.BlockSpec(memory_space=pl.ANY)] * len(before),
         out_specs=out_specs,
         out_shape=outs,
@@ -196,6 +193,42 @@
     return dq, dkv
 
 
+def pack_kernel(at, _, up_ref, out_ref, attn_ref, all_ref):
+    part, wide = up_ref.shape[1], attn_ref.shape[0]
+    after = part + out_ref.shape[1]
+    all_ref[:, :part] = up_ref[...]
+    all_ref[:, part:after] = out_ref[...]
+    if at > after:
+        all_ref[:, after:at] = jnp.zeros((all_ref.shape[0], at - after), BF)
+    attn = attn_ref[...].T
+    spare = all_ref.shape[1] - at - wide
+    if spare:
+        attn = jnp.concatenate([attn, jnp.zeros((attn.shape[0], spare), BF)], axis=1)
+    all_ref[:, at:] = attn
+
+
+def pack(member, each, up, out, attn_t, at, total):
+    return pl.pallas_call(
+        functools.partial(pack_kernel, at),
+        grid_spec=pltpu.PrefetchScalarGridSpec(
+            num_scalar_prefetch=1,
+            grid=(1,),
+            in_specs=[
+                pl.BlockSpec((each, up.shape[1]), lambda i, w: (w[0], 0)),
+                pl.BlockSpec((each, out.shape[1]), lambda i, w: (w[0], 0)),
+                pl.BlockSpec((attn_t.shape[0], each), lambda i, w: (0, w[0])),
+            ],
+            out_specs=pl.BlockSpec((each, total), lambda i, w: (0, 0)),
+        ),
+        out_shape=jax.ShapeDtypeStruct((each, total), BF),
+        compiler_params=params(),
+        cost_estimate=pl.CostEstimate(
+            flops=0, transcendentals=0, bytes_accessed=4 * each * total
+        ),
+        name="pack",
+    )(member.astype(jnp.int32).reshape(1), up, out, attn_t)
+
+
 def assemble_kernel(wide, held_ref, full_ref):
     full_ref[...] = jnp.concatenate(
         [held_ref[z][:, :wide] for z in range(held_ref.shape[0])], axis=1
@@ -219,70 +252,103 @@
     )(held)
 
 
-def entry_body(x, norm_ref, dn_ref, up_ref, w_ref, a_ref, u_ref, kv_ref):
-    a = layer_norm(x.astype(F32), norm_ref[0:1, :], norm_ref[1:2, :]).astype(BF)
+def ranks_of(rows, norm_ref, dn_ref):
+    a = layer_norm(rows.astype(F32), norm_ref[0:1, :], norm_ref[1:2, :]).astype(BF)
+    return a, dot(a, dn_ref[...], NT)
+
+
+def entry_kernel(x_ref, norm_ref, dn_ref, up_ref, w_ref, a_ref, u_ref, kv_ref):
+    a, u = ranks_of(x_ref[...], norm_ref, dn_ref)
     a_ref[...] = a
-    u = (2.0 * dot(a, dn_ref[...], NT)).astype(BF)
+    u = (2.0 * u).astype(BF)
     u_ref[...] = u
     kv_ref[...] = (dot(a, w_ref[...]) + dot(u, up_ref[...])).astype(BF)
 
 
-def entry_own_kernel(own_ref, *refs):
-    entry_body(own_ref[...], *refs)
-
-
-def entry_arrived_kernel(before, flag_ref, own_ref, arrived_ref, *refs):
-    given, (a_ref, u_ref, kv_ref, x_all, a_all, u_all) = refs[:4], refs[4 + before :]
+def entry(tree, trees, x, norm, dn, up, w):
+    rows = x.shape[0] // trees
+    wide = 2 * HEAD_DIM
+    last = D // wide
+    whole = lambda i: (0, 0)
+    return pl.pallas_call(
+        entry_kernel,
+        grid=(1,),
+        in_specs=[
+            pl.BlockSpec((rows, D), lambda i: (tree, 0)),
+            pl.BlockSpec((2, D), whole),
+            pl.BlockSpec((RANK, D), lambda i: (tree, 0)),
+            pl.BlockSpec((RANK, wide), lambda i: (tree, last)),
+            pl.BlockSpec((D, wide), lambda i: (0, last)),
+        ],
+        out_specs=[
+            pl.BlockSpec((rows, D), whole),
+            pl.BlockSpec((rows, RANK), whole),
+            pl.BlockSpec((rows, wide), whole),
+        ],
+        out_shape=[
+            jax.ShapeDtypeStruct((rows, D), BF),
+            jax.ShapeDtypeStruct((rows, RANK), BF),
+            jax.ShapeDtypeStruct((rows, wide), BF),
+        ],
+        compiler_params=params(),
+        cost_estimate=pl.CostEstimate(
+            flops=3 * rows * D * wide, transcendentals=0, bytes_accessed=8 * rows * D
+        ),
+        name="entry",
+    )(x, norm, dn, up, w)
+
+
+def enter_kernel(before, flag_ref, own_ref, arrived_ref, norm_ref, dn_ref, *refs):
+    a_ref, u_ref, x_all, a_all, u_all = refs[before:]
     x = jnp.where(flag_ref[0] == 1, own_ref[...], arrived_ref[...])
     x_all[...] = x
-    entry_body(x, *given, a_ref, u_ref, kv_ref)
-    a_all[...] = a_ref[...]
-    u_all[0] = u_ref[...]
-
-
-def entry(tree, trees, own, norm, dn, up, w, arrived=None, flag=None, before=()):
+    a, u = ranks_of(x, norm_ref, dn_ref)
+    a_ref[...] = a
+    a_all[...] = a
+    u = (2.0 * u).astype(BF)
+    u_ref[...] = u
+    u_all[0] = u
+
+
+def enter(tree, trees, own, arrived, flag, norm, dn, before):
     rows = own.shape[0] // trees
-    wide = 2 * HEAD_DIM
-    last = D // wide
-    whole = lambda i, *_: (0, 0)
-    mine = pl.BlockSpec((rows, D), lambda i, *_: (tree, 0))
+    whole = lambda i, f: (0, 0)
+    mine = pl.BlockSpec((rows, D), lambda i, f: (tree, 0))
     row = pl.BlockSpec((rows, D), whole)
-    ins, ins_specs = ([own], [mine]) if arrived is None else ([own, arrived], [mine, row])
-    outs = [
-        jax.ShapeDtypeStruct((rows, D), BF),
-        jax.ShapeDtypeStruct((rows, RANK), BF),
-        jax.ShapeDtypeStruct((rows, wide), BF),
-    ]
-    out_specs = [row, pl.BlockSpec((rows, RANK), whole), pl.BlockSpec((rows, wide), whole)]
-    kernel = entry_own_kernel
-    if arrived is not None:
-        kernel = functools.partial(entry_arrived_kernel, len(before))
-        outs += [jax.ShapeDtypeStruct((trees * rows, D), BF)] * 2
-        outs += [jax.ShapeDtypeStruct((trees, rows, RANK), BF)]
-        out_specs += [mine, mine, pl.BlockSpec((1, rows, RANK), lambda i, *_: (tree, 0, 0))]
-    return pl.pallas_call(
-        kernel,
+    return pl.pallas_call(
+        functools.partial(enter_kernel, len(before)),
         grid_spec=pltpu.PrefetchScalarGridSpec(
-            num_scalar_prefetch=0 if arrived is None else 1,
+            num_scalar_prefetch=1,
             grid=(1,),
-            in_specs=ins_specs
-            + [
+            in_specs=[
+                mine,
+                row,
                 pl.BlockSpec((2, D), whole),
-                pl.BlockSpec((RANK, D), lambda i, *_: (tree, 0)),
-                pl.BlockSpec((RANK, wide), lambda i, *_: (tree, last)),
-                pl.BlockSpec((D, wide), lambda i, *_: (0, last)),
+                pl.BlockSpec((RANK, D), lambda i, f: (tree, 0)),
             ]
             + [pl.BlockSpec(memory_space=pl.ANY)] * len(before),
-            out_specs=out_specs,
-        ),
-        out_shape=outs,
-        input_output_aliases={7 + i: 3 + i for i in range(len(before))},
-        compiler_params=params(),
-        cost_estimate=pl.CostEstimate(
-            flops=3 * rows * D * wide, transcendentals=0, bytes_accessed=8 * rows * D
-        ),
-        name="entry",
-    )(*([] if arrived is None else [flag]), *ins, norm, dn, up, w, *before)
+            out_specs=[
+                row,
+                pl.BlockSpec((rows, RANK), whole),
+                mine,
+                mine,
+                pl.BlockSpec((1, rows, RANK), lambda i, f: (tree, 0, 0)),
+            ],
+        ),
+        out_shape=[
+            jax.ShapeDtypeStruct((rows, D), BF),
+            jax.ShapeDtypeStruct((rows, RANK), BF),
+            jax.ShapeDtypeStruct((trees * rows, D), BF),
+            jax.ShapeDtypeStruct((trees * rows, D), BF),
+            jax.ShapeDtypeStruct((trees, rows, RANK), BF),
+        ],
+        input_output_aliases={5 + i: 2 + i for i in range(len(before))},
+        compiler_params=params(),
+        cost_estimate=pl.CostEstimate(
+            flops=2 * rows * D * 256, transcendentals=0, bytes_accessed=10 * rows * D
+        ),
+        name="enter",
+    )(flag, own, arrived, norm, dn, *before)
 
 
 def queries_kernel(a_ref, u_ref, up_ref, w_ref, q_ref):
@@ -366,16 +432,15 @@
     )(o, x, norm, dn, up, held)
 
 
-def query_leaving_kernel(_, dq_ref, u_ref, up_ref, w_ref, da_ref, du_ref, gup_ref):
+def query_leaving_kernel(_, dq_ref, up_ref, w_ref, da_ref, du_ref):
     @pl.when(pl.program_id(0) == 0)
     def _():
         du_ref[...] = dot(dq_ref[...], up_ref[...], NT)
-        gup_ref[...] = dot(u_ref[0], dq_ref[...], TN).astype(BF)
 
     da_ref[...] = dot(dq_ref[...], w_ref[...], NT)
 
 
-def query_leaving(which, dq, u, up, w, block=1024):
+def query_leaving(which, dq, up, w, block=1024):
     rows = dq.shape[0]
     whole = lambda i, w: (0, 0)
     return pl.pallas_call(
@@ -385,30 +450,27 @@
             grid=(D // block,),
             in_specs=[
                 pl.BlockSpec((rows, D), whole),
-                pl.BlockSpec((1, rows, RANK), lambda i, w: (w[1], 0, 0)),
                 pl.BlockSpec((RANK, D), lambda i, w: (w[1], 0)),
                 pl.BlockSpec((block, D), lambda i, w: (i, 0)),
             ],
             out_specs=[
                 pl.BlockSpec((rows, block), lambda i, w: (0, i)),
                 pl.BlockSpec((rows, RANK), whole),
-                pl.BlockSpec((RANK, D), whole),
             ],
         ),
         out_shape=[
             jax.ShapeDtypeStruct((rows, D), F32),
             jax.ShapeDtypeStruct((rows, RANK), F32),
-            jax.ShapeDtypeStruct((RANK, D), BF),
         ],
         compiler_params=params(),
         cost_estimate=pl.CostEstimate(
             flops=2 * rows * D * D, transcendentals=0, bytes_accessed=2 * D * D
         ),
         name="query_leaving",
-    )(which, dq, u, up, w)
-
-
-def leaving_kernel(blocks, _, da_ref, du_ref, *refs):
+    )(which, dq, up, w)
+
+
+def leaving_kernel(blocks, _, dq_ref, da_ref, du_ref, *refs):
     dkv_refs = refs[:blocks]
     (a_ref, u_ref, x_ref, dr_ref, gain_ref, dn_ref, up_ref, w_ref,
      dx_ref, gdn_ref, gup_ref) = refs[blocks:]
@@ -417,7 +479,8 @@
         total = total + ref[...].astype(F32)
     dkv = total.astype(BF)
     du = (2.0 * (du_ref[...] + dot(dkv, up_ref[...], NT))).astype(BF)
-    gup_ref[...] = dot(u_ref[0], dkv, TN).astype(BF)
+    gup_ref[:, :D] = dot(u_ref[0], dq_ref[...], TN).astype(BF)
+    gup_ref[:, D:] = dot(u_ref[0], dkv, TN).astype(BF)
     gdn_ref[...] = dot(du, a_ref[...], TN).astype(BF)
     da = da_ref[...] + dot(dkv, w_ref[...], NT) + dot(du, dn_ref[...])
     back = layer_norm_back(
@@ -426,7 +489,7 @@
     dx_ref[...] = (dr_ref[...].astype(F32) + back).astype(BF)
 
 
-def leaving(which, da, du, dkv, a, u, x, dr, gain, dn, up, w):
+def leaving(which, dq, da, du, dkv, a, u, x, dr, gain, dn, up, w):
     rows = da.shape[0]
     wide = 2 * HEAD_DIM
     last = D // wide
@@ -437,7 +500,8 @@
         grid_spec=pltpu.PrefetchScalarGridSpec(
             num_scalar_prefetch=1,
             grid=(1,),
-            in_specs=[pl.BlockSpec((rows, D), whole), pl.BlockSpec((rows, RANK), whole)]
+            in_specs=[pl.BlockSpec((rows, D), whole)] * 2
+            + [pl.BlockSpec((rows, RANK), whole)]
             + [pl.BlockSpec((rows, wide), whole)] * len(dkv)
             + [
                 pl.BlockSpec((rows, D), mine),
@@ -452,20 +516,20 @@
             out_specs=[
                 pl.BlockSpec((rows, D), whole),
                 pl.BlockSpec((RANK, D), whole),
-                pl.BlockSpec((RANK, wide), whole),
+                pl.BlockSpec((RANK, D + wide), whole),
             ],
         ),
         out_shape=[
             jax.ShapeDtypeStruct((rows, D), BF),
             jax.ShapeDtypeStruct((RANK, D), BF),
-            jax.ShapeDtypeStruct((RANK, wide), BF),
+            jax.ShapeDtypeStruct((RANK, D + wide), BF),
         ],
         compiler_params=params(),
         cost_estimate=pl.CostEstimate(
             flops=4 * rows * D * wide, transcendentals=0, bytes_accessed=14 * rows * D
         ),
         name="leaving",
-    )(which, da, du, *dkv, a, u, x, dr, gain, dn, up, w)
+    )(which, dq, da, du, *dkv, a, u, x, dr, gain, dn, up, w)
 
 
 def gelu_parts(f):
@@ -513,8 +577,10 @@
     )(b, held, up_up, down_up)
 
 
-def mlp_down_kernel(trees, g_ref, x2_ref, wd_ref, dnd_ref, upd_ref, *refs):
-    y_refs, (sum_ref, acc_ref) = refs[:trees], refs[trees:]
+def mlp_down_kernel(
+    trees, g_ref, x2_ref, wd_ref, dnd_ref, upd_ref, norm_ref, dn_ref, up_ref, w_ref, *refs
+):
+    y_refs, (kv_ref, sum_ref, acc_ref) = refs[:trees], refs[trees:]
     step = pl.program_id(0)
     rows = g_ref.shape[0] // trees
 
@@ -533,11 +599,14 @@
         y = (sum_ref[...] + dot(u4, upd_ref[...])).astype(BF)
         for m in range(trees):
             y_refs[m][...] = y[m * rows : (m + 1) * rows]
-
-
-def mlp_down(trees, g, x2, w_down, down_down, up_down, block=1024):
+        a, u = ranks_of(y, norm_ref, dn_ref)
+        kv_ref[...] = (dot(a, w_ref[...]) + dot(masked(u, rows), up_ref[...])).astype(BF)
+
+
+def mlp_down(trees, g, x2, w_down, down_down, up_down, of_next, block=1024):
     total, hidden = g.shape
     rows, wide = total // trees, trees * RANK
+    pair = 2 * HEAD_DIM
     once = lambda j: (0, 0)
     return pl.pallas_call(
         functools.partial(mlp_down_kernel, trees),
@@ -548,9 +617,14 @@
             pl.BlockSpec((block, D), lambda j: (j, 0)),
             pl.BlockSpec((wide, block), lambda j: (0, j)),
             pl.BlockSpec((wide, D), once),
-        ],
-        out_specs=[pl.BlockSpec((rows, D), once)] * trees,
-        out_shape=[jax.ShapeDtypeStruct((rows, D), BF)] * trees,
+            pl.BlockSpec((2, D), once),
+            pl.BlockSpec((wide, D), once),
+            pl.BlockSpec((wide, pair), once),
+            pl.BlockSpec((D, pair), once),
+        ],
+        out_specs=[pl.BlockSpec((rows, D), once)] * trees + [pl.BlockSpec((total, pair), once)],
+        out_shape=[jax.ShapeDtypeStruct((rows, D), BF)] * trees
+        + [jax.ShapeDtypeStruct((total, pair), BF)],
         scratch_shapes=[pltpu.VMEM((total, D), F32), pltpu.VMEM((wide, total), F32)],
         compiler_params=params(),
         cost_estimate=pl.CostEstimate(
@@ -559,7 +633,7 @@
             bytes_accessed=2 * D * hidden + 2 * total * hidden,
         ),
         name="mlp_down",
-    )(g, x2, w_down, down_down, up_down)
+    )(g, x2, w_down, down_down, up_down, *of_next)
 
 
 def by_tree(u_ref, u, rows):
@@ -673,8 +747,24 @@
         arrived_ref, *refs = refs
     (b_ref, x2_ref, gain_ref, wu_ref, wd_ref, g_ref, gp_ref, u3_ref, u4_ref, upu_ref, dnd_ref,
      dnu_ref, upd_ref, o_ref, u2_ref, dno_ref, upo_ref, wo_ref,
-     dr_ref, do_ref, gdno_ref, gupo_ref, gdnu_ref, gupu_ref, gdnd_ref, gupd_ref,
+     dr_ref, do_ref, slab_ref,
      dy_ref, sum_ref, du4_ref, du3_ref, du2_ref) = refs
+    shards = slab_ref.shape[0]
+    small = D // shards
+    large = (slab_ref.shape[2] - 4 * small) // 2
+    at = [0, small, 2 * small, 3 * small, 3 * small + large, 3 * small + 2 * large]
+
+    def put(which, grad):
+        for z in range(shards):
+            part = grad[:, z * small : (z + 1) * small].astype(BF)
+            slab_ref[z, :, at[which] : at[which] + small] = part
+
+    def put_block(which, index, grad):
+        block = grad.shape[1]
+        per = large // block
+        cols = pl.ds(pl.multiple_of(at[which] + lax.rem(index, per) * block, 128), block)
+        slab_ref[index // per, :, cols] = grad.astype(BF)
+
     step = pl.program_id(0)
 
     @pl.when(step == 0)
@@ -684,7 +774,7 @@
             dy = jnp.where(flag_ref[0] == 1, dy, arrived_ref[...])
         dy_ref[...] = dy
         du4_ref[...] = (2.0 * dot(dy, upd_ref[...], NT)).astype(BF)
-        gupd_ref[...] = dot(u4_ref[0], dy, TN).astype(BF)
+        put(5, dot(u4_ref[0], dy, TN))
         sum_ref[...] = jnp.zeros_like(sum_ref)
         du3_ref[...] = jnp.zeros_like(du3_ref)
 
@@ -693,21 +783,21 @@
         du4 = du4_ref[...]
         dg = dot(dy_ref[...], wd_ref[...], NT) + dot(du4, dnd_ref[...])
         df = (gp_ref[...].astype(F32) * dg).astype(BF)
-        gdnd_ref[...] = dot(du4, g_ref[...], TN).astype(BF)
-        gupu_ref[...] = dot(u3_ref[0], df, TN).astype(BF)
+        put_block(4, step, dot(du4, g_ref[...], TN))
+        put_block(3, step, dot(u3_ref[0], df, TN))
         du3_ref[...] += dot(upu_ref[...], df, NT)
         sum_ref[...] += dot(df, wu_ref[0], NT)
 
     @pl.when(step == first - 1)
     def _():
         du3 = (2.0 * du3_ref[...].T).astype(BF)
-        gdnu_ref[...] = dot(du3, b_ref[...], TN).astype(BF)
+        put(2, dot(du3, b_ref[...], TN))
         db = (sum_ref[...] + dot(du3, dnu_ref[...])).astype(BF).astype(F32)
         back = layer_norm_back(x2_ref[...].astype(F32), gain_ref[...], db)
         dr = (dy_ref[...].astype(F32) + back).astype(BF)
         dr_ref[...] = dr
         du2_ref[...] = (2.0 * dot(dr, upo_ref[...], NT)).astype(BF)
-        gupo_ref[...] = dot(u2_ref[0], dr, TN).astype(BF)
+        put(1, dot(u2_ref[0], dr, TN))
 
     @pl.when(step >= first)
     def _():
@@ -717,7 +807,10 @@
         for z in range(wo_ref.shape[0]):
             do = do + dot(dr_ref[:, z * wide : (z + 1) * wide], wo_ref[z], NT)
         do_ref[...] = do.astype(BF)
-        gdno_ref[...] = dot(du2, o_ref[...], TN).astype(BF)
+        grad = dot(du2, o_ref[...], TN).astype(BF)
+        deep = grad.shape[1]
+        for z in range(deep // small):
+            slab_ref[(step - first) * (deep // small) + z, :, :small] = grad[:, z * small : (z + 1) * small]
 
 
 def backward_rest(
@@ -745,7 +838,8 @@
     ranks = pl.BlockSpec((1, rows, RANK), lambda i, w: (w[1], 0, 0))
     across = pl.BlockSpec((RANK, D), mine)
     shape = jax.ShapeDtypeStruct
-    dr, do, *grads = pl.pallas_call(
+    columns = 4 * (D // shards) + 2 * part
+    return pl.pallas_call(
         functools.partial(backward_kernel, given, first),
         grid_spec=pltpu.PrefetchScalarGridSpec(
             num_scalar_prefetch=1,
@@ -775,12 +869,7 @@
             out_specs=[
                 pl.BlockSpec((rows, D), once),
                 pl.BlockSpec((rows, deep), lambda i, w: (0, late(i))),
-                pl.BlockSpec((RANK, deep), lambda i, w: (0, late(i))),
-                pl.BlockSpec((RANK, D), once),
-                pl.BlockSpec((RANK, D), once),
-                pl.BlockSpec((RANK, block), lambda i, w: (0, early(i))),
-                pl.BlockSpec((RANK, block), lambda i, w: (0, early(i))),
-                pl.BlockSpec((RANK, D), once),
+                pl.BlockSpec((shards, RANK, columns), lambda i, w: (0, 0, 0)),
             ],
             scratch_shapes=[
                 pltpu.VMEM((rows, D), BF),
@@ -790,10 +879,7 @@
                 pltpu.VMEM((rows, RANK), BF),
             ],
         ),
-        out_shape=[shape((rows, D), BF)] * 2
-        + [shape((RANK, D), BF)] * 3
-        + [shape((RANK, hidden), BF)] * 2
-        + [shape((RANK, D), BF)],
+        out_shape=[shape((rows, D), BF)] * 2 + [shape((shards, RANK, columns), BF)],
         compiler_params=params(),
         cost_estimate=pl.CostEstimate(
             flops=4 * rows * D * hidden + 2 * rows * D * D,
@@ -806,7 +892,36 @@
         b, x2, gain, held, w_down, g, gp, u3, u4, up_up, dn_down, dn_up, up_down,
         o, u2, dn_out, up_out, held,
     )
-    return dr, do, grads
+
+
+def place_kernel(parts, ids_ref, *refs):
+    slab_refs, grad_refs = refs[: -len(parts)], refs[-len(parts) :]
+    for ref in grad_refs:
+        ref[...] = jnp.zeros_like(ref)
+    for m, slab_ref in enumerate(slab_refs):
+        for r in range(slab_ref.shape[0]):
+            name = ids_ref[r * len(slab_refs) + m]
+            for ref, (at, width) in zip(grad_refs, parts):
+                ref[name] += slab_ref[r, :, at : at + width].astype(F32)
+
+
+def place(ids, slabs, parts, adapters):
+    every = lambda i, ids: (0, 0, 0)
+    return pl.pallas_call(
+        functools.partial(place_kernel, parts),
+        grid_spec=pltpu.PrefetchScalarGridSpec(
+            num_scalar_prefetch=1,
+            grid=(1,),
+            in_specs=[pl.BlockSpec(slab.shape, every) for slab in slabs],
+            out_specs=[pl.BlockSpec((adapters, RANK, width), every) for _, width in parts],
+        ),
+        out_shape=[jax.ShapeDtypeStruct((adapters, RANK, width), F32) for _, width in parts],
+        compiler_params=params(),
+        cost_estimate=pl.CostEstimate(
+            flops=0, transcendentals=0, bytes_accessed=6 * slabs[0].size * len(slabs)
+        ),
+        name="place",
+    )(ids, *slabs)
 
 
 def segment_of(places, lengths):
@@ -881,16 +996,7 @@
     padded = -(-attn_wide // 128) * 128
     attn_at = -(-(part + out_wide) // padded) * padded
     each = D // members
-    own = jnp.concatenate(
-        [
-            quarter(w_up[0]),
-            quarter(w_out[0]),
-            jnp.zeros((each, attn_at - part - out_wide), BF),
-            quarter(w_attn[0]),
-            jnp.zeros((each, padded - attn_wide), BF),
-        ],
-        axis=1,
-    )
+    own = pack(member, each, w_up[0], w_out[0], w_attn[0].T, attn_at, attn_at + padded)
     held = gathered(own).reshape(shards, D, own.shape[1])
     down_full = gathered(quarter(w_down[0]))
     attn_full = assemble(held, attn_at, attn_wide)
@@ -911,7 +1017,13 @@
     )
     owners = lax.all_gather(chosen, "replica", axis=0, tiled=True)
     owners, picked = lax.optimization_barrier((owners, picked))
-    behind = jnp.stack([picked] + [shifted(picked, "fsdp", k) for k in range(1, shards)])
+    ups, downs = [picked], [picked]
+    for k in range(1, shards):
+        ups.append(lax.ppermute(ups[-1], "fsdp", [(i, i + 1) for i in range(shards - 1)]))
+        downs.append(lax.ppermute(downs[-1], "fsdp", [(i + 1, i) for i in range(shards - 1)]))
+    behind = jnp.stack(
+        [picked] + [jnp.where(shard >= k, ups[k], downs[shards - k]) for k in range(1, shards)]
+    )
     ordered = [
         lax.dynamic_index_in_dim(behind, lax.rem(shard - z + shards, shards), 0, keepdims=False)
         for z in range(shards)
@@ -941,36 +1053,43 @@
         return [kv] + [to_higher(kv, s) for s in range(1, shards)]
 
     own_rows = inputs.reshape(trees * per_tree, D)
-    before = ()
-    for m in range(trees):
-        a, u1, kv = entry(m, trees, own_rows, norms[0], dn_attn, up_attn_, attn_full)
-        blocks = with_lower(kv)
-        before = attention_forward(
-            m, trees, queries(m, a, u1, up_attn_, attn_full), blocks, biases[m][0], before, False
-        )
-    x2, b = mixing(before[0], own_rows, norms[1], dn_out, up_out_, held, part)
+    entered = [
+        entry(m, trees, own_rows, norms[0], dn_attn, up_attn_, attn_full) for m in range(trees)
+    ]
+    own_kv = jnp.concatenate([part[2] for part in entered], axis=0)
+    blocks = with_lower(own_kv)
+    attended = ()
+    for m, (a, u1, _) in enumerate(entered):
+        q = queries(m, a, u1, up_attn_, attn_full)
+        attended = attention_forward(m, trees, q, blocks, biases[m][0], attended, False)
+    x2, b = mixing(attended[0], own_rows, norms[1], dn_out, up_out_, held, part)
     g = mlp_up(b, held, part, up_up_, dn_up)
-    sent = mlp_down(trees, g, x2, down_full, dn_down, up_down_)
+    of_last = [
+        lax.ppermute(value, "section", [(1, 0)])
+        for value in (norms[0], dn_attn, up_attn_[:, D:], attn_full[:, D:])
+    ]
+    bias = jnp.concatenate([pair[1] for pair in biases], axis=0)
+    g, of_last, bias = lax.optimization_barrier((g, of_last, bias))
+    *sent, sent_kv = mlp_down(trees, g, x2, down_full, dn_down, up_down_, of_last)
+    arrived_kv = lax.ppermute(sent_kv, "section", [(0, 1)])
+    sent, arrived_kv = lax.optimization_barrier((sent, arrived_kv))
     arrived = [lax.ppermute(rows, "section", [(0, 1)]) for rows in sent]
+    blocks = with_lower(jnp.where(section == 0, own_kv, arrived_kv))
     entered, attended = (), ()
     for m in range(trees):
         rows = arrived[m]
         if m:
             rows, attended = lax.optimization_barrier((rows, attended))
-        a, u1, kv, *entered = entry(
-            m, trees, own_rows, norms[0], dn_attn, up_attn_, attn_full, rows, is_first, entered
+        a, u1, *entered = enter(
+            m, trees, own_rows, rows, is_first, norms[0], dn_attn, entered
         )
-        blocks = with_lower(kv)
-        attended = attention_forward(
-            m, trees, queries(m, a, u1, up_attn_, attn_full), blocks, biases[m][0], attended, True
-        )
+        q = queries(m, a, u1, up_attn_, attn_full)
+        attended = attention_forward(m, trees, q, blocks, biases[m][0], attended, True)
     x, a, u1 = entered
-    o, lse, q, *blocks = attended
+    o, lse, q = attended
     layer_out, x2, b, g, gp, u2, u3, u4 = forward_rest(
         trees, o, x, norms[1], held, part, down_full, maps
     )
-    bias = jnp.concatenate([pair[1] for pair in biases], axis=0)
-
     def by_shard(grads, parts):
         return jnp.stack(
             [
@@ -1008,50 +1127,42 @@
             arrived, ready = lax.optimization_barrier((arrived, ready))
             in_grads.append(ready[0])
             total = scattered(ready[1])
-        dr, do, early = backward_rest(
+        dr, do, slab = backward_rest(
             which, own_grads, b, x2, gain[1:2], held, part, down_full, g, gp, u2, u3, u4,
             o, maps, arrived,
         )
         if total is not None:
             do, total = lax.optimization_barrier((do, total))
             total = all_replicas(total)
-        if step == trees:
-            slabs = by_shard(early, widths[2:])
-            do, slabs = lax.optimization_barrier((do, slabs))
-            early_sum = scattered(slabs)
+        early_sum = scattered(slab) if step == trees else None
         dq, dkv = attention_backward(which, q, do, o, blocks, bias, lse)
         dkv = [dkv[0]] + [to_lower(dkv[s], s) for s in range(1, shards)]
-        da, du, g_up_q = query_leaving(which, dq, u1, up_attn_, attn_full)
         if total is not None:
-            da, total = lax.optimization_barrier((da, total))
-            sums.append((step - 2, total))
-        dx, g_dn, g_up_kv = leaving(
-            which, da, du, dkv, a, u1, x, dr, gain[0:1], dn_attn, up_attn_, attn_full
+            dq, total = lax.optimization_barrier((dq, total))
+            sums.append(total)
+        da, du = query_leaving(which, dq, up_attn_, attn_full)
+        if early_sum is not None:
+            da, early_sum = lax.optimization_barrier((da, early_sum))
+        dx, *late = leaving(
+            which, dq, da, du, dkv, a, u1, x, dr, gain[0:1], dn_attn, up_attn_, attn_full
         )
         if step < trees:
             arrived = lax.ppermute(dx, "section", [(1, 0)])
-        late = (g_dn, jnp.concatenate([g_up_q, g_up_kv], axis=1))
-        now = (dx, *late, *early)
+        late = by_shard(late, widths[:2])
+        now = (dx, slab, late)
         ready = None
         if 0 < step < trees:
             dx_ready, *grads = (
                 jnp.where(section == 1, was, new) for was, new in zip(before, now)
             )
-            ready = (dx_ready, by_shard(grads, widths))
+            ready = (dx_ready, jnp.concatenate(grads, axis=2))
         before = now
     in_grads.append(dx)
-    late_sum = permuted(by_shard(late, widths[:2]))
-    sums.append((trees - 1, all_replicas(jnp.concatenate([late_sum, early_sum], axis=1))))
-
-    finals = []
-    names = jnp.arange(down_attn.shape[1], dtype=jnp.int32)[:, None, None]
-    for at, width in zip(starts, widths):
-        total = jnp.zeros((down_attn.shape[1], RANK, width), F32)
-        for m, slabs in sums:
-            for r in range(members):
-                addend = slabs[r, :, at : at + width].astype(F32)[None]
-                total = total + jnp.where(names == cyclic[r * trees + m], addend, 0.0)
-        finals.append(total[None])
+    sums.append(all_replicas(jnp.concatenate([early_sum, permuted(late)], axis=1)))
+    order = [2, 3, 4, 5, 6, 7, 0, 1]
+    parts = [(sum(widths[i] for i in order[:at]), widths[i]) for at, i in enumerate(order)]
+    placed = place(cyclic, sums, parts, down_attn.shape[1])
+    finals = [placed[order.index(i)][None] for i in range(len(stacks))]
     return (
         layer_out.reshape(1, trees, per_tree, D),
         jnp.stack(in_grads)[None],

time: 1050 us -> 1000 us (0.952)
  other arithmetic: 43.2 us -> 17.1 us
  local copies, waits for them, and re-layouts: 51.4 us -> 25.8 us
  Pallas kernels: 439 us -> 450 us
    ppermute x0 -> x11, waiting for transfers between devices: none -> 53.7 us  [the longest x3 46.3 us: local(): lax.ppermute(downs[-1], 'fsdp', [(i + 1, i) for i in range(shards - 1)])]
    ppermute x12 -> x9, waiting for transfers between devices: 57.7 us -> 8.76 us  [shifted(): lax.ppermute(value, axis, [(i, (i + steps) % count) for i in range(count)])]
    all_gather x2, waiting for transfers between devices: 276 us -> 249 us  [gathered(): return lax.all_gather(own[None], ('fsdp', 'replica'), axis=1, tiled=True)[0]]
    ppermute x0 -> x11, starting transfers between devices: none -> 26.4 us  [the longest x3 13.6 us: local(): lax.ppermute(ups[-1], 'fsdp', [(i, i + 1) for i in range(shards - 1)])]
    ppermute x12 -> x6, starting transfers between devices: 46.4 us -> 24 us  [to_higher(): lax.ppermute(value, 'fsdp', [(i, i + steps) for i in range(shards - steps)])]
    ppermute x2, waiting for transfers between devices: 19.5 us -> 37.7 us  [local(): arrived = lax.ppermute(dx, 'section', [(1, 0)])]
    ppermute x12 -> x6, waiting for transfers between devices: 1.14 us -> 13.7 us  [to_higher(): lax.ppermute(value, 'fsdp', [(i, i + steps) for i in range(shards - steps)])]
    ppermute x2, waiting for transfers between devices: 16.7 us -> 4.85 us  [local(): arrived = [lax.ppermute(rows, 'section', [(0, 1)]) for rows in sent]]
  transfers between devices with their start and end apart: 41 -> 43, of which waited for: 16 -> 23; matrix products, arithmetic and copies ran while one was open for 6% -> 4% of each run, Pallas kernels for 20% -> 19%
where the time goes in v3:
time: 1000 us; the launch traced here: 992 us
  Pallas kernels  450 us (45%)
  waiting for transfers between devices  386 us (39%)
  starting transfers between devices  80.8 us (8%)
  local copies, waits for them, and re-layouts  25.8 us (3%)
  between operations  20 us (2%)
  other arithmetic  17.1 us (2%)
    all_gather x2, waiting for transfers between devices, gathered(): return lax.all_gather(own[None], ('fsdp', 'replica'), axis=1, tiled=True)[0]  249 us
    pallas_call x3, Pallas kernels, backward_rest(): pl.pallas_call(functools.partial(backward_kernel, given, first), grid_spe...  127 us
    pallas_call x1, Pallas kernels, forward_rest(): pl.pallas_call(functools.partial(forward_kernel, trees, shards), grid=(sh...  66.3 us
    ppermute x3, waiting for transfers between devices, local(): lax.ppermute(downs[-1], 'fsdp', [(i + 1, i) for i in range(shards - 1)])  46.3 us
    pallas_call x3, Pallas kernels, attention_backward(): pl.pallas_call(functools.partial(attention_backward_kernel, blocks, heads...  43.9 us
    ppermute x2, waiting for transfers between devices, local(): arrived = lax.ppermute(dx, 'section', [(1, 0)])  37.7 us
    pallas_call x4, Pallas kernels, attention_forward(): pl.pallas_call(functools.partial(attention_forward_kernel, blocks, heads,...  35 us
    pallas_call x1, Pallas kernels, mlp_down(): pl.pallas_call(functools.partial(mlp_down_kernel, trees), grid=(hidden //...  31.9 us
  transfers between devices with their start and end apart: 43, of which 23 were waited for; matrix products, arithmetic and copies ran while one was open for 4% of the time, Pallas kernels for 19%

profile of v3, /device:TPU:0, one launch (start us, length us, event | category | flops | bytes accessed | tf_op | source)
XLA Modules:
  0.0 991.9 jit_solution(13105204802045449038)
XLA Ops:
  7.2 3.9 pack.1
  11.2 3.2 constant_dynamic-slice_fusion
  16.5 6.8 all-reduce
  33.5 4.6 collective-permute-start
  41.8 1.6 fusion.3.refs_4_
  43.8 1.6 fusion.1.refs_4_
  45.9 11.2 %collective-permute-done.1 = bf16[32,7232]{1,0:T(8,128)(2,1)S(1)} collective-permute-done((bf16[32,7232]{1,0:T(8,128)(2,1)S(1)}, bf16[32,7232]{1,0:T(8,128)(2,1)S(1)}, u32[]{:S(2)}, u32[]{:S(2)}) %collective-permute-start.1) | collective-permute-done | bytes 462880 | tf_op jit(solution)/shard_map/ppermute | solution.py:1023
  58.5 4.5 collective-permute-start.4
  63.6 1.5 pad_maximum_fusion.refs_4_
  65.1 16.7 %collective-permute-done.2 = bf16[32,7232]{1,0:T(8,128)(2,1)S(1)} collective-permute-done((bf16[32,7232]{1,0:T(8,128)(2,1)S(1)}, bf16[32,7232]{1,0:T(8,128)(2,1)S(1)}, u32[]{:S(2)}, u32[]{:S(2)}) %collective-permute-start.2) | collective-permute-done | bytes 462880 | tf_op jit(solution)/shard_map/ppermute | solution.py:1023
  83.2 4.5 collective-permute-start.5
  87.8 18.5 %collective-permute-done.3 = bf16[32,7232]{1,0:T(8,128)(2,1)S(1)} collective-permute-done((bf16[32,7232]{1,0:T(8,128)(2,1)S(1)}, bf16[32,7232]{1,0:T(8,128)(2,1)S(1)}, u32[]{:S(2)}, u32[]{:S(2)}) %collective-permute-start.3) | collective-permute-done | bytes 462880 | tf_op jit(solution)/shard_map/ppermute | solution.py:1023
  115.7 185.3 %all-gather.7.cloned.1.call-done = bf16[8192,3200]{1,0:T(8,128)(2,1)} async-done(((bf16[512,3200]{1,0:T(8,128)(2,1)}), bf16[8192,3200]{1,0:T(8,128)(2,1)}) %all-gather.7.cloned.1.call-update) | async-done | bytes 52428816 | tf_op jit(solution)/shard_map/all_gather | solution.py:993
  301.0 10.9 %assemble.1.w_ref.refs_11_ = bf16[2048,2304]{1,0:T(8,128)(2,1)} custom-call(bf16[4,2048,3200]{2,1,0:T(8,128)(2,1)} %bitcast.145), custom_call_target="tpu_custom_call" | custom-call | bytes 20971520 | tf_op jit(solution)/shard_map/assemble/pallas_call | solution.py:241
  312.0 4.1 entry.3
  316.1 4.2 entry.2
  321.2 3.4 collective-permute-start.6
  324.6 3.1 collective-permute-start.7
  329.0 6.2 queries.5.q_ref
  336.5 6.1 queries.4.q_ref
  343.9 4.2 collective-permute-done.7.refs_2_
  349.6 9.5 collective-permute-done.8.refs_3_
  359.8 8.6 attention_forward.4
  368.4 8.7 attention_forward.5
  377.1 13.6 %mixing.1 = (f32[512,2048]{1,0:T(8,128)}, bf16[512,2048]{1,0:T(8,128)(2,1)}) custom-call(bf16[512,2048]{1,0:T(8,128)(2,1)} %get-tuple-element.128.o_ref, bf16[512,2048]{1,0:T(8,128)(2,1)} %bitcast.163, f32[2,2048]{1,0:T(2,128)} %pad_maximum_fusion.23.norm_ref.refs_2_, bf16[32,2048]{1,0:T(8,128)(2,1)} %pad_maximum_fusion.12.dn_ref.refs_3_.refs_17_.refs_18_, ...), custom_call_target="tpu_custom_call" | custom-call | flops 4294967296 | bytes 18874368 | tf_op jit(solution)/shard_map/mixing/pallas_call | solution.py:411
  390.7 28.4 %mlp_up.1.g_ref = bf16[512,8192]{1,0:T(8,128)(2,1)} custom-call(bf16[512,2048]{1,0:T(8,128)(2,1)} %get-tuple-element.129.b_ref, bf16[4,2048,3200]{2,1,0:T(8,128)(2,1)} %bitcast.147, bf16[32,8192]{1,0:T(8,128)(2,1)} %pad_maximum_fusion.5.upu_ref.refs_8_.refs_11_.refs_12_, bf16[32,2048]{1,0:T(8,128)(2,1)} %pad_maximum_fusion.14.dnu_ref.refs_10_.refs_13_.refs_14_), custom_call_target="tpu_custom_call" | custom-call | flops 17179869184 | bytes 41943040 | tf_op jit(solution)/shard_map/mlp_up/pallas_call | solution.py:558
  419.2 64.1 %all-gather.5.cloned.1.call-done = bf16[1,8192,2048]{2,1,0:T(8,128)(2,1)} async-done(((bf16[1,512,2048]{2,1,0:T(8,128)(2,1)}), bf16[1,8192,2048]{2,1,0:T(8,128)(2,1)}) %all-gather.5.cloned.1.call-update) | async-done | bytes 33554448 | tf_op jit(solution)/shard_map/all_gather | solution.py:993
  483.3 31.9 %mlp_down.1 = (bf16[256,2048]{1,0:T(8,128)(2,1)}, bf16[256,2048]{1,0:T(8,128)(2,1)}, bf16[512,256]{1,0:T(8,128)(2,1)}) custom-call(bf16[512,8192]{1,0:T(8,128)(2,1)} %mlp_up.1.g_ref, f32[512,2048]{1,0:T(8,128)} %get-tuple-element.131.x2_ref, bf16[8192,2048]{1,0:T(8,128)(2,1)} %bitcast.156, ...), custom_call_target="tpu_custom_call" | custom-call | flops 17179869184 | bytes 41943040 | tf_op jit(solution)/shard_map/mlp_down/pallas_call | solution.py:611
  515.2 3.6 collective-permute-start.13
  518.8 5.9 collective-permute-done.13
  524.7 4.3 collective-permute-start.15
  531.1 9.0 collective-permute-start.16
  540.1 6.0 collective-permute-start.17
  548.0 4.9 collective-permute-done.15.arrived_ref
  553.9 4.2 enter.2
  558.0 6.2 queries.6.q_ref
  565.8 8.9 attention_forward.6
  575.6 4.2 enter.3
  579.8 6.1 queries.7.q_ref
  585.8 8.8 attention_forward.7
  594.7 66.3 %forward_rest.1 = (bf16[512,2048]{1,0:T(8,128)(2,1)}, bf16[512,2048]{1,0:T(8,128)(2,1)}, bf16[512,2048]{1,0:T(8,128)(2,1)}, bf16[512,8192]{1,0:T(8,128)(2,1)}, b...) custom-call(bf16[512,2048]{1,0:T(8,128)(2,1)} %get-tuple-element.156, ...), custom_call_target="tpu_custom_call" | custom-call | flops 38654705664 | bytes 92274688 | tf_op jit(solution)/shard_map/forward_rest/pallas_call | solution.py:699
  661.0 42.0 %backward_rest.3 = (bf16[256,2048]{1,0:T(8,128)(2,1)}, bf16[256,2048]{1,0:T(8,128)(2,1)}, bf16[4,16,6144]{2,1,0:T(8,128)(2,1)}) custom-call(s32[2]{0:T(128)} %constant.143.clone.refs_0_._, bf16[512,2048]{1,0:T(8,128)(2,1)} %bitcast.166, bf16[512,2048]{1,0:T(8,128)(2,1)} %get-tuple-element.160.refs_2_.refs_3_, ...), custom_call_target="tpu_custom_call" | custom-call | flops 19327352832 | bytes 83886080 | tf_op jit(solution)/shard_map/backward_rest/pallas_call | solution.py:842
  703.0 14.8 %attention_backward.3 = (bf16[256,2048]{1,0:T(8,128)(2,1)}, bf16[256,256]{1,0:T(8,128)(2,1)}, bf16[256,256]{1,0:T(8,128)(2,1)}, bf16[256,256]{1,0:T(8,128)(2,1)}, bf16[256,256]{1,0:T(8,128)(2,1)}) custom-call(s32[2]{0:T(128)} %constant.143.clone.refs_0_._, bf16[512,2048]{1,0:T(8,128)(2,1)} %get-tuple-element.159.q_ref, ...), custom_call_target="tpu_custom_call" | custom-call | flops 10737418240 | bytes 5242880 | tf_op jit(solution)/shard_map/attention_backward/pallas_call | solution.py:165
  721.7 7.2 query_leaving.3
  730.0 10.9 %collective-permute-done.20.refs_2_ = bf16[256,256]{1,0:T(8,128)(2,1)S(1)} collective-permute-done((bf16[256,256]{1,0:T(8,128)(2,1)}, bf16[256,256]{1,0:T(8,128)(2,1)S(1)}, u32[]{:S(2)}, u32[]{:S(2)}) %collective-permute-start.20) | collective-permute-done | bytes 131104 | tf_op jit(solution)/shard_map/ppermute | solution.py:1050
  741.5 7.3 leaving.3
  751.8 19.0 %collective-permute-done.22.refs_2_ = bf16[256,2048]{1,0:T(8,128)(2,1)S(1)} collective-permute-done((bf16[256,2048]{1,0:T(8,128)(2,1)}, bf16[256,2048]{1,0:T(8,128)(2,1)S(1)}, u32[]{:S(2)}, u32[]{:S(2)}) %collective-permute-start.22) | collective-permute-done | bytes 1048608 | tf_op jit(solution)/shard_map/ppermute | solution.py:1150
  771.8 42.5 %backward_rest.4 = (bf16[256,2048]{1,0:T(8,128)(2,1)}, bf16[256,2048]{1,0:T(8,128)(2,1)}, bf16[4,16,6144]{2,1,0:T(8,128)(2,1)}) custom-call(s32[2]{0:T(128)} %pad_add_fusion.1.refs_0_._, bf16[512,2048]{1,0:T(8,128)(2,1)} %bitcast.167, bf16[256,2048]{1,0:T(8,128)(2,1)} %copy-done.2, bf16[512,2048]{1,0:T(8,128)(2,1)} %get-tuple-element.160.refs_2_.refs_3_, ...), custom_call_target="tpu_custom_call" | custom-call | flops 19327352832 | bytes 83886080 | tf_op jit(solution)/shard_map/backward_rest/pallas_call | solution.py:842
  814.3 14.5 %attention_backward.4 = (bf16[256,2048]{1,0:T(8,128)(2,1)}, bf16[256,256]{1,0:T(8,128)(2,1)}, bf16[256,256]{1,0:T(8,128)(2,1)}, bf16[256,256]{1,0:T(8,128)(2,1)}, bf16[256,256]{1,0:T(8,128)(2,1)}) custom-call(s32[2]{0:T(128)} %pad_add_fusion.1.refs_0_._, bf16[512,2048]{1,0:T(8,128)(2,1)} %get-tuple-element.159.q_ref, ...), custom_call_target="tpu_custom_call" | custom-call | flops 10737418240 | bytes 5242880 | tf_op jit(solution)/shard_map/attention_backward/pallas_call | solution.py:165
  832.8 7.4 query_leaving.4
  842.2 7.4 leaving.4
  853.7 18.7 %collective-permute-done.26.refs_2_ = bf16[256,2048]{1,0:T(8,128)(2,1)S(1)} collective-permute-done((bf16[256,2048]{1,0:T(8,128)(2,1)S(1)}, bf16[256,2048]{1,0:T(8,128)(2,1)S(1)}, u32[]{:S(2)}, u32[]{:S(2)}) %collective-permute-start.26) | collective-permute-done | bytes 1048608 | tf_op jit(solution)/shard_map/ppermute | solution.py:1150
  873.4 42.4 %backward_rest.5 = (bf16[256,2048]{1,0:T(8,128)(2,1)}, bf16[256,2048]{1,0:T(8,128)(2,1)}, bf16[4,16,6144]{2,1,0:T(8,128)(2,1)}) custom-call(s32[2]{0:T(128)} %pad_add_fusion.2.refs_0_._, bf16[512,2048]{1,0:T(8,128)(2,1)} %bitcast.168, bf16[256,2048]{1,0:T(8,128)(2,1)} %copy-done.1, bf16[512,2048]{1,0:T(8,128)(2,1)} %get-tuple-element.160.refs_2_.refs_3_, ...), custom_call_target="tpu_custom_call" | custom-call | flops 19327352832 | bytes 83886080 | tf_op jit(solution)/shard_map/backward_rest/pallas_call | solution.py:842
  916.0 1.9 collective-permute-start.28
  919.3 14.6 %attention_backward.5 = (bf16[256,2048]{1,0:T(8,128)(2,1)}, bf16[256,256]{1,0:T(8,128)(2,1)}, bf16[256,256]{1,0:T(8,128)(2,1)}, bf16[256,256]{1,0:T(8,128)(2,1)}, bf16[256,256]{1,0:T(8,128)(2,1)}) custom-call(s32[2]{0:T(128)} %pad_add_fusion.2.refs_0_._, bf16[512,2048]{1,0:T(8,128)(2,1)} %get-tuple-element.159.q_ref, ...), custom_call_target="tpu_custom_call" | custom-call | flops 10737418240 | bytes 5242880 | tf_op jit(solution)/shard_map/attention_backward/pallas_call | solution.py:165
  938.9 7.2 query_leaving.5
  946.2 4.9 collective-permute-done.31.refs_2_
  951.8 7.4 leaving.5
  962.4 2.5 collective-permute-start.35
  967.6 1.6 collective-permute-start.37
  970.6 1.5 maximum_bitcast_fusion
  972.1 2.9 collective-permute-done.36
  976.2 3.4 collective-permute-done.38
  980.7 4.3 place.1
  (269 shorter events, 76.3 us)
Async XLA Ops:
  7.2 293.8 %all-gather.7.cloned.1.call-start = ((), (), s32[]{:S(2)}) async-start(), calls=%async_computation.5 | async-start | bytes 55705600 | tf_op jit(solution)/shard_map/all_gather | solution.py:993
  11.2 472.1 %all-gather.5.cloned.1.call-start = ((), (), s32[]{:S(2)}) async-start(), calls=%async_computation.2 | async-start | bytes 35651584 | tf_op jit(solution)/shard_map/all_gather | solution.py:993
  14.4 23.7 %copy-start.30 = (bf16[1,2,2048]{2,1,0:T(2,128)(2,1)S(1)}, bf16[1,2,2048]{2,1,0:T(2,128)(2,1)}, u32[]{:S(2)}) copy-start(bf16[1,2,2048]{2,1,0:T(2,128)(2,1)} %param.22) | copy-start | bytes 24580
  14.5 23.7 %copy-start.31 = (bf16[1,2,2048]{2,1,0:T(2,128)(2,1)S(1)}, bf16[1,2,2048]{2,1,0:T(2,128)(2,1)}, u32[]{:S(2)}) copy-start(bf16[1,2,2048]{2,1,0:T(2,128)(2,1)} %param.23) | copy-start | bytes 24580
  14.5 25.2 %copy-start.33 = (s32[2,1,5]{2,1,0:T(1,128)S(1)}, s32[2,1,5]{2,1,0:T(1,128)}, u32[]{:S(2)}) copy-start(s32[2,1,5]{2,1,0:T(1,128)} %param.37) | copy-start | bytes 124
  14.5 25.4 %copy-start.34 = (s32[2,1,5]{2,1,0:T(1,128)S(1)}, s32[2,1,5]{2,1,0:T(1,128)}, u32[]{:S(2)}) copy-start(s32[2,1,5]{2,1,0:T(1,128)} %param.36) | copy-start | bytes 124
  14.5 901.4 %reduce-scatter.3.cloned.1.call-start = ((), (), s32[]{:S(2)}) async-start(), calls=%async_computation.3 | async-start | bytes 1167360 | tf_op jit(solution)/shard_map/reduce_scatter | solution.py:1104
  32.2 24.9 %collective-permute-start.1 = (bf16[32,7232]{1,0:T(8,128)(2,1)S(1)}, bf16[32,7232]{1,0:T(8,128)(2,1)S(1)}, u32[]{:S(2)}, u32[]{:S(2)}) collective-permute-start(bf16[32,7232]{1,0:T(8,128)(2,1)S(1)} %concatenate.118), channel_id=1, source_target_pairs={{4,0},{8,4},{12,8},{5,1},{9,5},{13,9},{6,2},{10,6},{14,10},{7,3},{... | collective-permute-start | bytes 1388552 | tf_op jit(solution)/shard_map/ppermute | solution.py:1023
  33.5 25.0 %collective-permute-start = (bf16[32,7232]{1,0:T(8,128)(2,1)S(1)}, bf16[32,7232]{1,0:T(8,128)(2,1)S(1)}, u32[]{:S(2)}, u32[]{:S(2)}) collective-permute-start(bf16[32,7232]{1,0:T(8,128)(2,1)S(1)} %concatenate.118), channel_id=1, source_target_pairs={{0,4},{4,8},{8,12},{1,5},{5,9},{9,13},{2,6},{6,10},{10,14},{3,7},{... | collective-permute-start | bytes 1388552 | tf_op jit(solution)/shard_map/ppermute | solution.py:1022
  38.2 24.8 %copy-start.16 = (f32[1,2048]{1,0:T(1,128)}, f32[1,2048]{1,0:T(1,128)S(1)}, u32[]{:S(2)}) copy-start(f32[1,2048]{1,0:T(1,128)S(1)} %get-tuple-element.309.refs_4_.refs_5_) | copy-start | bytes 24580
  38.3 380.8 %collective-permute-start.9 = (f32[2,2048]{1,0:T(2,128)S(1)}, f32[2,2048]{1,0:T(2,128)S(1)}, u32[]{:S(2)}, u32[]{:S(2)}) collective-permute-start(f32[2,2048]{1,0:T(2,128)S(1)} %pad_maximum_fusion.22.norm_ref), channel_id=1, source_target_pairs={{16,0},{17,1},{18,2},{19,3},{20,4},{21,5},{22,6},{23,7},{24,8},{25... | collective-permute-start | bytes 49160 | tf_op jit(solution)/shard_map/ppermute | solution.py:1068
  57.1 24.7 %collective-permute-start.2 = (bf16[32,7232]{1,0:T(8,128)(2,1)S(1)}, bf16[32,7232]{1,0:T(8,128)(2,1)S(1)}, u32[]{:S(2)}, u32[]{:S(2)}) collective-permute-start(bf16[32,7232]{1,0:T(8,128)(2,1)S(1)} %collective-permute-done.1), channel_id=1, source_target_pairs={{4,0},{8,4},{12,8},{5,1},{9,5},{13,9},{6,2},{10,6},{14,10},{7,3},{... | collective-permute-start | bytes 1388552 | tf_op jit(solution)/shard_map/ppermute | solution.py:1023
  58.5 24.7 %collective-permute-start.4 = (bf16[32,7232]{1,0:T(8,128)(2,1)S(1)}, bf16[32,7232]{1,0:T(8,128)(2,1)S(1)}, u32[]{:S(2)}, u32[]{:S(2)}) collective-permute-start(bf16[32,7232]{1,0:T(8,128)(2,1)S(1)} %collective-permute-done), channel_id=1, source_target_pairs={{0,4},{4,8},{8,12},{1,5},{5,9},{9,13},{2,6},{6,10},{10,14},{3,7},{... | collective-permute-start | bytes 1388552 | tf_op jit(solution)/shard_map/ppermute | solution.py:1022
  81.8 24.4 %collective-permute-start.3 = (bf16[32,7232]{1,0:T(8,128)(2,1)S(1)}, bf16[32,7232]{1,0:T(8,128)(2,1)S(1)}, u32[]{:S(2)}, u32[]{:S(2)}) collective-permute-start(bf16[32,7232]{1,0:T(8,128)(2,1)S(1)} %collective-permute-done.2), channel_id=1, source_target_pairs={{4,0},{8,4},{12,8},{5,1},{9,5},{13,9},{6,2},{10,6},{14,10},{7,3},{... | collective-permute-start | bytes 1388552 | tf_op jit(solution)/shard_map/ppermute | solution.py:1023
  83.2 24.4 %collective-permute-start.5 = (bf16[32,7232]{1,0:T(8,128)(2,1)S(1)}, bf16[32,7232]{1,0:T(8,128)(2,1)S(1)}, u32[]{:S(2)}, u32[]{:S(2)}) collective-permute-start(bf16[32,7232]{1,0:T(8,128)(2,1)S(1)} %collective-permute-done.4), channel_id=1, source_target_pairs={{0,4},{4,8},{8,12},{1,5},{5,9},{9,13},{2,6},{6,10},{10,14},{3,7},{... | collective-permute-start | bytes 1388552 | tf_op jit(solution)/shard_map/ppermute | solution.py:1022
  108.7 310.4 %collective-permute-start.10 = (bf16[32,2048]{1,0:T(8,128)(2,1)S(1)}, bf16[32,2048]{1,0:T(8,128)(2,1)S(1)}, u32[]{:S(2)}, u32[]{:S(2)}) collective-permute-start(bf16[32,2048]{1,0:T(8,128)(2,1)S(1)} %pad_maximum_fusion.11.dn_ref.refs_9_), channel_id=1, source_target_pairs={{16,0},{17,1},{18,2},{19,3},{20,4},{21,5},{22,6},{23,7},{24,8},{25... | collective-permute-start | bytes 393224 | tf_op jit(solution)/shard_map/ppermute | solution.py:1068
  321.2 14.0 %copy-start.10 = (bf16[512,256]{1,0:T(8,128)(2,1)}, bf16[512,256]{1,0:T(8,128)(2,1)S(1)}, u32[]{:S(2)}) copy-start(bf16[512,256]{1,0:T(8,128)(2,1)S(1)} %constant_dynamic-update-slice_fusion.refs_0_) | copy-start | bytes 786436
  321.2 21.4 %collective-permute-start.6 = (bf16[512,256]{1,0:T(8,128)(2,1)S(1)}, bf16[512,256]{1,0:T(8,128)(2,1)S(1)}, u32[]{:S(2)}, u32[]{:S(2)}) collective-permute-start(bf16[512,256]{1,0:T(8,128)(2,1)S(1)} %constant_dynamic-update-slice_fusion.refs_0_), channel_id=1, source_target_pairs={{0,4},{4,8},{8,12},{1,5},{5,9},{9,13},{2,6},{6,10},{10,14},{3,7},{... | collective-permute-start | bytes 786440 | tf_op jit(solution)/shard_map/ppermute | solution.py:1047
  324.6 23.5 %collective-permute-start.7 = (bf16[512,256]{1,0:T(8,128)(2,1)S(1)}, bf16[512,256]{1,0:T(8,128)(2,1)S(1)}, u32[]{:S(2)}, u32[]{:S(2)}) collective-permute-start(bf16[512,256]{1,0:T(8,128)(2,1)S(1)} %constant_dynamic-update-slice_fusion.refs_0_), channel_id=1, source_target_pairs={{0,8},{4,12},{1,9},{5,13},{2,10},{6,14},{3,11},{7,15},{16,24},{20,... | collective-permute-start | bytes 786440 | tf_op jit(solution)/shard_map/ppermute | solution.py:1047
  327.6 31.4 %collective-permute-start.8 = (bf16[512,256]{1,0:T(8,128)(2,1)S(1)}, bf16[512,256]{1,0:T(8,128)(2,1)S(1)}, u32[]{:S(2)}, u32[]{:S(2)}) collective-permute-start(bf16[512,256]{1,0:T(8,128)(2,1)S(1)} %constant_dynamic-update-slice_fusion.refs_0_), channel_id=1, source_target_pairs={{0,12},{1,13},{2,14},{3,15},{16,28},{17,29},{18,30},{19,31}} | collective-permute-start | bytes 786440 | tf_op jit(solution)/shard_map/ppermute | solution.py:1047
  342.6 16.5 %copy-start.41 = (bf16[512,256]{1,0:T(8,128)(2,1)}, bf16[512,256]{1,0:T(8,128)(2,1)S(1)}, u32[]{:S(2)}) copy-start(bf16[512,256]{1,0:T(8,128)(2,1)S(1)} %collective-permute-done.6.refs_1_) | copy-start | bytes 786436
  342.6 76.5 %collective-permute-start.11 = (bf16[32,256]{1,0:T(8,128)(2,1)S(1)}, bf16[32,256]{1,0:T(8,128)(2,1)S(1)}, u32[]{:S(2)}, u32[]{:S(2)}) collective-permute-start(bf16[32,256]{1,0:T(8,128)(2,1)S(1)} %slice.341), channel_id=1, source_target_pairs={{16,0},{17,1},{18,2},{19,3},{20,4},{21,5},{22,6},{23,7},{24,8},{25... | collective-permute-start | bytes 49160 | tf_op jit(solution)/shard_map/ppermute | solution.py:1068
  348.1 11.0 %copy-start.42 = (bf16[512,256]{1,0:T(8,128)(2,1)}, bf16[512,256]{1,0:T(8,128)(2,1)S(1)}, u32[]{:S(2)}) copy-start(bf16[512,256]{1,0:T(8,128)(2,1)S(1)} %collective-permute-done.7.refs_2_) | copy-start | bytes 786436
  348.1 71.1 %collective-permute-start.12 = (bf16[2048,256]{1,0:T(8,128)(2,1)S(1)}, bf16[2048,256]{1,0:T(8,128)(2,1)S(1)}, u32[]{:S(2)}, u32[]{:S(2)}) collective-permute-start(bf16[2048,256]{1,0:T(8,128)(2,1)S(1)} %slice.342), channel_id=1, source_target_pairs={{16,0},{17,1},{18,2},{19,3},{20,4},{21,5},{22,6},{23,7},{24,8},{25... | collective-permute-start | bytes 3145736 | tf_op jit(solution)/shard_map/ppermute | solution.py:1068
  419.1 64.1 %copy-start.45 = (f32[2,2048]{1,0:T(2,128)}, f32[2,2048]{1,0:T(2,128)S(1)}, u32[]{:S(2)}) copy-start(f32[2,2048]{1,0:T(2,128)S(1)} %collective-permute-done.9.norm_ref) | copy-start | bytes 49156
  419.1 64.1 %copy-start.46 = (bf16[32,256]{1,0:T(8,128)(2,1)}, bf16[32,256]{1,0:T(8,128)(2,1)S(1)}, u32[]{:S(2)}) copy-start(bf16[32,256]{1,0:T(8,128)(2,1)S(1)} %collective-permute-done.11.up_ref) | copy-start | bytes 49156
  419.2 64.1 %copy-start.44 = (bf16[32,2048]{1,0:T(8,128)(2,1)}, bf16[32,2048]{1,0:T(8,128)(2,1)S(1)}, u32[]{:S(2)}) copy-start(bf16[32,2048]{1,0:T(8,128)(2,1)S(1)} %collective-permute-done.10.dn_ref) | copy-start | bytes 393220
  419.2 64.1 %copy-start.37 = (bf16[2048,256]{1,0:T(8,128)(2,1)}, bf16[2048,256]{1,0:T(8,128)(2,1)S(1)}, u32[]{:S(2)}) copy-start(bf16[2048,256]{1,0:T(8,128)(2,1)S(1)} %collective-permute-done.12.w_ref) | copy-start | bytes 3145732
  483.3 47.7 %copy-start.11 = (bf16[512,256]{1,0:T(8,128)(2,1)S(1)}, bf16[512,256]{1,0:T(8,128)(2,1)}, u32[]{:S(2)}) copy-start(bf16[512,256]{1,0:T(8,128)(2,1)} %copy-done.10) | copy-start | bytes 786436
  515.2 9.5 collective-permute-start.13
  524.7 28.2 %collective-permute-start.15 = (bf16[256,2048]{1,0:T(8,128)(2,1)}, bf16[256,2048]{1,0:T(8,128)(2,1)S(1)}, u32[]{:S(2)}, u32[]{:S(2)}) collective-permute-start(bf16[256,2048]{1,0:T(8,128)(2,1)} %get-tuple-element.140), channel_id=1, source_target_pairs={{0,16},{1,17},{2,18},{3,19},{4,20},{5,21},{6,22},{7,23},{8,24},{9,... | collective-permute-start | bytes 3145736 | tf_op jit(solution)/shard_map/ppermute | solution.py:1076
  529.1 45.6 %collective-permute-start.14 = (bf16[256,2048]{1,0:T(8,128)(2,1)}, bf16[256,2048]{1,0:T(8,128)(2,1)S(1)}, u32[]{:S(2)}, u32[]{:S(2)}) collective-permute-start(bf16[256,2048]{1,0:T(8,128)(2,1)} %get-tuple-element.139), channel_id=1, source_target_pairs={{0,16},{1,17},{2,18},{3,19},{4,20},{5,21},{6,22},{7,23},{8,24},{9,... | collective-permute-start | bytes 3145736 | tf_op jit(solution)/shard_map/ppermute | solution.py:1076
  531.0 33.2 %copy-start.13 = (bf16[512,256]{1,0:T(8,128)(2,1)}, bf16[512,256]{1,0:T(8,128)(2,1)S(1)}, u32[]{:S(2)}) copy-start(bf16[512,256]{1,0:T(8,128)(2,1)S(1)} %broadcast_select_fusion.2.refs_0_) | copy-start | bytes 786436
  531.1 33.2 %collective-permute-start.16 = (bf16[512,256]{1,0:T(8,128)(2,1)S(1)}, bf16[512,256]{1,0:T(8,128)(2,1)S(1)}, u32[]{:S(2)}, u32[]{:S(2)}) collective-permute-start(bf16[512,256]{1,0:T(8,128)(2,1)S(1)} %broadcast_select_fusion.2.refs_0_), channel_id=1, source_target_pairs={{0,4},{4,8},{8,12},{1,5},{5,9},{9,13},{2,6},{6,10},{10,14},{3,7},{... | collective-permute-start | bytes 786440 | tf_op jit(solution)/shard_map/ppermute | solution.py:1047
  540.1 24.2 %collective-permute-start.17 = (bf16[512,256]{1,0:T(8,128)(2,1)S(1)}, bf16[512,256]{1,0:T(8,128)(2,1)S(1)}, u32[]{:S(2)}, u32[]{:S(2)}) collective-permute-start(bf16[512,256]{1,0:T(8,128)(2,1)S(1)} %broadcast_select_fusion.2.refs_0_), channel_id=1, source_target_pairs={{0,8},{4,12},{1,9},{5,13},{2,10},{6,14},{3,11},{7,15},{16,24},{20,... | collective-permute-start | bytes 786440 | tf_op jit(solution)/shard_map/ppermute | solution.py:1047
  546.1 18.2 %collective-permute-start.18 = (bf16[512,256]{1,0:T(8,128)(2,1)S(1)}, bf16[512,256]{1,0:T(8,128)(2,1)S(1)}, u32[]{:S(2)}, u32[]{:S(2)}) collective-permute-start(bf16[512,256]{1,0:T(8,128)(2,1)S(1)} %broadcast_select_fusion.2.refs_0_), channel_id=1, source_target_pairs={{0,12},{1,13},{2,14},{3,15},{16,28},{17,29},{18,30},{19,31}} | collective-permute-start | bytes 786440 | tf_op jit(solution)/shard_map/ppermute | solution.py:1047
  717.8 12.2 %collective-permute-start.19 = (bf16[256,256]{1,0:T(8,128)(2,1)}, bf16[256,256]{1,0:T(8,128)(2,1)S(1)}, u32[]{:S(2)}, u32[]{:S(2)}) collective-permute-start(bf16[256,256]{1,0:T(8,128)(2,1)} %get-tuple-element.174), channel_id=1, source_target_pairs={{4,0},{8,4},{12,8},{5,1},{9,5},{13,9},{6,2},{10,6},{14,10},{7,3},{... | collective-permute-start | bytes 393224 | tf_op jit(solution)/shard_map/ppermute | solution.py:1050
  719.1 21.8 %collective-permute-start.20 = (bf16[256,256]{1,0:T(8,128)(2,1)}, bf16[256,256]{1,0:T(8,128)(2,1)S(1)}, u32[]{:S(2)}, u32[]{:S(2)}) collective-permute-start(bf16[256,256]{1,0:T(8,128)(2,1)} %get-tuple-element.175), channel_id=1, source_target_pairs={{8,0},{12,4},{9,1},{13,5},{10,2},{14,6},{11,3},{15,7},{24,16},{28,... | collective-permute-start | bytes 393224 | tf_op jit(solution)/shard_map/ppermute | solution.py:1050
  720.4 20.5 %collective-permute-start.21 = (bf16[256,256]{1,0:T(8,128)(2,1)}, bf16[256,256]{1,0:T(8,128)(2,1)S(1)}, u32[]{:S(2)}, u32[]{:S(2)}) collective-permute-start(bf16[256,256]{1,0:T(8,128)(2,1)} %get-tuple-element.176), channel_id=1, source_target_pairs={{12,0},{13,1},{14,2},{15,3},{28,16},{29,17},{30,18},{31,19}} | collective-permute-start | bytes 393224 | tf_op jit(solution)/shard_map/ppermute | solution.py:1050
  748.8 22.0 %collective-permute-start.22 = (bf16[256,2048]{1,0:T(8,128)(2,1)}, bf16[256,2048]{1,0:T(8,128)(2,1)S(1)}, u32[]{:S(2)}, u32[]{:S(2)}) collective-permute-start(bf16[256,2048]{1,0:T(8,128)(2,1)} %get-tuple-element.180), channel_id=1, source_target_pairs={{16,0},{17,1},{18,2},{19,3},{20,4},{21,5},{22,6},{23,7},{24,8},{25... | collective-permute-start | bytes 3145736 | tf_op jit(solution)/shard_map/ppermute | solution.py:1150
  814.3 18.4 %copy-start.8 = (bf16[4,16,6144]{2,1,0:T(8,128)(2,1)S(1)}, bf16[4,16,6144]{2,1,0:T(8,128)(2,1)}, u32[]{:S(2)}) copy-start(bf16[4,16,6144]{2,1,0:T(8,128)(2,1)} %get-tuple-element.191) | copy-start | bytes 2359300
  814.3 18.4 %copy-start.9 = (bf16[4,16,6144]{2,1,0:T(8,128)(2,1)S(1)}, bf16[4,16,6144]{2,1,0:T(8,128)(2,1)}, u32[]{:S(2)}) copy-start(bf16[4,16,6144]{2,1,0:T(8,128)(2,1)} %get-tuple-element.192) | copy-start | bytes 2359300
  828.8 11.4 %collective-permute-start.23 = (bf16[256,256]{1,0:T(8,128)(2,1)}, bf16[256,256]{1,0:T(8,128)(2,1)S(1)}, u32[]{:S(2)}, u32[]{:S(2)}) collective-permute-start(bf16[256,256]{1,0:T(8,128)(2,1)} %get-tuple-element.186), channel_id=1, source_target_pairs={{4,0},{8,4},{12,8},{5,1},{9,5},{13,9},{6,2},{10,6},{14,10},{7,3},{... | collective-permute-start | bytes 393224 | tf_op jit(solution)/shard_map/ppermute | solution.py:1050
  830.1 10.2 %collective-permute-start.24 = (bf16[256,256]{1,0:T(8,128)(2,1)}, bf16[256,256]{1,0:T(8,128)(2,1)S(1)}, u32[]{:S(2)}, u32[]{:S(2)}) collective-permute-start(bf16[256,256]{1,0:T(8,128)(2,1)} %get-tuple-element.187), channel_id=1, source_target_pairs={{8,0},{12,4},{9,1},{13,5},{10,2},{14,6},{11,3},{15,7},{24,16},{28,... | collective-permute-start | bytes 393224 | tf_op jit(solution)/shard_map/ppermute | solution.py:1050
  831.4 10.2 %collective-permute-start.25 = (bf16[256,256]{1,0:T(8,128)(2,1)}, bf16[256,256]{1,0:T(8,128)(2,1)S(1)}, u32[]{:S(2)}, u32[]{:S(2)}) collective-permute-start(bf16[256,256]{1,0:T(8,128)(2,1)} %get-tuple-element.188), channel_id=1, source_target_pairs={{12,0},{13,1},{14,2},{15,3},{28,16},{29,17},{30,18},{31,19}} | collective-permute-start | bytes 393224 | tf_op jit(solution)/shard_map/ppermute | solution.py:1050
  851.2 21.3 %collective-permute-start.26 = (bf16[256,2048]{1,0:T(8,128)(2,1)S(1)}, bf16[256,2048]{1,0:T(8,128)(2,1)S(1)}, u32[]{:S(2)}, u32[]{:S(2)}) collective-permute-start(bf16[256,2048]{1,0:T(8,128)(2,1)S(1)} %copy-done.4), channel_id=1, source_target_pairs={{16,0},{17,1},{18,2},{19,3},{20,4},{21,5},{22,6},{23,7},{24,8},{25... | collective-permute-start | bytes 3145736 | tf_op jit(solution)/shard_map/ppermute | solution.py:1150
  872.5 73.7 %reduce-scatter.5.cloned.1.call-start = ((), (), s32[]{:S(2)}) async-start(), calls=%async_computation.4 | async-start | bytes 983040 | tf_op jit(solution)/shard_map/reduce_scatter | solution.py:1104
  915.9 21.9 %copy-start.14 = (bf16[1,16,7232]{2,1,0:T(8,128)(2,1)S(1)}, bf16[1,16,7232]{2,1,0:T(8,128)(2,1)}, u32[]{:S(2)}) copy-start(bf16[1,16,7232]{2,1,0:T(8,128)(2,1)} %reduce-scatter.3.cloned.1.call-done) | copy-start | bytes 694276
  915.9 20.6 %collective-permute-start.27 = (bf16[16,7232]{1,0:T(8,128)(2,1)}, bf16[16,7232]{1,0:T(8,128)(2,1)S(1)}, u32[]{:S(2)}, u32[]{:S(2)}) collective-permute-start(bf16[16,7232]{1,0:T(8,128)(2,1)} %bitcast.175), channel_id=1, source_target_pairs={{0,1},{1,2},{2,3},{3,0},{4,5},{5,6},{6,7},{7,4},{8,9},{9,10},{10,1... | collective-permute-start | bytes 694280 | tf_op jit(solution)/shard_map/ppermute | solution.py:969
  916.0 21.8 %collective-permute-start.28 = (bf16[16,7232]{1,0:T(8,128)(2,1)}, bf16[16,7232]{1,0:T(8,128)(2,1)S(1)}, u32[]{:S(2)}, u32[]{:S(2)}) collective-permute-start(bf16[16,7232]{1,0:T(8,128)(2,1)} %bitcast.176), channel_id=1, source_target_pairs={{0,2},{1,3},{2,0},{3,1},{4,6},{5,7},{6,4},{7,5},{8,10},{9,11},{10,... | collective-permute-start | bytes 694280 | tf_op jit(solution)/shard_map/ppermute | solution.py:969
  917.9 19.9 %collective-permute-start.29 = (bf16[16,7232]{1,0:T(8,128)(2,1)}, bf16[16,7232]{1,0:T(8,128)(2,1)S(1)}, u32[]{:S(2)}, u32[]{:S(2)}) collective-permute-start(bf16[16,7232]{1,0:T(8,128)(2,1)} %bitcast.177), channel_id=1, source_target_pairs={{0,3},{1,0},{2,1},{3,2},{4,7},{5,4},{6,5},{7,6},{8,11},{9,8},{10,9... | collective-permute-start | bytes 694280 | tf_op jit(solution)/shard_map/ppermute | solution.py:969
  933.9 12.3 %collective-permute-start.30 = (bf16[256,256]{1,0:T(8,128)(2,1)}, bf16[256,256]{1,0:T(8,128)(2,1)S(1)}, u32[]{:S(2)}, u32[]{:S(2)}) collective-permute-start(bf16[256,256]{1,0:T(8,128)(2,1)} %get-tuple-element.210), channel_id=1, source_target_pairs={{4,0},{8,4},{12,8},{5,1},{9,5},{13,9},{6,2},{10,6},{14,10},{7,3},{... | collective-permute-start | bytes 393224 | tf_op jit(solution)/shard_map/ppermute | solution.py:1050
  935.2 15.9 %collective-permute-start.31 = (bf16[256,256]{1,0:T(8,128)(2,1)}, bf16[256,256]{1,0:T(8,128)(2,1)S(1)}, u32[]{:S(2)}, u32[]{:S(2)}) collective-permute-start(bf16[256,256]{1,0:T(8,128)(2,1)} %get-tuple-element.211), channel_id=1, source_target_pairs={{8,0},{12,4},{9,1},{13,5},{10,2},{14,6},{11,3},{15,7},{24,16},{28,... | collective-permute-start | bytes 393224 | tf_op jit(solution)/shard_map/ppermute | solution.py:1050
  936.5 14.6 %collective-permute-start.32 = (bf16[256,256]{1,0:T(8,128)(2,1)}, bf16[256,256]{1,0:T(8,128)(2,1)S(1)}, u32[]{:S(2)}, u32[]{:S(2)}) collective-permute-start(bf16[256,256]{1,0:T(8,128)(2,1)} %get-tuple-element.212), channel_id=1, source_target_pairs={{12,0},{13,1},{14,2},{15,3},{28,16},{29,17},{30,18},{31,19}} | collective-permute-start | bytes 393224 | tf_op jit(solution)/shard_map/ppermute | solution.py:1050
  951.8 13.2 %copy-start.36 = (s32[4]{0:T(128)S(1)}, s32[4]{0:T(128)}, u32[]{:S(2)}) copy-start(s32[4]{0:T(128)} %fusion.36) | copy-start | bytes 52
  951.8 13.2 %copy-start.35 = (s32[8]{0:T(128)S(1)}, s32[8]{0:T(128)}, u32[]{:S(2)}) copy-start(s32[8]{0:T(128)} %all-reduce) | copy-start | bytes 100
  951.8 15.7 %copy-start.17 = (bf16[1,16,6144]{2,1,0:T(8,128)(2,1)S(1)}, bf16[1,16,6144]{2,1,0:T(8,128)(2,1)}, u32[]{:S(2)}) copy-start(bf16[1,16,6144]{2,1,0:T(8,128)(2,1)} %reduce-scatter.5.cloned.1.call-done) | copy-start | bytes 589828
  959.2 11.4 %copy-start.6 = (bf16[256,2048]{1,0:T(8,128)(2,1)S(1)}, bf16[256,2048]{1,0:T(8,128)(2,1)}, u32[]{:S(2)}) copy-start(bf16[256,2048]{1,0:T(8,128)(2,1)} %get-tuple-element.214) | copy-start | bytes 3145732
  961.1 5.9 collective-permute-start.33
  961.1 5.8 collective-permute-start.34
  962.4 5.0 collective-permute-start.35
  967.5 7.4 collective-permute-start.36
  967.6 8.6 collective-permute-start.37
  969.2 10.4 %collective-permute-start.38 = (bf16[16,7232]{1,0:T(8,128)(2,1)S(1)}, bf16[16,7232]{1,0:T(8,128)(2,1)S(1)}, u32[]{:S(2)}, u32[]{:S(2)}) collective-permute-start(bf16[16,7232]{1,0:T(8,128)(2,1)S(1)} %get-tuple-element.269), channel_id=1, source_target_pairs={{0,3},{1,0},{2,1},{3,2},{4,7},{5,4},{6,5},{7,6},{8,11},{9,8},{10,9... | collective-permute-start | bytes 694280 | tf_op jit(solution)/shard_map/ppermute | solution.py:969
  (27 other events, 70.6 us)
Sparse Core Ops, SparseCore 0:
  11.3 289.6 all-gather.6
  302.6 180.6 all-gather.4
  872.6 27.4 reduce-scatter.2
  916.0 25.5 reduce-scatter.4

commit v4 on v3

--- a/solution.py
+++ b/solution.py
@@ -21,7 +21,8 @@
 LOG2E = math.log2(math.e)
 LN2 = math.log(2.0)
 GELU_C = math.sqrt(2.0 / math.pi)
-VMEM_LIMIT = 56 * 1024 * 1024
+VMEM_LIMIT = 52 * 1024 * 1024
+SLICE = 512
 
 NN = (((1,), (0,)), ((), ()))
 NT = (((1,), (1,)), ((), ()))
@@ -67,14 +68,10 @@
     return jnp.where(tree_mask(value.shape[0], per_tree), 2.0 * value, 0.0).astype(BF)
 
 
-def attention_forward_kernel(blocks, heads, before, keep, q_ref, *refs):
-    kv_refs, (bias_ref, *refs) = refs[:blocks], refs[blocks:]
-    o_ref, lse_ref, *kept_refs = refs[before:]
+def attend(heads, q_ref, kv_refs, bias_ref, o_ref, lse_ref):
     keys = jnp.concatenate([r[:, :HEAD_DIM] for r in kv_refs], axis=0)
     vals = jnp.concatenate([r[:, HEAD_DIM:] for r in kv_refs], axis=0)
     vals = jnp.concatenate([vals, jnp.ones_like(vals)], axis=1)
-    if keep:
-        kept_refs[0][...] = q_ref[...]
     for h in range(heads):
         cols = slice(h * HEAD_DIM, (h + 1) * HEAD_DIM)
         scores = dot(q_ref[:, cols], keys, NT) + bias_ref[...]
@@ -86,27 +83,31 @@
         lse_ref[0, h : h + 1, :] = (top + jnp.log2(total)).T[0:1, :]
 
 
-def attention_forward(tree, trees, q, kv, bias, before, keep, heads=8):
+def attention_forward_kernel(blocks, heads, before, q_ref, *refs):
+    kv_refs, (bias_ref, *refs) = refs[:blocks], refs[blocks:]
+    attend(heads, q_ref, kv_refs, bias_ref, *refs[before:])
+
+
+def attention_forward(tree, trees, q, kv, bias, before, heads=8):
     rows = q.shape[0]
     blocks = len(kv)
     wide = heads * HEAD_DIM
     steps = HEADS // heads
-    mine = pl.BlockSpec((rows, wide), lambda i: (tree, i))
-    tall = jax.ShapeDtypeStruct((trees * rows, D), BF)
-    outs = [tall, jax.ShapeDtypeStruct((trees * steps, heads, rows), F32)]
-    out_specs = [mine, pl.BlockSpec((1, heads, rows), lambda i: (tree * steps + i, 0, 0))]
-    if keep:
-        outs.append(tall)
-        out_specs.append(mine)
-    return pl.pallas_call(
-        functools.partial(attention_forward_kernel, blocks, heads, len(before), keep),
+    return pl.pallas_call(
+        functools.partial(attention_forward_kernel, blocks, heads, len(before)),
         grid=(steps,),
         in_specs=[pl.BlockSpec((rows, wide), lambda i: (0, i))]
         + [pl.BlockSpec((rows, 2 * HEAD_DIM), lambda i: (tree, 0))] * blocks
         + [pl.BlockSpec((rows, blocks * rows), lambda i: (0, 0))]
         + [pl.BlockSpec(memory_space=pl.ANY)] * len(before),
-        out_specs=out_specs,
-        out_shape=outs,
+        out_specs=[
+            pl.BlockSpec((rows, wide), lambda i: (tree, i)),
+            pl.BlockSpec((1, heads, rows), lambda i: (tree * steps + i, 0, 0)),
+        ],
+        out_shape=[
+            jax.ShapeDtypeStruct((trees * rows, D), BF),
+            jax.ShapeDtypeStruct((trees * steps, heads, rows), F32),
+        ],
         input_output_aliases={blocks + 2 + i: i for i in range(len(before))},
         compiler_params=params(),
         cost_estimate=pl.CostEstimate(
@@ -298,57 +299,76 @@
     )(x, norm, dn, up, w)
 
 
-def enter_kernel(before, flag_ref, own_ref, arrived_ref, norm_ref, dn_ref, *refs):
-    a_ref, u_ref, x_all, a_all, u_all = refs[before:]
-    x = jnp.where(flag_ref[0] == 1, own_ref[...], arrived_ref[...])
-    x_all[...] = x
-    a, u = ranks_of(x, norm_ref, dn_ref)
-    a_ref[...] = a
-    a_all[...] = a
-    u = (2.0 * u).astype(BF)
-    u_ref[...] = u
-    u_all[0] = u
-
-
-def enter(tree, trees, own, arrived, flag, norm, dn, before):
+def enter_kernel(
+    blocks, heads, before, flag_ref, own_ref, arrived_ref, norm_ref, dn_ref, up_ref, w_ref, *refs
+):
+    kv_refs, (bias_ref, *refs) = refs[:blocks], refs[blocks:]
+    o_ref, lse_ref, q_ref, x_all, a_ref, u_ref = refs[before:]
+
+    @pl.when(pl.program_id(0) == 0)
+    def _():
+        x = jnp.where(flag_ref[0] == 1, own_ref[...], arrived_ref[...])
+        x_all[...] = x
+        a, u = ranks_of(x, norm_ref, dn_ref)
+        a_ref[...] = a
+        u_ref[0] = (2.0 * u).astype(BF)
+
+    q = dot(a_ref[...], w_ref[...]) + dot(u_ref[0], up_ref[...])
+    q_ref[...] = (q * (INV_ROOT * LOG2E)).astype(BF)
+    attend(heads, q_ref, kv_refs, bias_ref, o_ref, lse_ref)
+
+
+def enter(tree, trees, own, arrived, flag, norm, dn, up, w, kv, bias, before, heads=8):
     rows = own.shape[0] // trees
+    blocks = len(kv)
+    wide = heads * HEAD_DIM
+    steps = HEADS // heads
     whole = lambda i, f: (0, 0)
     mine = pl.BlockSpec((rows, D), lambda i, f: (tree, 0))
-    row = pl.BlockSpec((rows, D), whole)
-    return pl.pallas_call(
-        functools.partial(enter_kernel, len(before)),
+    part = pl.BlockSpec((rows, wide), lambda i, f: (tree, i))
+    tall = jax.ShapeDtypeStruct((trees * rows, D), BF)
+    return pl.pallas_call(
+        functools.partial(enter_kernel, blocks, heads, len(before)),
         grid_spec=pltpu.PrefetchScalarGridSpec(
             num_scalar_prefetch=1,
-            grid=(1,),
+            grid=(steps,),
             in_specs=[
                 mine,
-                row,
+                pl.BlockSpec((rows, D), whole),
                 pl.BlockSpec((2, D), whole),
                 pl.BlockSpec((RANK, D), lambda i, f: (tree, 0)),
+                pl.BlockSpec((RANK, wide), lambda i, f: (tree, i)),
+                pl.BlockSpec((D, wide), lambda i, f: (0, i)),
             ]
+            + [pl.BlockSpec((rows, 2 * HEAD_DIM), lambda i, f: (tree, 0))] * blocks
+            + [pl.BlockSpec((rows, blocks * rows), whole)]
             + [pl.BlockSpec(memory_space=pl.ANY)] * len(before),
             out_specs=[
-                row,
-                pl.BlockSpec((rows, RANK), whole),
+                part,
+                pl.BlockSpec((1, heads, rows), lambda i, f: (tree * steps + i, 0, 0)),
+                part,
                 mine,
                 mine,
                 pl.BlockSpec((1, rows, RANK), lambda i, f: (tree, 0, 0)),
             ],
         ),
         out_shape=[
-            jax.ShapeDtypeStruct((rows, D), BF),
-            jax.ShapeDtypeStruct((rows, RANK), BF),
-            jax.ShapeDtypeStruct((trees * rows, D), BF),
-            jax.ShapeDtypeStruct((trees * rows, D), BF),
+            tall,
+            jax.ShapeDtypeStruct((trees * steps, heads, rows), F32),
+            tall,
+            tall,
+            tall,
             jax.ShapeDtypeStruct((trees, rows, RANK), BF),
         ],
-        input_output_aliases={5 + i: 2 + i for i in range(len(before))},
-        compiler_params=params(),
-        cost_estimate=pl.CostEstimate(
-            flops=2 * rows * D * 256, transcendentals=0, bytes_accessed=10 * rows * D
+        input_output_aliases={8 + blocks + i: i for i in range(len(before))},
+        compiler_params=params(),
+        cost_estimate=pl.CostEstimate(
+            flops=2 * rows * D * D + 8 * rows * rows * blocks * D,
+            transcendentals=rows * rows * blocks * HEADS,
+            bytes_accessed=2 * D * D + 16 * rows * D + 4 * rows * rows * blocks,
         ),
         name="enter",
-    )(flag, own, arrived, norm, dn, *before)
+    )(flag, own, arrived, norm, dn, up, w, *kv, bias, *before)
 
 
 def queries_kernel(a_ref, u_ref, up_ref, w_ref, q_ref):
@@ -470,66 +490,91 @@
     )(which, dq, up, w)
 
 
-def leaving_kernel(blocks, _, dq_ref, da_ref, du_ref, *refs):
+def leaving_kernel(blocks, shards, _, dq_ref, da_ref, du_ref, *refs):
     dkv_refs = refs[:blocks]
     (a_ref, u_ref, x_ref, dr_ref, gain_ref, dn_ref, up_ref, w_ref,
-     dx_ref, gdn_ref, gup_ref) = refs[blocks:]
+     dx_ref, slab_ref, gdn_ref, gup_ref) = refs[blocks:]
+    step = pl.program_id(0)
+
+    @pl.when(step == 0)
+    def _():
+        gdn_ref[...] = jnp.zeros_like(gdn_ref)
+        gup_ref[...] = jnp.zeros_like(gup_ref)
+
     total = dkv_refs[0][...].astype(F32)
     for ref in dkv_refs[1:]:
         total = total + ref[...].astype(F32)
     dkv = total.astype(BF)
     du = (2.0 * (du_ref[...] + dot(dkv, up_ref[...], NT))).astype(BF)
-    gup_ref[:, :D] = dot(u_ref[0], dq_ref[...], TN).astype(BF)
-    gup_ref[:, D:] = dot(u_ref[0], dkv, TN).astype(BF)
-    gdn_ref[...] = dot(du, a_ref[...], TN).astype(BF)
+    gup_ref[:, :D] += dot(u_ref[0], dq_ref[...], TN)
+    gup_ref[:, D:] += dot(u_ref[0], dkv, TN)
+    gdn_ref[...] += dot(du, a_ref[...], TN)
     da = da_ref[...] + dot(dkv, w_ref[...], NT) + dot(du, dn_ref[...])
     back = layer_norm_back(
-        x_ref[...].astype(F32), gain_ref[...], da.astype(BF).astype(F32)
+        x_ref[...].astype(F32), gain_ref[0:1, :], da.astype(BF).astype(F32)
     )
     dx_ref[...] = (dr_ref[...].astype(F32) + back).astype(BF)
 
-
-def leaving(which, dq, da, du, dkv, a, u, x, dr, gain, dn, up, w):
-    rows = da.shape[0]
+    @pl.when(step == pl.num_programs(0) - 1)
+    def _():
+        small, large = D // shards, gup_ref.shape[1] // shards
+        for z in range(shards):
+            slab_ref[z] = jnp.concatenate(
+                [
+                    gdn_ref[:, z * small : (z + 1) * small],
+                    gup_ref[...][:, z * large : (z + 1) * large],
+                ],
+                axis=1,
+            ).astype(BF)
+
+
+def leaving(which, dq, da, du, dkv, a, u, x, dr, gain, dn, up, w, shards, steps=2):
+    rows = da.shape[0] // steps
     wide = 2 * HEAD_DIM
     last = D // wide
+    columns = (D + D + wide) // shards
     whole = lambda i, w: (0, 0)
-    mine = lambda i, w: (w[1], 0)
-    return pl.pallas_call(
-        functools.partial(leaving_kernel, len(dkv)),
+    here = pl.BlockSpec((rows, D), lambda i, w: (i, 0))
+    mine = pl.BlockSpec((rows, D), lambda i, w: (w[1] * steps + i, 0))
+    return pl.pallas_call(
+        functools.partial(leaving_kernel, len(dkv), shards),
         grid_spec=pltpu.PrefetchScalarGridSpec(
             num_scalar_prefetch=1,
-            grid=(1,),
-            in_specs=[pl.BlockSpec((rows, D), whole)] * 2
-            + [pl.BlockSpec((rows, RANK), whole)]
-            + [pl.BlockSpec((rows, wide), whole)] * len(dkv)
+            grid=(steps,),
+            in_specs=[here, here, pl.BlockSpec((rows, RANK), lambda i, w: (i, 0))]
+            + [pl.BlockSpec((rows, wide), lambda i, w: (i, 0))] * len(dkv)
             + [
-                pl.BlockSpec((rows, D), mine),
-                pl.BlockSpec((1, rows, RANK), lambda i, w: (w[1], 0, 0)),
-                pl.BlockSpec((rows, D), mine),
-                pl.BlockSpec((rows, D), whole),
-                pl.BlockSpec((1, D), whole),
-                pl.BlockSpec((RANK, D), mine),
+                mine,
+                pl.BlockSpec((1, rows, RANK), lambda i, w: (w[1], i, 0)),
+                mine,
+                here,
+                pl.BlockSpec((2, D), whole),
+                pl.BlockSpec((RANK, D), lambda i, w: (w[1], 0)),
                 pl.BlockSpec((RANK, wide), lambda i, w: (w[1], last)),
                 pl.BlockSpec((D, wide), lambda i, w: (0, last)),
             ],
-            out_specs=[
-                pl.BlockSpec((rows, D), whole),
-                pl.BlockSpec((RANK, D), whole),
-                pl.BlockSpec((RANK, D + wide), whole),
-            ],
+            out_specs=[here, pl.BlockSpec((shards, RANK, columns), lambda i, w: (0, 0, 0))],
+            scratch_shapes=[pltpu.VMEM((RANK, D), F32), pltpu.VMEM((RANK, D + wide), F32)],
         ),
         out_shape=[
-            jax.ShapeDtypeStruct((rows, D), BF),
-            jax.ShapeDtypeStruct((RANK, D), BF),
-            jax.ShapeDtypeStruct((RANK, D + wide), BF),
-        ],
-        compiler_params=params(),
-        cost_estimate=pl.CostEstimate(
-            flops=4 * rows * D * wide, transcendentals=0, bytes_accessed=14 * rows * D
+            jax.ShapeDtypeStruct(da.shape, BF),
+            jax.ShapeDtypeStruct((shards, RANK, columns), BF),
+        ],
+        compiler_params=params(),
+        cost_estimate=pl.CostEstimate(
+            flops=8 * rows * D * wide, transcendentals=0, bytes_accessed=28 * rows * D
         ),
         name="leaving",
     )(which, dq, da, du, *dkv, a, u, x, dr, gain, dn, up, w)
+
+
+def joined(ref):
+    return jnp.concatenate([ref[i] for i in range(ref.shape[0])], axis=1)
+
+
+def sliced(ref, value):
+    for i in range(ref.shape[0]):
+        ref[i] = value[:, i * SLICE : (i + 1) * SLICE]
 
 
 def gelu_parts(f):
@@ -544,7 +589,7 @@
         u3_ref[...] = masked(dot(b_ref[...], dnu_ref[...], NT), per_tree)
 
     f = dot(b_ref[...], wu_ref[0]) + dot(u3_ref[...], upu_ref[...])
-    g_ref[...] = (f * gelu_parts(f)[1]).astype(BF)
+    sliced(g_ref, (f * gelu_parts(f)[1]).astype(BF))
 
 
 def mlp_up(b, held, part, up_up, down_up, block=1024):
@@ -564,8 +609,8 @@
             pl.BlockSpec((wide, block), lambda j: (0, j)),
             pl.BlockSpec((wide, D), once),
         ],
-        out_specs=pl.BlockSpec((rows, block), lambda j: (0, j)),
-        out_shape=jax.ShapeDtypeStruct((rows, hidden), BF),
+        out_specs=pl.BlockSpec((block // SLICE, rows, SLICE), lambda j: (j, 0, 0)),
+        out_shape=jax.ShapeDtypeStruct((hidden // SLICE, rows, SLICE), BF),
         scratch_shapes=[pltpu.VMEM((rows, wide), BF)],
         compiler_params=params(),
         cost_estimate=pl.CostEstimate(
@@ -582,14 +627,14 @@
 ):
     y_refs, (kv_ref, sum_ref, acc_ref) = refs[:trees], refs[trees:]
     step = pl.program_id(0)
-    rows = g_ref.shape[0] // trees
+    rows = g_ref.shape[1] // trees
 
     @pl.when(step == 0)
     def _():
         sum_ref[...] = x2_ref[...]
         acc_ref[...] = jnp.zeros_like(acc_ref)
 
-    g = g_ref[...]
+    g = joined(g_ref)
     sum_ref[...] += dot(g, wd_ref[...])
     acc_ref[...] += dot(dnd_ref[...], g, NT)
 
@@ -604,7 +649,7 @@
 
 
 def mlp_down(trees, g, x2, w_down, down_down, up_down, of_next, block=1024):
-    total, hidden = g.shape
+    total, hidden = g.shape[1], g.shape[0] * SLICE
     rows, wide = total // trees, trees * RANK
     pair = 2 * HEAD_DIM
     once = lambda j: (0, 0)
@@ -612,7 +657,7 @@
         functools.partial(mlp_down_kernel, trees),
         grid=(hidden // block,),
         in_specs=[
-            pl.BlockSpec((total, block), lambda j: (0, j)),
+            pl.BlockSpec((block // SLICE, total, SLICE), lambda j: (j, 0, 0)),
             pl.BlockSpec((total, D), once, pipeline_mode=pl.Buffered(1)),
             pl.BlockSpec((block, D), lambda j: (j, 0)),
             pl.BlockSpec((wide, block), lambda j: (0, j)),
@@ -668,9 +713,9 @@
         f = dot(b_ref[...], wu_ref[0]) + dot(inner_ref[...], upu_ref[...])
         square, half = gelu_parts(f)
         g = (f * half).astype(BF)
-        g_ref[...] = g
+        sliced(g_ref, g)
         slope = f * ((2 * GELU_C) + (6 * GELU_C * 0.044715) * square)
-        gp_ref[...] = (half + (half * (1.0 - half)) * slope).astype(BF)
+        sliced(gp_ref, (half + (half * (1.0 - half)) * slope).astype(BF))
         sum_ref[...] += dot(g, wd_ref[...])
         acc_ref[...] += dot(dnd_ref[...], g, NT)
 
@@ -695,6 +740,7 @@
     late = lambda i: jnp.maximum(i - shards, 0)
     single = pl.Buffered(1)
     full = pl.BlockSpec((total, D), once)
+    hid = pl.BlockSpec((block // SLICE, total, SLICE), lambda i: (late(i), 0, 0))
     ranks = pl.BlockSpec((trees, rows, RANK), lambda i: (0, 0, 0))
     return pl.pallas_call(
         functools.partial(forward_kernel, trees, shards),
@@ -716,14 +762,14 @@
             full,
             full,
             full,
-            pl.BlockSpec((total, block), lambda i: (0, late(i))),
-            pl.BlockSpec((total, block), lambda i: (0, late(i))),
+            hid,
+            hid,
             ranks,
             ranks,
             ranks,
         ],
         out_shape=[jax.ShapeDtypeStruct((total, D), BF)] * 3
-        + [jax.ShapeDtypeStruct((total, hidden), BF)] * 2
+        + [jax.ShapeDtypeStruct((hidden // SLICE, total, SLICE), BF)] * 2
         + [jax.ShapeDtypeStruct((trees, rows, RANK), BF)] * 3,
         scratch_shapes=[
             pltpu.VMEM((total, D), F32),
@@ -782,8 +828,8 @@
     def _():
         du4 = du4_ref[...]
         dg = dot(dy_ref[...], wd_ref[...], NT) + dot(du4, dnd_ref[...])
-        df = (gp_ref[...].astype(F32) * dg).astype(BF)
-        put_block(4, step, dot(du4, g_ref[...], TN))
+        df = (joined(gp_ref).astype(F32) * dg).astype(BF)
+        put_block(4, step, dot(du4, joined(g_ref), TN))
         put_block(3, step, dot(u3_ref[0], df, TN))
         du3_ref[...] += dot(upu_ref[...], df, NT)
         sum_ref[...] += dot(df, wu_ref[0], NT)
@@ -793,7 +839,7 @@
         du3 = (2.0 * du3_ref[...].T).astype(BF)
         put(2, dot(du3, b_ref[...], TN))
         db = (sum_ref[...] + dot(du3, dnu_ref[...])).astype(BF).astype(F32)
-        back = layer_norm_back(x2_ref[...].astype(F32), gain_ref[...], db)
+        back = layer_norm_back(x2_ref[...].astype(F32), gain_ref[0:1, :], db)
         dr = (dy_ref[...].astype(F32) + back).astype(BF)
         dr_ref[...] = dr
         du2_ref[...] = (2.0 * dot(dr, upo_ref[...], NT)).astype(BF)
@@ -833,7 +879,7 @@
     single = pl.Buffered(1)
     row = pl.BlockSpec((rows, D), mine, pipeline_mode=single)
     given = 1 if arrived is None else 2
-    hid = pl.BlockSpec((rows, block), lambda i, w: (w[1], early(i)))
+    hid = pl.BlockSpec((block // SLICE, rows, SLICE), lambda i, w: (early(i), w[1], 0))
     thin = pl.BlockSpec((RANK, block), lambda i, w: (w[1], early(i)))
     ranks = pl.BlockSpec((1, rows, RANK), lambda i, w: (w[1], 0, 0))
     across = pl.BlockSpec((RANK, D), mine)
@@ -849,7 +895,7 @@
             + [
                 row,
                 row,
-                pl.BlockSpec((1, D), once),
+                pl.BlockSpec((2, D), once),
                 pl.BlockSpec((1, D, block), lambda i, w: (early(i) // per, 0, early(i) % per)),
                 pl.BlockSpec((block, D), lambda i, w: (early(i), 0)),
                 hid,
@@ -894,31 +940,37 @@
     )
 
 
-def place_kernel(parts, ids_ref, *refs):
-    slab_refs, grad_refs = refs[: -len(parts)], refs[-len(parts) :]
+def place_kernel(groups, trees, ids_ref, *refs):
+    count = sum(members for _, members, _ in groups)
+    slab_refs, grad_refs = refs[:count], refs[count:]
     for ref in grad_refs:
         ref[...] = jnp.zeros_like(ref)
-    for m, slab_ref in enumerate(slab_refs):
-        for r in range(slab_ref.shape[0]):
-            name = ids_ref[r * len(slab_refs) + m]
-            for ref, (at, width) in zip(grad_refs, parts):
-                ref[name] += slab_ref[r, :, at : at + width].astype(F32)
-
-
-def place(ids, slabs, parts, adapters):
+    at = 0
+    for tree, members, parts in groups:
+        for r in range(members):
+            name = ids_ref[r * trees + tree]
+            for which, start, width in parts:
+                grad_refs[which][name] += slab_refs[at][:, start : start + width].astype(F32)
+            at += 1
+
+
+def place(ids, groups, trees, widths, adapters):
+    slabs = [slab for _, slabs, _ in groups for slab in slabs]
     every = lambda i, ids: (0, 0, 0)
     return pl.pallas_call(
-        functools.partial(place_kernel, parts),
+        functools.partial(
+            place_kernel, [(tree, len(held), parts) for tree, held, parts in groups], trees
+        ),
         grid_spec=pltpu.PrefetchScalarGridSpec(
             num_scalar_prefetch=1,
             grid=(1,),
-            in_specs=[pl.BlockSpec(slab.shape, every) for slab in slabs],
-            out_specs=[pl.BlockSpec((adapters, RANK, width), every) for _, width in parts],
-        ),
-        out_shape=[jax.ShapeDtypeStruct((adapters, RANK, width), F32) for _, width in parts],
-        compiler_params=params(),
-        cost_estimate=pl.CostEstimate(
-            flops=0, transcendentals=0, bytes_accessed=6 * slabs[0].size * len(slabs)
+            in_specs=[pl.BlockSpec(slab.shape, lambda i, ids: (0, 0)) for slab in slabs],
+            out_specs=[pl.BlockSpec((adapters, RANK, width), every) for width in widths],
+        ),
+        out_shape=[jax.ShapeDtypeStruct((adapters, RANK, width), F32) for width in widths],
+        compiler_params=params(),
+        cost_estimate=pl.CostEstimate(
+            flops=0, transcendentals=0, bytes_accessed=6 * sum(slab.size for slab in slabs)
         ),
         name="place",
     )(ids, *slabs)
@@ -1061,7 +1113,7 @@
     attended = ()
     for m, (a, u1, _) in enumerate(entered):
         q = queries(m, a, u1, up_attn_, attn_full)
-        attended = attention_forward(m, trees, q, blocks, biases[m][0], attended, False)
+        attended = attention_forward(m, trees, q, blocks, biases[m][0], attended)
     x2, b = mixing(attended[0], own_rows, norms[1], dn_out, up_out_, held, part)
     g = mlp_up(b, held, part, up_up_, dn_up)
     of_last = [
@@ -1069,37 +1121,25 @@
         for value in (norms[0], dn_attn, up_attn_[:, D:], attn_full[:, D:])
     ]
     bias = jnp.concatenate([pair[1] for pair in biases], axis=0)
-    g, of_last, bias = lax.optimization_barrier((g, of_last, bias))
+    g, of_last = lax.optimization_barrier((g, of_last))
     *sent, sent_kv = mlp_down(trees, g, x2, down_full, dn_down, up_down_, of_last)
     arrived_kv = lax.ppermute(sent_kv, "section", [(0, 1)])
     sent, arrived_kv = lax.optimization_barrier((sent, arrived_kv))
     arrived = [lax.ppermute(rows, "section", [(0, 1)]) for rows in sent]
     blocks = with_lower(jnp.where(section == 0, own_kv, arrived_kv))
-    entered, attended = (), ()
+    entered = ()
     for m in range(trees):
         rows = arrived[m]
         if m:
-            rows, attended = lax.optimization_barrier((rows, attended))
-        a, u1, *entered = enter(
-            m, trees, own_rows, rows, is_first, norms[0], dn_attn, entered
+            rows, entered = lax.optimization_barrier((rows, entered))
+        entered = enter(
+            m, trees, own_rows, rows, is_first, norms[0], dn_attn, up_attn_, attn_full, blocks,
+            biases[m][0], entered,
         )
-        q = queries(m, a, u1, up_attn_, attn_full)
-        attended = attention_forward(m, trees, q, blocks, biases[m][0], attended, True)
-    x, a, u1 = entered
-    o, lse, q = attended
+    o, lse, q, x, a, u1 = entered
     layer_out, x2, b, g, gp, u2, u3, u4 = forward_rest(
         trees, o, x, norms[1], held, part, down_full, maps
     )
-    def by_shard(grads, parts):
-        return jnp.stack(
-            [
-                jnp.concatenate(
-                    [g[:, z * part : (z + 1) * part] for g, part in zip(grads, parts)], axis=1
-                )
-                for z in range(shards)
-            ]
-        )
-
     def scattered(slabs):
         return lax.psum_scatter(slabs, "fsdp", scatter_dimension=0)
 
@@ -1111,11 +1151,16 @@
         return total.astype(BF)
 
     def all_replicas(total):
-        return jnp.stack([total] + [shifted(total, "replica", i) for i in range(1, members)])
+        return [total] + [shifted(total, "replica", i) for i in range(1, members)]
 
     own_grads = cotangent.reshape(trees * per_tree, D)
     order = lax.rem(member - jnp.arange(members, dtype=jnp.int32) + members, members)
     cyclic = owners.reshape(members, trees)[order].reshape(-1)
+    early_ones, late_ones = tuple(range(2, len(stacks))), (0, 1)
+
+    def columns(order):
+        return [(i, sum(widths[j] for j in order[:at]), widths[i]) for at, i in enumerate(order)]
+
     in_grads, sums, arrived, before, total, ready = [], [], None, None, None, None
     for step in range(trees + 1):
         tree = jnp.clip(step - 1 + section, 0, trees - 1)
@@ -1128,7 +1173,7 @@
             in_grads.append(ready[0])
             total = scattered(ready[1])
         dr, do, slab = backward_rest(
-            which, own_grads, b, x2, gain[1:2], held, part, down_full, g, gp, u2, u3, u4,
+            which, own_grads, b, x2, norms[1], held, part, down_full, g, gp, u2, u3, u4,
             o, maps, arrived,
         )
         if total is not None:
@@ -1139,16 +1184,15 @@
         dkv = [dkv[0]] + [to_lower(dkv[s], s) for s in range(1, shards)]
         if total is not None:
             dq, total = lax.optimization_barrier((dq, total))
-            sums.append(total)
+            sums.append((step - 2, total, columns(early_ones + late_ones)))
         da, du = query_leaving(which, dq, up_attn_, attn_full)
         if early_sum is not None:
             da, early_sum = lax.optimization_barrier((da, early_sum))
-        dx, *late = leaving(
-            which, dq, da, du, dkv, a, u1, x, dr, gain[0:1], dn_attn, up_attn_, attn_full
+        dx, late = leaving(
+            which, dq, da, du, dkv, a, u1, x, dr, norms[0], dn_attn, up_attn_, attn_full, shards
         )
         if step < trees:
             arrived = lax.ppermute(dx, "section", [(1, 0)])
-        late = by_shard(late, widths[:2])
         now = (dx, slab, late)
         ready = None
         if 0 < step < trees:
@@ -1158,11 +1202,11 @@
             ready = (dx_ready, jnp.concatenate(grads, axis=2))
         before = now
     in_grads.append(dx)
-    sums.append(all_replicas(jnp.concatenate([early_sum, permuted(late)], axis=1)))
-    order = [2, 3, 4, 5, 6, 7, 0, 1]
-    parts = [(sum(widths[i] for i in order[:at]), widths[i]) for at, i in enumerate(order)]
-    placed = place(cyclic, sums, parts, down_attn.shape[1])
-    finals = [placed[order.index(i)][None] for i in range(len(stacks))]
+    early_sums, late = lax.optimization_barrier((all_replicas(early_sum), late))
+    sums.append((trees - 1, early_sums, columns(early_ones)))
+    sums.append((trees - 1, all_replicas(permuted(late)), columns(late_ones)))
+    placed = place(cyclic, sums, trees, widths, down_attn.shape[1])
+    finals = [grad[None] for grad in placed]
     return (
         layer_out.reshape(1, trees, per_tree, D),
         jnp.stack(in_grads)[None],

time: 1000 us -> 987 us (0.987)
  Pallas kernels: 450 us -> 425 us
  waiting for transfers between devices: 386 us -> 407 us
    pallas_call x4 -> x2, Pallas kernels: 35 us -> 17 us  [attention_forward(): pl.pallas_call(functools.partial(attention_forward_kernel, blocks, heads,...]
    pallas_call x6, Pallas kernels: 34.7 us -> 49.6 us  [the longest x2 27.7 us: enter(): pl.pallas_call(functools.partial(enter_kernel, blocks, heads, len(before)...]
    pallas_call x4 -> x2, Pallas kernels: 24.6 us -> 11.1 us  [queries(): pl.pallas_call(queries_kernel, grid=(D // block,), in_specs=[pl.BlockSpec...]
  transfers between devices with their start and end apart: 43 -> 46, of which waited for: 23 -> 24; matrix products, arithmetic and copies ran while one was open for 4% -> 3% of each run, Pallas kernels for 19% -> 19%
where the time goes in v4:
time: 987 us; the launch traced here: 977 us
  Pallas kernels  425 us (43%)
  waiting for transfers between devices  407 us (41%)
  starting transfers between devices  81.2 us (8%)
  local copies, waits for them, and re-layouts  20.8 us (2%)
  between operations  19.8 us (2%)
  other arithmetic  10.6 us (1%)
    all_gather x2, waiting for transfers between devices, gathered(): return lax.all_gather(own[None], ('fsdp', 'replica'), axis=1, tiled=True)[0]  255 us
    pallas_call x3, Pallas kernels, backward_rest(): pl.pallas_call(functools.partial(backward_kernel, given, first), grid_spe...  125 us
    pallas_call x1, Pallas kernels, forward_rest(): pl.pallas_call(functools.partial(forward_kernel, trees, shards), grid=(sh...  66.1 us
    ppermute x3, waiting for transfers between devices, local(): lax.ppermute(downs[-1], 'fsdp', [(i + 1, i) for i in range(shards - 1)])  49.5 us
    pallas_call x3, Pallas kernels, attention_backward(): pl.pallas_call(functools.partial(attention_backward_kernel, blocks, heads...  42.2 us
    ppermute x2, waiting for transfers between devices, local(): arrived = lax.ppermute(dx, 'section', [(1, 0)])  41.5 us
    pallas_call x1, Pallas kernels, mlp_down(): pl.pallas_call(functools.partial(mlp_down_kernel, trees), grid=(hidden //...  30.5 us
    pallas_call x1, Pallas kernels, mlp_up(): pl.pallas_call(functools.partial(mlp_up_kernel, rows * RANK // wide), gri...  28.3 us
  transfers between devices with their start and end apart: 46, of which 24 were waited for; matrix products, arithmetic and copies ran while one was open for 3% of the time, Pallas kernels for 19%

profile of v4, /device:TPU:0, one launch (start us, length us, event | category | flops | bytes accessed | tf_op | source)
XLA Modules:
  0.0 976.5 jit_solution(13329741491135551859)
XLA Ops:
  7.2 4.0 pack.1
  11.3 3.2 constant_dynamic-slice_fusion
  16.5 6.9 all-reduce
  33.6 4.6 collective-permute-start
  41.5 1.6 fusion.3.refs_4_
  43.1 14.0 %collective-permute-done.1 = bf16[32,7232]{1,0:T(8,128)(2,1)S(1)} collective-permute-done((bf16[32,7232]{1,0:T(8,128)(2,1)S(1)}, bf16[32,7232]{1,0:T(8,128)(2,1)S(1)}, u32[]{:S(2)}, u32[]{:S(2)}) %collective-permute-start.1) | collective-permute-done | bytes 462880 | tf_op jit(solution)/shard_map/ppermute | solution.py:1075
  58.5 4.5 collective-permute-start.4
  63.3 1.6 fusion.1.refs_4_
  64.9 16.9 %collective-permute-done.2 = bf16[32,7232]{1,0:T(8,128)(2,1)S(1)} collective-permute-done((bf16[32,7232]{1,0:T(8,128)(2,1)S(1)}, bf16[32,7232]{1,0:T(8,128)(2,1)S(1)}, u32[]{:S(2)}, u32[]{:S(2)}) %collective-permute-start.2) | collective-permute-done | bytes 462880 | tf_op jit(solution)/shard_map/ppermute | solution.py:1075
  83.2 4.5 collective-permute-start.5
  87.8 18.5 %collective-permute-done.3 = bf16[32,7232]{1,0:T(8,128)(2,1)S(1)} collective-permute-done((bf16[32,7232]{1,0:T(8,128)(2,1)S(1)}, bf16[32,7232]{1,0:T(8,128)(2,1)S(1)}, u32[]{:S(2)}, u32[]{:S(2)}) %collective-permute-start.3) | collective-permute-done | bytes 462880 | tf_op jit(solution)/shard_map/ppermute | solution.py:1075
  110.9 190.1 %all-gather.7.cloned.1.call-done = bf16[8192,3200]{1,0:T(8,128)(2,1)} async-done(((bf16[512,3200]{1,0:T(8,128)(2,1)}), bf16[8192,3200]{1,0:T(8,128)(2,1)}) %all-gather.7.cloned.1.call-update) | async-done | bytes 52428816 | tf_op jit(solution)/shard_map/all_gather | solution.py:1045
  301.1 11.0 %assemble.1.w_ref.refs_11_ = bf16[2048,2304]{1,0:T(8,128)(2,1)} custom-call(bf16[4,2048,3200]{2,1,0:T(8,128)(2,1)} %bitcast.120), custom_call_target="tpu_custom_call" | custom-call | bytes 20971520 | tf_op jit(solution)/shard_map/assemble/pallas_call | solution.py:242
  312.0 3.4 entry.3
  316.4 3.4 entry.2
  320.8 3.9 collective-permute-start.8
  326.1 2.5 collective-permute-start.6
  328.6 5.6 queries.3.q_ref
  334.2 1.7 slice.240
  335.9 5.4 queries.2.q_ref
  343.7 4.6 collective-permute-done.7.refs_2_
  349.7 9.5 collective-permute-done.6.refs_1_
  359.2 8.5 attention_forward.2
  367.7 8.6 attention_forward.3
  376.3 13.6 %mixing.1 = (f32[512,2048]{1,0:T(8,128)}, bf16[512,2048]{1,0:T(8,128)(2,1)}) custom-call(bf16[512,2048]{1,0:T(8,128)(2,1)} %get-tuple-element.131.o_ref, bf16[512,2048]{1,0:T(8,128)(2,1)} %bitcast.141, f32[2,2048]{1,0:T(2,128)S(1)} %pad_maximum_fusion.19.norm_ref.refs_2_.refs_4_.refs_5_, ...), custom_call_target="tpu_custom_call" | custom-call | flops 4294967296 | bytes 18874368 | tf_op jit(solution)/shard_map/mixing/pallas_call | solution.py:431
  389.9 28.3 %mlp_up.1.g_ref = bf16[16,512,512]{2,1,0:T(8,128)(2,1)} custom-call(bf16[512,2048]{1,0:T(8,128)(2,1)} %get-tuple-element.132.b_ref, bf16[4,2048,3200]{2,1,0:T(8,128)(2,1)} %bitcast.122, bf16[32,8192]{1,0:T(8,128)(2,1)S(1)} %pad_maximum_fusion.3.upu_ref.refs_8_.refs_11_.refs_12_, bf16[32,2048]{1,0:T(8,128)(2,1)S(1)} %pad_maximum_fusion.10.dnu_ref.refs_10_.refs_13_.refs_14_), custom_call_target="tpu_custom_call" | custom-call | flops 17179869184 | bytes 41943040 | tf_op jit(solution)/shard_map/mlp_up/pallas_call | solution.py:603
  418.2 65.1 %all-gather.5.cloned.1.call-done = bf16[1,8192,2048]{2,1,0:T(8,128)(2,1)} async-done(((bf16[1,512,2048]{2,1,0:T(8,128)(2,1)}), bf16[1,8192,2048]{2,1,0:T(8,128)(2,1)}) %all-gather.5.cloned.1.call-update) | async-done | bytes 33554448 | tf_op jit(solution)/shard_map/all_gather | solution.py:1045
  483.3 30.5 %mlp_down.1 = (bf16[256,2048]{1,0:T(8,128)(2,1)}, bf16[256,2048]{1,0:T(8,128)(2,1)}, bf16[512,256]{1,0:T(8,128)(2,1)S(1)}) custom-call(bf16[16,512,512]{2,1,0:T(8,128)(2,1)} %mlp_up.1.g_ref, f32[512,2048]{1,0:T(8,128)} %get-tuple-element.134.x2_ref, bf16[8192,2048]{1,0:T(8,128)(2,1)} %bitcast.131, ...), custom_call_target="tpu_custom_call" | custom-call | flops 17179869184 | bytes 41943040 | tf_op jit(solution)/shard_map/mlp_down/pallas_call | solution.py:656
  513.8 3.6 collective-permute-start.13
  517.4 5.5 collective-permute-done.13
  523.0 5.4 collective-permute-start.15
  531.0 8.4 collective-permute-start.18
  539.4 5.4 collective-permute-start.17
  547.6 3.9 collective-permute-done.17.refs_2_
  551.5 4.0 collective-permute-done.16.refs_1_
  555.5 13.9 %enter.2 = (bf16[512,2048]{1,0:T(8,128)(2,1)}, f32[4,8,256]{2,1,0:T(8,128)S(1)}, bf16[512,2048]{1,0:T(8,128)(2,1)}, bf16[512,2048]{1,0:T(8,128)(2,1)}, bf16[512,...) custom-call(s32[1]{0:T(128)} %bitcast.flag_ref, bf16[512,2048]{1,0:T(8,128)(2,1)} %bitcast.142, ...), custom_call_target="tpu_custom_call" | custom-call | flops 6442450944 | bytes 17825792 | tf_op jit(solution)/shard_map/enter/pallas_call | solution.py:330
  569.5 2.1 collective-permute-done.14.arrived_ref
  572.6 13.7 %enter.3 = (bf16[512,2048]{1,0:T(8,128)(2,1)}, f32[4,8,256]{2,1,0:T(8,128)S(1)}, bf16[512,2048]{1,0:T(8,128)(2,1)}, bf16[512,2048]{1,0:T(8,128)(2,1)}, bf16[512,...) custom-call(s32[1]{0:T(128)} %bitcast.flag_ref, ...), custom_call_target="tpu_custom_call", output_to_operand_aliasing={{0}: (12, {}), {1}: (13, {}), {2}: (14, {}), {3}: (15, {}),... | custom-call | flops 6442450944 | bytes 17825792 | tf_op jit(solution)/shard_map/enter/pallas_call | solution.py:330
  586.3 66.1 %forward_rest.1 = (bf16[512,2048]{1,0:T(8,128)(2,1)}, bf16[512,2048]{1,0:T(8,128)(2,1)}, bf16[512,2048]{1,0:T(8,128)(2,1)}, bf16[16,512,512]{2,1,0:T(8,128)(2,1)...) custom-call(bf16[512,2048]{1,0:T(8,128)(2,1)} %get-tuple-element.158, ...), custom_call_target="tpu_custom_call" | custom-call | flops 38654705664 | bytes 92274688 | tf_op jit(solution)/shard_map/forward_rest/pallas_call | solution.py:745
  652.4 41.3 %backward_rest.3 = (bf16[256,2048]{1,0:T(8,128)(2,1)}, bf16[256,2048]{1,0:T(8,128)(2,1)}, bf16[4,16,6144]{2,1,0:T(8,128)(2,1)}) custom-call(s32[2]{0:T(128)S(1)} %copy-done.9, bf16[512,2048]{1,0:T(8,128)(2,1)} %bitcast.136, bf16[512,2048]{1,0:T(8,128)(2,1)} %get-tuple-element.162.refs_2_.refs_3_, bf16[512,2048]{1,0:T(8,128)(2,1)} %get-tuple-element.163.refs_3_.refs_4_, ...), custom_call_target="tpu_custom_call" | custom-call | flops 19327352832 | bytes 83886080 | tf_op jit(solution)/shard_map/backward_rest/pallas_call | solution.py:888
  693.8 14.3 %attention_backward.3 = (bf16[256,2048]{1,0:T(8,128)(2,1)}, bf16[256,256]{1,0:T(8,128)(2,1)S(1)}, bf16[256,256]{1,0:T(8,128)(2,1)S(1)}, bf16[256,256]{1,0:T(8,128)(2,1)S(1)}, bf16[256,256]{1,0:T(8,128)(2,1)S(1)}) custom-call(s32[2]{0:T(128)S(1)} %copy-done.9, bf16[512,2048]{1,0:T(8,128)(2,1)} %get-tuple-element.161.q_ref, ...), custom_call_target="tpu_custom_call" | custom-call | flops 10737418240 | bytes 5242880 | tf_op jit(solution)/shard_map/attention_backward/pallas_call | solution.py:166
  713.1 6.8 query_leaving.3
  720.0 12.2 %collective-permute-done.20.refs_2_ = bf16[256,256]{1,0:T(8,128)(2,1)S(1)} collective-permute-done((bf16[256,256]{1,0:T(8,128)(2,1)S(1)}, bf16[256,256]{1,0:T(8,128)(2,1)S(1)}, u32[]{:S(2)}, u32[]{:S(2)}) %collective-permute-start.20) | collective-permute-done | bytes 131104 | tf_op jit(solution)/shard_map/ppermute | solution.py:1102
  732.2 6.4 leaving.3
  739.9 21.8 %collective-permute-done.22.refs_2_ = bf16[256,2048]{1,0:T(8,128)(2,1)} collective-permute-done((bf16[256,2048]{1,0:T(8,128)(2,1)}, bf16[256,2048]{1,0:T(8,128)(2,1)}, u32[]{:S(2)}, u32[]{:S(2)}) %collective-permute-start.22) | collective-permute-done | bytes 1048608 | tf_op jit(solution)/shard_map/ppermute | solution.py:1195
  761.8 41.8 %backward_rest.4 = (bf16[256,2048]{1,0:T(8,128)(2,1)}, bf16[256,2048]{1,0:T(8,128)(2,1)}, bf16[4,16,6144]{2,1,0:T(8,128)(2,1)}) custom-call(s32[2]{0:T(128)S(1)} %pad_add_fusion.1.refs_0_._, bf16[512,2048]{1,0:T(8,128)(2,1)} %bitcast.137, bf16[256,2048]{1,0:T(8,128)(2,1)} %collective-permute-done.22.refs_2_, ...), custom_call_target="tpu_custom_call" | custom-call | flops 19327352832 | bytes 83886080 | tf_op jit(solution)/shard_map/backward_rest/pallas_call | solution.py:888
  803.5 13.9 %attention_backward.4 = (bf16[256,2048]{1,0:T(8,128)(2,1)}, bf16[256,256]{1,0:T(8,128)(2,1)S(1)}, bf16[256,256]{1,0:T(8,128)(2,1)S(1)}, bf16[256,256]{1,0:T(8,128)(2,1)S(1)}, bf16[256,256]{1,0:T(8,128)(2,1)S(1)}) custom-call(s32[2]{0:T(128)S(1)} %pad_add_fusion.1.refs_0_._, bf16[512,2048]{1,0:T(8,128)(2,1)} %get-tuple-element.161.q_ref, ...), custom_call_target="tpu_custom_call" | custom-call | flops 10737418240 | bytes 5242880 | tf_op jit(solution)/shard_map/attention_backward/pallas_call | solution.py:166
  821.5 7.0 query_leaving.4
  828.5 2.7 collective-permute-done.24.refs_2_
  831.2 6.4 leaving.4
  837.6 2.3 broadcast_select_fusion
  842.3 19.7 %collective-permute-done.26.refs_2_ = bf16[256,2048]{1,0:T(8,128)(2,1)} collective-permute-done((bf16[256,2048]{1,0:T(8,128)(2,1)}, bf16[256,2048]{1,0:T(8,128)(2,1)}, u32[]{:S(2)}, u32[]{:S(2)}) %collective-permute-start.26) | collective-permute-done | bytes 1048608 | tf_op jit(solution)/shard_map/ppermute | solution.py:1195
  862.1 41.7 %backward_rest.5 = (bf16[256,2048]{1,0:T(8,128)(2,1)}, bf16[256,2048]{1,0:T(8,128)(2,1)}, bf16[4,16,6144]{2,1,0:T(8,128)(2,1)}) custom-call(s32[2]{0:T(128)S(1)} %pad_add_fusion.2.refs_0_._, bf16[512,2048]{1,0:T(8,128)(2,1)} %bitcast.138, bf16[256,2048]{1,0:T(8,128)(2,1)} %collective-permute-done.26.refs_2_, ...), custom_call_target="tpu_custom_call" | custom-call | flops 19327352832 | bytes 83886080 | tf_op jit(solution)/shard_map/backward_rest/pallas_call | solution.py:888
  904.0 1.9 collective-permute-start.28
  907.0 14.1 %attention_backward.5 = (bf16[256,2048]{1,0:T(8,128)(2,1)}, bf16[256,256]{1,0:T(8,128)(2,1)S(1)}, bf16[256,256]{1,0:T(8,128)(2,1)S(1)}, bf16[256,256]{1,0:T(8,128)(2,1)S(1)}, bf16[256,256]{1,0:T(8,128)(2,1)S(1)}) custom-call(s32[2]{0:T(128)S(1)} %pad_add_fusion.2.refs_0_._, bf16[512,2048]{1,0:T(8,128)(2,1)} %get-tuple-element.161.q_ref, ...), custom_call_target="tpu_custom_call" | custom-call | flops 10737418240 | bytes 5242880 | tf_op jit(solution)/shard_map/attention_backward/pallas_call | solution.py:166
  923.6 6.7 query_leaving.5
  934.7 5.6 collective-permute-done.31.refs_2_
  940.3 4.7 collective-permute-done.32.refs_3_
  945.0 6.5 leaving.5
  951.6 3.8 collective-permute-start.38
  957.3 3.1 collective-permute-done.37
  961.1 2.4 collective-permute-start.40
  963.6 3.1 maximum_bitcast_fusion
  966.9 2.7 place.1
  (202 shorter events, 55.8 us)
Async XLA Ops:
  7.2 293.9 %all-gather.7.cloned.1.call-start = ((), (), s32[]{:S(2)}) async-start(), calls=%async_computation.5 | async-start | bytes 55705600 | tf_op jit(solution)/shard_map/all_gather | solution.py:1045
  11.2 472.1 %all-gather.5.cloned.1.call-start = ((), (), s32[]{:S(2)}) async-start(), calls=%async_computation.2 | async-start | bytes 35651584 | tf_op jit(solution)/shard_map/all_gather | solution.py:1045
  14.5 1.9 copy-start.18
  14.5 23.7 %copy-start.16 = (bf16[1,2,2048]{2,1,0:T(2,128)(2,1)S(1)}, bf16[1,2,2048]{2,1,0:T(2,128)(2,1)}, u32[]{:S(2)}) copy-start(bf16[1,2,2048]{2,1,0:T(2,128)(2,1)} %param.22) | copy-start | bytes 24580
  14.5 23.7 %copy-start.17 = (bf16[1,2,2048]{2,1,0:T(2,128)(2,1)S(1)}, bf16[1,2,2048]{2,1,0:T(2,128)(2,1)}, u32[]{:S(2)}) copy-start(bf16[1,2,2048]{2,1,0:T(2,128)(2,1)} %param.23) | copy-start | bytes 24580
  14.5 25.2 %copy-start.19 = (s32[2,1,5]{2,1,0:T(1,128)S(1)}, s32[2,1,5]{2,1,0:T(1,128)}, u32[]{:S(2)}) copy-start(s32[2,1,5]{2,1,0:T(1,128)} %param.37) | copy-start | bytes 124
  14.5 25.4 %copy-start.20 = (s32[2,1,5]{2,1,0:T(1,128)S(1)}, s32[2,1,5]{2,1,0:T(1,128)}, u32[]{:S(2)}) copy-start(s32[2,1,5]{2,1,0:T(1,128)} %param.36) | copy-start | bytes 124
  14.5 889.4 %reduce-scatter.3.cloned.1.call-start = ((), (), s32[]{:S(2)}) async-start(), calls=%async_computation.3 | async-start | bytes 1167360 | tf_op jit(solution)/shard_map/reduce_scatter | solution.py:1144
  32.3 24.9 %collective-permute-start.1 = (bf16[32,7232]{1,0:T(8,128)(2,1)S(1)}, bf16[32,7232]{1,0:T(8,128)(2,1)S(1)}, u32[]{:S(2)}, u32[]{:S(2)}) collective-permute-start(bf16[32,7232]{1,0:T(8,128)(2,1)S(1)} %concatenate.79), channel_id=1, source_target_pairs={{4,0},{8,4},{12,8},{5,1},{9,5},{13,9},{6,2},{10,6},{14,10},{7,3},{... | collective-permute-start | bytes 1388552 | tf_op jit(solution)/shard_map/ppermute | solution.py:1075
  33.6 25.0 %collective-permute-start = (bf16[32,7232]{1,0:T(8,128)(2,1)S(1)}, bf16[32,7232]{1,0:T(8,128)(2,1)S(1)}, u32[]{:S(2)}, u32[]{:S(2)}) collective-permute-start(bf16[32,7232]{1,0:T(8,128)(2,1)S(1)} %concatenate.79), channel_id=1, source_target_pairs={{0,4},{4,8},{8,12},{1,5},{5,9},{9,13},{2,6},{6,10},{10,14},{3,7},{... | collective-permute-start | bytes 1388552 | tf_op jit(solution)/shard_map/ppermute | solution.py:1074
  38.3 379.9 %collective-permute-start.9 = (f32[2,2048]{1,0:T(2,128)S(1)}, f32[2,2048]{1,0:T(2,128)S(1)}, u32[]{:S(2)}, u32[]{:S(2)}) collective-permute-start(f32[2,2048]{1,0:T(2,128)S(1)} %pad_maximum_fusion.18.norm_ref.refs_8_), channel_id=1, source_target_pairs={{16,0},{17,1},{18,2},{19,3},{20,4},{21,5},{22,6},{23,7},{24,8},{25... | collective-permute-start | bytes 49160 | tf_op jit(solution)/shard_map/ppermute | solution.py:1120
  57.2 24.7 %collective-permute-start.2 = (bf16[32,7232]{1,0:T(8,128)(2,1)S(1)}, bf16[32,7232]{1,0:T(8,128)(2,1)S(1)}, u32[]{:S(2)}, u32[]{:S(2)}) collective-permute-start(bf16[32,7232]{1,0:T(8,128)(2,1)S(1)} %collective-permute-done.1), channel_id=1, source_target_pairs={{4,0},{8,4},{12,8},{5,1},{9,5},{13,9},{6,2},{10,6},{14,10},{7,3},{... | collective-permute-start | bytes 1388552 | tf_op jit(solution)/shard_map/ppermute | solution.py:1075
  58.5 24.7 %collective-permute-start.4 = (bf16[32,7232]{1,0:T(8,128)(2,1)S(1)}, bf16[32,7232]{1,0:T(8,128)(2,1)S(1)}, u32[]{:S(2)}, u32[]{:S(2)}) collective-permute-start(bf16[32,7232]{1,0:T(8,128)(2,1)S(1)} %collective-permute-done), channel_id=1, source_target_pairs={{0,4},{4,8},{8,12},{1,5},{5,9},{9,13},{2,6},{6,10},{10,14},{3,7},{... | collective-permute-start | bytes 1388552 | tf_op jit(solution)/shard_map/ppermute | solution.py:1074
  81.8 24.4 %collective-permute-start.3 = (bf16[32,7232]{1,0:T(8,128)(2,1)S(1)}, bf16[32,7232]{1,0:T(8,128)(2,1)S(1)}, u32[]{:S(2)}, u32[]{:S(2)}) collective-permute-start(bf16[32,7232]{1,0:T(8,128)(2,1)S(1)} %collective-permute-done.2), channel_id=1, source_target_pairs={{4,0},{8,4},{12,8},{5,1},{9,5},{13,9},{6,2},{10,6},{14,10},{7,3},{... | collective-permute-start | bytes 1388552 | tf_op jit(solution)/shard_map/ppermute | solution.py:1075
  83.2 24.4 %collective-permute-start.5 = (bf16[32,7232]{1,0:T(8,128)(2,1)S(1)}, bf16[32,7232]{1,0:T(8,128)(2,1)S(1)}, u32[]{:S(2)}, u32[]{:S(2)}) collective-permute-start(bf16[32,7232]{1,0:T(8,128)(2,1)S(1)} %collective-permute-done.4), channel_id=1, source_target_pairs={{0,4},{4,8},{8,12},{1,5},{5,9},{9,13},{2,6},{6,10},{10,14},{3,7},{... | collective-permute-start | bytes 1388552 | tf_op jit(solution)/shard_map/ppermute | solution.py:1074
  108.7 309.5 %collective-permute-start.10 = (bf16[32,2048]{1,0:T(8,128)(2,1)S(1)}, bf16[32,2048]{1,0:T(8,128)(2,1)S(1)}, u32[]{:S(2)}, u32[]{:S(2)}) collective-permute-start(bf16[32,2048]{1,0:T(8,128)(2,1)S(1)} %pad_maximum_fusion.7.dn_ref.refs_9_), channel_id=1, source_target_pairs={{16,0},{17,1},{18,2},{19,3},{20,4},{21,5},{22,6},{23,7},{24,8},{25... | collective-permute-start | bytes 393224 | tf_op jit(solution)/shard_map/ppermute | solution.py:1120
  320.8 21.5 %collective-permute-start.8 = (bf16[512,256]{1,0:T(8,128)(2,1)S(1)}, bf16[512,256]{1,0:T(8,128)(2,1)S(1)}, u32[]{:S(2)}, u32[]{:S(2)}) collective-permute-start(bf16[512,256]{1,0:T(8,128)(2,1)S(1)} %constant_dynamic-update-slice_fusion.refs_0_), channel_id=1, source_target_pairs={{0,12},{1,13},{2,14},{3,15},{16,28},{17,29},{18,30},{19,31}} | collective-permute-start | bytes 786440 | tf_op jit(solution)/shard_map/ppermute | solution.py:1099
  324.8 23.5 %collective-permute-start.7 = (bf16[512,256]{1,0:T(8,128)(2,1)S(1)}, bf16[512,256]{1,0:T(8,128)(2,1)S(1)}, u32[]{:S(2)}, u32[]{:S(2)}) collective-permute-start(bf16[512,256]{1,0:T(8,128)(2,1)S(1)} %constant_dynamic-update-slice_fusion.refs_0_), channel_id=1, source_target_pairs={{0,8},{4,12},{1,9},{5,13},{2,10},{6,14},{3,11},{7,15},{16,24},{20,... | collective-permute-start | bytes 786440 | tf_op jit(solution)/shard_map/ppermute | solution.py:1099
  326.1 33.2 %collective-permute-start.6 = (bf16[512,256]{1,0:T(8,128)(2,1)S(1)}, bf16[512,256]{1,0:T(8,128)(2,1)S(1)}, u32[]{:S(2)}, u32[]{:S(2)}) collective-permute-start(bf16[512,256]{1,0:T(8,128)(2,1)S(1)} %constant_dynamic-update-slice_fusion.refs_0_), channel_id=1, source_target_pairs={{0,4},{4,8},{8,12},{1,5},{5,9},{9,13},{2,6},{6,10},{10,14},{3,7},{... | collective-permute-start | bytes 786440 | tf_op jit(solution)/shard_map/ppermute | solution.py:1099
  334.2 1.7 copy-start.4
  342.4 75.8 %collective-permute-start.11 = (bf16[32,256]{1,0:T(8,128)(2,1)S(1)}, bf16[32,256]{1,0:T(8,128)(2,1)S(1)}, u32[]{:S(2)}, u32[]{:S(2)}) collective-permute-start(bf16[32,256]{1,0:T(8,128)(2,1)S(1)} %slice.239), channel_id=1, source_target_pairs={{16,0},{17,1},{18,2},{19,3},{20,4},{21,5},{22,6},{23,7},{24,8},{25... | collective-permute-start | bytes 49160 | tf_op jit(solution)/shard_map/ppermute | solution.py:1120
  348.2 70.0 %collective-permute-start.12 = (bf16[2048,256]{1,0:T(8,128)(2,1)S(1)}, bf16[2048,256]{1,0:T(8,128)(2,1)}, u32[]{:S(2)}, u32[]{:S(2)}) collective-permute-start(bf16[2048,256]{1,0:T(8,128)(2,1)S(1)} %slice.240), channel_id=1, source_target_pairs={{16,0},{17,1},{18,2},{19,3},{20,4},{21,5},{22,6},{23,7},{24,8},{25... | collective-permute-start | bytes 3145736 | tf_op jit(solution)/shard_map/ppermute | solution.py:1120
  513.8 9.2 collective-permute-start.13
  523.0 32.5 %collective-permute-start.15 = (bf16[256,2048]{1,0:T(8,128)(2,1)}, bf16[256,2048]{1,0:T(8,128)(2,1)}, u32[]{:S(2)}, u32[]{:S(2)}) collective-permute-start(bf16[256,2048]{1,0:T(8,128)(2,1)} %get-tuple-element.143), channel_id=1, source_target_pairs={{0,16},{1,17},{2,18},{3,19},{4,20},{5,21},{6,22},{7,23},{8,24},{9,... | collective-permute-start | bytes 3145736 | tf_op jit(solution)/shard_map/ppermute | solution.py:1128
  529.6 42.0 %collective-permute-start.14 = (bf16[256,2048]{1,0:T(8,128)(2,1)S(1)}, bf16[256,2048]{1,0:T(8,128)(2,1)S(1)}, u32[]{:S(2)}, u32[]{:S(2)}) collective-permute-start(bf16[256,2048]{1,0:T(8,128)(2,1)S(1)} %copy-done.22), channel_id=1, source_target_pairs={{0,16},{1,17},{2,18},{3,19},{4,20},{5,21},{6,22},{7,23},{8,24},{9,... | collective-permute-start | bytes 3145736 | tf_op jit(solution)/shard_map/ppermute | solution.py:1128
  531.0 16.6 %collective-permute-start.18 = (bf16[512,256]{1,0:T(8,128)(2,1)S(1)}, bf16[512,256]{1,0:T(8,128)(2,1)S(1)}, u32[]{:S(2)}, u32[]{:S(2)}) collective-permute-start(bf16[512,256]{1,0:T(8,128)(2,1)S(1)} %broadcast_select_fusion.2.refs_0_), channel_id=1, source_target_pairs={{0,12},{1,13},{2,14},{3,15},{16,28},{17,29},{18,30},{19,31}} | collective-permute-start | bytes 786440 | tf_op jit(solution)/shard_map/ppermute | solution.py:1099
  539.4 12.1 %collective-permute-start.17 = (bf16[512,256]{1,0:T(8,128)(2,1)S(1)}, bf16[512,256]{1,0:T(8,128)(2,1)S(1)}, u32[]{:S(2)}, u32[]{:S(2)}) collective-permute-start(bf16[512,256]{1,0:T(8,128)(2,1)S(1)} %broadcast_select_fusion.2.refs_0_), channel_id=1, source_target_pairs={{0,8},{4,12},{1,9},{5,13},{2,10},{6,14},{3,11},{7,15},{16,24},{20,... | collective-permute-start | bytes 786440 | tf_op jit(solution)/shard_map/ppermute | solution.py:1099
  544.7 10.8 %collective-permute-start.16 = (bf16[512,256]{1,0:T(8,128)(2,1)S(1)}, bf16[512,256]{1,0:T(8,128)(2,1)S(1)}, u32[]{:S(2)}, u32[]{:S(2)}) collective-permute-start(bf16[512,256]{1,0:T(8,128)(2,1)S(1)} %broadcast_select_fusion.2.refs_0_), channel_id=1, source_target_pairs={{0,4},{4,8},{8,12},{1,5},{5,9},{9,13},{2,6},{6,10},{10,14},{3,7},{... | collective-permute-start | bytes 786440 | tf_op jit(solution)/shard_map/ppermute | solution.py:1099
  555.5 138.2 %copy-start.10 = (bf16[512,256]{1,0:T(8,128)(2,1)}, bf16[512,256]{1,0:T(8,128)(2,1)S(1)}, u32[]{:S(2)}) copy-start(bf16[512,256]{1,0:T(8,128)(2,1)S(1)} %collective-permute-done.16.refs_1_) | copy-start | bytes 786436
  586.3 66.1 %copy-start.9 = (s32[2]{0:T(128)S(1)}, s32[2]{0:T(128)}, u32[]{:S(2)}) copy-start(s32[2]{0:T(128)} %constant.143.clone.refs_0_._) | copy-start | bytes 28
  708.0 11.9 %collective-permute-start.19 = (bf16[256,256]{1,0:T(8,128)(2,1)S(1)}, bf16[256,256]{1,0:T(8,128)(2,1)S(1)}, u32[]{:S(2)}, u32[]{:S(2)}) collective-permute-start(bf16[256,256]{1,0:T(8,128)(2,1)S(1)} %get-tuple-element.175), channel_id=1, source_target_pairs={{4,0},{8,4},{12,8},{5,1},{9,5},{13,9},{6,2},{10,6},{14,10},{7,3},{... | collective-permute-start | bytes 393224 | tf_op jit(solution)/shard_map/ppermute | solution.py:1102
  709.3 22.8 %collective-permute-start.20 = (bf16[256,256]{1,0:T(8,128)(2,1)S(1)}, bf16[256,256]{1,0:T(8,128)(2,1)S(1)}, u32[]{:S(2)}, u32[]{:S(2)}) collective-permute-start(bf16[256,256]{1,0:T(8,128)(2,1)S(1)} %get-tuple-element.176), channel_id=1, source_target_pairs={{8,0},{12,4},{9,1},{13,5},{10,2},{14,6},{11,3},{15,7},{24,16},{28,... | collective-permute-start | bytes 393224 | tf_op jit(solution)/shard_map/ppermute | solution.py:1102
  710.6 21.5 %collective-permute-start.21 = (bf16[256,256]{1,0:T(8,128)(2,1)S(1)}, bf16[256,256]{1,0:T(8,128)(2,1)S(1)}, u32[]{:S(2)}, u32[]{:S(2)}) collective-permute-start(bf16[256,256]{1,0:T(8,128)(2,1)S(1)} %get-tuple-element.177), channel_id=1, source_target_pairs={{12,0},{13,1},{14,2},{15,3},{28,16},{29,17},{30,18},{31,19}} | collective-permute-start | bytes 393224 | tf_op jit(solution)/shard_map/ppermute | solution.py:1102
  711.9 1.2 copy-start.2
  738.6 23.2 %collective-permute-start.22 = (bf16[256,2048]{1,0:T(8,128)(2,1)}, bf16[256,2048]{1,0:T(8,128)(2,1)}, u32[]{:S(2)}, u32[]{:S(2)}) collective-permute-start(bf16[256,2048]{1,0:T(8,128)(2,1)} %get-tuple-element.181), channel_id=1, source_target_pairs={{16,0},{17,1},{18,2},{19,3},{20,4},{21,5},{22,6},{23,7},{24,8},{25... | collective-permute-start | bytes 3145736 | tf_op jit(solution)/shard_map/ppermute | solution.py:1195
  739.9 63.6 %copy-start.11 = (bf16[512,256]{1,0:T(8,128)(2,1)S(1)}, bf16[512,256]{1,0:T(8,128)(2,1)}, u32[]{:S(2)}) copy-start(bf16[512,256]{1,0:T(8,128)(2,1)} %copy-done.10) | copy-start | bytes 786436
  803.5 17.9 %copy-start.14 = (bf16[4,16,6144]{2,1,0:T(8,128)(2,1)S(1)}, bf16[4,16,6144]{2,1,0:T(8,128)(2,1)}, u32[]{:S(2)}) copy-start(bf16[4,16,6144]{2,1,0:T(8,128)(2,1)} %get-tuple-element.192) | copy-start | bytes 2359300
  803.5 17.9 %copy-start.15 = (bf16[4,16,6144]{2,1,0:T(8,128)(2,1)S(1)}, bf16[4,16,6144]{2,1,0:T(8,128)(2,1)}, u32[]{:S(2)}) copy-start(bf16[4,16,6144]{2,1,0:T(8,128)(2,1)} %get-tuple-element.193) | copy-start | bytes 2359300
  817.4 4.1 copy-start.1
  817.4 11.1 %collective-permute-start.23 = (bf16[256,256]{1,0:T(8,128)(2,1)S(1)}, bf16[256,256]{1,0:T(8,128)(2,1)S(1)}, u32[]{:S(2)}, u32[]{:S(2)}) collective-permute-start(bf16[256,256]{1,0:T(8,128)(2,1)S(1)} %get-tuple-element.187), channel_id=1, source_target_pairs={{4,0},{8,4},{12,8},{5,1},{9,5},{13,9},{6,2},{10,6},{14,10},{7,3},{... | collective-permute-start | bytes 393224 | tf_op jit(solution)/shard_map/ppermute | solution.py:1102
  818.8 12.4 %collective-permute-start.24 = (bf16[256,256]{1,0:T(8,128)(2,1)S(1)}, bf16[256,256]{1,0:T(8,128)(2,1)S(1)}, u32[]{:S(2)}, u32[]{:S(2)}) collective-permute-start(bf16[256,256]{1,0:T(8,128)(2,1)S(1)} %get-tuple-element.188), channel_id=1, source_target_pairs={{8,0},{12,4},{9,1},{13,5},{10,2},{14,6},{11,3},{15,7},{24,16},{28,... | collective-permute-start | bytes 393224 | tf_op jit(solution)/shard_map/ppermute | solution.py:1102
  820.1 11.1 %collective-permute-start.25 = (bf16[256,256]{1,0:T(8,128)(2,1)S(1)}, bf16[256,256]{1,0:T(8,128)(2,1)S(1)}, u32[]{:S(2)}, u32[]{:S(2)}) collective-permute-start(bf16[256,256]{1,0:T(8,128)(2,1)S(1)} %get-tuple-element.189), channel_id=1, source_target_pairs={{12,0},{13,1},{14,2},{15,3},{28,16},{29,17},{30,18},{31,19}} | collective-permute-start | bytes 393224 | tf_op jit(solution)/shard_map/ppermute | solution.py:1102
  831.2 6.4 copy-start.13
  839.9 22.1 %collective-permute-start.26 = (bf16[256,2048]{1,0:T(8,128)(2,1)}, bf16[256,2048]{1,0:T(8,128)(2,1)}, u32[]{:S(2)}, u32[]{:S(2)}) collective-permute-start(bf16[256,2048]{1,0:T(8,128)(2,1)} %get-tuple-element.191), channel_id=1, source_target_pairs={{16,0},{17,1},{18,2},{19,3},{20,4},{21,5},{22,6},{23,7},{24,8},{25... | collective-permute-start | bytes 3145736 | tf_op jit(solution)/shard_map/ppermute | solution.py:1195
  862.0 68.3 %reduce-scatter.5.cloned.1.call-start = ((), (), s32[]{:S(2)}) async-start(), calls=%async_computation.4 | async-start | bytes 983040 | tf_op jit(solution)/shard_map/reduce_scatter | solution.py:1144
  903.9 18.5 %collective-permute-start.29 = (bf16[16,7232]{1,0:T(8,128)(2,1)}, bf16[16,7232]{1,0:T(8,128)(2,1)S(1)}, u32[]{:S(2)}, u32[]{:S(2)}) collective-permute-start(bf16[16,7232]{1,0:T(8,128)(2,1)} %bitcast.112), channel_id=1, source_target_pairs={{0,3},{1,0},{2,1},{3,2},{4,7},{5,4},{6,5},{7,6},{8,11},{9,8},{10,9... | collective-permute-start | bytes 694280 | tf_op jit(solution)/shard_map/ppermute | solution.py:1021
  904.0 18.4 %collective-permute-start.28 = (bf16[16,7232]{1,0:T(8,128)(2,1)}, bf16[16,7232]{1,0:T(8,128)(2,1)S(1)}, u32[]{:S(2)}, u32[]{:S(2)}) collective-permute-start(bf16[16,7232]{1,0:T(8,128)(2,1)} %bitcast.113), channel_id=1, source_target_pairs={{0,2},{1,3},{2,0},{3,1},{4,6},{5,7},{6,4},{7,5},{8,10},{9,11},{10,... | collective-permute-start | bytes 694280 | tf_op jit(solution)/shard_map/ppermute | solution.py:1021
  905.8 16.5 %collective-permute-start.27 = (bf16[16,7232]{1,0:T(8,128)(2,1)}, bf16[16,7232]{1,0:T(8,128)(2,1)S(1)}, u32[]{:S(2)}, u32[]{:S(2)}) collective-permute-start(bf16[16,7232]{1,0:T(8,128)(2,1)} %bitcast.114), channel_id=1, source_target_pairs={{0,1},{1,2},{2,3},{3,0},{4,5},{5,6},{6,7},{7,4},{8,9},{9,10},{10,1... | collective-permute-start | bytes 694280 | tf_op jit(solution)/shard_map/ppermute | solution.py:1021
  921.1 12.4 %collective-permute-start.30 = (bf16[256,256]{1,0:T(8,128)(2,1)S(1)}, bf16[256,256]{1,0:T(8,128)(2,1)S(1)}, u32[]{:S(2)}, u32[]{:S(2)}) collective-permute-start(bf16[256,256]{1,0:T(8,128)(2,1)S(1)} %get-tuple-element.209), channel_id=1, source_target_pairs={{4,0},{8,4},{12,8},{5,1},{9,5},{13,9},{6,2},{10,6},{14,10},{7,3},{... | collective-permute-start | bytes 393224 | tf_op jit(solution)/shard_map/ppermute | solution.py:1102
  922.4 1.2 copy-start
  930.3 21.1 %collective-permute-start.35 = (bf16[16,6144]{1,0:T(8,128)(2,1)}, bf16[16,6144]{1,0:T(8,128)(2,1)S(1)}, u32[]{:S(2)}, u32[]{:S(2)}) collective-permute-start(bf16[16,6144]{1,0:T(8,128)(2,1)} %bitcast.116), channel_id=1, source_target_pairs={{0,3},{1,0},{2,1},{3,2},{4,7},{5,4},{6,5},{7,6},{8,11},{9,8},{10,9... | collective-permute-start | bytes 589832 | tf_op jit(solution)/shard_map/ppermute | solution.py:1021
  931.9 19.6 %collective-permute-start.34 = (bf16[16,6144]{1,0:T(8,128)(2,1)}, bf16[16,6144]{1,0:T(8,128)(2,1)S(1)}, u32[]{:S(2)}, u32[]{:S(2)}) collective-permute-start(bf16[16,6144]{1,0:T(8,128)(2,1)} %bitcast.117), channel_id=1, source_target_pairs={{0,2},{1,3},{2,0},{3,1},{4,6},{5,7},{6,4},{7,5},{8,10},{9,11},{10,... | collective-permute-start | bytes 589832 | tf_op jit(solution)/shard_map/ppermute | solution.py:1021
  932.1 19.4 %collective-permute-start.33 = (bf16[16,6144]{1,0:T(8,128)(2,1)}, bf16[16,6144]{1,0:T(8,128)(2,1)S(1)}, u32[]{:S(2)}, u32[]{:S(2)}) collective-permute-start(bf16[16,6144]{1,0:T(8,128)(2,1)} %bitcast.118), channel_id=1, source_target_pairs={{0,1},{1,2},{2,3},{3,0},{4,5},{5,6},{6,7},{7,4},{8,9},{9,10},{10,1... | collective-permute-start | bytes 589832 | tf_op jit(solution)/shard_map/ppermute | solution.py:1021
  932.1 8.2 collective-permute-start.31
  933.4 11.6 %collective-permute-start.32 = (bf16[256,256]{1,0:T(8,128)(2,1)S(1)}, bf16[256,256]{1,0:T(8,128)(2,1)S(1)}, u32[]{:S(2)}, u32[]{:S(2)}) collective-permute-start(bf16[256,256]{1,0:T(8,128)(2,1)S(1)} %get-tuple-element.211), channel_id=1, source_target_pairs={{12,0},{13,1},{14,2},{15,3},{28,16},{29,17},{30,18},{31,19}} | collective-permute-start | bytes 393224 | tf_op jit(solution)/shard_map/ppermute | solution.py:1102
  945.0 10.4 %copy-start.21 = (s32[8]{0:T(128)S(1)}, s32[8]{0:T(128)}, u32[]{:S(2)}) copy-start(s32[8]{0:T(128)} %all-reduce) | copy-start | bytes 100
  951.5 5.8 collective-permute-start.36
  951.6 5.7 collective-permute-start.38
  955.4 5.1 collective-permute-start.37
  960.5 6.2 collective-permute-start.41
  961.1 5.7 collective-permute-start.40
  963.5 3.4 collective-permute-start.39
  963.6 3.2 copy-start.7
  963.6 3.2 copy-start.8
  (7 other events, 6.7 us)
Sparse Core Ops, SparseCore 0:
  11.3 289.6 all-gather.6
  302.6 180.6 all-gather.4
  862.1 26.6 reduce-scatter.2
  904.0 24.6 reduce-scatter.4

commit v5 on v4

--- a/solution.py
+++ b/solution.py
@@ -21,7 +21,7 @@
 LOG2E = math.log2(math.e)
 LN2 = math.log(2.0)
 GELU_C = math.sqrt(2.0 / math.pi)
-VMEM_LIMIT = 52 * 1024 * 1024
+VMEM_LIMIT = 53 * 1024 * 1024
 SLICE = 512
 
 NN = (((1,), (0,)), ((), ()))

time: 987 us -> 991 us (level)
  no operation moved by 1% of the time
where the time goes in v5:
time: 991 us; the launch traced here: 980 us
  Pallas kernels  433 us (44%)
  waiting for transfers between devices  410 us (41%)
  starting transfers between devices  79.5 us (8%)
  between operations  19.8 us (2%)
  local copies, waits for them, and re-layouts  16.3 us (2%)
  other arithmetic  10.9 us (1%)
    all_gather x2, waiting for transfers between devices, gathered(): return lax.all_gather(own[None], ('fsdp', 'replica'), axis=1, tiled=True)[0]  256 us
    pallas_call x3, Pallas kernels, backward_rest(): pl.pallas_call(functools.partial(backward_kernel, given, first), grid_spe...  125 us
    pallas_call x1, Pallas kernels, forward_rest(): pl.pallas_call(functools.partial(forward_kernel, trees, shards), grid=(sh...  66 us
    ppermute x3, waiting for transfers between devices, local(): lax.ppermute(downs[-1], 'fsdp', [(i + 1, i) for i in range(shards - 1)])  49.4 us
    pallas_call x3, Pallas kernels, attention_backward(): pl.pallas_call(functools.partial(attention_backward_kernel, blocks, heads...  42.7 us
    ppermute x2, waiting for transfers between devices, local(): arrived = lax.ppermute(dx, 'section', [(1, 0)])  41.2 us
    pallas_call x1, Pallas kernels, mlp_down(): pl.pallas_call(functools.partial(mlp_down_kernel, trees), grid=(hidden //...  31.7 us
    pallas_call x1, Pallas kernels, mlp_up(): pl.pallas_call(functools.partial(mlp_up_kernel, rows * RANK // wide), gri...  28.1 us
  transfers between devices with their start and end apart: 46, of which 24 were waited for; matrix products, arithmetic and copies ran while one was open for 3% of the time, Pallas kernels for 19%

profile of v5, /device:TPU:0, one launch (start us, length us, event | category | flops | bytes accessed | tf_op | source)
XLA Modules:
  0.0 980.4 jit_solution(18062175897656991366)
XLA Ops:
  7.2 4.0 pack.1
  11.3 3.2 constant_dynamic-slice_fusion
  16.5 6.9 all-reduce
  33.6 4.6 collective-permute-start
  41.6 1.6 fusion.3.refs_4_
  43.2 14.0 %collective-permute-done.1 = bf16[32,7232]{1,0:T(8,128)(2,1)S(1)} collective-permute-done((bf16[32,7232]{1,0:T(8,128)(2,1)S(1)}, bf16[32,7232]{1,0:T(8,128)(2,1)S(1)}, u32[]{:S(2)}, u32[]{:S(2)}) %collective-permute-start.1) | collective-permute-done | bytes 462880 | tf_op jit(solution)/shard_map/ppermute | solution.py:1075
  58.6 4.5 collective-permute-start.4
  63.3 1.6 fusion.1.refs_4_
  65.0 16.9 %collective-permute-done.2 = bf16[32,7232]{1,0:T(8,128)(2,1)S(1)} collective-permute-done((bf16[32,7232]{1,0:T(8,128)(2,1)S(1)}, bf16[32,7232]{1,0:T(8,128)(2,1)S(1)}, u32[]{:S(2)}, u32[]{:S(2)}) %collective-permute-start.2) | collective-permute-done | bytes 462880 | tf_op jit(solution)/shard_map/ppermute | solution.py:1075
  83.3 4.5 collective-permute-start.5
  87.8 18.5 %collective-permute-done.3 = bf16[32,7232]{1,0:T(8,128)(2,1)S(1)} collective-permute-done((bf16[32,7232]{1,0:T(8,128)(2,1)S(1)}, bf16[32,7232]{1,0:T(8,128)(2,1)S(1)}, u32[]{:S(2)}, u32[]{:S(2)}) %collective-permute-start.3) | collective-permute-done | bytes 462880 | tf_op jit(solution)/shard_map/ppermute | solution.py:1075
  111.7 189.3 %all-gather.7.cloned.1.call-done = bf16[8192,3200]{1,0:T(8,128)(2,1)} async-done(((bf16[512,3200]{1,0:T(8,128)(2,1)}), bf16[8192,3200]{1,0:T(8,128)(2,1)}) %all-gather.7.cloned.1.call-update) | async-done | bytes 52428816 | tf_op jit(solution)/shard_map/all_gather | solution.py:1045
  301.1 11.0 %assemble.1.w_ref.refs_11_ = bf16[2048,2304]{1,0:T(8,128)(2,1)} custom-call(bf16[4,2048,3200]{2,1,0:T(8,128)(2,1)} %bitcast.116), custom_call_target="tpu_custom_call" | custom-call | bytes 20971520 | tf_op jit(solution)/shard_map/assemble/pallas_call | solution.py:242
  312.0 3.7 entry.3
  315.7 3.7 entry.2
  319.5 3.9 collective-permute-start.8
  324.8 2.5 collective-permute-start.6
  327.2 6.3 queries.3.q_ref
  334.8 6.2 queries.2.q_ref
  342.3 4.6 collective-permute-done.7.refs_2_
  346.9 1.5 collective-permute-start.12
  348.4 9.5 collective-permute-done.6.refs_1_
  357.9 8.5 attention_forward.2
  366.4 8.5 attention_forward.3
  374.9 13.7 %mixing.1 = (f32[512,2048]{1,0:T(8,128)}, bf16[512,2048]{1,0:T(8,128)(2,1)}) custom-call(bf16[512,2048]{1,0:T(8,128)(2,1)} %get-tuple-element.131.o_ref, bf16[512,2048]{1,0:T(8,128)(2,1)} %bitcast.137, f32[2,2048]{1,0:T(2,128)S(1)} %pad_maximum_fusion.19.norm_ref.refs_2_.refs_4_.refs_5_, ...), custom_call_target="tpu_custom_call" | custom-call | flops 4294967296 | bytes 18874368 | tf_op jit(solution)/shard_map/mixing/pallas_call | solution.py:431
  388.6 28.1 %mlp_up.1.g_ref = bf16[16,512,512]{2,1,0:T(8,128)(2,1)} custom-call(bf16[512,2048]{1,0:T(8,128)(2,1)} %get-tuple-element.132.b_ref, bf16[4,2048,3200]{2,1,0:T(8,128)(2,1)} %bitcast.118, bf16[32,8192]{1,0:T(8,128)(2,1)S(1)} %pad_maximum_fusion.3.upu_ref.refs_8_.refs_11_.refs_12_, bf16[32,2048]{1,0:T(8,128)(2,1)S(1)} %pad_maximum_fusion.10.dnu_ref.refs_10_.refs_13_.refs_14_), custom_call_target="tpu_custom_call" | custom-call | flops 17179869184 | bytes 41943040 | tf_op jit(solution)/shard_map/mlp_up/pallas_call | solution.py:603
  416.7 66.6 %all-gather.5.cloned.1.call-done = bf16[1,8192,2048]{2,1,0:T(8,128)(2,1)} async-done(((bf16[1,512,2048]{2,1,0:T(8,128)(2,1)}), bf16[1,8192,2048]{2,1,0:T(8,128)(2,1)}) %all-gather.5.cloned.1.call-update) | async-done | bytes 33554448 | tf_op jit(solution)/shard_map/all_gather | solution.py:1045
  483.3 31.7 %mlp_down.1 = (bf16[256,2048]{1,0:T(8,128)(2,1)}, bf16[256,2048]{1,0:T(8,128)(2,1)}, bf16[512,256]{1,0:T(8,128)(2,1)S(1)}) custom-call(bf16[16,512,512]{2,1,0:T(8,128)(2,1)} %mlp_up.1.g_ref, f32[512,2048]{1,0:T(8,128)} %get-tuple-element.134.x2_ref, bf16[8192,2048]{1,0:T(8,128)(2,1)} %bitcast.127, ...), custom_call_target="tpu_custom_call" | custom-call | flops 17179869184 | bytes 41943040 | tf_op jit(solution)/shard_map/mlp_down/pallas_call | solution.py:656
  515.0 3.7 collective-permute-start.13
  518.7 5.5 collective-permute-done.13
  524.3 5.3 collective-permute-start.15
  530.6 1.4 collective-permute-start.14
  532.0 8.4 collective-permute-start.18
  540.4 5.4 collective-permute-start.17
  547.1 1.5 pad_maximum_fusion.refs_4_
  548.6 3.9 collective-permute-done.17.refs_2_
  552.5 4.0 collective-permute-done.16.refs_1_
  557.2 14.1 %enter.2 = (bf16[512,2048]{1,0:T(8,128)(2,1)}, f32[4,8,256]{2,1,0:T(8,128)S(1)}, bf16[512,2048]{1,0:T(8,128)(2,1)}, bf16[512,2048]{1,0:T(8,128)(2,1)}, bf16[512,...) custom-call(s32[1]{0:T(128)} %bitcast.flag_ref, bf16[512,2048]{1,0:T(8,128)(2,1)} %bitcast.138, ...), custom_call_target="tpu_custom_call" | custom-call | flops 6442450944 | bytes 17825792 | tf_op jit(solution)/shard_map/enter/pallas_call | solution.py:330
  571.3 1.6 collective-permute-done.14.arrived_ref
  573.9 13.9 %enter.3 = (bf16[512,2048]{1,0:T(8,128)(2,1)}, f32[4,8,256]{2,1,0:T(8,128)S(1)}, bf16[512,2048]{1,0:T(8,128)(2,1)}, bf16[512,2048]{1,0:T(8,128)(2,1)}, bf16[512,...) custom-call(s32[1]{0:T(128)} %bitcast.flag_ref, ...), custom_call_target="tpu_custom_call", output_to_operand_aliasing={{0}: (12, {}), {1}: (13, {}), {2}: (14, {}), {3}: (15, {}),... | custom-call | flops 6442450944 | bytes 17825792 | tf_op jit(solution)/shard_map/enter/pallas_call | solution.py:330
  587.7 66.0 %forward_rest.1 = (bf16[512,2048]{1,0:T(8,128)(2,1)}, bf16[512,2048]{1,0:T(8,128)(2,1)}, bf16[512,2048]{1,0:T(8,128)(2,1)}, bf16[16,512,512]{2,1,0:T(8,128)(2,1)...) custom-call(bf16[512,2048]{1,0:T(8,128)(2,1)} %get-tuple-element.158, ...), custom_call_target="tpu_custom_call" | custom-call | flops 38654705664 | bytes 92274688 | tf_op jit(solution)/shard_map/forward_rest/pallas_call | solution.py:745
  653.7 41.4 %backward_rest.3 = (bf16[256,2048]{1,0:T(8,128)(2,1)}, bf16[256,2048]{1,0:T(8,128)(2,1)}, bf16[4,16,6144]{2,1,0:T(8,128)(2,1)}) custom-call(s32[2]{0:T(128)S(1)} %copy-done.5, bf16[512,2048]{1,0:T(8,128)(2,1)} %bitcast.132, bf16[512,2048]{1,0:T(8,128)(2,1)} %get-tuple-element.162.refs_2_.refs_3_, bf16[512,2048]{1,0:T(8,128)(2,1)} %get-tuple-element.163.refs_3_.refs_4_, ...), custom_call_target="tpu_custom_call" | custom-call | flops 19327352832 | bytes 83886080 | tf_op jit(solution)/shard_map/backward_rest/pallas_call | solution.py:888
  695.1 14.4 %attention_backward.3 = (bf16[256,2048]{1,0:T(8,128)(2,1)}, bf16[256,256]{1,0:T(8,128)(2,1)S(1)}, bf16[256,256]{1,0:T(8,128)(2,1)S(1)}, bf16[256,256]{1,0:T(8,128)(2,1)S(1)}, bf16[256,256]{1,0:T(8,128)(2,1)S(1)}) custom-call(s32[2]{0:T(128)S(1)} %copy-done.5, bf16[512,2048]{1,0:T(8,128)(2,1)} %get-tuple-element.161.q_ref, ...), custom_call_target="tpu_custom_call" | custom-call | flops 10737418240 | bytes 5242880 | tf_op jit(solution)/shard_map/attention_backward/pallas_call | solution.py:166
  713.4 7.0 query_leaving.3
  721.5 12.2 %collective-permute-done.20.refs_2_ = bf16[256,256]{1,0:T(8,128)(2,1)S(1)} collective-permute-done((bf16[256,256]{1,0:T(8,128)(2,1)S(1)}, bf16[256,256]{1,0:T(8,128)(2,1)S(1)}, u32[]{:S(2)}, u32[]{:S(2)}) %collective-permute-start.20) | collective-permute-done | bytes 131104 | tf_op jit(solution)/shard_map/ppermute | solution.py:1102
  733.7 6.9 leaving.3
  742.0 21.7 %collective-permute-done.22.refs_2_ = bf16[256,2048]{1,0:T(8,128)(2,1)S(1)} collective-permute-done((bf16[256,2048]{1,0:T(8,128)(2,1)}, bf16[256,2048]{1,0:T(8,128)(2,1)S(1)}, u32[]{:S(2)}, u32[]{:S(2)}) %collective-permute-start.22) | collective-permute-done | bytes 1048608 | tf_op jit(solution)/shard_map/ppermute | solution.py:1195
  764.6 41.8 %backward_rest.4 = (bf16[256,2048]{1,0:T(8,128)(2,1)}, bf16[256,2048]{1,0:T(8,128)(2,1)}, bf16[4,16,6144]{2,1,0:T(8,128)(2,1)}) custom-call(s32[2]{0:T(128)S(1)} %pad_add_fusion.1.refs_0_._, bf16[512,2048]{1,0:T(8,128)(2,1)} %bitcast.133, bf16[256,2048]{1,0:T(8,128)(2,1)} %copy-done.6, bf16[512,2048]{1,0:T(8,128)(2,1)} %get-tuple-element.162.refs_2_.refs_3_, ...), custom_call_target="tpu_custom_call" | custom-call | flops 19327352832 | bytes 83886080 | tf_op jit(solution)/shard_map/backward_rest/pallas_call | solution.py:888
  806.5 14.0 %attention_backward.4 = (bf16[256,2048]{1,0:T(8,128)(2,1)}, bf16[256,256]{1,0:T(8,128)(2,1)S(1)}, bf16[256,256]{1,0:T(8,128)(2,1)S(1)}, bf16[256,256]{1,0:T(8,128)(2,1)S(1)}, bf16[256,256]{1,0:T(8,128)(2,1)S(1)}) custom-call(s32[2]{0:T(128)S(1)} %pad_add_fusion.1.refs_0_._, bf16[512,2048]{1,0:T(8,128)(2,1)} %get-tuple-element.161.q_ref, ...), custom_call_target="tpu_custom_call" | custom-call | flops 10737418240 | bytes 5242880 | tf_op jit(solution)/shard_map/attention_backward/pallas_call | solution.py:166
  820.4 1.4 collective-permute-start.23
  824.6 7.2 query_leaving.4
  833.1 6.9 leaving.4
  840.1 1.4 broadcast_select_fusion
  843.8 19.5 %collective-permute-done.26.refs_2_ = bf16[256,2048]{1,0:T(8,128)(2,1)} collective-permute-done((bf16[256,2048]{1,0:T(8,128)(2,1)}, bf16[256,2048]{1,0:T(8,128)(2,1)}, u32[]{:S(2)}, u32[]{:S(2)}) %collective-permute-start.26) | collective-permute-done | bytes 1048608 | tf_op jit(solution)/shard_map/ppermute | solution.py:1195
  863.5 41.7 %backward_rest.5 = (bf16[256,2048]{1,0:T(8,128)(2,1)}, bf16[256,2048]{1,0:T(8,128)(2,1)}, bf16[4,16,6144]{2,1,0:T(8,128)(2,1)}) custom-call(s32[2]{0:T(128)S(1)} %pad_add_fusion.2.refs_0_._, bf16[512,2048]{1,0:T(8,128)(2,1)} %bitcast.134, bf16[256,2048]{1,0:T(8,128)(2,1)} %collective-permute-done.26.refs_2_, ...), custom_call_target="tpu_custom_call" | custom-call | flops 19327352832 | bytes 83886080 | tf_op jit(solution)/shard_map/backward_rest/pallas_call | solution.py:888
  905.4 1.9 collective-permute-start.28
  907.4 14.3 %attention_backward.5 = (bf16[256,2048]{1,0:T(8,128)(2,1)}, bf16[256,256]{1,0:T(8,128)(2,1)S(1)}, bf16[256,256]{1,0:T(8,128)(2,1)S(1)}, bf16[256,256]{1,0:T(8,128)(2,1)S(1)}, bf16[256,256]{1,0:T(8,128)(2,1)S(1)}) custom-call(s32[2]{0:T(128)S(1)} %pad_add_fusion.2.refs_0_._, bf16[512,2048]{1,0:T(8,128)(2,1)} %get-tuple-element.161.q_ref, ...), custom_call_target="tpu_custom_call" | custom-call | flops 10737418240 | bytes 5242880 | tf_op jit(solution)/shard_map/attention_backward/pallas_call | solution.py:166
  923.0 7.0 query_leaving.5
  935.8 11.9 %collective-permute-done.31.refs_2_ = bf16[256,256]{1,0:T(8,128)(2,1)S(1)} collective-permute-done((bf16[256,256]{1,0:T(8,128)(2,1)S(1)}, bf16[256,256]{1,0:T(8,128)(2,1)S(1)}, u32[]{:S(2)}, u32[]{:S(2)}) %collective-permute-start.31) | collective-permute-done | bytes 131104 | tf_op jit(solution)/shard_map/ppermute | solution.py:1102
  947.7 6.9 leaving.5
  955.5 3.8 collective-permute-start.38
  961.3 2.9 collective-permute-done.37
  965.8 2.8 maximum_bitcast_fusion
  969.4 4.0 place.1
  (208 shorter events, 53.4 us)
Async XLA Ops:
  7.2 293.9 %all-gather.7.cloned.1.call-start = ((), (), s32[]{:S(2)}) async-start(), calls=%async_computation.5 | async-start | bytes 55705600 | tf_op jit(solution)/shard_map/all_gather | solution.py:1045
  11.2 472.1 %all-gather.5.cloned.1.call-start = ((), (), s32[]{:S(2)}) async-start(), calls=%async_computation.2 | async-start | bytes 35651584 | tf_op jit(solution)/shard_map/all_gather | solution.py:1045
  14.5 23.7 %copy-start.15 = (bf16[1,2,2048]{2,1,0:T(2,128)(2,1)S(1)}, bf16[1,2,2048]{2,1,0:T(2,128)(2,1)}, u32[]{:S(2)}) copy-start(bf16[1,2,2048]{2,1,0:T(2,128)(2,1)} %param.22) | copy-start | bytes 24580
  14.5 23.7 %copy-start.16 = (bf16[1,2,2048]{2,1,0:T(2,128)(2,1)S(1)}, bf16[1,2,2048]{2,1,0:T(2,128)(2,1)}, u32[]{:S(2)}) copy-start(bf16[1,2,2048]{2,1,0:T(2,128)(2,1)} %param.23) | copy-start | bytes 24580
  14.5 25.2 %copy-start.18 = (s32[2,1,5]{2,1,0:T(1,128)S(1)}, s32[2,1,5]{2,1,0:T(1,128)}, u32[]{:S(2)}) copy-start(s32[2,1,5]{2,1,0:T(1,128)} %param.37) | copy-start | bytes 124
  14.5 25.4 %copy-start.19 = (s32[2,1,5]{2,1,0:T(1,128)S(1)}, s32[2,1,5]{2,1,0:T(1,128)}, u32[]{:S(2)}) copy-start(s32[2,1,5]{2,1,0:T(1,128)} %param.36) | copy-start | bytes 124
  14.5 890.8 %reduce-scatter.3.cloned.1.call-start = ((), (), s32[]{:S(2)}) async-start(), calls=%async_computation.3 | async-start | bytes 1167360 | tf_op jit(solution)/shard_map/reduce_scatter | solution.py:1144
  32.3 24.9 %collective-permute-start.1 = (bf16[32,7232]{1,0:T(8,128)(2,1)S(1)}, bf16[32,7232]{1,0:T(8,128)(2,1)S(1)}, u32[]{:S(2)}, u32[]{:S(2)}) collective-permute-start(bf16[32,7232]{1,0:T(8,128)(2,1)S(1)} %concatenate.79), channel_id=1, source_target_pairs={{4,0},{8,4},{12,8},{5,1},{9,5},{13,9},{6,2},{10,6},{14,10},{7,3},{... | collective-permute-start | bytes 1388552 | tf_op jit(solution)/shard_map/ppermute | solution.py:1075
  33.6 25.0 %collective-permute-start = (bf16[32,7232]{1,0:T(8,128)(2,1)S(1)}, bf16[32,7232]{1,0:T(8,128)(2,1)S(1)}, u32[]{:S(2)}, u32[]{:S(2)}) collective-permute-start(bf16[32,7232]{1,0:T(8,128)(2,1)S(1)} %concatenate.79), channel_id=1, source_target_pairs={{0,4},{4,8},{8,12},{1,5},{5,9},{9,13},{2,6},{6,10},{10,14},{3,7},{... | collective-permute-start | bytes 1388552 | tf_op jit(solution)/shard_map/ppermute | solution.py:1074
  38.3 378.4 %collective-permute-start.9 = (f32[2,2048]{1,0:T(2,128)S(1)}, f32[2,2048]{1,0:T(2,128)S(1)}, u32[]{:S(2)}, u32[]{:S(2)}) collective-permute-start(f32[2,2048]{1,0:T(2,128)S(1)} %pad_maximum_fusion.18.norm_ref.refs_8_), channel_id=1, source_target_pairs={{16,0},{17,1},{18,2},{19,3},{20,4},{21,5},{22,6},{23,7},{24,8},{25... | collective-permute-start | bytes 49160 | tf_op jit(solution)/shard_map/ppermute | solution.py:1120
  57.2 24.7 %collective-permute-start.2 = (bf16[32,7232]{1,0:T(8,128)(2,1)S(1)}, bf16[32,7232]{1,0:T(8,128)(2,1)S(1)}, u32[]{:S(2)}, u32[]{:S(2)}) collective-permute-start(bf16[32,7232]{1,0:T(8,128)(2,1)S(1)} %collective-permute-done.1), channel_id=1, source_target_pairs={{4,0},{8,4},{12,8},{5,1},{9,5},{13,9},{6,2},{10,6},{14,10},{7,3},{... | collective-permute-start | bytes 1388552 | tf_op jit(solution)/shard_map/ppermute | solution.py:1075
  58.6 24.7 %collective-permute-start.4 = (bf16[32,7232]{1,0:T(8,128)(2,1)S(1)}, bf16[32,7232]{1,0:T(8,128)(2,1)S(1)}, u32[]{:S(2)}, u32[]{:S(2)}) collective-permute-start(bf16[32,7232]{1,0:T(8,128)(2,1)S(1)} %collective-permute-done), channel_id=1, source_target_pairs={{0,4},{4,8},{8,12},{1,5},{5,9},{9,13},{2,6},{6,10},{10,14},{3,7},{... | collective-permute-start | bytes 1388552 | tf_op jit(solution)/shard_map/ppermute | solution.py:1074
  81.9 24.4 %collective-permute-start.3 = (bf16[32,7232]{1,0:T(8,128)(2,1)S(1)}, bf16[32,7232]{1,0:T(8,128)(2,1)S(1)}, u32[]{:S(2)}, u32[]{:S(2)}) collective-permute-start(bf16[32,7232]{1,0:T(8,128)(2,1)S(1)} %collective-permute-done.2), channel_id=1, source_target_pairs={{4,0},{8,4},{12,8},{5,1},{9,5},{13,9},{6,2},{10,6},{14,10},{7,3},{... | collective-permute-start | bytes 1388552 | tf_op jit(solution)/shard_map/ppermute | solution.py:1075
  83.3 24.4 %collective-permute-start.5 = (bf16[32,7232]{1,0:T(8,128)(2,1)S(1)}, bf16[32,7232]{1,0:T(8,128)(2,1)S(1)}, u32[]{:S(2)}, u32[]{:S(2)}) collective-permute-start(bf16[32,7232]{1,0:T(8,128)(2,1)S(1)} %collective-permute-done.4), channel_id=1, source_target_pairs={{0,4},{4,8},{8,12},{1,5},{5,9},{9,13},{2,6},{6,10},{10,14},{3,7},{... | collective-permute-start | bytes 1388552 | tf_op jit(solution)/shard_map/ppermute | solution.py:1074
  108.8 307.9 %collective-permute-start.10 = (bf16[32,2048]{1,0:T(8,128)(2,1)S(1)}, bf16[32,2048]{1,0:T(8,128)(2,1)S(1)}, u32[]{:S(2)}, u32[]{:S(2)}) collective-permute-start(bf16[32,2048]{1,0:T(8,128)(2,1)S(1)} %pad_maximum_fusion.7.dn_ref.refs_9_), channel_id=1, source_target_pairs={{16,0},{17,1},{18,2},{19,3},{20,4},{21,5},{22,6},{23,7},{24,8},{25... | collective-permute-start | bytes 393224 | tf_op jit(solution)/shard_map/ppermute | solution.py:1120
  110.2 603.2 %copy-start = (bf16[32,2304]{1,0:T(8,128)(2,1)}, bf16[32,2304]{1,0:T(8,128)(2,1)S(1)}, u32[]{:S(2)}) copy-start(bf16[32,2304]{1,0:T(8,128)(2,1)S(1)} %concatenate.81.up_ref.refs_10_) | copy-start | bytes 442372
  111.7 276.9 %copy-start.3 = (bf16[32,8192]{1,0:T(8,128)(2,1)}, bf16[32,8192]{1,0:T(8,128)(2,1)S(1)}, u32[]{:S(2)}) copy-start(bf16[32,8192]{1,0:T(8,128)(2,1)S(1)} %pad_maximum_fusion.3.upu_ref.refs_8_.refs_11_.refs_12_) | copy-start | bytes 1572868
  319.5 21.5 %collective-permute-start.8 = (bf16[512,256]{1,0:T(8,128)(2,1)S(1)}, bf16[512,256]{1,0:T(8,128)(2,1)S(1)}, u32[]{:S(2)}, u32[]{:S(2)}) collective-permute-start(bf16[512,256]{1,0:T(8,128)(2,1)S(1)} %constant_dynamic-update-slice_fusion.refs_0_), channel_id=1, source_target_pairs={{0,12},{1,13},{2,14},{3,15},{16,28},{17,29},{18,30},{19,31}} | collective-permute-start | bytes 786440 | tf_op jit(solution)/shard_map/ppermute | solution.py:1099
  323.4 23.5 %collective-permute-start.7 = (bf16[512,256]{1,0:T(8,128)(2,1)S(1)}, bf16[512,256]{1,0:T(8,128)(2,1)S(1)}, u32[]{:S(2)}, u32[]{:S(2)}) collective-permute-start(bf16[512,256]{1,0:T(8,128)(2,1)S(1)} %constant_dynamic-update-slice_fusion.refs_0_), channel_id=1, source_target_pairs={{0,8},{4,12},{1,9},{5,13},{2,10},{6,14},{3,11},{7,15},{16,24},{20,... | collective-permute-start | bytes 786440 | tf_op jit(solution)/shard_map/ppermute | solution.py:1099
  324.8 33.2 %collective-permute-start.6 = (bf16[512,256]{1,0:T(8,128)(2,1)S(1)}, bf16[512,256]{1,0:T(8,128)(2,1)S(1)}, u32[]{:S(2)}, u32[]{:S(2)}) collective-permute-start(bf16[512,256]{1,0:T(8,128)(2,1)S(1)} %constant_dynamic-update-slice_fusion.refs_0_), channel_id=1, source_target_pairs={{0,4},{4,8},{8,12},{1,5},{5,9},{9,13},{2,6},{6,10},{10,14},{3,7},{... | collective-permute-start | bytes 786440 | tf_op jit(solution)/shard_map/ppermute | solution.py:1099
  341.0 16.9 %copy-start.26 = (bf16[512,256]{1,0:T(8,128)(2,1)}, bf16[512,256]{1,0:T(8,128)(2,1)S(1)}, u32[]{:S(2)}) copy-start(bf16[512,256]{1,0:T(8,128)(2,1)S(1)} %collective-permute-done.8.refs_3_) | copy-start | bytes 786436
  341.0 75.6 %collective-permute-start.11 = (bf16[32,256]{1,0:T(8,128)(2,1)S(1)}, bf16[32,256]{1,0:T(8,128)(2,1)S(1)}, u32[]{:S(2)}, u32[]{:S(2)}) collective-permute-start(bf16[32,256]{1,0:T(8,128)(2,1)S(1)} %slice.239), channel_id=1, source_target_pairs={{16,0},{17,1},{18,2},{19,3},{20,4},{21,5},{22,6},{23,7},{24,8},{25... | collective-permute-start | bytes 49160 | tf_op jit(solution)/shard_map/ppermute | solution.py:1120
  346.9 69.8 %collective-permute-start.12 = (bf16[2048,256]{1,0:T(8,128)(2,1)S(1)}, bf16[2048,256]{1,0:T(8,128)(2,1)}, u32[]{:S(2)}, u32[]{:S(2)}) collective-permute-start(bf16[2048,256]{1,0:T(8,128)(2,1)S(1)} %slice.240), channel_id=1, source_target_pairs={{16,0},{17,1},{18,2},{19,3},{20,4},{21,5},{22,6},{23,7},{24,8},{25... | collective-permute-start | bytes 3145736 | tf_op jit(solution)/shard_map/ppermute | solution.py:1120
  515.0 15.6 %copy-start.21 = (bf16[256,2048]{1,0:T(8,128)(2,1)S(1)}, bf16[256,2048]{1,0:T(8,128)(2,1)}, u32[]{:S(2)}) copy-start(bf16[256,2048]{1,0:T(8,128)(2,1)} %get-tuple-element.142) | copy-start | bytes 3145732
  515.0 9.3 collective-permute-start.13
  524.3 32.2 %collective-permute-start.15 = (bf16[256,2048]{1,0:T(8,128)(2,1)}, bf16[256,2048]{1,0:T(8,128)(2,1)}, u32[]{:S(2)}, u32[]{:S(2)}) collective-permute-start(bf16[256,2048]{1,0:T(8,128)(2,1)} %get-tuple-element.143), channel_id=1, source_target_pairs={{0,16},{1,17},{2,18},{3,19},{4,20},{5,21},{6,22},{7,23},{8,24},{9,... | collective-permute-start | bytes 3145736 | tf_op jit(solution)/shard_map/ppermute | solution.py:1128
  530.6 42.3 %collective-permute-start.14 = (bf16[256,2048]{1,0:T(8,128)(2,1)S(1)}, bf16[256,2048]{1,0:T(8,128)(2,1)S(1)}, u32[]{:S(2)}, u32[]{:S(2)}) collective-permute-start(bf16[256,2048]{1,0:T(8,128)(2,1)S(1)} %copy-done.21), channel_id=1, source_target_pairs={{0,16},{1,17},{2,18},{3,19},{4,20},{5,21},{6,22},{7,23},{8,24},{9,... | collective-permute-start | bytes 3145736 | tf_op jit(solution)/shard_map/ppermute | solution.py:1128
  532.0 16.6 %collective-permute-start.18 = (bf16[512,256]{1,0:T(8,128)(2,1)S(1)}, bf16[512,256]{1,0:T(8,128)(2,1)S(1)}, u32[]{:S(2)}, u32[]{:S(2)}) collective-permute-start(bf16[512,256]{1,0:T(8,128)(2,1)S(1)} %broadcast_select_fusion.2.refs_0_), channel_id=1, source_target_pairs={{0,12},{1,13},{2,14},{3,15},{16,28},{17,29},{18,30},{19,31}} | collective-permute-start | bytes 786440 | tf_op jit(solution)/shard_map/ppermute | solution.py:1099
  540.4 12.1 %collective-permute-start.17 = (bf16[512,256]{1,0:T(8,128)(2,1)S(1)}, bf16[512,256]{1,0:T(8,128)(2,1)S(1)}, u32[]{:S(2)}, u32[]{:S(2)}) collective-permute-start(bf16[512,256]{1,0:T(8,128)(2,1)S(1)} %broadcast_select_fusion.2.refs_0_), channel_id=1, source_target_pairs={{0,8},{4,12},{1,9},{5,13},{2,10},{6,14},{3,11},{7,15},{16,24},{20,... | collective-permute-start | bytes 786440 | tf_op jit(solution)/shard_map/ppermute | solution.py:1099
  545.8 10.8 %collective-permute-start.16 = (bf16[512,256]{1,0:T(8,128)(2,1)S(1)}, bf16[512,256]{1,0:T(8,128)(2,1)S(1)}, u32[]{:S(2)}, u32[]{:S(2)}) collective-permute-start(bf16[512,256]{1,0:T(8,128)(2,1)S(1)} %broadcast_select_fusion.2.refs_0_), channel_id=1, source_target_pairs={{0,4},{4,8},{8,12},{1,5},{5,9},{9,13},{2,6},{6,10},{10,14},{3,7},{... | collective-permute-start | bytes 786440 | tf_op jit(solution)/shard_map/ppermute | solution.py:1099
  548.6 7.9 copy-start.23
  587.7 66.0 %copy-start.5 = (s32[2]{0:T(128)S(1)}, s32[2]{0:T(128)}, u32[]{:S(2)}) copy-start(s32[2]{0:T(128)} %constant.143.clone.refs_0_._) | copy-start | bytes 28
  709.5 11.9 %collective-permute-start.19 = (bf16[256,256]{1,0:T(8,128)(2,1)S(1)}, bf16[256,256]{1,0:T(8,128)(2,1)S(1)}, u32[]{:S(2)}, u32[]{:S(2)}) collective-permute-start(bf16[256,256]{1,0:T(8,128)(2,1)S(1)} %get-tuple-element.175), channel_id=1, source_target_pairs={{4,0},{8,4},{12,8},{5,1},{9,5},{13,9},{6,2},{10,6},{14,10},{7,3},{... | collective-permute-start | bytes 393224 | tf_op jit(solution)/shard_map/ppermute | solution.py:1102
  710.8 22.8 %collective-permute-start.20 = (bf16[256,256]{1,0:T(8,128)(2,1)S(1)}, bf16[256,256]{1,0:T(8,128)(2,1)S(1)}, u32[]{:S(2)}, u32[]{:S(2)}) collective-permute-start(bf16[256,256]{1,0:T(8,128)(2,1)S(1)} %get-tuple-element.176), channel_id=1, source_target_pairs={{8,0},{12,4},{9,1},{13,5},{10,2},{14,6},{11,3},{15,7},{24,16},{28,... | collective-permute-start | bytes 393224 | tf_op jit(solution)/shard_map/ppermute | solution.py:1102
  712.1 21.5 %collective-permute-start.21 = (bf16[256,256]{1,0:T(8,128)(2,1)S(1)}, bf16[256,256]{1,0:T(8,128)(2,1)S(1)}, u32[]{:S(2)}, u32[]{:S(2)}) collective-permute-start(bf16[256,256]{1,0:T(8,128)(2,1)S(1)} %get-tuple-element.177), channel_id=1, source_target_pairs={{12,0},{13,1},{14,2},{15,3},{28,16},{29,17},{30,18},{31,19}} | collective-permute-start | bytes 393224 | tf_op jit(solution)/shard_map/ppermute | solution.py:1102
  740.6 23.1 %collective-permute-start.22 = (bf16[256,2048]{1,0:T(8,128)(2,1)}, bf16[256,2048]{1,0:T(8,128)(2,1)S(1)}, u32[]{:S(2)}, u32[]{:S(2)}) collective-permute-start(bf16[256,2048]{1,0:T(8,128)(2,1)} %get-tuple-element.181), channel_id=1, source_target_pairs={{16,0},{17,1},{18,2},{19,3},{20,4},{21,5},{22,6},{23,7},{24,8},{25... | collective-permute-start | bytes 3145736 | tf_op jit(solution)/shard_map/ppermute | solution.py:1195
  806.5 18.0 %copy-start.8 = (bf16[4,16,6144]{2,1,0:T(8,128)(2,1)S(1)}, bf16[4,16,6144]{2,1,0:T(8,128)(2,1)}, u32[]{:S(2)}) copy-start(bf16[4,16,6144]{2,1,0:T(8,128)(2,1)} %get-tuple-element.192) | copy-start | bytes 2359300
  806.5 18.0 %copy-start.9 = (bf16[4,16,6144]{2,1,0:T(8,128)(2,1)S(1)}, bf16[4,16,6144]{2,1,0:T(8,128)(2,1)}, u32[]{:S(2)}) copy-start(bf16[4,16,6144]{2,1,0:T(8,128)(2,1)} %get-tuple-element.193) | copy-start | bytes 2359300
  820.4 11.4 %collective-permute-start.23 = (bf16[256,256]{1,0:T(8,128)(2,1)S(1)}, bf16[256,256]{1,0:T(8,128)(2,1)S(1)}, u32[]{:S(2)}, u32[]{:S(2)}) collective-permute-start(bf16[256,256]{1,0:T(8,128)(2,1)S(1)} %get-tuple-element.187), channel_id=1, source_target_pairs={{4,0},{8,4},{12,8},{5,1},{9,5},{13,9},{6,2},{10,6},{14,10},{7,3},{... | collective-permute-start | bytes 393224 | tf_op jit(solution)/shard_map/ppermute | solution.py:1102
  821.9 9.9 %collective-permute-start.24 = (bf16[256,256]{1,0:T(8,128)(2,1)S(1)}, bf16[256,256]{1,0:T(8,128)(2,1)S(1)}, u32[]{:S(2)}, u32[]{:S(2)}) collective-permute-start(bf16[256,256]{1,0:T(8,128)(2,1)S(1)} %get-tuple-element.188), channel_id=1, source_target_pairs={{8,0},{12,4},{9,1},{13,5},{10,2},{14,6},{11,3},{15,7},{24,16},{28,... | collective-permute-start | bytes 393224 | tf_op jit(solution)/shard_map/ppermute | solution.py:1102
  823.2 9.9 %collective-permute-start.25 = (bf16[256,256]{1,0:T(8,128)(2,1)S(1)}, bf16[256,256]{1,0:T(8,128)(2,1)S(1)}, u32[]{:S(2)}, u32[]{:S(2)}) collective-permute-start(bf16[256,256]{1,0:T(8,128)(2,1)S(1)} %get-tuple-element.189), channel_id=1, source_target_pairs={{12,0},{13,1},{14,2},{15,3},{28,16},{29,17},{30,18},{31,19}} | collective-permute-start | bytes 393224 | tf_op jit(solution)/shard_map/ppermute | solution.py:1102
  833.1 6.9 copy-start.7
  841.5 21.9 %collective-permute-start.26 = (bf16[256,2048]{1,0:T(8,128)(2,1)}, bf16[256,2048]{1,0:T(8,128)(2,1)}, u32[]{:S(2)}, u32[]{:S(2)}) collective-permute-start(bf16[256,2048]{1,0:T(8,128)(2,1)} %get-tuple-element.191), channel_id=1, source_target_pairs={{16,0},{17,1},{18,2},{19,3},{20,4},{21,5},{22,6},{23,7},{24,8},{25... | collective-permute-start | bytes 3145736 | tf_op jit(solution)/shard_map/ppermute | solution.py:1195
  863.4 67.5 %reduce-scatter.5.cloned.1.call-start = ((), (), s32[]{:S(2)}) async-start(), calls=%async_computation.4 | async-start | bytes 983040 | tf_op jit(solution)/shard_map/reduce_scatter | solution.py:1144
  905.3 17.7 %copy-start.2 = (bf16[32,2304]{1,0:T(8,128)(2,1)S(1)}, bf16[32,2304]{1,0:T(8,128)(2,1)}, u32[]{:S(2)}) copy-start(bf16[32,2304]{1,0:T(8,128)(2,1)} %copy-done) | copy-start | bytes 442372
  905.3 17.6 %collective-permute-start.29 = (bf16[16,7232]{1,0:T(8,128)(2,1)}, bf16[16,7232]{1,0:T(8,128)(2,1)S(1)}, u32[]{:S(2)}, u32[]{:S(2)}) collective-permute-start(bf16[16,7232]{1,0:T(8,128)(2,1)} %bitcast.146), channel_id=1, source_target_pairs={{0,3},{1,0},{2,1},{3,2},{4,7},{5,4},{6,5},{7,6},{8,11},{9,8},{10,9... | collective-permute-start | bytes 694280 | tf_op jit(solution)/shard_map/ppermute | solution.py:1021
  905.4 17.6 %collective-permute-start.28 = (bf16[16,7232]{1,0:T(8,128)(2,1)}, bf16[16,7232]{1,0:T(8,128)(2,1)S(1)}, u32[]{:S(2)}, u32[]{:S(2)}) collective-permute-start(bf16[16,7232]{1,0:T(8,128)(2,1)} %bitcast.147), channel_id=1, source_target_pairs={{0,2},{1,3},{2,0},{3,1},{4,6},{5,7},{6,4},{7,5},{8,10},{9,11},{10,... | collective-permute-start | bytes 694280 | tf_op jit(solution)/shard_map/ppermute | solution.py:1021
  907.2 15.8 %collective-permute-start.27 = (bf16[16,7232]{1,0:T(8,128)(2,1)}, bf16[16,7232]{1,0:T(8,128)(2,1)S(1)}, u32[]{:S(2)}, u32[]{:S(2)}) collective-permute-start(bf16[16,7232]{1,0:T(8,128)(2,1)} %bitcast.148), channel_id=1, source_target_pairs={{0,1},{1,2},{2,3},{3,0},{4,5},{5,6},{6,7},{7,4},{8,9},{9,10},{10,1... | collective-permute-start | bytes 694280 | tf_op jit(solution)/shard_map/ppermute | solution.py:1021
  921.7 12.8 %collective-permute-start.30 = (bf16[256,256]{1,0:T(8,128)(2,1)S(1)}, bf16[256,256]{1,0:T(8,128)(2,1)S(1)}, u32[]{:S(2)}, u32[]{:S(2)}) collective-permute-start(bf16[256,256]{1,0:T(8,128)(2,1)S(1)} %get-tuple-element.209), channel_id=1, source_target_pairs={{4,0},{8,4},{12,8},{5,1},{9,5},{13,9},{6,2},{10,6},{14,10},{7,3},{... | collective-permute-start | bytes 393224 | tf_op jit(solution)/shard_map/ppermute | solution.py:1102
  923.0 7.1 copy-start.10
  923.0 7.1 copy-start.11
  923.0 7.1 copy-start.12
  930.9 23.7 %collective-permute-start.35 = (bf16[16,6144]{1,0:T(8,128)(2,1)}, bf16[16,6144]{1,0:T(8,128)(2,1)S(1)}, u32[]{:S(2)}, u32[]{:S(2)}) collective-permute-start(bf16[16,6144]{1,0:T(8,128)(2,1)} %bitcast.112), channel_id=1, source_target_pairs={{0,3},{1,0},{2,1},{3,2},{4,7},{5,4},{6,5},{7,6},{8,11},{9,8},{10,9... | collective-permute-start | bytes 589832 | tf_op jit(solution)/shard_map/ppermute | solution.py:1021
  931.7 22.9 %collective-permute-start.34 = (bf16[16,6144]{1,0:T(8,128)(2,1)}, bf16[16,6144]{1,0:T(8,128)(2,1)S(1)}, u32[]{:S(2)}, u32[]{:S(2)}) collective-permute-start(bf16[16,6144]{1,0:T(8,128)(2,1)} %bitcast.113), channel_id=1, source_target_pairs={{0,2},{1,3},{2,0},{3,1},{4,6},{5,7},{6,4},{7,5},{8,10},{9,11},{10,... | collective-permute-start | bytes 589832 | tf_op jit(solution)/shard_map/ppermute | solution.py:1021
  933.0 21.6 %collective-permute-start.33 = (bf16[16,6144]{1,0:T(8,128)(2,1)}, bf16[16,6144]{1,0:T(8,128)(2,1)S(1)}, u32[]{:S(2)}, u32[]{:S(2)}) collective-permute-start(bf16[16,6144]{1,0:T(8,128)(2,1)} %bitcast.114), channel_id=1, source_target_pairs={{0,1},{1,2},{2,3},{3,0},{4,5},{5,6},{6,7},{7,4},{8,9},{9,10},{10,1... | collective-permute-start | bytes 589832 | tf_op jit(solution)/shard_map/ppermute | solution.py:1021
  933.2 14.5 %collective-permute-start.31 = (bf16[256,256]{1,0:T(8,128)(2,1)S(1)}, bf16[256,256]{1,0:T(8,128)(2,1)S(1)}, u32[]{:S(2)}, u32[]{:S(2)}) collective-permute-start(bf16[256,256]{1,0:T(8,128)(2,1)S(1)} %get-tuple-element.210), channel_id=1, source_target_pairs={{8,0},{12,4},{9,1},{13,5},{10,2},{14,6},{11,3},{15,7},{24,16},{28,... | collective-permute-start | bytes 393224 | tf_op jit(solution)/shard_map/ppermute | solution.py:1102
  934.5 13.2 %collective-permute-start.32 = (bf16[256,256]{1,0:T(8,128)(2,1)S(1)}, bf16[256,256]{1,0:T(8,128)(2,1)S(1)}, u32[]{:S(2)}, u32[]{:S(2)}) collective-permute-start(bf16[256,256]{1,0:T(8,128)(2,1)S(1)} %get-tuple-element.211), channel_id=1, source_target_pairs={{12,0},{13,1},{14,2},{15,3},{28,16},{29,17},{30,18},{31,19}} | collective-permute-start | bytes 393224 | tf_op jit(solution)/shard_map/ppermute | solution.py:1102
  947.7 11.7 %copy-start.20 = (s32[8]{0:T(128)S(1)}, s32[8]{0:T(128)}, u32[]{:S(2)}) copy-start(s32[8]{0:T(128)} %all-reduce) | copy-start | bytes 100
  955.4 5.8 collective-permute-start.36
  955.5 5.8 collective-permute-start.38
  959.3 4.9 collective-permute-start.37
  965.0 3.6 collective-permute-start.41
  965.0 4.4 collective-permute-start.40
  965.7 3.8 collective-permute-start.39
  (10 other events, 22.5 us)
Sparse Core Ops, SparseCore 0:
  11.3 289.6 all-gather.6
  302.7 180.6 all-gather.4
  863.5 27.0 reduce-scatter.2
  905.4 25.4 reduce-scatter.4
